TPU v7x, 128 devices: a whole 4x4x4 slice. The times are simulated.
128 devices in a mesh: gx: 8 (over y, x_lo), gy: 16 (over z, x_hi, core).
Axes of the slice: x: 4 (x_hi: 2, x_lo: 2; x = x_hi * 2 + x_lo), y: 4, z: 4, core: 2. Of those that a mesh axis runs over, the one named last changes fastest.
Arguments:
- pressure: float32 [192, 384, 256], P('gx', 'gy'), may hold values from -6 to 6
- pressure_old: float32 [192, 384, 256], P('gx', 'gy'), may hold values from -6 to 6
- speed_term: float32 [192, 384, 256], P('gx', 'gy'), may hold values from 0.03 to 0.15
- layer_width: int32 [4], replicated, may hold values from 8 to 16
- source_x: int32 [4], replicated, may hold values from 0 to 191
- source_y: int32 [4], replicated, may hold values from 0 to 383
- source_z: int32 [4], replicated, may hold values from 0 to 255
- source_amp: float32 [8, 4], replicated, may hold values from -8 to 8
- receiver_x: int32 [64], replicated, may hold values from 0 to 191
- receiver_y: int32 [64], replicated, may hold values from 0 to 383
- receiver_z: int32 [64], replicated, may hold values from 0 to 255
Outputs:
- pressure_final: float32 [192, 384, 256], P('gx', 'gy')
- traces: float32 [64, 8], replicated
- energy: float32 [8], replicated
All inputs are finite; a program needn't handle non-finite values.
Results may differ from a plain program's by a relative error of at most 0.00026.
Values sent between devices are 32-bit elements; how exact they have to be, the bound alone decides.
No kernel may reach another device: no remote copies, remote signals or barrier semaphores. Data moves between devices by JAX's collectives and lax.ppermute only.
A program may use at most 64 MiB of HBM per device.

v0:
```python
import functools

import jax
import jax.numpy as jnp
from jax import lax
from jax.sharding import Mesh
from jax.sharding import PartitionSpec as P

STEPS = 8
GX = ("gx_0", "gx_1")
GY = ("gy_0", "gy_1", "gy_2")
GX_GY = ("gx_0", "gx_1", "gy_0", "gy_1", "gy_2")


first_coef = (0.8, -0.2, 4.0 / 105.0, -1.0 / 280.0)
second_coef = (1.6, -0.2, 8.0 / 315.0, -1.0 / 560.0)
centre_coef = -205.0 / 72.0
damping = 0.6
radius = 4


def with_halo(array, sides, width):
    edges = {}
    for axis, dim in sides:
        size, length = (lax.axis_size(axis), array.shape[dim])
        up = [(i, (i + 1) % size) for i in range(size - 1)]
        last = lax.slice_in_dim(array, length - width, length, axis=dim)
        initial = lax.slice_in_dim(array, 0, width, axis=dim)
        edges[dim] = (
            lax.ppermute(last, axis, up),
            lax.ppermute(initial, axis, [(b, a) for a, b in up]),
        )
    done = []
    for _, dim in sides:
        low, high = edges[dim]
        around = [(width, width) if d in done else (0, 0) for d in range(array.ndim)]
        array = jnp.concatenate([jnp.pad(low, around), array, jnp.pad(high, around)], axis=dim)
        done.append(dim)
    return array


def by_axis(array, axes):
    return functools.reduce(lax.psum, axes, array)


def shifted(padded, axis_id, offset, length):
    return lax.slice_in_dim(padded, radius + offset, radius + offset + length, axis=axis_id)


def first_diff(padded, axis_id, length):
    summed = first_coef[0] * (
        shifted(padded, axis_id, 1, length) - shifted(padded, axis_id, -1, length)
    )
    for shift_by in range(2, 5):
        summed = summed + first_coef[shift_by - 1] * (
            shifted(padded, axis_id, shift_by, length) - shifted(padded, axis_id, -shift_by, length)
        )
    return summed


def second_diff(padded, axis_id, length):
    summed = centre_coef * shifted(padded, axis_id, 0, length)
    for shift_by in range(1, 5):
        summed = summed + second_coef[shift_by - 1] * (
            shifted(padded, axis_id, shift_by, length) + shifted(padded, axis_id, -shift_by, length)
        )
    return summed


def profile(position, low_width, high_width, length):
    inward_low = jnp.clip((low_width - position) / low_width, 0.0, 1.0)
    inward_high = jnp.clip((position - (length - 1 - high_width)) / high_width, 0.0, 1.0)
    return jnp.exp(-damping * (inward_low * inward_low + inward_high * inward_high))


def per_device(
    pressure,
    pressure_old,
    speed_term,
    layer_width,
    source_x,
    source_y,
    source_z,
    source_amp,
    receiver_x,
    receiver_y,
    receiver_z,
):
    cells_x, cells_y, depth = pressure.shape
    count_x = cells_x * lax.axis_size(GX)
    count_y = cells_y * lax.axis_size(GY)
    start_x = lax.axis_index(GX) * cells_x
    start_y = lax.axis_index(GY) * cells_y
    widths = layer_width.astype(jnp.float32)
    global_x = profile(
        jnp.arange(count_x, dtype=jnp.int32).astype(jnp.float32), widths[0], widths[1], count_x
    )
    global_y = profile(
        jnp.arange(count_y, dtype=jnp.int32).astype(jnp.float32), widths[2], widths[3], count_y
    )
    keep_x = lax.dynamic_slice_in_dim(global_x, start_x, cells_x)[:, None, None]
    take_x = keep_x - 1.0
    keep_y = lax.dynamic_slice_in_dim(global_y, start_y, cells_y)[None, :, None]
    take_y = keep_y - 1.0
    weight = 1.0 - keep_x * keep_y
    normaliser = depth * (float(count_x * count_y) - jnp.sum(global_x) * jnp.sum(global_y))
    source_lx = source_x - start_x
    source_ly = source_y - start_y
    source_owned = (
        (source_lx >= 0) & (source_lx < cells_x) & (source_ly >= 0) & (source_ly < cells_y)
    ).astype(jnp.float32)
    source_lx = jnp.clip(source_lx, 0, cells_x - 1)
    source_ly = jnp.clip(source_ly, 0, cells_y - 1)
    receiver_lx = receiver_x - start_x
    receiver_ly = receiver_y - start_y
    receiver_owned = (
        (receiver_lx >= 0) & (receiver_lx < cells_x) & (receiver_ly >= 0) & (receiver_ly < cells_y)
    ).astype(jnp.float32)
    receiver_lx = jnp.clip(receiver_lx, 0, cells_x - 1)
    receiver_ly = jnp.clip(receiver_ly, 0, cells_y - 1)
    current = pressure
    previous = pressure_old
    memory_x = jnp.zeros_like(pressure)
    memory_y = jnp.zeros_like(pressure)
    zeta_x = jnp.zeros_like(pressure)
    zeta_y = jnp.zeros_like(pressure)
    energies = []
    traces = []
    for step_index in range(STEPS):
        wave_pad = with_halo(current, ((GX, 0), (GY, 1)), 4)
        flux_x = jnp.pad(memory_x, ((radius, radius), (0, 0), (0, 0)))
        flux_y = jnp.pad(memory_y, ((0, 0), (radius, radius), (0, 0)))
        wave_pad, flux_x, flux_y = (wave_pad, flux_x, flux_y)
        pad_x = wave_pad[:, radius : radius + cells_y]
        pad_y = wave_pad[radius : radius + cells_x, :]
        pad_z = jnp.pad(current, ((0, 0), (0, 0), (radius, radius)))
        grad_x = first_diff(pad_x, 0, cells_x)
        grad_y = first_diff(pad_y, 1, cells_y)
        bend_x = second_diff(pad_x, 0, cells_x) + first_diff(flux_x, 0, cells_x)
        zeta_x = keep_x * zeta_x + take_x * bend_x
        bend_y = second_diff(pad_y, 1, cells_y) + first_diff(flux_y, 1, cells_y)
        zeta_y = keep_y * zeta_y + take_y * bend_y
        laplace = bend_x + zeta_x + bend_y + zeta_y + second_diff(pad_z, 2, depth)
        following = 2.0 * current - previous + speed_term * laplace
        following = following.at[source_lx, source_ly, source_z].add(
            source_amp[step_index] * source_owned
        )
        memory_x = keep_x * memory_x + take_x * grad_x
        memory_y = keep_y * memory_y + take_y * grad_y
        energy_local = jnp.sum(weight * following * following)
        trace_local = following[receiver_lx, receiver_ly, receiver_z] * receiver_owned
        energies.append(energy_local)
        traces.append(trace_local)
        previous = current
        current = following
    energy_sum, trace_table = (
        by_axis(jnp.stack(energies), GX_GY),
        by_axis(jnp.stack(traces, axis=1), GX_GY),
    )
    energy = energy_sum / normaliser
    return (current, trace_table, energy)


def solution(mesh):
    split = Mesh(mesh.devices.reshape(4, 2, 4, 2, 2), ("gx_0", "gx_1", "gy_0", "gy_1", "gy_2"))
    return jax.shard_map(
        per_device,
        mesh=split,
        in_specs=(
            P(GX, GY, None),
            P(GX, GY, None),
            P(GX, GY, None),
            P(),
            P(),
            P(),
            P(),
            P(),
            P(),
            P(),
            P(),
        ),
        out_specs=(P(GX, GY, None), P(), P()),
        check_vma=False,
    )
```

profile of v0, /device:TPU:0, one launch (start us, length us, event | category | flops | bytes accessed | tf_op | source)
XLA Modules:
  0.0 286.9 jit_solution(16289942052447889101)
XLA Ops:
  1.7 3.5 %collective-permute-start.1 = (f32[4,24,256]{2,1,0:T(8,128)S(1)}, f32[4,24,256]{2,1,0:T(8,128)S(1)}, u32[]{:S(2)}, u32[]{:S(2)}) collective-permute-start(f32[4,24,256]{2,1,0:T(8,128)S(1)} %get-tuple-element.143), channel_id=1, source_target_pairs={{0,16},{16,32},{32,48},{48,64},{64,80},{80,96},{96,112},{1,17},{17... | collective-permute-start | bytes 294920 | tf_op jit(solution)/shard_map/ppermute | solution.py:30
  8.8 3.0 %collective-permute-start.3 = (f32[24,4,256]{2,1,0:T(4,128)S(1)}, f32[24,4,256]{2,1,0:T(4,128)S(1)}, u32[]{:S(2)}, u32[]{:S(2)}) collective-permute-start(f32[24,4,256]{2,1,0:T(4,128)S(1)} %get-tuple-element.138), channel_id=1, source_target_pairs={{0,1},{1,2},{2,3},{3,4},{4,5},{5,6},{6,7},{7,8},{8,9},{9,10},{10,1... | collective-permute-start | bytes 294920 | tf_op jit(solution)/shard_map/ppermute | solution.py:30
  13.8 1.9 multiply_exponential_fusion
  18.3 1.9 fusion.351
  26.8 3.7 %fusion.184 = (f32[24,24,256]{2,1,0:T(8,128)S(1)}, f32[24,24,256]{2,1,0:T(8,128)}, f32[24,24,256]{2,1,0:T(8,128)}) fusion(f32[24,24,256]{2,1,0:T(8,128)S(1)} %copy-done, f32[24,24,256]{2,1,0:T(8,128)S(1)} %copy-done.31, f32[24,24,256]{2,1,0:T(8,128)S(1)} %copy-done.65, f32[24]{0:T(128)S(1)} %broadcast_add_fusion, f32[24]{0:T(128)S(1)} %get-tuple-element.70, ...), kind=kLoop, calls=%fused_computation.418 | loop fusion | flops 10764288 | bytes 13566336 | tf_op jit(solution)/shard_map/add | solution.py:144
  31.3 4.5 %collective-permute-start.5 = (f32[4,24,256]{2,1,0:T(8,128)S(1)}, f32[4,24,256]{2,1,0:T(8,128)S(1)}, u32[]{:S(2)}, u32[]{:S(2)}) collective-permute-start(f32[4,24,256]{2,1,0:T(8,128)S(1)} %get-tuple-element.136), channel_id=1, source_target_pairs={{0,16},{16,32},{32,48},{48,64},{64,80},{80,96},{96,112},{1,17},{17... | collective-permute-start | bytes 294920 | tf_op jit(solution)/shard_map/ppermute | solution.py:30
  38.5 4.3 %collective-permute-start.7 = (f32[24,4,256]{2,1,0:T(4,128)S(1)}, f32[24,4,256]{2,1,0:T(4,128)S(1)}, u32[]{:S(2)}, u32[]{:S(2)}) collective-permute-start(f32[24,4,256]{2,1,0:T(4,128)S(1)} %get-tuple-element.131), channel_id=1, source_target_pairs={{0,1},{1,2},{2,3},{3,4},{4,5},{5,6},{6,7},{7,8},{8,9},{9,10},{10,1... | collective-permute-start | bytes 294920 | tf_op jit(solution)/shard_map/ppermute | solution.py:30
  42.8 1.5 gather_fusion
  47.0 3.9 %fusion.199 = (f32[24,24,256]{2,1,0:T(8,128)S(1)}, f32[24,24,256]{2,1,0:T(8,128)}, f32[24,24,256]{2,1,0:T(8,128)}) fusion(f32[24,24,256]{2,1,0:T(8,128)S(1)} %copy-done, f32[24,24,256]{2,1,0:T(8,128)S(1)} %scatter_fusion, f32[24,24,256]{2,1,0:T(8,128)S(1)} %copy-done.32, f32[24,24,256]{2,1,0:T(8,128)S(1)} %copy-done.51, f32[24]{0:T(128)S(1)} %copy-done.68, ...), kind=kLoop, calls=%fused_computation.433 | loop fusion | flops 11649024 | bytes 15336000 | tf_op jit(solution)/shard_map/add | solution.py:144
  53.1 6.2 %collective-permute-start.9 = (f32[4,24,256]{2,1,0:T(8,128)}, f32[4,24,256]{2,1,0:T(8,128)}, u32[]{:S(2)}, u32[]{:S(2)}) collective-permute-start(f32[4,24,256]{2,1,0:T(8,128)} %get-tuple-element.129), channel_id=1, source_target_pairs={{0,16},{16,32},{32,48},{48,64},{64,80},{80,96},{96,112},{1,17},{17... | collective-permute-start | bytes 294920 | tf_op jit(solution)/shard_map/ppermute | solution.py:30
  59.3 1.5 gather_fusion.1
  63.5 5.5 %collective-permute-start.11 = (f32[24,4,256]{2,1,0:T(4,128)S(1)}, f32[24,4,256]{2,1,0:T(4,128)S(1)}, u32[]{:S(2)}, u32[]{:S(2)}) collective-permute-start(f32[24,4,256]{2,1,0:T(4,128)S(1)} %get-tuple-element.127), channel_id=1, source_target_pairs={{0,1},{1,2},{2,3},{3,4},{4,5},{5,6},{6,7},{7,8},{8,9},{9,10},{10,1... | collective-permute-start | bytes 294920 | tf_op jit(solution)/shard_map/ppermute | solution.py:30
  71.0 1.4 multiply_add_fusion.17
  74.1 1.9 multiply_add_fusion.15
  76.6 4.0 %fusion.214 = (f32[24,24,256]{2,1,0:T(8,128)S(1)}, f32[24,24,256]{2,1,0:T(8,128)}, f32[24,24,256]{2,1,0:T(8,128)}) fusion(f32[24,24,256]{2,1,0:T(8,128)S(1)} %copy-done, f32[24,24,256]{2,1,0:T(8,128)S(1)} %copy-done.9, f32[24,24,256]{2,1,0:T(8,128)S(1)} %scatter_fusion, f32[24]{0:T(128)S(1)} %copy-done.76, f32[24]{0:T(128)S(1)} %broadcast_add_fusion.1, ...), kind=kLoop, calls=%fused_computation.448 | loop fusion | flops 12533760 | bytes 16515648 | tf_op jit(solution)/shard_map/add | solution.py:144
  82.0 4.7 %collective-permute-start.13 = (f32[4,24,256]{2,1,0:T(8,128)S(1)}, f32[4,24,256]{2,1,0:T(8,128)S(1)}, u32[]{:S(2)}, u32[]{:S(2)}) collective-permute-start(f32[4,24,256]{2,1,0:T(8,128)S(1)} %get-tuple-element.122), channel_id=1, source_target_pairs={{0,16},{16,32},{32,48},{48,64},{64,80},{80,96},{96,112},{1,17},{17... | collective-permute-start | bytes 294920 | tf_op jit(solution)/shard_map/ppermute | solution.py:30
  86.8 1.6 gather_fusion.2
  90.9 6.3 %collective-permute-start.15 = (f32[24,4,256]{2,1,0:T(4,128)S(1)}, f32[24,4,256]{2,1,0:T(4,128)S(1)}, u32[]{:S(2)}, u32[]{:S(2)}) collective-permute-start(f32[24,4,256]{2,1,0:T(4,128)S(1)} %get-tuple-element.117), channel_id=1, source_target_pairs={{0,1},{1,2},{2,3},{3,4},{4,5},{5,6},{6,7},{7,8},{8,9},{9,10},{10,1... | collective-permute-start | bytes 294920 | tf_op jit(solution)/shard_map/ppermute | solution.py:30
  100.8 3.9 %fusion.229 = (f32[24,24,256]{2,1,0:T(8,128)S(1)}, f32[24,24,256]{2,1,0:T(8,128)}, f32[24,24,256]{2,1,0:T(8,128)}) fusion(f32[24,24,256]{2,1,0:T(8,128)S(1)} %copy-done, f32[24,24,256]{2,1,0:T(8,128)S(1)} %scatter_fusion.2, f32[24,24,256]{2,1,0:T(8,128)S(1)} %copy-done.10, f32[24,24,256]{2,1,0:T(8,128)S(1)} %copy-done.37, f32[24]{0:T(128)S(1)} %copy-done.69, ...), kind=kLoop, calls=%fused_computation.463 | loop fusion | flops 12238848 | bytes 16515552 | tf_op jit(solution)/shard_map/add | solution.py:144
  106.8 6.1 %collective-permute-start.17 = (f32[4,24,256]{2,1,0:T(8,128)}, f32[4,24,256]{2,1,0:T(8,128)}, u32[]{:S(2)}, u32[]{:S(2)}) collective-permute-start(f32[4,24,256]{2,1,0:T(8,128)} %get-tuple-element.115), channel_id=1, source_target_pairs={{0,16},{16,32},{32,48},{48,64},{64,80},{80,96},{96,112},{1,17},{17... | collective-permute-start | bytes 294920 | tf_op jit(solution)/shard_map/ppermute | solution.py:30
  112.9 1.5 gather_fusion.3
  117.0 6.1 %collective-permute-start.19 = (f32[24,4,256]{2,1,0:T(4,128)S(1)}, f32[24,4,256]{2,1,0:T(4,128)S(1)}, u32[]{:S(2)}, u32[]{:S(2)}) collective-permute-start(f32[24,4,256]{2,1,0:T(4,128)S(1)} %get-tuple-element.113), channel_id=1, source_target_pairs={{0,1},{1,2},{2,3},{3,4},{4,5},{5,6},{6,7},{7,8},{8,9},{9,10},{10,1... | collective-permute-start | bytes 294920 | tf_op jit(solution)/shard_map/ppermute | solution.py:30
  128.2 1.9 multiply_add_fusion.7
  130.2 3.9 %fusion.244 = (f32[24,24,256]{2,1,0:T(8,128)S(1)}, f32[24,24,256]{2,1,0:T(8,128)}, f32[24,24,256]{2,1,0:T(8,128)}) fusion(f32[24,24,256]{2,1,0:T(8,128)S(1)} %copy-done, f32[24,24,256]{2,1,0:T(8,128)S(1)} %copy-done.4, f32[24,24,256]{2,1,0:T(8,128)S(1)} %scatter_fusion.2, f32[24,24,256]{2,1,0:T(8,128)S(1)} %copy-done.39, f32[24]{0:T(128)S(1)} %copy-done.78, ...), kind=kLoop, calls=%fused_computation.478 | loop fusion | flops 11501568 | bytes 15925632 | tf_op jit(solution)/shard_map/add | solution.py:144
  136.1 5.4 %collective-permute-start.21 = (f32[4,24,256]{2,1,0:T(8,128)S(1)}, f32[4,24,256]{2,1,0:T(8,128)S(1)}, u32[]{:S(2)}, u32[]{:S(2)}) collective-permute-start(f32[4,24,256]{2,1,0:T(8,128)S(1)} %get-tuple-element.108), channel_id=1, source_target_pairs={{0,16},{16,32},{32,48},{48,64},{64,80},{80,96},{96,112},{1,17},{17... | collective-permute-start | bytes 294920 | tf_op jit(solution)/shard_map/ppermute | solution.py:30
  141.6 1.5 gather_fusion.4
  145.7 5.8 %collective-permute-start.23 = (f32[24,4,256]{2,1,0:T(4,128)S(1)}, f32[24,4,256]{2,1,0:T(4,128)S(1)}, u32[]{:S(2)}, u32[]{:S(2)}) collective-permute-start(f32[24,4,256]{2,1,0:T(4,128)S(1)} %get-tuple-element.103), channel_id=1, source_target_pairs={{0,1},{1,2},{2,3},{3,4},{4,5},{5,6},{6,7},{7,8},{8,9},{9,10},{10,1... | collective-permute-start | bytes 294920 | tf_op jit(solution)/shard_map/ppermute | solution.py:30
  155.0 4.0 %fusion.259 = (f32[24,24,256]{2,1,0:T(8,128)}, f32[24,24,256]{2,1,0:T(8,128)}, f32[24,24,256]{2,1,0:T(8,128)}) fusion(f32[24,24,256]{2,1,0:T(8,128)S(1)} %copy-done, f32[24,24,256]{2,1,0:T(8,128)S(1)} %scatter_fusion.4, f32[24,24,256]{2,1,0:T(8,128)S(1)} %copy-done.5, f32[24,24,256]{2,1,0:T(8,128)S(1)} %copy-done.25, f32[24]{0:T(128)S(1)} %copy-done.71, ...), kind=kLoop, calls=%fused_computation.493 | loop fusion | flops 11501568 | bytes 15925632 | tf_op jit(solution)/shard_map/add | solution.py:144
  159.6 2.0 scatter_fusion.5
  161.6 1.6 fusion.365
  163.3 6.6 %collective-permute-start.25 = (f32[4,24,256]{2,1,0:T(8,128)}, f32[4,24,256]{2,1,0:T(8,128)}, u32[]{:S(2)}, u32[]{:S(2)}) collective-permute-start(f32[4,24,256]{2,1,0:T(8,128)} %get-tuple-element.101), channel_id=1, source_target_pairs={{0,16},{16,32},{32,48},{48,64},{64,80},{80,96},{96,112},{1,17},{17... | collective-permute-start | bytes 294920 | tf_op jit(solution)/shard_map/ppermute | solution.py:30
  171.0 3.0 %gather_fusion.5 = f32[64]{0:T(128)} fusion(f32[24,24,256]{2,1,0:T(8,128)} %scatter_fusion.5, s32[64]{0:T(128)S(1)} %fusion.344), kind=kCustom, calls=%fused_computation.5 | custom fusion | bytes 1280 | tf_op jit(solution)/shard_map/gather | solution.py:151
  176.5 6.3 %collective-permute-start.27 = (f32[24,4,256]{2,1,0:T(4,128)S(1)}, f32[24,4,256]{2,1,0:T(4,128)S(1)}, u32[]{:S(2)}, u32[]{:S(2)}) collective-permute-start(f32[24,4,256]{2,1,0:T(4,128)S(1)} %get-tuple-element.96), channel_id=1, source_target_pairs={{0,1},{1,2},{2,3},{3,4},{4,5},{5,6},{6,7},{7,8},{8,9},{9,10},{10,1... | collective-permute-start | bytes 294920 | tf_op jit(solution)/shard_map/ppermute | solution.py:30
  188.8 1.9 multiply_add_fusion
  190.7 3.9 %fusion.274 = (f32[24,24,256]{2,1,0:T(8,128)S(1)}, f32[24,24,256]{2,1,0:T(8,128)}, f32[24,24,256]{2,1,0:T(8,128)}) fusion(f32[24,24,256]{2,1,0:T(8,128)S(1)} %copy-done, f32[24,24,256]{2,1,0:T(8,128)S(1)} %copy-done.7, f32[24,24,256]{2,1,0:T(8,128)S(1)} %scatter_fusion.4, f32[24,24,256]{2,1,0:T(8,128)S(1)} %copy-done.41, f32[24]{0:T(128)S(1)} %copy-done.80, ...), kind=kLoop, calls=%fused_computation.508 | loop fusion | flops 11501568 | bytes 15925632 | tf_op jit(solution)/shard_map/add | solution.py:144
  196.7 5.9 %collective-permute-start.29 = (f32[4,24,256]{2,1,0:T(8,128)}, f32[4,24,256]{2,1,0:T(8,128)}, u32[]{:S(2)}, u32[]{:S(2)}) collective-permute-start(f32[4,24,256]{2,1,0:T(8,128)} %get-tuple-element.94), channel_id=1, source_target_pairs={{0,16},{16,32},{32,48},{48,64},{64,80},{80,96},{96,112},{1,17},{17... | collective-permute-start | bytes 294920 | tf_op jit(solution)/shard_map/ppermute | solution.py:30
  202.6 1.5 gather_fusion.6
  206.8 5.7 %collective-permute-start.31 = (f32[24,4,256]{2,1,0:T(4,128)S(1)}, f32[24,4,256]{2,1,0:T(4,128)S(1)}, u32[]{:S(2)}, u32[]{:S(2)}) collective-permute-start(f32[24,4,256]{2,1,0:T(4,128)S(1)} %get-tuple-element.92), channel_id=1, source_target_pairs={{0,1},{1,2},{2,3},{3,4},{4,5},{5,6},{6,7},{7,8},{8,9},{9,10},{10,1... | collective-permute-start | bytes 294920 | tf_op jit(solution)/shard_map/ppermute | solution.py:30
  215.6 3.9 %fusion.289 = f32[24,24,256]{2,1,0:T(8,128)} fusion(f32[24,24,256]{2,1,0:T(8,128)S(1)} %copy-done, f32[24,24,256]{2,1,0:T(8,128)S(1)} %scatter_fusion.6, f32[24,24,256]{2,1,0:T(8,128)S(1)} %copy-done.58, f32[32,28,256]{2,1,0:T(8,128)S(1)} %get-tuple-element.73, f32[32,28,256]{2,1,0:T(8,128)S(1)} %get-tuple-element.72, f32[24,24,256]{2,1,0:T(8,128)S(1)} %copy-done.57, ...), kind=kLoop, calls=%fused_computation.523 | loop fusion | flops 12386304 | bytes 15925632 | tf_op jit(solution)/shard_map/add | solution.py:144
  220.1 2.0 scatter_fusion.7
  222.2 2.9 %gather_fusion.7 = f32[64]{0:T(128)} fusion(f32[24,24,256]{2,1,0:T(8,128)} %scatter_fusion.7, s32[64]{0:T(128)S(1)} %fusion.344), kind=kCustom, calls=%fused_computation.7 | custom fusion | bytes 1280 | tf_op jit(solution)/shard_map/gather | solution.py:151
  226.3 2.7 fusion.7
  230.3 5.1 %stack.71 = f32[8]{0:T(128)S(1)} concatenate(f32[1]{0:T(128)} %bitcast.16, f32[1]{0:T(128)} %bitcast.17, f32[1]{0:T(128)} %bitcast.18, f32[1]{0:T(128)} %bitcast.19, f32[1]{0:T(128)} %bitcast.20, f32[1]{0:T(128)} %bitcast.21, f32[1]{0:T(128)} %bitcast.22, f32[1]{0:T(128)} %bitcast.23), dimensions={0} | concatenate | bytes 64 | tf_op jit(solution)/shard_map/stack | solution.py:157
  235.4 14.1 %all-reduce.41 = (f32[64,8]{0,1:T(8,128)S(1)}, f32[8]{0:T(128)S(1)}) all-reduce(f32[64,8]{0,1:T(8,128)S(1)} %stack.62, f32[8]{0:T(128)S(1)} %stack.71), channel_id=1, replica_groups=mesh['gx_0'=4,'gx_1'=2,'gy_0'=4,'gy_1'=2,'gy_2'=2] {'gx_0'}, use_global_device_ids=true, to_apply=%region_8.9 | all-reduce | flops 520 | bytes 4160 | tf_op jit(solution)/shard_map/psum | solution.py:43
  249.5 5.0 %all-reduce.44 = (f32[64,8]{0,1:T(8,128)S(1)}, f32[8]{0:T(128)S(1)}) all-reduce(f32[64,8]{0,1:T(8,128)S(1)} %get-tuple-element.21, f32[8]{0:T(128)S(1)} %get-tuple-element.22), channel_id=1, replica_groups=mesh['gx_0'=4,'gx_1'=2,'gy_0'=4,'gy_1'=2,'gy_2'=2] {'gx_1'}, use_global_device_ids=true, to_apply=%region_9.10 | all-reduce | flops 520 | bytes 4160 | tf_op jit(solution)/shard_map/psum | solution.py:43
  254.5 22.3 %all-reduce.40 = (f32[64,8]{0,1:T(8,128)S(1)}, f32[8]{0:T(128)S(1)}) all-reduce(f32[64,8]{0,1:T(8,128)S(1)} %get-tuple-element.27, f32[8]{0:T(128)S(1)} %get-tuple-element.28), channel_id=1, replica_groups=mesh['gx_0'=4,'gx_1'=2,'gy_0'=4,'gy_1'=2,'gy_2'=2] {'gy_0'}, use_global_device_ids=true, to_apply=%region_10.11 | all-reduce | flops 520 | bytes 4160 | tf_op jit(solution)/shard_map/psum | solution.py:43
  276.8 6.5 %all-reduce.43 = (f32[64,8]{0,1:T(8,128)S(1)}, f32[8]{0:T(128)S(1)}) all-reduce(f32[64,8]{0,1:T(8,128)S(1)} %get-tuple-element.19, f32[8]{0:T(128)S(1)} %get-tuple-element.20), channel_id=1, replica_groups=mesh['gx_0'=4,'gx_1'=2,'gy_0'=4,'gy_1'=2,'gy_2'=2] {'gy_1'}, use_global_device_ids=true, to_apply=%region_11.12 | all-reduce | flops 520 | bytes 4160 | tf_op jit(solution)/shard_map/psum | solution.py:43
  283.3 3.1 %all-reduce.42 = (f32[64,8]{0,1:T(8,128)}, f32[8]{0:T(128)S(1)}) all-reduce(f32[64,8]{0,1:T(8,128)S(1)} %get-tuple-element.25, f32[8]{0:T(128)S(1)} %get-tuple-element.26), channel_id=1, replica_groups=mesh['gx_0'=4,'gx_1'=2,'gy_0'=4,'gy_1'=2,'gy_2'=2] {'gy_2'}, use_global_device_ids=true, to_apply=%region_12.13 | all-reduce | flops 520 | bytes 4160 | tf_op jit(solution)/shard_map/psum | solution.py:43
  (344 shorter events, 74.6 us)
Async XLA Ops:
  0.6 22.2 %copy-start.31 = (f32[24,24,256]{2,1,0:T(8,128)S(1)}, f32[24,24,256]{2,1,0:T(8,128)}, u32[]{:S(2)}) copy-start(f32[24,24,256]{2,1,0:T(8,128)} %param.11) | copy-start | bytes 1769476
  1.7 21.2 %collective-permute-start.1 = (f32[4,24,256]{2,1,0:T(8,128)S(1)}, f32[4,24,256]{2,1,0:T(8,128)S(1)}, u32[]{:S(2)}, u32[]{:S(2)}) collective-permute-start(f32[4,24,256]{2,1,0:T(8,128)S(1)} %get-tuple-element.143), channel_id=1, source_target_pairs={{0,16},{16,32},{32,48},{48,64},{64,80},{80,96},{96,112},{1,17},{17... | collective-permute-start | bytes 294920 | tf_op jit(solution)/shard_map/ppermute | solution.py:30
  5.2 17.9 %collective-permute-start = (f32[4,24,256]{2,1,0:T(8,128)S(1)}, f32[4,24,256]{2,1,0:T(8,128)S(1)}, u32[]{:S(2)}, u32[]{:S(2)}) collective-permute-start(f32[4,24,256]{2,1,0:T(8,128)S(1)} %get-tuple-element.142), channel_id=1, source_target_pairs={{16,0},{32,16},{48,32},{64,48},{80,64},{96,80},{112,96},{17,1},{33... | collective-permute-start | bytes 294920 | tf_op jit(solution)/shard_map/ppermute | solution.py:31
  7.5 16.6 %collective-permute-start.2 = (f32[24,4,256]{2,1,0:T(4,128)S(1)}, f32[24,4,256]{2,1,0:T(4,128)S(1)}, u32[]{:S(2)}, u32[]{:S(2)}) collective-permute-start(f32[24,4,256]{2,1,0:T(4,128)S(1)} %get-tuple-element.137), channel_id=1, source_target_pairs={{1,0},{2,1},{3,2},{4,3},{5,4},{6,5},{7,6},{8,7},{9,8},{10,9},{11,1... | collective-permute-start | bytes 294920 | tf_op jit(solution)/shard_map/ppermute | solution.py:31
  8.8 15.3 %collective-permute-start.3 = (f32[24,4,256]{2,1,0:T(4,128)S(1)}, f32[24,4,256]{2,1,0:T(4,128)S(1)}, u32[]{:S(2)}, u32[]{:S(2)}) collective-permute-start(f32[24,4,256]{2,1,0:T(4,128)S(1)} %get-tuple-element.138), channel_id=1, source_target_pairs={{0,1},{1,2},{2,3},{3,4},{4,5},{5,6},{6,7},{7,8},{8,9},{9,10},{10,1... | collective-permute-start | bytes 294920 | tf_op jit(solution)/shard_map/ppermute | solution.py:30
  15.8 10.0 %copy-start.86 = (f32[24]{0:T(128)}, f32[24]{0:T(128)S(1)}, u32[]{:S(2)}) copy-start(f32[24]{0:T(128)S(1)} %get-tuple-element.70) | copy-start | bytes 292
  20.3 5.5 %copy-start.83 = (f32[24]{0:T(128)}, f32[24]{0:T(128)S(1)}, u32[]{:S(2)}) copy-start(f32[24]{0:T(128)S(1)} %get-tuple-element.68) | copy-start | bytes 292
  31.3 44.7 %copy-start.1 = (f32[24,24,256]{2,1,0:T(8,128)}, f32[24,24,256]{2,1,0:T(8,128)S(1)}, u32[]{:S(2)}) copy-start(f32[24,24,256]{2,1,0:T(8,128)S(1)} %scatter_fusion) | copy-start | bytes 1769476
  31.3 13.0 %collective-permute-start.5 = (f32[4,24,256]{2,1,0:T(8,128)S(1)}, f32[4,24,256]{2,1,0:T(8,128)S(1)}, u32[]{:S(2)}, u32[]{:S(2)}) collective-permute-start(f32[4,24,256]{2,1,0:T(8,128)S(1)} %get-tuple-element.136), channel_id=1, source_target_pairs={{0,16},{16,32},{32,48},{48,64},{64,80},{80,96},{96,112},{1,17},{17... | collective-permute-start | bytes 294920 | tf_op jit(solution)/shard_map/ppermute | solution.py:30
  35.9 8.5 %collective-permute-start.4 = (f32[4,24,256]{2,1,0:T(8,128)S(1)}, f32[4,24,256]{2,1,0:T(8,128)S(1)}, u32[]{:S(2)}, u32[]{:S(2)}) collective-permute-start(f32[4,24,256]{2,1,0:T(8,128)S(1)} %get-tuple-element.135), channel_id=1, source_target_pairs={{16,0},{32,16},{48,32},{64,48},{80,64},{96,80},{112,96},{17,1},{33... | collective-permute-start | bytes 294920 | tf_op jit(solution)/shard_map/ppermute | solution.py:31
  37.2 7.3 %collective-permute-start.6 = (f32[24,4,256]{2,1,0:T(4,128)S(1)}, f32[24,4,256]{2,1,0:T(4,128)S(1)}, u32[]{:S(2)}, u32[]{:S(2)}) collective-permute-start(f32[24,4,256]{2,1,0:T(4,128)S(1)} %get-tuple-element.130), channel_id=1, source_target_pairs={{1,0},{2,1},{3,2},{4,3},{5,4},{6,5},{7,6},{8,7},{9,8},{10,9},{11,1... | collective-permute-start | bytes 294920 | tf_op jit(solution)/shard_map/ppermute | solution.py:31
  38.5 6.0 %collective-permute-start.7 = (f32[24,4,256]{2,1,0:T(4,128)S(1)}, f32[24,4,256]{2,1,0:T(4,128)S(1)}, u32[]{:S(2)}, u32[]{:S(2)}) collective-permute-start(f32[24,4,256]{2,1,0:T(4,128)S(1)} %get-tuple-element.131), channel_id=1, source_target_pairs={{0,1},{1,2},{2,3},{3,4},{4,5},{5,6},{6,7},{7,8},{8,9},{9,10},{10,1... | collective-permute-start | bytes 294920 | tf_op jit(solution)/shard_map/ppermute | solution.py:30
  44.8 6.2 %copy-start.20 = (f32[32,28,256]{2,1,0:T(8,128)}, f32[32,28,256]{2,1,0:T(8,128)S(1)}, u32[]{:S(2)}) copy-start(f32[32,28,256]{2,1,0:T(8,128)S(1)} %get-tuple-element.84) | copy-start | bytes 2752516
  44.8 6.1 %copy-start.22 = (f32[32,28,256]{2,1,0:T(8,128)}, f32[32,28,256]{2,1,0:T(8,128)S(1)}, u32[]{:S(2)}) copy-start(f32[32,28,256]{2,1,0:T(8,128)S(1)} %get-tuple-element.85) | copy-start | bytes 2752516
  52.3 17.6 %copy-start.8 = (f32[24,24,256]{2,1,0:T(8,128)}, f32[24,24,256]{2,1,0:T(8,128)S(1)}, u32[]{:S(2)}) copy-start(f32[24,24,256]{2,1,0:T(8,128)S(1)} %scatter_fusion.1) | copy-start | bytes 1769476
  53.1 15.9 %collective-permute-start.9 = (f32[4,24,256]{2,1,0:T(8,128)}, f32[4,24,256]{2,1,0:T(8,128)}, u32[]{:S(2)}, u32[]{:S(2)}) collective-permute-start(f32[4,24,256]{2,1,0:T(8,128)} %get-tuple-element.129), channel_id=1, source_target_pairs={{0,16},{16,32},{32,48},{48,64},{64,80},{80,96},{96,112},{1,17},{17... | collective-permute-start | bytes 294920 | tf_op jit(solution)/shard_map/ppermute | solution.py:30
  60.9 9.2 %collective-permute-start.8 = (f32[4,24,256]{2,1,0:T(8,128)}, f32[4,24,256]{2,1,0:T(8,128)S(1)}, u32[]{:S(2)}, u32[]{:S(2)}) collective-permute-start(f32[4,24,256]{2,1,0:T(8,128)} %get-tuple-element.128), channel_id=1, source_target_pairs={{16,0},{32,16},{48,32},{64,48},{80,64},{96,80},{112,96},{17,1},{33... | collective-permute-start | bytes 294920 | tf_op jit(solution)/shard_map/ppermute | solution.py:31
  62.2 10.2 %collective-permute-start.10 = (f32[24,4,256]{2,1,0:T(4,128)S(1)}, f32[24,4,256]{2,1,0:T(4,128)S(1)}, u32[]{:S(2)}, u32[]{:S(2)}) collective-permute-start(f32[24,4,256]{2,1,0:T(4,128)S(1)} %get-tuple-element.126), channel_id=1, source_target_pairs={{1,0},{2,1},{3,2},{4,3},{5,4},{6,5},{7,6},{8,7},{9,8},{10,9},{11,1... | collective-permute-start | bytes 294920 | tf_op jit(solution)/shard_map/ppermute | solution.py:31
  63.5 8.9 %collective-permute-start.11 = (f32[24,4,256]{2,1,0:T(4,128)S(1)}, f32[24,4,256]{2,1,0:T(4,128)S(1)}, u32[]{:S(2)}, u32[]{:S(2)}) collective-permute-start(f32[24,4,256]{2,1,0:T(4,128)S(1)} %get-tuple-element.127), channel_id=1, source_target_pairs={{0,1},{1,2},{2,3},{3,4},{4,5},{5,6},{6,7},{7,8},{8,9},{9,10},{10,1... | collective-permute-start | bytes 294920 | tf_op jit(solution)/shard_map/ppermute | solution.py:30
  82.0 15.3 %collective-permute-start.13 = (f32[4,24,256]{2,1,0:T(8,128)S(1)}, f32[4,24,256]{2,1,0:T(8,128)S(1)}, u32[]{:S(2)}, u32[]{:S(2)}) collective-permute-start(f32[4,24,256]{2,1,0:T(8,128)S(1)} %get-tuple-element.122), channel_id=1, source_target_pairs={{0,16},{16,32},{32,48},{48,64},{64,80},{80,96},{96,112},{1,17},{17... | collective-permute-start | bytes 294920 | tf_op jit(solution)/shard_map/ppermute | solution.py:30
  88.4 9.1 %collective-permute-start.14 = (f32[24,4,256]{2,1,0:T(4,128)S(1)}, f32[24,4,256]{2,1,0:T(4,128)S(1)}, u32[]{:S(2)}, u32[]{:S(2)}) collective-permute-start(f32[24,4,256]{2,1,0:T(4,128)S(1)} %get-tuple-element.116), channel_id=1, source_target_pairs={{1,0},{2,1},{3,2},{4,3},{5,4},{6,5},{7,6},{8,7},{9,8},{10,9},{11,1... | collective-permute-start | bytes 294920 | tf_op jit(solution)/shard_map/ppermute | solution.py:31
  89.6 7.8 %collective-permute-start.12 = (f32[4,24,256]{2,1,0:T(8,128)S(1)}, f32[4,24,256]{2,1,0:T(8,128)S(1)}, u32[]{:S(2)}, u32[]{:S(2)}) collective-permute-start(f32[4,24,256]{2,1,0:T(8,128)S(1)} %get-tuple-element.121), channel_id=1, source_target_pairs={{16,0},{32,16},{48,32},{64,48},{80,64},{96,80},{112,96},{17,1},{33... | collective-permute-start | bytes 294920 | tf_op jit(solution)/shard_map/ppermute | solution.py:31
  90.9 7.3 %collective-permute-start.15 = (f32[24,4,256]{2,1,0:T(4,128)S(1)}, f32[24,4,256]{2,1,0:T(4,128)S(1)}, u32[]{:S(2)}, u32[]{:S(2)}) collective-permute-start(f32[24,4,256]{2,1,0:T(4,128)S(1)} %get-tuple-element.117), channel_id=1, source_target_pairs={{0,1},{1,2},{2,3},{3,4},{4,5},{5,6},{6,7},{7,8},{8,9},{9,10},{10,1... | collective-permute-start | bytes 294920 | tf_op jit(solution)/shard_map/ppermute | solution.py:30
  98.5 6.3 %copy-start.12 = (f32[32,28,256]{2,1,0:T(8,128)}, f32[32,28,256]{2,1,0:T(8,128)S(1)}, u32[]{:S(2)}) copy-start(f32[32,28,256]{2,1,0:T(8,128)S(1)} %get-tuple-element.80) | copy-start | bytes 2752516
  98.5 6.3 %copy-start.14 = (f32[32,28,256]{2,1,0:T(8,128)}, f32[32,28,256]{2,1,0:T(8,128)S(1)}, u32[]{:S(2)}) copy-start(f32[32,28,256]{2,1,0:T(8,128)S(1)} %get-tuple-element.81) | copy-start | bytes 2752516
  106.1 18.0 %copy-start.3 = (f32[24,24,256]{2,1,0:T(8,128)}, f32[24,24,256]{2,1,0:T(8,128)S(1)}, u32[]{:S(2)}) copy-start(f32[24,24,256]{2,1,0:T(8,128)S(1)} %scatter_fusion.3) | copy-start | bytes 1769476
  106.8 16.3 %collective-permute-start.17 = (f32[4,24,256]{2,1,0:T(8,128)}, f32[4,24,256]{2,1,0:T(8,128)}, u32[]{:S(2)}, u32[]{:S(2)}) collective-permute-start(f32[4,24,256]{2,1,0:T(8,128)} %get-tuple-element.115), channel_id=1, source_target_pairs={{0,16},{16,32},{32,48},{48,64},{64,80},{80,96},{96,112},{1,17},{17... | collective-permute-start | bytes 294920 | tf_op jit(solution)/shard_map/ppermute | solution.py:30
  114.4 9.8 %collective-permute-start.16 = (f32[4,24,256]{2,1,0:T(8,128)}, f32[4,24,256]{2,1,0:T(8,128)S(1)}, u32[]{:S(2)}, u32[]{:S(2)}) collective-permute-start(f32[4,24,256]{2,1,0:T(8,128)} %get-tuple-element.114), channel_id=1, source_target_pairs={{16,0},{32,16},{48,32},{64,48},{80,64},{96,80},{112,96},{17,1},{33... | collective-permute-start | bytes 294920 | tf_op jit(solution)/shard_map/ppermute | solution.py:31
  115.7 10.8 %collective-permute-start.18 = (f32[24,4,256]{2,1,0:T(4,128)S(1)}, f32[24,4,256]{2,1,0:T(4,128)S(1)}, u32[]{:S(2)}, u32[]{:S(2)}) collective-permute-start(f32[24,4,256]{2,1,0:T(4,128)S(1)} %get-tuple-element.112), channel_id=1, source_target_pairs={{1,0},{2,1},{3,2},{4,3},{5,4},{6,5},{7,6},{8,7},{9,8},{10,9},{11,1... | collective-permute-start | bytes 294920 | tf_op jit(solution)/shard_map/ppermute | solution.py:31
  117.0 9.5 %collective-permute-start.19 = (f32[24,4,256]{2,1,0:T(4,128)S(1)}, f32[24,4,256]{2,1,0:T(4,128)S(1)}, u32[]{:S(2)}, u32[]{:S(2)}) collective-permute-start(f32[24,4,256]{2,1,0:T(4,128)S(1)} %get-tuple-element.113), channel_id=1, source_target_pairs={{0,1},{1,2},{2,3},{3,4},{4,5},{5,6},{6,7},{7,8},{8,9},{9,10},{10,1... | collective-permute-start | bytes 294920 | tf_op jit(solution)/shard_map/ppermute | solution.py:30
  136.1 15.4 %collective-permute-start.21 = (f32[4,24,256]{2,1,0:T(8,128)S(1)}, f32[4,24,256]{2,1,0:T(8,128)S(1)}, u32[]{:S(2)}, u32[]{:S(2)}) collective-permute-start(f32[4,24,256]{2,1,0:T(8,128)S(1)} %get-tuple-element.108), channel_id=1, source_target_pairs={{0,16},{16,32},{32,48},{48,64},{64,80},{80,96},{96,112},{1,17},{17... | collective-permute-start | bytes 294920 | tf_op jit(solution)/shard_map/ppermute | solution.py:30
  143.1 8.6 %collective-permute-start.22 = (f32[24,4,256]{2,1,0:T(4,128)S(1)}, f32[24,4,256]{2,1,0:T(4,128)S(1)}, u32[]{:S(2)}, u32[]{:S(2)}) collective-permute-start(f32[24,4,256]{2,1,0:T(4,128)S(1)} %get-tuple-element.102), channel_id=1, source_target_pairs={{1,0},{2,1},{3,2},{4,3},{5,4},{6,5},{7,6},{8,7},{9,8},{10,9},{11,1... | collective-permute-start | bytes 294920 | tf_op jit(solution)/shard_map/ppermute | solution.py:31
  144.4 7.3 %collective-permute-start.20 = (f32[4,24,256]{2,1,0:T(8,128)}, f32[4,24,256]{2,1,0:T(8,128)S(1)}, u32[]{:S(2)}, u32[]{:S(2)}) collective-permute-start(f32[4,24,256]{2,1,0:T(8,128)} %get-tuple-element.107), channel_id=1, source_target_pairs={{16,0},{32,16},{48,32},{64,48},{80,64},{96,80},{112,96},{17,1},{33... | collective-permute-start | bytes 294920 | tf_op jit(solution)/shard_map/ppermute | solution.py:31
  145.7 6.8 %collective-permute-start.23 = (f32[24,4,256]{2,1,0:T(4,128)S(1)}, f32[24,4,256]{2,1,0:T(4,128)S(1)}, u32[]{:S(2)}, u32[]{:S(2)}) collective-permute-start(f32[24,4,256]{2,1,0:T(4,128)S(1)} %get-tuple-element.103), channel_id=1, source_target_pairs={{0,1},{1,2},{2,3},{3,4},{4,5},{5,6},{6,7},{7,8},{8,9},{9,10},{10,1... | collective-permute-start | bytes 294920 | tf_op jit(solution)/shard_map/ppermute | solution.py:30
  152.7 6.3 %copy-start.16 = (f32[32,28,256]{2,1,0:T(8,128)}, f32[32,28,256]{2,1,0:T(8,128)S(1)}, u32[]{:S(2)}) copy-start(f32[32,28,256]{2,1,0:T(8,128)S(1)} %get-tuple-element.76) | copy-start | bytes 2752516
  152.7 6.3 %copy-start.18 = (f32[32,28,256]{2,1,0:T(8,128)}, f32[32,28,256]{2,1,0:T(8,128)S(1)}, u32[]{:S(2)}) copy-start(f32[32,28,256]{2,1,0:T(8,128)S(1)} %get-tuple-element.77) | copy-start | bytes 2752516
  163.3 19.5 %collective-permute-start.25 = (f32[4,24,256]{2,1,0:T(8,128)}, f32[4,24,256]{2,1,0:T(8,128)}, u32[]{:S(2)}, u32[]{:S(2)}) collective-permute-start(f32[4,24,256]{2,1,0:T(8,128)} %get-tuple-element.101), channel_id=1, source_target_pairs={{0,16},{16,32},{32,48},{48,64},{64,80},{80,96},{96,112},{1,17},{17... | collective-permute-start | bytes 294920 | tf_op jit(solution)/shard_map/ppermute | solution.py:30
  173.9 11.1 %collective-permute-start.24 = (f32[4,24,256]{2,1,0:T(8,128)}, f32[4,24,256]{2,1,0:T(8,128)S(1)}, u32[]{:S(2)}, u32[]{:S(2)}) collective-permute-start(f32[4,24,256]{2,1,0:T(8,128)} %get-tuple-element.100), channel_id=1, source_target_pairs={{16,0},{32,16},{48,32},{64,48},{80,64},{96,80},{112,96},{17,1},{33... | collective-permute-start | bytes 294920 | tf_op jit(solution)/shard_map/ppermute | solution.py:31
  175.2 11.9 %collective-permute-start.26 = (f32[24,4,256]{2,1,0:T(4,128)S(1)}, f32[24,4,256]{2,1,0:T(4,128)S(1)}, u32[]{:S(2)}, u32[]{:S(2)}) collective-permute-start(f32[24,4,256]{2,1,0:T(4,128)S(1)} %get-tuple-element.95), channel_id=1, source_target_pairs={{1,0},{2,1},{3,2},{4,3},{5,4},{6,5},{7,6},{8,7},{9,8},{10,9},{11,1... | collective-permute-start | bytes 294920 | tf_op jit(solution)/shard_map/ppermute | solution.py:31
  176.5 10.6 %collective-permute-start.27 = (f32[24,4,256]{2,1,0:T(4,128)S(1)}, f32[24,4,256]{2,1,0:T(4,128)S(1)}, u32[]{:S(2)}, u32[]{:S(2)}) collective-permute-start(f32[24,4,256]{2,1,0:T(4,128)S(1)} %get-tuple-element.96), channel_id=1, source_target_pairs={{0,1},{1,2},{2,3},{3,4},{4,5},{5,6},{6,7},{7,8},{8,9},{9,10},{10,1... | collective-permute-start | bytes 294920 | tf_op jit(solution)/shard_map/ppermute | solution.py:30
  196.0 17.9 %copy-start.24 = (f32[24,24,256]{2,1,0:T(8,128)}, f32[24,24,256]{2,1,0:T(8,128)S(1)}, u32[]{:S(2)}) copy-start(f32[24,24,256]{2,1,0:T(8,128)S(1)} %scatter_fusion.6) | copy-start | bytes 1769476
  196.7 15.8 %collective-permute-start.29 = (f32[4,24,256]{2,1,0:T(8,128)}, f32[4,24,256]{2,1,0:T(8,128)}, u32[]{:S(2)}, u32[]{:S(2)}) collective-permute-start(f32[4,24,256]{2,1,0:T(8,128)} %get-tuple-element.94), channel_id=1, source_target_pairs={{0,16},{16,32},{32,48},{48,64},{64,80},{80,96},{96,112},{1,17},{17... | collective-permute-start | bytes 294920 | tf_op jit(solution)/shard_map/ppermute | solution.py:30
  204.2 9.5 %collective-permute-start.30 = (f32[24,4,256]{2,1,0:T(4,128)S(1)}, f32[24,4,256]{2,1,0:T(4,128)S(1)}, u32[]{:S(2)}, u32[]{:S(2)}) collective-permute-start(f32[24,4,256]{2,1,0:T(4,128)S(1)} %get-tuple-element.91), channel_id=1, source_target_pairs={{1,0},{2,1},{3,2},{4,3},{5,4},{6,5},{7,6},{8,7},{9,8},{10,9},{11,1... | collective-permute-start | bytes 294920 | tf_op jit(solution)/shard_map/ppermute | solution.py:31
  205.5 8.1 %collective-permute-start.28 = (f32[4,24,256]{2,1,0:T(8,128)S(1)}, f32[4,24,256]{2,1,0:T(8,128)S(1)}, u32[]{:S(2)}, u32[]{:S(2)}) collective-permute-start(f32[4,24,256]{2,1,0:T(8,128)S(1)} %get-tuple-element.93), channel_id=1, source_target_pairs={{16,0},{32,16},{48,32},{64,48},{80,64},{96,80},{112,96},{17,1},{33... | collective-permute-start | bytes 294920 | tf_op jit(solution)/shard_map/ppermute | solution.py:31
  206.8 6.9 %collective-permute-start.31 = (f32[24,4,256]{2,1,0:T(4,128)S(1)}, f32[24,4,256]{2,1,0:T(4,128)S(1)}, u32[]{:S(2)}, u32[]{:S(2)}) collective-permute-start(f32[24,4,256]{2,1,0:T(4,128)S(1)} %get-tuple-element.92), channel_id=1, source_target_pairs={{0,1},{1,2},{2,3},{3,4},{4,5},{5,6},{6,7},{7,8},{8,9},{9,10},{10,1... | collective-permute-start | bytes 294920 | tf_op jit(solution)/shard_map/ppermute | solution.py:30
  215.6 10.6 %copy-start.11 = (f32[24,24,256]{2,1,0:T(8,128)S(1)}, f32[24,24,256]{2,1,0:T(8,128)}, u32[]{:S(2)}) copy-start(f32[24,24,256]{2,1,0:T(8,128)} %copy-done.8) | copy-start | bytes 1769476
  220.1 6.1 %copy-start.2 = (f32[24,24,256]{2,1,0:T(8,128)S(1)}, f32[24,24,256]{2,1,0:T(8,128)}, u32[]{:S(2)}) copy-start(f32[24,24,256]{2,1,0:T(8,128)} %copy-done.1) | copy-start | bytes 1769476
  220.1 6.1 %copy-start.6 = (f32[24,24,256]{2,1,0:T(8,128)S(1)}, f32[24,24,256]{2,1,0:T(8,128)}, u32[]{:S(2)}) copy-start(f32[24,24,256]{2,1,0:T(8,128)} %copy-done.3) | copy-start | bytes 1769476
  (95 other events, 147.7 us)
where the time goes:
time: 290 us; the launch traced here: 287 us
  starting transfers between devices  107 us (37%)
  other arithmetic  63.8 us (22%)
  local copies, waits for them, and re-layouts  59.2 us (20%)
  blocking collectives  51 us (18%)
  between operations  4.68 us (2%)
    ppermute x16, starting transfers between devices, with_halo(): lax.ppermute(last, axis, up)  86.1 us
    psum x5, blocking collectives, by_axis(): return functools.reduce(lax.psum, axes, array)  51 us
    add x8, other arithmetic, per_device(): following = 2.0 * current - previous + speed_term * laplace  31.1 us
    unnamed x238, local copies, waits for them, and re-layouts  30.2 us
    ppermute x16, starting transfers between devices, with_halo(): lax.ppermute(initial, axis, [(b, a) for a, b in up])  20.6 us
    gather x8, local copies, waits for them, and re-layouts, per_device(): following[receiver_lx, receiver_ly, receiver_z] * receiver_owned  15 us
    scatter-add x8, other arithmetic, per_device(): following.at[source_lx, source_ly, source_z]  8.39 us
    slice x16, local copies, waits for them, and re-layouts, with_halo(): initial = lax.slice_in_dim(array, 0, width, axis=dim)  7.9 us
  transfers between devices with their start and end apart: 32, of which 2 were waited for; matrix products, arithmetic and copies ran while one was open for 11% of the time, Pallas kernels for 0%

commit v1 on v0

v1 whole, which is shorter than its diff:
```python
import functools

import jax
import jax.numpy as jnp
import ml_dtypes
import numpy as np
from jax import lax
from jax.experimental import pallas as pl
from jax.experimental.pallas import tpu as pltpu
from jax.sharding import PartitionSpec as P

STEPS = 8
NSRC = 4
NREC = 64
NX = 192
NY = 384
NZ = 256
CX = 24
CY = 24
H = 4
LO = 8
LANES = 128
GX = "gx"
GY = "gy"
BOTH = (GX, GY)

first_coef = (0.8, -0.2, 4.0 / 105.0, -1.0 / 280.0)
second_coef = (1.6, -0.2, 8.0 / 315.0, -1.0 / 560.0)
centre_coef = -205.0 / 72.0
damping = 0.6

FIELD = (CX + 2 * H, 2, CY + 2 * LO, LANES)
MEM_X = (CX + 2 * H, 2, CY, LANES)
MEM_Y = (CX, 2, CY + 2 * LO, LANES)
BLOCK = (CX, 2, CY, LANES)
STRIP_X = (H, 2, CY, LANES)
STRIP_Y = (CX, 2, H, LANES)
SEEN = (2 * STEPS, LANES)


def band_matrix():
    band = np.zeros((NZ, NZ), np.float64)
    for i in range(NZ):
        band[i, i] = centre_coef
        for k in range(1, 5):
            if i + k < NZ:
                band[i + k, i] = second_coef[k - 1]
            if i - k >= 0:
                band[i - k, i] = second_coef[k - 1]
    high = band.astype(ml_dtypes.bfloat16)
    low = (band - high.astype(np.float64)).astype(ml_dtypes.bfloat16)
    return np.concatenate([high, high, low], axis=0)


def profile(position, low_width, high_width, length):
    inward_low = jnp.clip((low_width - position) / low_width, 0.0, 1.0)
    inward_high = jnp.clip((position - (length - 1 - high_width)) / high_width, 0.0, 1.0)
    return jnp.exp(-damping * (inward_low * inward_low + inward_high * inward_high))


def wide(value):
    return jnp.full((1, LANES), value, jnp.float32)


def keep_of_row(widths_ref, start_x, i):
    position = (start_x + i).astype(jnp.float32)
    low, high = (widths_ref[0].astype(jnp.float32), widths_ref[1].astype(jnp.float32))
    return profile(wide(position), wide(low), wide(high), NX)


def keep_of_columns(widths_ref, start_y):
    position = (start_y + lax.broadcasted_iota(jnp.int32, (CY, LANES), 0)).astype(jnp.float32)
    low, high = (widths_ref[2].astype(jnp.float32), widths_ref[3].astype(jnp.float32))
    return profile(position, wide(low), wide(high), NY)


def whole_sum(low_width, high_width, length):
    rows = length // LANES + (1 if length % LANES else 0)
    index = lax.broadcasted_iota(jnp.int32, (rows, LANES), 0) * LANES
    index = index + lax.broadcasted_iota(jnp.int32, (rows, LANES), 1)
    low, high = (wide(low_width.astype(jnp.float32)), wide(high_width.astype(jnp.float32)))
    value = profile(index.astype(jnp.float32), low, high, length)
    return jnp.sum(jnp.where(index < length, value, 0.0))


def place():
    gx, gy = (lax.axis_index(GX), lax.axis_index(GY))
    edge_x = (gx == 0) | (gx == lax.axis_size(GX) - 1)
    edge_y = (gy == 0) | (gy == lax.axis_size(GY) - 1)
    return gx, gy, edge_x, edge_y


def observe(field, seen, step, widths_ref, rx, ry, rz):
    gx, gy, edge_x, edge_y = place()
    start_x, start_y = (gx * CX, gy * CY)

    @pl.when(edge_x | edge_y)
    def _():
        keep_y = keep_of_columns(widths_ref, start_y)

        def add_row(i, total):
            weight = 1.0 - keep_of_row(widths_ref, start_x, i) * keep_y
            value = field[i + H, :, LO : LO + CY, :]
            return total + weight * (value[0] * value[0] + value[1] * value[1])

        total = lax.fori_loop(0, CX, add_row, jnp.zeros((CY, LANES), jnp.float32))
        sum_x = whole_sum(widths_ref[0], widths_ref[1], NX)
        sum_y = whole_sum(widths_ref[2], widths_ref[3], NY)
        normaliser = wide(float(NZ) * (float(NX * NY) - sum_x * sum_y))
        seen[STEPS + step : STEPS + step + 1, :] = jnp.sum(total, axis=0, keepdims=True) / normaliser

    lane = lax.broadcasted_iota(jnp.int32, (1, LANES), 1)

    def sample(r, carry):
        lx, ly, z = (rx[r] - start_x, ry[r] - start_y, rz[r])

        @pl.when((lx >= 0) & (lx < CX) & (ly >= 0) & (ly < CY))
        def _():
            line = field[lx + H, z >> 7, pl.ds(ly + LO, 1), :]
            turned = pltpu.roll(line, (r - (z & 127)) & 127, axis=1)
            seen[step : step + 1, :] = jnp.where(lane == r, turned, seen[step : step + 1, :])

        return carry

    lax.fori_loop(0, NREC, sample, 0)


def pack_kernel(pressure, field, up_x, down_x, up_y, down_y):
    field[...] = jnp.zeros(FIELD, jnp.float32)
    for half in range(2):
        part = pressure[:, :, half * LANES : (half + 1) * LANES]
        field[H : H + CX, half, LO : LO + CY, :] = part
    up_x[...] = field[CX : CX + H, :, LO : LO + CY, :]
    down_x[...] = field[H : 2 * H, :, LO : LO + CY, :]
    up_y[...] = field[H : H + CX, :, LO + CY - H : LO + CY, :]
    down_y[...] = field[H : H + CX, :, LO : LO + H, :]


def begin_kernel(old, speed_term, field, speed, memory_x, memory_y, zeta_x, zeta_y, seen):
    field[...] = jnp.zeros(FIELD, jnp.float32)
    for half in range(2):
        lanes = slice(half * LANES, (half + 1) * LANES)
        field[H : H + CX, half, LO : LO + CY, :] = old[:, :, lanes]
        speed[:, half, :, :] = speed_term[:, :, lanes]
    memory_x[...] = jnp.zeros(MEM_X, jnp.float32)
    memory_y[...] = jnp.zeros(MEM_Y, jnp.float32)
    zeta_x[...] = jnp.zeros(BLOCK, jnp.float32)
    zeta_y[...] = jnp.zeros(BLOCK, jnp.float32)
    seen[...] = jnp.zeros(SEEN, jnp.float32)


def inner_kernel(
    step,
    widths_ref,
    sx,
    sy,
    sz,
    amp,
    rx,
    ry,
    rz,
    band,
    current,
    speed,
    previous_in,
    memory_x_in,
    memory_y_in,
    zeta_x_in,
    zeta_y_in,
    seen_in,
    following,
    memory_x,
    memory_y,
    zeta_x,
    zeta_y,
    seen,
    bend_z,
):
    gx, gy, edge_x, edge_y = place()
    start_x, start_y = (gx * CX, gy * CY)
    halves = [current[H : H + CX, h, LO : LO + CY, :].reshape(CX * CY, LANES) for h in range(2)]
    whole = jnp.concatenate(halves, axis=1)
    high = whole.astype(jnp.bfloat16)
    low = (whole - high.astype(jnp.float32)).astype(jnp.bfloat16)
    bent = jnp.dot(
        jnp.concatenate([high, low, high], axis=1), band[...], preferred_element_type=jnp.float32
    )
    for h in range(2):
        bend_z[:, h, :, :] = bent[:, h * LANES : (h + 1) * LANES].reshape(CX, CY, LANES)

    def second_x(i):
        total = centre_coef * current[i + H, :, LO : LO + CY, :]
        for k in range(1, 5):
            pair = current[i + H + k, :, LO : LO + CY, :] + current[i + H - k, :, LO : LO + CY, :]
            total = total + second_coef[k - 1] * pair
        return total

    def second_y(i):
        total = centre_coef * current[i + H, :, LO : LO + CY, :]
        for k in range(1, 5):
            pair = current[i + H, :, LO + k : LO + CY + k, :]
            pair = pair + current[i + H, :, LO - k : LO + CY - k, :]
            total = total + second_coef[k - 1] * pair
        return total

    def first_x(ref, i, lo):
        total = 0.0
        for k in range(1, 5):
            pair = ref[i + H + k, :, lo : lo + CY, :] - ref[i + H - k, :, lo : lo + CY, :]
            total = total + first_coef[k - 1] * pair
        return total

    def first_y(ref, i, off):
        total = 0.0
        for k in range(1, 5):
            pair = ref[i + off, :, LO + k : LO + CY + k, :]
            pair = pair - ref[i + off, :, LO - k : LO + CY - k, :]
            total = total + first_coef[k - 1] * pair
        return total

    def plain(i, carry):
        laplace = second_x(i) + second_y(i) + bend_z[i]
        value = 2.0 * current[i + H, :, LO : LO + CY, :] - previous_in[i + H, :, LO : LO + CY, :]
        following[i + H, :, LO : LO + CY, :] = value + speed[i] * laplace
        return carry

    lax.fori_loop(0, CX, plain, 0)

    @pl.when(edge_x)
    def _():
        def layer(i, carry):
            keep = keep_of_row(widths_ref, start_x, i)[None]
            flux = first_x(memory_x_in, i, 0)
            bend = second_x(i) + flux
            zeta = keep * zeta_x_in[i] + (keep - 1.0) * bend
            zeta_x[i] = zeta
            inside = slice(LO, LO + CY)
            following[i + H, :, inside, :] = following[i + H, :, inside, :] + speed[i] * (flux + zeta)
            return carry

        lax.fori_loop(0, CX, layer, 0)

        def keep_memory(i, carry):
            keep = keep_of_row(widths_ref, start_x, i)[None]
            grad = first_x(current, i, LO)
            memory_x[i + H] = keep * memory_x_in[i + H] + (keep - 1.0) * grad
            return carry

        lax.fori_loop(0, CX, keep_memory, 0)

    @pl.when(edge_y)
    def _():
        keep = keep_of_columns(widths_ref, start_y)[None]

        def layer(i, carry):
            flux = first_y(memory_y_in, i, 0)
            bend = second_y(i) + flux
            zeta = keep * zeta_y_in[i] + (keep - 1.0) * bend
            zeta_y[i] = zeta
            inside = slice(LO, LO + CY)
            following[i + H, :, inside, :] = following[i + H, :, inside, :] + speed[i] * (flux + zeta)
            grad = first_y(current, i, H)
            memory_y[i, :, inside, :] = keep * memory_y_in[i, :, inside, :] + (keep - 1.0) * grad
            return carry

        lax.fori_loop(0, CX, layer, 0)

    lane = lax.broadcasted_iota(jnp.int32, (1, LANES), 1)
    for s in range(NSRC):
        lx, ly, z = (sx[s] - start_x, sy[s] - start_y, sz[s])

        @pl.when((lx >= 0) & (lx < CX) & (ly >= 0) & (ly < CY))
        def _():
            at = (lx + H, z >> 7, pl.ds(ly + LO, 1), slice(None))
            added = jnp.where(lane == (z & 127), amp[step, s], 0.0)
            following[at] = following[at] + added

    if step > 0:
        observe(current, seen, step - 1, widths_ref, rx, ry, rz)


def join_kernel(last, *refs):
    if last:
        widths_ref, rx, ry, rz, speed, lo_x, hi_x, lo_y, hi_y, _, _, field, seen, beside = refs
    else:
        speed, lo_x, hi_x, lo_y, hi_y, _, field, up_x, down_x, up_y, down_y, beside = refs
    gx, gy, _, _ = place()
    has = [
        (gx > 0).astype(jnp.float32),
        (gx < lax.axis_size(GX) - 1).astype(jnp.float32),
        (gy > 0).astype(jnp.float32),
        (gy < lax.axis_size(GY) - 1).astype(jnp.float32),
    ]
    low_x, high_x, low_y, high_y = [[e * m for e in second_coef] for m in has]
    beside[:, :, 4:8, :] = lo_y[...]
    beside[:, :, 8:16, :] = jnp.zeros((CX, 2, 8, LANES), jnp.float32)
    beside[:, :, 16:20, :] = hi_y[...]

    def ends(i):
        first, final = (0.0, 0.0)
        for k in range(1, 5):
            first = first + low_y[k - 1] * beside[i, :, 8 - k : 16 - k, :]
            final = final + high_y[k - 1] * beside[i, :, 8 + k : 16 + k, :]
        return first, final

    def inside(i, carry):
        first, final = ends(i)
        for at, extra in ((0, first), (16, final)):
            rows = slice(LO + at, LO + at + 8)
            field[i + H, :, rows, :] = (
                field[i + H, :, rows, :] + speed[i, :, at : at + 8, :] * extra
            )
        return carry

    lax.fori_loop(H, CX - H, inside, 0, unroll=4)
    for r in range(H):
        for i, coef, halo in ((r, low_x, lo_x), (CX - H + r, high_x, hi_x)):
            across = 0.0
            for k in range(1, 5):
                at = H + i - k if i < H else i + k - CX
                if 0 <= at < H:
                    across = across + coef[k - 1] * halo[at]
            first, final = ends(i)
            for at, extra in ((0, first), (8, None), (16, final)):
                rows = slice(LO + at, LO + at + 8)
                part = across[:, at : at + 8, :]
                part = part if extra is None else part + extra
                field[i + H, :, rows, :] = (
                    field[i + H, :, rows, :] + speed[i, :, at : at + 8, :] * part
                )
    if last:
        observe(field, seen, STEPS - 1, widths_ref, rx, ry, rz)
    else:
        up_x[...] = field[CX : CX + H, :, LO : LO + CY, :]
        down_x[...] = field[H : 2 * H, :, LO : LO + CY, :]
        up_y[...] = field[H : H + CX, :, LO + CY - H : LO + CY, :]
        down_y[...] = field[H : H + CX, :, LO : LO + H, :]


def finish_kernel(field, pressure):
    for half in range(2):
        part = field[H : H + CX, half, LO : LO + CY, :]
        pressure[:, :, half * LANES : (half + 1) * LANES] = part


def vmem(count):
    return [pl.BlockSpec(memory_space=pltpu.VMEM)] * count


def smem(count):
    return [pl.BlockSpec(memory_space=pltpu.SMEM)] * count


def shape(*sizes):
    return [jax.ShapeDtypeStruct(size, jnp.float32) for size in sizes]


def ring(strip, axis, by):
    size = lax.axis_size(axis)
    return lax.ppermute(strip, axis, [(i, (i + by) % size) for i in range(size)])


def exchange(strips):
    up_x, down_x, up_y, down_y = strips
    return (ring(up_x, GX, 1), ring(down_x, GX, -1), ring(up_y, GY, 1), ring(down_y, GY, -1))


def spread(value, move):
    columns = lax.axis_size(GY)
    pairs = []
    for gx in range(lax.axis_size(GX)):
        for gy in range(columns):
            to_x, to_y = move(gx, gy)
            pairs.append((gx * columns + gy, to_x * columns + to_y))
    return lax.ppermute(value, BOTH, pairs)


def move_x(by, gx, gy):
    x = ((gy // 2) % 2) * 2 + gx % 2
    x = (x + by) % 4
    return (gx // 2) * 2 + x % 2, (gy // 4) * 4 + (x // 2) * 2 + gy % 2


def total(value):
    if (lax.axis_size(GX), lax.axis_size(GY)) != (8, 16):
        return lax.psum(value, BOTH)
    value = value + spread(value, lambda gx, gy: (gx, gy ^ 1))
    parts = [spread(value, functools.partial(move_x, by)) for by in (1, 2, 3)]
    value = value + parts[0] + parts[1] + parts[2]
    parts = [spread(value, lambda gx, gy, by=by: (gx, (gy + 4 * by) % 16)) for by in (1, 2, 3)]
    value = value + parts[0] + parts[1] + parts[2]
    parts = [spread(value, lambda gx, gy, by=by: ((gx + 2 * by) % 8, gy)) for by in (1, 2, 3)]
    return value + parts[0] + parts[1] + parts[2]


def per_device(
    pressure,
    pressure_old,
    speed_term,
    layer_width,
    source_x,
    source_y,
    source_z,
    source_amp,
    receiver_x,
    receiver_y,
    receiver_z,
):
    receivers = (receiver_x, receiver_y, receiver_z)
    limit = pltpu.CompilerParams(vmem_limit_bytes=48 * 1024 * 1024)
    strips_out = shape(STRIP_X, STRIP_X, STRIP_Y, STRIP_Y)
    current, *strips = pl.pallas_call(
        pack_kernel,
        out_shape=shape(FIELD) + strips_out,
        in_specs=vmem(1),
        out_specs=vmem(5),
        compiler_params=limit,
    )(pressure)
    previous, speed, *state = pl.pallas_call(
        begin_kernel,
        out_shape=shape(FIELD, BLOCK, MEM_X, MEM_Y, BLOCK, BLOCK, SEEN),
        in_specs=vmem(2),
        out_specs=vmem(7),
        compiler_params=limit,
    )(pressure_old, speed_term)
    band = jnp.asarray(band_matrix())
    for step in range(STEPS):
        halos = exchange(strips)
        following, *state = pl.pallas_call(
            functools.partial(inner_kernel, step),
            out_shape=shape(FIELD, MEM_X, MEM_Y, BLOCK, BLOCK, SEEN),
            in_specs=smem(8) + vmem(9),
            out_specs=vmem(6),
            scratch_shapes=[pltpu.VMEM(BLOCK, jnp.float32)],
            input_output_aliases={11: 0, 12: 1, 13: 2, 14: 3, 15: 4, 16: 5},
            compiler_params=limit,
        )(
            layer_width,
            source_x,
            source_y,
            source_z,
            source_amp,
            *receivers,
            band,
            current,
            speed,
            previous,
            *state,
        )
        previous = current
        beside = pltpu.VMEM((CX, 2, 24, LANES), jnp.float32)
        if step < STEPS - 1:
            current, *strips = pl.pallas_call(
                functools.partial(join_kernel, False),
                out_shape=shape(FIELD) + strips_out,
                in_specs=vmem(6),
                out_specs=vmem(5),
                scratch_shapes=[beside],
                input_output_aliases={5: 0},
                compiler_params=limit,
            )(speed, *halos, following)
        else:
            current, seen = pl.pallas_call(
                functools.partial(join_kernel, True),
                out_shape=shape(FIELD, SEEN),
                in_specs=smem(4) + vmem(7),
                out_specs=vmem(2),
                scratch_shapes=[beside],
                input_output_aliases={9: 0, 10: 1},
                compiler_params=limit,
            )(layer_width, *receivers, speed, *halos, following, state[-1])
    final = pl.pallas_call(
        finish_kernel,
        out_shape=jax.ShapeDtypeStruct(pressure.shape, jnp.float32),
        in_specs=vmem(1),
        out_specs=pl.BlockSpec(memory_space=pltpu.VMEM),
        compiler_params=limit,
    )(current)
    seen = total(seen)
    return final, seen[:STEPS, :NREC].T, jnp.sum(seen[STEPS:], axis=1)


def solution(mesh):
    block = P(GX, GY, None)
    return jax.shard_map(
        per_device,
        mesh=mesh,
        in_specs=(block, block, block) + (P(),) * 8,
        out_specs=(block, P(), P()),
        check_vma=False,
    )
```

time: 290 us -> 172 us (0.59)
  other arithmetic: 63.8 us -> 0.64 us
  Pallas kernels: 0 us -> 61.1 us
  blocking collectives: 51 us -> 0 us
  local copies, waits for them, and re-layouts: 59.2 us -> 13.1 us
  starting transfers between devices: 107 us -> 82.3 us
  waiting for transfers between devices: 1.5 us -> 13.3 us
  between operations: 4.68 us -> 1.26 us
    pallas_call x0 -> x19, Pallas kernels: none -> 61.1 us  [the longest x8 54.9 us: per_device(): pl.pallas_call(functools.partial(inner_kernel, step), out_shape=shape(FIE...]
    psum x5 -> x0, blocking collectives: 51 us -> none  [by_axis(): return functools.reduce(lax.psum, axes, array)]
    add x16 -> x4, other arithmetic: 43.4 us -> 0.02 us  [the longest x2 0.01 us: total(): value = value + parts[0] + parts[1] + parts[2]]
    ppermute x32 -> x42, starting transfers between devices: 107 us -> 82.3 us  [the longest x32 76.1 us: ring(): lax.ppermute(strip, axis, [(i, (i + by) % size) for i in range(size)])]
    unnamed x238 -> x53, local copies, waits for them, and re-layouts: 30.2 us -> 12.5 us
    gather x8 -> x0, local copies, waits for them, and re-layouts: 15 us -> none  [per_device(): following[receiver_lx, receiver_ly, receiver_z] * receiver_owned]
    ppermute x32 -> x42, waiting for transfers between devices: 1.5 us -> 13.3 us  [the longest x10 13.2 us: spread(): return lax.ppermute(value, BOTH, pairs)]
    slice x18 -> x0, local copies, waits for them, and re-layouts: 8.8 us -> none  [the longest x16 7.9 us: with_halo(): initial = lax.slice_in_dim(array, 0, width, axis=dim)]
  transfers between devices with their start and end apart: 32 -> 42, of which waited for: 2 -> 9; matrix products, arithmetic and copies ran while one was open for 11% -> 0% of each run, Pallas kernels for 0% -> 33%
where the time goes in v1:
time: 172 us
  starting transfers between devices  82.3 us (48%)
  Pallas kernels  61.1 us (36%)
  waiting for transfers between devices  13.3 us (8%)
  local copies, waits for them, and re-layouts  13.1 us (8%)
    ppermute x32, starting transfers between devices, ring(): lax.ppermute(strip, axis, [(i, (i + by) % size) for i in range(size)])  76.1 us
    pallas_call x8, Pallas kernels, per_device(): pl.pallas_call(functools.partial(inner_kernel, step), out_shape=shape(FIE...  54.9 us
    ppermute x10, waiting for transfers between devices, spread(): return lax.ppermute(value, BOTH, pairs)  13.2 us
    unnamed x53, local copies, waits for them, and re-layouts  12.5 us
    ppermute x10, starting transfers between devices, spread(): return lax.ppermute(value, BOTH, pairs)  6.24 us
  transfers between devices with their start and end apart: 42, of which 9 were waited for; matrix products, arithmetic and copies ran while one was open for 0% of the time, Pallas kernels for 33%

profile of v1, /device:TPU:0, one launch (start us, length us, event | category | flops | bytes accessed | tf_op | source)
XLA Modules:
  0.0 171.7 jit_solution(13276001148518993579)
XLA Ops:
  0.7 1.1 copy-done.16
  1.9 1.1 copy-done
  3.0 1.6 collective-permute-start
  4.6 2.6 %collective-permute-start.1 = (f32[4,2,24,128]{3,2,1,0:T(8,128)S(1)}, f32[4,2,24,128]{3,2,1,0:T(8,128)S(1)}, u32[]{:S(2)}, u32[]{:S(2)}) collective-permute-start(f32[4,2,24,128]{3,2,1,0:T(8,128)S(1)} %get-tuple-element.98), channel_id=1, source_target_pairs={{0,112},{16,0},{32,16},{48,32},{64,48},{80,64},{96,80},{112,96},{1... | collective-permute-start | bytes 294920 | tf_op jit(solution)/shard_map/ppermute | solution.py:360
  7.1 5.5 %collective-permute-start.3 = (f32[24,2,4,128]{3,2,1,0:T(4,128)S(1)}, f32[24,2,4,128]{3,2,1,0:T(4,128)S(1)}, u32[]{:S(2)}, u32[]{:S(2)}) collective-permute-start(f32[24,2,4,128]{3,2,1,0:T(4,128)S(1)} %get-tuple-element.100), channel_id=1, source_target_pairs={{0,15},{1,0},{2,1},{3,2},{4,3},{5,4},{6,5},{7,6},{8,7},{9,8},{10,9... | collective-permute-start | bytes 294920 | tf_op jit(solution)/shard_map/ppermute | solution.py:360
  13.4 1.1 copy-done.17
  14.4 1.1 copy-done.18
  15.9 5.2 %shard_map.141 = (f32[32,2,40,128]{3,2,1,0:T(8,128)S(1)}, f32[32,2,24,128]{3,2,1,0:T(8,128)S(1)}, f32[24,2,40,128]{3,2,1,0:T(8,128)S(1)}, f32[24,2,24,128]{3,2,1...) custom-call(s32[4]{0:T(128)S(1)} %copy-done.19, ...), custom_call_target="tpu_custom_call", output_to_operand_aliasing={{0}: (11, {}), {1}: (12, {}), {2}: (13, {}), {3}: (14, {}),... | custom-call | tf_op jit(solution)/shard_map/pallas_call | solution.py:429
  21.5 1.1 copy-done.8
  22.5 4.1 %collective-permute-start.5 = (f32[4,2,24,128]{3,2,1,0:T(8,128)S(1)}, f32[4,2,24,128]{3,2,1,0:T(8,128)S(1)}, u32[]{:S(2)}, u32[]{:S(2)}) collective-permute-start(f32[4,2,24,128]{3,2,1,0:T(8,128)S(1)} %get-tuple-element.110), channel_id=1, source_target_pairs={{0,112},{16,0},{32,16},{48,32},{64,48},{80,64},{96,80},{112,96},{1... | collective-permute-start | bytes 294920 | tf_op jit(solution)/shard_map/ppermute | solution.py:360
  26.7 5.4 %collective-permute-start.7 = (f32[24,2,4,128]{3,2,1,0:T(4,128)S(1)}, f32[24,2,4,128]{3,2,1,0:T(4,128)S(1)}, u32[]{:S(2)}, u32[]{:S(2)}) collective-permute-start(f32[24,2,4,128]{3,2,1,0:T(4,128)S(1)} %get-tuple-element.112), channel_id=1, source_target_pairs={{0,15},{1,0},{2,1},{3,2},{4,3},{5,4},{6,5},{7,6},{8,7},{9,8},{10,9... | collective-permute-start | bytes 294920 | tf_op jit(solution)/shard_map/ppermute | solution.py:360
  32.0 7.1 %shard_map.143 = (f32[32,2,40,128]{3,2,1,0:T(8,128)S(1)}, f32[32,2,24,128]{3,2,1,0:T(8,128)S(1)}, f32[24,2,40,128]{3,2,1,0:T(8,128)S(1)}, f32[24,2,24,128]{3,2,1...) custom-call(s32[4]{0:T(128)S(1)} %copy-done.19, ...), custom_call_target="tpu_custom_call", output_to_operand_aliasing={{0}: (11, {}), {1}: (12, {}), {2}: (13, {}), {3}: (14, {}),... | custom-call | tf_op jit(solution)/shard_map/pallas_call | solution.py:429
  39.5 1.1 copy-done.2
  40.5 4.1 %collective-permute-start.9 = (f32[4,2,24,128]{3,2,1,0:T(8,128)S(1)}, f32[4,2,24,128]{3,2,1,0:T(8,128)S(1)}, u32[]{:S(2)}, u32[]{:S(2)}) collective-permute-start(f32[4,2,24,128]{3,2,1,0:T(8,128)S(1)} %get-tuple-element.121), channel_id=1, source_target_pairs={{0,112},{16,0},{32,16},{48,32},{64,48},{80,64},{96,80},{112,96},{1... | collective-permute-start | bytes 294920 | tf_op jit(solution)/shard_map/ppermute | solution.py:360
  44.7 5.4 %collective-permute-start.11 = (f32[24,2,4,128]{3,2,1,0:T(4,128)S(1)}, f32[24,2,4,128]{3,2,1,0:T(4,128)S(1)}, u32[]{:S(2)}, u32[]{:S(2)}) collective-permute-start(f32[24,2,4,128]{3,2,1,0:T(4,128)S(1)} %get-tuple-element.123), channel_id=1, source_target_pairs={{0,15},{1,0},{2,1},{3,2},{4,3},{5,4},{6,5},{7,6},{8,7},{9,8},{10,9... | collective-permute-start | bytes 294920 | tf_op jit(solution)/shard_map/ppermute | solution.py:360
  50.0 7.1 %shard_map.145 = (f32[32,2,40,128]{3,2,1,0:T(8,128)S(1)}, f32[32,2,24,128]{3,2,1,0:T(8,128)S(1)}, f32[24,2,40,128]{3,2,1,0:T(8,128)S(1)}, f32[24,2,24,128]{3,2,1...) custom-call(s32[4]{0:T(128)S(1)} %copy-done.19, ...), custom_call_target="tpu_custom_call", output_to_operand_aliasing={{0}: (11, {}), {1}: (12, {}), {2}: (13, {}), {3}: (14, {}),... | custom-call | tf_op jit(solution)/shard_map/pallas_call | solution.py:429
  57.5 1.1 copy-done.10
  58.6 4.1 %collective-permute-start.13 = (f32[4,2,24,128]{3,2,1,0:T(8,128)S(1)}, f32[4,2,24,128]{3,2,1,0:T(8,128)S(1)}, u32[]{:S(2)}, u32[]{:S(2)}) collective-permute-start(f32[4,2,24,128]{3,2,1,0:T(8,128)S(1)} %get-tuple-element.132), channel_id=1, source_target_pairs={{0,112},{16,0},{32,16},{48,32},{64,48},{80,64},{96,80},{112,96},{1... | collective-permute-start | bytes 294920 | tf_op jit(solution)/shard_map/ppermute | solution.py:360
  62.7 5.4 %collective-permute-start.15 = (f32[24,2,4,128]{3,2,1,0:T(4,128)S(1)}, f32[24,2,4,128]{3,2,1,0:T(4,128)S(1)}, u32[]{:S(2)}, u32[]{:S(2)}) collective-permute-start(f32[24,2,4,128]{3,2,1,0:T(4,128)S(1)} %get-tuple-element.134), channel_id=1, source_target_pairs={{0,15},{1,0},{2,1},{3,2},{4,3},{5,4},{6,5},{7,6},{8,7},{9,8},{10,9... | collective-permute-start | bytes 294920 | tf_op jit(solution)/shard_map/ppermute | solution.py:360
  68.1 7.1 %shard_map.147 = (f32[32,2,40,128]{3,2,1,0:T(8,128)S(1)}, f32[32,2,24,128]{3,2,1,0:T(8,128)S(1)}, f32[24,2,40,128]{3,2,1,0:T(8,128)S(1)}, f32[24,2,24,128]{3,2,1...) custom-call(s32[4]{0:T(128)S(1)} %copy-done.19, ...), custom_call_target="tpu_custom_call", output_to_operand_aliasing={{0}: (11, {}), {1}: (12, {}), {2}: (13, {}), {3}: (14, {}),... | custom-call | tf_op jit(solution)/shard_map/pallas_call | solution.py:429
  75.5 1.1 copy-done.4
  76.6 4.1 %collective-permute-start.17 = (f32[4,2,24,128]{3,2,1,0:T(8,128)S(1)}, f32[4,2,24,128]{3,2,1,0:T(8,128)S(1)}, u32[]{:S(2)}, u32[]{:S(2)}) collective-permute-start(f32[4,2,24,128]{3,2,1,0:T(8,128)S(1)} %get-tuple-element.143), channel_id=1, source_target_pairs={{0,112},{16,0},{32,16},{48,32},{64,48},{80,64},{96,80},{112,96},{1... | collective-permute-start | bytes 294920 | tf_op jit(solution)/shard_map/ppermute | solution.py:360
  80.7 5.4 %collective-permute-start.19 = (f32[24,2,4,128]{3,2,1,0:T(4,128)S(1)}, f32[24,2,4,128]{3,2,1,0:T(4,128)S(1)}, u32[]{:S(2)}, u32[]{:S(2)}) collective-permute-start(f32[24,2,4,128]{3,2,1,0:T(4,128)S(1)} %get-tuple-element.145), channel_id=1, source_target_pairs={{0,15},{1,0},{2,1},{3,2},{4,3},{5,4},{6,5},{7,6},{8,7},{9,8},{10,9... | collective-permute-start | bytes 294920 | tf_op jit(solution)/shard_map/ppermute | solution.py:360
  86.1 7.1 %shard_map.149 = (f32[32,2,40,128]{3,2,1,0:T(8,128)S(1)}, f32[32,2,24,128]{3,2,1,0:T(8,128)S(1)}, f32[24,2,40,128]{3,2,1,0:T(8,128)S(1)}, f32[24,2,24,128]{3,2,1...) custom-call(s32[4]{0:T(128)S(1)} %copy-done.19, ...), custom_call_target="tpu_custom_call", output_to_operand_aliasing={{0}: (11, {}), {1}: (12, {}), {2}: (13, {}), {3}: (14, {}),... | custom-call | tf_op jit(solution)/shard_map/pallas_call | solution.py:429
  93.6 1.1 copy-done.12
  94.6 4.1 %collective-permute-start.21 = (f32[4,2,24,128]{3,2,1,0:T(8,128)S(1)}, f32[4,2,24,128]{3,2,1,0:T(8,128)S(1)}, u32[]{:S(2)}, u32[]{:S(2)}) collective-permute-start(f32[4,2,24,128]{3,2,1,0:T(8,128)S(1)} %get-tuple-element.154), channel_id=1, source_target_pairs={{0,112},{16,0},{32,16},{48,32},{64,48},{80,64},{96,80},{112,96},{1... | collective-permute-start | bytes 294920 | tf_op jit(solution)/shard_map/ppermute | solution.py:360
  98.8 5.4 %collective-permute-start.23 = (f32[24,2,4,128]{3,2,1,0:T(4,128)S(1)}, f32[24,2,4,128]{3,2,1,0:T(4,128)S(1)}, u32[]{:S(2)}, u32[]{:S(2)}) collective-permute-start(f32[24,2,4,128]{3,2,1,0:T(4,128)S(1)} %get-tuple-element.156), channel_id=1, source_target_pairs={{0,15},{1,0},{2,1},{3,2},{4,3},{5,4},{6,5},{7,6},{8,7},{9,8},{10,9... | collective-permute-start | bytes 294920 | tf_op jit(solution)/shard_map/ppermute | solution.py:360
  104.1 7.1 %shard_map.151 = (f32[32,2,40,128]{3,2,1,0:T(8,128)S(1)}, f32[32,2,24,128]{3,2,1,0:T(8,128)S(1)}, f32[24,2,40,128]{3,2,1,0:T(8,128)S(1)}, f32[24,2,24,128]{3,2,1...) custom-call(s32[4]{0:T(128)S(1)} %copy-done.19, ...), custom_call_target="tpu_custom_call", output_to_operand_aliasing={{0}: (11, {}), {1}: (12, {}), {2}: (13, {}), {3}: (14, {}),... | custom-call | tf_op jit(solution)/shard_map/pallas_call | solution.py:429
  111.6 1.1 copy-done.6
  112.6 4.1 %collective-permute-start.25 = (f32[4,2,24,128]{3,2,1,0:T(8,128)S(1)}, f32[4,2,24,128]{3,2,1,0:T(8,128)S(1)}, u32[]{:S(2)}, u32[]{:S(2)}) collective-permute-start(f32[4,2,24,128]{3,2,1,0:T(8,128)S(1)} %get-tuple-element.165), channel_id=1, source_target_pairs={{0,112},{16,0},{32,16},{48,32},{64,48},{80,64},{96,80},{112,96},{1... | collective-permute-start | bytes 294920 | tf_op jit(solution)/shard_map/ppermute | solution.py:360
  116.8 5.4 %collective-permute-start.27 = (f32[24,2,4,128]{3,2,1,0:T(4,128)S(1)}, f32[24,2,4,128]{3,2,1,0:T(4,128)S(1)}, u32[]{:S(2)}, u32[]{:S(2)}) collective-permute-start(f32[24,2,4,128]{3,2,1,0:T(4,128)S(1)} %get-tuple-element.167), channel_id=1, source_target_pairs={{0,15},{1,0},{2,1},{3,2},{4,3},{5,4},{6,5},{7,6},{8,7},{9,8},{10,9... | collective-permute-start | bytes 294920 | tf_op jit(solution)/shard_map/ppermute | solution.py:360
  122.1 7.1 %shard_map.153 = (f32[32,2,40,128]{3,2,1,0:T(8,128)S(1)}, f32[32,2,24,128]{3,2,1,0:T(8,128)S(1)}, f32[24,2,40,128]{3,2,1,0:T(8,128)S(1)}, f32[24,2,24,128]{3,2,1...) custom-call(s32[4]{0:T(128)S(1)} %copy-done.19, ...), custom_call_target="tpu_custom_call", output_to_operand_aliasing={{0}: (11, {}), {1}: (12, {}), {2}: (13, {}), {3}: (14, {}),... | custom-call | tf_op jit(solution)/shard_map/pallas_call | solution.py:429
  129.6 1.1 copy-done.14
  130.7 4.1 %collective-permute-start.29 = (f32[4,2,24,128]{3,2,1,0:T(8,128)S(1)}, f32[4,2,24,128]{3,2,1,0:T(8,128)S(1)}, u32[]{:S(2)}, u32[]{:S(2)}) collective-permute-start(f32[4,2,24,128]{3,2,1,0:T(8,128)S(1)} %get-tuple-element.176), channel_id=1, source_target_pairs={{0,112},{16,0},{32,16},{48,32},{64,48},{80,64},{96,80},{112,96},{1... | collective-permute-start | bytes 294920 | tf_op jit(solution)/shard_map/ppermute | solution.py:360
  134.8 5.4 %collective-permute-start.31 = (f32[24,2,4,128]{3,2,1,0:T(4,128)S(1)}, f32[24,2,4,128]{3,2,1,0:T(4,128)S(1)}, u32[]{:S(2)}, u32[]{:S(2)}) collective-permute-start(f32[24,2,4,128]{3,2,1,0:T(4,128)S(1)} %get-tuple-element.178), channel_id=1, source_target_pairs={{0,15},{1,0},{2,1},{3,2},{4,3},{5,4},{6,5},{7,6},{8,7},{9,8},{10,9... | collective-permute-start | bytes 294920 | tf_op jit(solution)/shard_map/ppermute | solution.py:360
  140.2 7.1 %shard_map.155 = (f32[32,2,40,128]{3,2,1,0:T(8,128)S(1)}, f32[32,2,24,128]{3,2,1,0:T(8,128)S(1)}, f32[24,2,40,128]{3,2,1,0:T(8,128)S(1)}, f32[24,2,24,128]{3,2,1...) custom-call(s32[4]{0:T(128)S(1)} %copy-done.19, ...), custom_call_target="tpu_custom_call", output_to_operand_aliasing={{0}: (11, {}), {1}: (12, {}), {2}: (13, {}), {3}: (14, {}),... | custom-call | tf_op jit(solution)/shard_map/pallas_call | solution.py:429
  147.3 2.8 %shard_map.156 = (f32[32,2,40,128]{3,2,1,0:T(8,128)S(1)}, f32[16,128]{1,0:T(8,128)S(1)}) custom-call(s32[4]{0:T(128)S(1)} %copy-done.19, s32[64]{0:T(128)S(1)} %copy-done.20, s32[64]{0:T(128)S(1)} %copy-done.21, s32[64]{0:T(128)S(1)} %copy-done.22, ...), custom_call_target="tpu_custom_call", output_to_operand_aliasing={{0}: (9, {}), {1}: (10, {})} | custom-call | tf_op jit(solution)/shard_map/pallas_call | solution.py:463
  150.2 1.2 collective-permute-done.32
  151.4 2.0 %collective-permute-start.33 = (f32[16,128]{1,0:T(8,128)S(1)}, f32[16,128]{1,0:T(8,128)S(1)}, u32[]{:S(2)}, u32[]{:S(2)}) collective-permute-start(f32[16,128]{1,0:T(8,128)S(1)} %add.30), channel_id=1, source_target_pairs={{0,16},{1,17},{2,18},{3,19},{4,20},{5,21},{6,22},{7,23},{8,24},{9,... | collective-permute-start | bytes 24584 | tf_op jit(solution)/shard_map/ppermute | solution.py:375
  153.4 1.6 collective-permute-done.35
  155.0 1.5 collective-permute-done.34
  156.5 1.2 collective-permute-done.33
  157.8 1.9 %collective-permute-start.36 = (f32[16,128]{1,0:T(8,128)S(1)}, f32[16,128]{1,0:T(8,128)S(1)}, u32[]{:S(2)}, u32[]{:S(2)}) collective-permute-start(f32[16,128]{1,0:T(8,128)S(1)} %add_add_fusion.2), channel_id=1, source_target_pairs={{0,4},{1,5},{2,6},{3,7},{4,8},{5,9},{6,10},{7,11},{8,12},{9,13},{1... | collective-permute-start | bytes 24584 | tf_op jit(solution)/shard_map/ppermute | solution.py:375
  159.7 1.6 collective-permute-done.38
  161.3 1.6 collective-permute-done.37
  163.0 1.0 collective-permute-done.36
  164.0 1.2 collective-permute-start.41
  167.7 2.8 %collective-permute-done.40 = f32[16,128]{1,0:T(8,128)S(1)} collective-permute-done((f32[16,128]{1,0:T(8,128)S(1)}, f32[16,128]{1,0:T(8,128)S(1)}, u32[]{:S(2)}, u32[]{:S(2)}) %collective-permute-start.40) | collective-permute-done | bytes 8224 | tf_op jit(solution)/shard_map/ppermute | solution.py:375
  (114 shorter events, 7.4 us)
Async XLA Ops:
  0.6 15.2 %copy-start.15 = (bf16[768,256]{1,0:T(8,128)(2,1)S(1)}, bf16[768,256]{1,0:T(8,128)(2,1)}, u32[]{:S(2)}) copy-start(bf16[768,256]{1,0:T(8,128)(2,1)} %constant.4.clone.band) | copy-start | bytes 1179652
  1.8 14.1 %copy-start.21 = (s32[64]{0:T(128)S(1)}, s32[64]{0:T(128)}, u32[]{:S(2)}) copy-start(s32[64]{0:T(128)} %refs_2_.1) | copy-start | bytes 772
  1.8 14.1 %copy-start.22 = (s32[64]{0:T(128)S(1)}, s32[64]{0:T(128)}, u32[]{:S(2)}) copy-start(s32[64]{0:T(128)} %refs_3_.1) | copy-start | bytes 772
  1.8 14.1 %copy-start.23 = (s32[4]{0:T(128)S(1)}, s32[4]{0:T(128)}, u32[]{:S(2)}) copy-start(s32[4]{0:T(128)} %sx.15) | copy-start | bytes 52
  1.8 14.1 %copy-start.24 = (s32[4]{0:T(128)S(1)}, s32[4]{0:T(128)}, u32[]{:S(2)}) copy-start(s32[4]{0:T(128)} %sy.15) | copy-start | bytes 52
  1.8 14.1 %copy-start.25 = (s32[4]{0:T(128)S(1)}, s32[4]{0:T(128)}, u32[]{:S(2)}) copy-start(s32[4]{0:T(128)} %sz.15) | copy-start | bytes 52
  3.0 18.1 %collective-permute-start = (f32[4,2,24,128]{3,2,1,0:T(8,128)S(1)}, f32[4,2,24,128]{3,2,1,0:T(8,128)S(1)}, u32[]{:S(2)}, u32[]{:S(2)}) collective-permute-start(f32[4,2,24,128]{3,2,1,0:T(8,128)S(1)} %get-tuple-element.97), channel_id=1, source_target_pairs={{0,16},{16,32},{32,48},{48,64},{64,80},{80,96},{96,112},{112,0},{1... | collective-permute-start | bytes 294920 | tf_op jit(solution)/shard_map/ppermute | solution.py:360
  4.6 16.5 %collective-permute-start.1 = (f32[4,2,24,128]{3,2,1,0:T(8,128)S(1)}, f32[4,2,24,128]{3,2,1,0:T(8,128)S(1)}, u32[]{:S(2)}, u32[]{:S(2)}) collective-permute-start(f32[4,2,24,128]{3,2,1,0:T(8,128)S(1)} %get-tuple-element.98), channel_id=1, source_target_pairs={{0,112},{16,0},{32,16},{48,32},{64,48},{80,64},{96,80},{112,96},{1... | collective-permute-start | bytes 294920 | tf_op jit(solution)/shard_map/ppermute | solution.py:360
  7.1 14.0 %collective-permute-start.2 = (f32[24,2,4,128]{3,2,1,0:T(4,128)S(1)}, f32[24,2,4,128]{3,2,1,0:T(4,128)S(1)}, u32[]{:S(2)}, u32[]{:S(2)}) collective-permute-start(f32[24,2,4,128]{3,2,1,0:T(4,128)S(1)} %get-tuple-element.99), channel_id=1, source_target_pairs={{0,1},{1,2},{2,3},{3,4},{4,5},{5,6},{6,7},{7,8},{8,9},{9,10},{10,1... | collective-permute-start | bytes 294920 | tf_op jit(solution)/shard_map/ppermute | solution.py:360
  7.1 14.0 %collective-permute-start.3 = (f32[24,2,4,128]{3,2,1,0:T(4,128)S(1)}, f32[24,2,4,128]{3,2,1,0:T(4,128)S(1)}, u32[]{:S(2)}, u32[]{:S(2)}) collective-permute-start(f32[24,2,4,128]{3,2,1,0:T(4,128)S(1)} %get-tuple-element.100), channel_id=1, source_target_pairs={{0,15},{1,0},{2,1},{3,2},{4,3},{5,4},{6,5},{7,6},{8,7},{9,8},{10,9... | collective-permute-start | bytes 294920 | tf_op jit(solution)/shard_map/ppermute | solution.py:360
  22.5 16.6 %collective-permute-start.4 = (f32[4,2,24,128]{3,2,1,0:T(8,128)S(1)}, f32[4,2,24,128]{3,2,1,0:T(8,128)S(1)}, u32[]{:S(2)}, u32[]{:S(2)}) collective-permute-start(f32[4,2,24,128]{3,2,1,0:T(8,128)S(1)} %get-tuple-element.109), channel_id=1, source_target_pairs={{0,16},{16,32},{32,48},{48,64},{64,80},{80,96},{96,112},{112,0},{1... | collective-permute-start | bytes 294920 | tf_op jit(solution)/shard_map/ppermute | solution.py:360
  22.5 16.6 %collective-permute-start.5 = (f32[4,2,24,128]{3,2,1,0:T(8,128)S(1)}, f32[4,2,24,128]{3,2,1,0:T(8,128)S(1)}, u32[]{:S(2)}, u32[]{:S(2)}) collective-permute-start(f32[4,2,24,128]{3,2,1,0:T(8,128)S(1)} %get-tuple-element.110), channel_id=1, source_target_pairs={{0,112},{16,0},{32,16},{48,32},{64,48},{80,64},{96,80},{112,96},{1... | collective-permute-start | bytes 294920 | tf_op jit(solution)/shard_map/ppermute | solution.py:360
  26.7 12.5 %collective-permute-start.6 = (f32[24,2,4,128]{3,2,1,0:T(4,128)S(1)}, f32[24,2,4,128]{3,2,1,0:T(4,128)S(1)}, u32[]{:S(2)}, u32[]{:S(2)}) collective-permute-start(f32[24,2,4,128]{3,2,1,0:T(4,128)S(1)} %get-tuple-element.111), channel_id=1, source_target_pairs={{0,1},{1,2},{2,3},{3,4},{4,5},{5,6},{6,7},{7,8},{8,9},{9,10},{10,1... | collective-permute-start | bytes 294920 | tf_op jit(solution)/shard_map/ppermute | solution.py:360
  26.7 12.5 %collective-permute-start.7 = (f32[24,2,4,128]{3,2,1,0:T(4,128)S(1)}, f32[24,2,4,128]{3,2,1,0:T(4,128)S(1)}, u32[]{:S(2)}, u32[]{:S(2)}) collective-permute-start(f32[24,2,4,128]{3,2,1,0:T(4,128)S(1)} %get-tuple-element.112), channel_id=1, source_target_pairs={{0,15},{1,0},{2,1},{3,2},{4,3},{5,4},{6,5},{7,6},{8,7},{9,8},{10,9... | collective-permute-start | bytes 294920 | tf_op jit(solution)/shard_map/ppermute | solution.py:360
  40.5 16.6 %collective-permute-start.8 = (f32[4,2,24,128]{3,2,1,0:T(8,128)S(1)}, f32[4,2,24,128]{3,2,1,0:T(8,128)S(1)}, u32[]{:S(2)}, u32[]{:S(2)}) collective-permute-start(f32[4,2,24,128]{3,2,1,0:T(8,128)S(1)} %get-tuple-element.120), channel_id=1, source_target_pairs={{0,16},{16,32},{32,48},{48,64},{64,80},{80,96},{96,112},{112,0},{1... | collective-permute-start | bytes 294920 | tf_op jit(solution)/shard_map/ppermute | solution.py:360
  40.5 16.6 %collective-permute-start.9 = (f32[4,2,24,128]{3,2,1,0:T(8,128)S(1)}, f32[4,2,24,128]{3,2,1,0:T(8,128)S(1)}, u32[]{:S(2)}, u32[]{:S(2)}) collective-permute-start(f32[4,2,24,128]{3,2,1,0:T(8,128)S(1)} %get-tuple-element.121), channel_id=1, source_target_pairs={{0,112},{16,0},{32,16},{48,32},{64,48},{80,64},{96,80},{112,96},{1... | collective-permute-start | bytes 294920 | tf_op jit(solution)/shard_map/ppermute | solution.py:360
  44.7 12.5 %collective-permute-start.10 = (f32[24,2,4,128]{3,2,1,0:T(4,128)S(1)}, f32[24,2,4,128]{3,2,1,0:T(4,128)S(1)}, u32[]{:S(2)}, u32[]{:S(2)}) collective-permute-start(f32[24,2,4,128]{3,2,1,0:T(4,128)S(1)} %get-tuple-element.122), channel_id=1, source_target_pairs={{0,1},{1,2},{2,3},{3,4},{4,5},{5,6},{6,7},{7,8},{8,9},{9,10},{10,1... | collective-permute-start | bytes 294920 | tf_op jit(solution)/shard_map/ppermute | solution.py:360
  44.7 12.5 %collective-permute-start.11 = (f32[24,2,4,128]{3,2,1,0:T(4,128)S(1)}, f32[24,2,4,128]{3,2,1,0:T(4,128)S(1)}, u32[]{:S(2)}, u32[]{:S(2)}) collective-permute-start(f32[24,2,4,128]{3,2,1,0:T(4,128)S(1)} %get-tuple-element.123), channel_id=1, source_target_pairs={{0,15},{1,0},{2,1},{3,2},{4,3},{5,4},{6,5},{7,6},{8,7},{9,8},{10,9... | collective-permute-start | bytes 294920 | tf_op jit(solution)/shard_map/ppermute | solution.py:360
  58.6 16.6 %collective-permute-start.12 = (f32[4,2,24,128]{3,2,1,0:T(8,128)S(1)}, f32[4,2,24,128]{3,2,1,0:T(8,128)S(1)}, u32[]{:S(2)}, u32[]{:S(2)}) collective-permute-start(f32[4,2,24,128]{3,2,1,0:T(8,128)S(1)} %get-tuple-element.131), channel_id=1, source_target_pairs={{0,16},{16,32},{32,48},{48,64},{64,80},{80,96},{96,112},{112,0},{1... | collective-permute-start | bytes 294920 | tf_op jit(solution)/shard_map/ppermute | solution.py:360
  58.6 16.6 %collective-permute-start.13 = (f32[4,2,24,128]{3,2,1,0:T(8,128)S(1)}, f32[4,2,24,128]{3,2,1,0:T(8,128)S(1)}, u32[]{:S(2)}, u32[]{:S(2)}) collective-permute-start(f32[4,2,24,128]{3,2,1,0:T(8,128)S(1)} %get-tuple-element.132), channel_id=1, source_target_pairs={{0,112},{16,0},{32,16},{48,32},{64,48},{80,64},{96,80},{112,96},{1... | collective-permute-start | bytes 294920 | tf_op jit(solution)/shard_map/ppermute | solution.py:360
  62.7 12.5 %collective-permute-start.14 = (f32[24,2,4,128]{3,2,1,0:T(4,128)S(1)}, f32[24,2,4,128]{3,2,1,0:T(4,128)S(1)}, u32[]{:S(2)}, u32[]{:S(2)}) collective-permute-start(f32[24,2,4,128]{3,2,1,0:T(4,128)S(1)} %get-tuple-element.133), channel_id=1, source_target_pairs={{0,1},{1,2},{2,3},{3,4},{4,5},{5,6},{6,7},{7,8},{8,9},{9,10},{10,1... | collective-permute-start | bytes 294920 | tf_op jit(solution)/shard_map/ppermute | solution.py:360
  62.7 12.5 %collective-permute-start.15 = (f32[24,2,4,128]{3,2,1,0:T(4,128)S(1)}, f32[24,2,4,128]{3,2,1,0:T(4,128)S(1)}, u32[]{:S(2)}, u32[]{:S(2)}) collective-permute-start(f32[24,2,4,128]{3,2,1,0:T(4,128)S(1)} %get-tuple-element.134), channel_id=1, source_target_pairs={{0,15},{1,0},{2,1},{3,2},{4,3},{5,4},{6,5},{7,6},{8,7},{9,8},{10,9... | collective-permute-start | bytes 294920 | tf_op jit(solution)/shard_map/ppermute | solution.py:360
  76.6 16.6 %collective-permute-start.16 = (f32[4,2,24,128]{3,2,1,0:T(8,128)S(1)}, f32[4,2,24,128]{3,2,1,0:T(8,128)S(1)}, u32[]{:S(2)}, u32[]{:S(2)}) collective-permute-start(f32[4,2,24,128]{3,2,1,0:T(8,128)S(1)} %get-tuple-element.142), channel_id=1, source_target_pairs={{0,16},{16,32},{32,48},{48,64},{64,80},{80,96},{96,112},{112,0},{1... | collective-permute-start | bytes 294920 | tf_op jit(solution)/shard_map/ppermute | solution.py:360
  76.6 16.6 %collective-permute-start.17 = (f32[4,2,24,128]{3,2,1,0:T(8,128)S(1)}, f32[4,2,24,128]{3,2,1,0:T(8,128)S(1)}, u32[]{:S(2)}, u32[]{:S(2)}) collective-permute-start(f32[4,2,24,128]{3,2,1,0:T(8,128)S(1)} %get-tuple-element.143), channel_id=1, source_target_pairs={{0,112},{16,0},{32,16},{48,32},{64,48},{80,64},{96,80},{112,96},{1... | collective-permute-start | bytes 294920 | tf_op jit(solution)/shard_map/ppermute | solution.py:360
  80.7 12.5 %collective-permute-start.18 = (f32[24,2,4,128]{3,2,1,0:T(4,128)S(1)}, f32[24,2,4,128]{3,2,1,0:T(4,128)S(1)}, u32[]{:S(2)}, u32[]{:S(2)}) collective-permute-start(f32[24,2,4,128]{3,2,1,0:T(4,128)S(1)} %get-tuple-element.144), channel_id=1, source_target_pairs={{0,1},{1,2},{2,3},{3,4},{4,5},{5,6},{6,7},{7,8},{8,9},{9,10},{10,1... | collective-permute-start | bytes 294920 | tf_op jit(solution)/shard_map/ppermute | solution.py:360
  80.7 12.5 %collective-permute-start.19 = (f32[24,2,4,128]{3,2,1,0:T(4,128)S(1)}, f32[24,2,4,128]{3,2,1,0:T(4,128)S(1)}, u32[]{:S(2)}, u32[]{:S(2)}) collective-permute-start(f32[24,2,4,128]{3,2,1,0:T(4,128)S(1)} %get-tuple-element.145), channel_id=1, source_target_pairs={{0,15},{1,0},{2,1},{3,2},{4,3},{5,4},{6,5},{7,6},{8,7},{9,8},{10,9... | collective-permute-start | bytes 294920 | tf_op jit(solution)/shard_map/ppermute | solution.py:360
  94.6 16.6 %collective-permute-start.20 = (f32[4,2,24,128]{3,2,1,0:T(8,128)S(1)}, f32[4,2,24,128]{3,2,1,0:T(8,128)S(1)}, u32[]{:S(2)}, u32[]{:S(2)}) collective-permute-start(f32[4,2,24,128]{3,2,1,0:T(8,128)S(1)} %get-tuple-element.153), channel_id=1, source_target_pairs={{0,16},{16,32},{32,48},{48,64},{64,80},{80,96},{96,112},{112,0},{1... | collective-permute-start | bytes 294920 | tf_op jit(solution)/shard_map/ppermute | solution.py:360
  94.6 16.6 %collective-permute-start.21 = (f32[4,2,24,128]{3,2,1,0:T(8,128)S(1)}, f32[4,2,24,128]{3,2,1,0:T(8,128)S(1)}, u32[]{:S(2)}, u32[]{:S(2)}) collective-permute-start(f32[4,2,24,128]{3,2,1,0:T(8,128)S(1)} %get-tuple-element.154), channel_id=1, source_target_pairs={{0,112},{16,0},{32,16},{48,32},{64,48},{80,64},{96,80},{112,96},{1... | collective-permute-start | bytes 294920 | tf_op jit(solution)/shard_map/ppermute | solution.py:360
  98.8 12.5 %collective-permute-start.22 = (f32[24,2,4,128]{3,2,1,0:T(4,128)S(1)}, f32[24,2,4,128]{3,2,1,0:T(4,128)S(1)}, u32[]{:S(2)}, u32[]{:S(2)}) collective-permute-start(f32[24,2,4,128]{3,2,1,0:T(4,128)S(1)} %get-tuple-element.155), channel_id=1, source_target_pairs={{0,1},{1,2},{2,3},{3,4},{4,5},{5,6},{6,7},{7,8},{8,9},{9,10},{10,1... | collective-permute-start | bytes 294920 | tf_op jit(solution)/shard_map/ppermute | solution.py:360
  98.8 12.5 %collective-permute-start.23 = (f32[24,2,4,128]{3,2,1,0:T(4,128)S(1)}, f32[24,2,4,128]{3,2,1,0:T(4,128)S(1)}, u32[]{:S(2)}, u32[]{:S(2)}) collective-permute-start(f32[24,2,4,128]{3,2,1,0:T(4,128)S(1)} %get-tuple-element.156), channel_id=1, source_target_pairs={{0,15},{1,0},{2,1},{3,2},{4,3},{5,4},{6,5},{7,6},{8,7},{9,8},{10,9... | collective-permute-start | bytes 294920 | tf_op jit(solution)/shard_map/ppermute | solution.py:360
  112.6 16.6 %collective-permute-start.24 = (f32[4,2,24,128]{3,2,1,0:T(8,128)S(1)}, f32[4,2,24,128]{3,2,1,0:T(8,128)S(1)}, u32[]{:S(2)}, u32[]{:S(2)}) collective-permute-start(f32[4,2,24,128]{3,2,1,0:T(8,128)S(1)} %get-tuple-element.164), channel_id=1, source_target_pairs={{0,16},{16,32},{32,48},{48,64},{64,80},{80,96},{96,112},{112,0},{1... | collective-permute-start | bytes 294920 | tf_op jit(solution)/shard_map/ppermute | solution.py:360
  112.6 16.6 %collective-permute-start.25 = (f32[4,2,24,128]{3,2,1,0:T(8,128)S(1)}, f32[4,2,24,128]{3,2,1,0:T(8,128)S(1)}, u32[]{:S(2)}, u32[]{:S(2)}) collective-permute-start(f32[4,2,24,128]{3,2,1,0:T(8,128)S(1)} %get-tuple-element.165), channel_id=1, source_target_pairs={{0,112},{16,0},{32,16},{48,32},{64,48},{80,64},{96,80},{112,96},{1... | collective-permute-start | bytes 294920 | tf_op jit(solution)/shard_map/ppermute | solution.py:360
  116.8 12.5 %collective-permute-start.26 = (f32[24,2,4,128]{3,2,1,0:T(4,128)S(1)}, f32[24,2,4,128]{3,2,1,0:T(4,128)S(1)}, u32[]{:S(2)}, u32[]{:S(2)}) collective-permute-start(f32[24,2,4,128]{3,2,1,0:T(4,128)S(1)} %get-tuple-element.166), channel_id=1, source_target_pairs={{0,1},{1,2},{2,3},{3,4},{4,5},{5,6},{6,7},{7,8},{8,9},{9,10},{10,1... | collective-permute-start | bytes 294920 | tf_op jit(solution)/shard_map/ppermute | solution.py:360
  116.8 12.5 %collective-permute-start.27 = (f32[24,2,4,128]{3,2,1,0:T(4,128)S(1)}, f32[24,2,4,128]{3,2,1,0:T(4,128)S(1)}, u32[]{:S(2)}, u32[]{:S(2)}) collective-permute-start(f32[24,2,4,128]{3,2,1,0:T(4,128)S(1)} %get-tuple-element.167), channel_id=1, source_target_pairs={{0,15},{1,0},{2,1},{3,2},{4,3},{5,4},{6,5},{7,6},{8,7},{9,8},{10,9... | collective-permute-start | bytes 294920 | tf_op jit(solution)/shard_map/ppermute | solution.py:360
  130.7 16.6 %collective-permute-start.28 = (f32[4,2,24,128]{3,2,1,0:T(8,128)S(1)}, f32[4,2,24,128]{3,2,1,0:T(8,128)S(1)}, u32[]{:S(2)}, u32[]{:S(2)}) collective-permute-start(f32[4,2,24,128]{3,2,1,0:T(8,128)S(1)} %get-tuple-element.175), channel_id=1, source_target_pairs={{0,16},{16,32},{32,48},{48,64},{64,80},{80,96},{96,112},{112,0},{1... | collective-permute-start | bytes 294920 | tf_op jit(solution)/shard_map/ppermute | solution.py:360
  130.7 16.6 %collective-permute-start.29 = (f32[4,2,24,128]{3,2,1,0:T(8,128)S(1)}, f32[4,2,24,128]{3,2,1,0:T(8,128)S(1)}, u32[]{:S(2)}, u32[]{:S(2)}) collective-permute-start(f32[4,2,24,128]{3,2,1,0:T(8,128)S(1)} %get-tuple-element.176), channel_id=1, source_target_pairs={{0,112},{16,0},{32,16},{48,32},{64,48},{80,64},{96,80},{112,96},{1... | collective-permute-start | bytes 294920 | tf_op jit(solution)/shard_map/ppermute | solution.py:360
  134.8 12.5 %collective-permute-start.30 = (f32[24,2,4,128]{3,2,1,0:T(4,128)S(1)}, f32[24,2,4,128]{3,2,1,0:T(4,128)S(1)}, u32[]{:S(2)}, u32[]{:S(2)}) collective-permute-start(f32[24,2,4,128]{3,2,1,0:T(4,128)S(1)} %get-tuple-element.177), channel_id=1, source_target_pairs={{0,1},{1,2},{2,3},{3,4},{4,5},{5,6},{6,7},{7,8},{8,9},{9,10},{10,1... | collective-permute-start | bytes 294920 | tf_op jit(solution)/shard_map/ppermute | solution.py:360
  134.8 12.5 %collective-permute-start.31 = (f32[24,2,4,128]{3,2,1,0:T(4,128)S(1)}, f32[24,2,4,128]{3,2,1,0:T(4,128)S(1)}, u32[]{:S(2)}, u32[]{:S(2)}) collective-permute-start(f32[24,2,4,128]{3,2,1,0:T(4,128)S(1)} %get-tuple-element.178), channel_id=1, source_target_pairs={{0,15},{1,0},{2,1},{3,2},{4,3},{5,4},{6,5},{7,6},{8,7},{9,8},{10,9... | collective-permute-start | bytes 294920 | tf_op jit(solution)/shard_map/ppermute | solution.py:360
  150.1 1.3 collective-permute-start.32
  151.4 3.7 %collective-permute-start.35 = (f32[16,128]{1,0:T(8,128)S(1)}, f32[16,128]{1,0:T(8,128)S(1)}, u32[]{:S(2)}, u32[]{:S(2)}) collective-permute-start(f32[16,128]{1,0:T(8,128)S(1)} %add.30), channel_id=1, source_target_pairs={{0,18},{1,19},{2,16},{3,17},{4,22},{5,23},{6,20},{7,21},{8,26},{9,... | collective-permute-start | bytes 24584 | tf_op jit(solution)/shard_map/ppermute | solution.py:375
  151.4 5.2 %collective-permute-start.34 = (f32[16,128]{1,0:T(8,128)S(1)}, f32[16,128]{1,0:T(8,128)S(1)}, u32[]{:S(2)}, u32[]{:S(2)}) collective-permute-start(f32[16,128]{1,0:T(8,128)S(1)} %add.30), channel_id=1, source_target_pairs={{0,2},{1,3},{2,0},{3,1},{4,6},{5,7},{6,4},{7,5},{8,10},{9,11},{10,... | collective-permute-start | bytes 24584 | tf_op jit(solution)/shard_map/ppermute | solution.py:375
  151.4 6.3 %collective-permute-start.33 = (f32[16,128]{1,0:T(8,128)S(1)}, f32[16,128]{1,0:T(8,128)S(1)}, u32[]{:S(2)}, u32[]{:S(2)}) collective-permute-start(f32[16,128]{1,0:T(8,128)S(1)} %add.30), channel_id=1, source_target_pairs={{0,16},{1,17},{2,18},{3,19},{4,20},{5,21},{6,22},{7,23},{8,24},{9,... | collective-permute-start | bytes 24584 | tf_op jit(solution)/shard_map/ppermute | solution.py:375
  157.7 3.7 %collective-permute-start.38 = (f32[16,128]{1,0:T(8,128)S(1)}, f32[16,128]{1,0:T(8,128)S(1)}, u32[]{:S(2)}, u32[]{:S(2)}) collective-permute-start(f32[16,128]{1,0:T(8,128)S(1)} %add_add_fusion.2), channel_id=1, source_target_pairs={{0,12},{1,13},{2,14},{3,15},{4,0},{5,1},{6,2},{7,3},{8,4},{9,5},{1... | collective-permute-start | bytes 24584 | tf_op jit(solution)/shard_map/ppermute | solution.py:375
  157.7 5.3 %collective-permute-start.37 = (f32[16,128]{1,0:T(8,128)S(1)}, f32[16,128]{1,0:T(8,128)S(1)}, u32[]{:S(2)}, u32[]{:S(2)}) collective-permute-start(f32[16,128]{1,0:T(8,128)S(1)} %add_add_fusion.2), channel_id=1, source_target_pairs={{0,8},{1,9},{2,10},{3,11},{4,12},{5,13},{6,14},{7,15},{8,0},{9,1},... | collective-permute-start | bytes 24584 | tf_op jit(solution)/shard_map/ppermute | solution.py:375
  157.8 6.2 %collective-permute-start.36 = (f32[16,128]{1,0:T(8,128)S(1)}, f32[16,128]{1,0:T(8,128)S(1)}, u32[]{:S(2)}, u32[]{:S(2)}) collective-permute-start(f32[16,128]{1,0:T(8,128)S(1)} %add_add_fusion.2), channel_id=1, source_target_pairs={{0,4},{1,5},{2,6},{3,7},{4,8},{5,9},{6,10},{7,11},{8,12},{9,13},{1... | collective-permute-start | bytes 24584 | tf_op jit(solution)/shard_map/ppermute | solution.py:375
  164.0 3.7 %collective-permute-start.41 = (f32[16,128]{1,0:T(8,128)S(1)}, f32[16,128]{1,0:T(8,128)S(1)}, u32[]{:S(2)}, u32[]{:S(2)}) collective-permute-start(f32[16,128]{1,0:T(8,128)S(1)} %add_add_fusion.1), channel_id=1, source_target_pairs={{0,96},{1,97},{2,98},{3,99},{4,100},{5,101},{6,102},{7,103},{8,104... | collective-permute-start | bytes 24584 | tf_op jit(solution)/shard_map/ppermute | solution.py:375
  165.2 5.2 %collective-permute-start.40 = (f32[16,128]{1,0:T(8,128)S(1)}, f32[16,128]{1,0:T(8,128)S(1)}, u32[]{:S(2)}, u32[]{:S(2)}) collective-permute-start(f32[16,128]{1,0:T(8,128)S(1)} %add_add_fusion.1), channel_id=1, source_target_pairs={{0,64},{1,65},{2,66},{3,67},{4,68},{5,69},{6,70},{7,71},{8,72},{9,... | collective-permute-start | bytes 24584 | tf_op jit(solution)/shard_map/ppermute | solution.py:375
  165.2 5.2 %collective-permute-start.39 = (f32[16,128]{1,0:T(8,128)S(1)}, f32[16,128]{1,0:T(8,128)S(1)}, u32[]{:S(2)}, u32[]{:S(2)}) collective-permute-start(f32[16,128]{1,0:T(8,128)S(1)} %add_add_fusion.1), channel_id=1, source_target_pairs={{0,32},{1,33},{2,34},{3,35},{4,36},{5,37},{6,38},{7,39},{8,40},{9,... | collective-permute-start | bytes 24584 | tf_op jit(solution)/shard_map/ppermute | solution.py:375
  (20 other events, 116.4 us)

commit v2 on v1

v2 whole, which is shorter than its diff:
```python
import functools

import jax
import jax.numpy as jnp
import ml_dtypes
import numpy as np
from jax import lax
from jax.experimental import pallas as pl
from jax.experimental.pallas import tpu as pltpu
from jax.sharding import PartitionSpec as P

STEPS = 8
NSRC = 4
NREC = 64
NX = 192
NY = 384
NZ = 256
CX = 24
CY = 24
H = 4
LO = 8
LANES = 128
GX = "gx"
GY = "gy"
BOTH = (GX, GY)

first_coef = (0.8, -0.2, 4.0 / 105.0, -1.0 / 280.0)
second_coef = (1.6, -0.2, 8.0 / 315.0, -1.0 / 560.0)
centre_coef = -205.0 / 72.0
damping = 0.6

FIELD = (CX + 2 * H, 2, CY + 2 * LO, LANES)
MEM_X = (2, CX + 2 * H, 2, CY, LANES)
MEM_Y = (CX, 2, CY + 2 * LO, LANES)
BLOCK = (CX, 2, CY, LANES)
STRIP_X = (H, 2, CY, LANES)
STRIP_Y = (CX, 2, H, LANES)
SEEN = (2 * STEPS, LANES)
KEEP_X = (CX, CY, LANES)
KEEP_Y = (CY, LANES)
NORM = (1, LANES)
RECEIVERS = 8
TABLE = RECEIVERS + NREC
COMMON = 5040.0
CHUNKS = 4
INSIDE = slice(LO, LO + CY)


def band_matrix():
    band = np.zeros((NZ, NZ), np.float32)
    for k, tap in enumerate((8064.0, -1008.0, 128.0, -9.0)):
        band += tap * (np.eye(NZ, k=k + 1) + np.eye(NZ, k=-k - 1)).astype(np.float32)
    return np.concatenate([band, band], axis=0).astype(ml_dtypes.bfloat16)


def profile(position, low_width, high_width, length):
    inward_low = jnp.clip((low_width - position) / low_width, 0.0, 1.0)
    inward_high = jnp.clip((position - (length - 1 - high_width)) / high_width, 0.0, 1.0)
    return jnp.exp(-damping * (inward_low * inward_low + inward_high * inward_high))


def wide(value):
    return jnp.full((1, LANES), value, jnp.float32)


def keep_of(widths, start, dims, dim, length):
    position = start + lax.broadcasted_iota(jnp.int32, dims, dim)
    low, high = [jnp.full(dims, w, jnp.float32) for w in widths]
    return profile(position.astype(jnp.float32), low, high, length)


def whole_sum(widths, length):
    rows = -(-length // LANES)
    index = lax.broadcasted_iota(jnp.int32, (rows, LANES), 0) * LANES
    index = index + lax.broadcasted_iota(jnp.int32, (rows, LANES), 1)
    value = profile(index.astype(jnp.float32), wide(widths[0]), wide(widths[1]), length)
    return jnp.sum(jnp.where(index < length, value, 0.0))


def place():
    gx, gy = (lax.axis_index(GX), lax.axis_index(GY))
    edge_x = (gx == 0) | (gx == lax.axis_size(GX) - 1)
    edge_y = (gy == 0) | (gy == lax.axis_size(GY) - 1)
    return gx, gy, edge_x, edge_y


def energy_row(field, i, keep_x, keep_y):
    weight = 1.0 - keep_x[i] * keep_y[...]
    value = field[i + H, :, INSIDE, :]
    return weight * (value[0] * value[0] + value[1] * value[1])


def note_energy(seen, step, summed, norm):
    at = STEPS + step
    seen[at : at + 1, :] = jnp.sum(summed, axis=0, keepdims=True) / norm[...]


def note_traces(field, seen, step, table):
    lane = lax.broadcasted_iota(jnp.int32, (1, LANES), 1)

    def sample(n, carry):
        code = table[RECEIVERS + n]
        r, z, ly, lx = (code & 63, (code >> 6) & 255, (code >> 14) & 31, code >> 19)
        line = field[lx + H, z >> 7, pl.ds(ly + LO, 1), :]
        turned = pltpu.roll(line, (r - (z & 127)) & 127, axis=1)
        seen[step : step + 1, :] = jnp.where(lane == r, turned, seen[step : step + 1, :])
        return carry

    lax.fori_loop(0, table[0], sample, 0)


def fetch(pairs, sems):
    copies = []
    for n, (source, target) in enumerate(pairs):
        for c in range(CHUNKS):
            rows = pl.ds(c * (CX // CHUNKS), CX // CHUNKS)
            copies.append(pltpu.make_async_copy(source.at[rows], target.at[rows], sems.at[n, c]))
    for copy in copies:
        copy.start()
    return copies


def split_strips(field, mine_x, mine_y, near_x, far_x, near_y, far_y):
    rows = [field[CX : CX + H, :, INSIDE, :], field[H : 2 * H, :, INSIDE, :]]
    near_x[...] = jnp.where(mine_x, rows[1], rows[0])
    far_x[...] = jnp.where(mine_x, rows[0], rows[1])
    high, low = (LO + CY - H, LO)
    columns = [field[H : H + CX, :, at : at + H, :] for at in (high, low)]
    near_y[...] = jnp.where(mine_y, columns[1], columns[0])
    far_y[...] = jnp.where(mine_y, columns[0], columns[1])


def odd():
    return lax.axis_index(GX) % 2 == 1, lax.axis_index(GY) % 2 == 1


def pack_kernel(pressure, field, near_x, far_x, near_y, far_y, staged, sems):
    copies = fetch([(pressure, staged)], sems)
    field[...] = jnp.zeros(FIELD, jnp.float32)
    for copy in copies:
        copy.wait()
    for half in range(2):
        part = staged[:, :, half * LANES : (half + 1) * LANES]
        field[H : H + CX, half, INSIDE, :] = part
    split_strips(field, *odd(), near_x, far_x, near_y, far_y)


def begin_kernel(
    widths_ref, sx, sy, sz, rx, ry, rz, old, speed_term,
    field, speed, memory_x, memory_y, zeta_x, zeta_y, seen, keep_x, keep_y, norm, table,
    staged_old, staged_speed, sems,
):
    copies = fetch([(old, staged_old), (speed_term, staged_speed)], sems)
    gx, gy, edge_x, edge_y = place()
    start_x, start_y = (gx * CX, gy * CY)
    seen[...] = jnp.zeros(SEEN, jnp.float32)
    field[...] = jnp.zeros(FIELD, jnp.float32)

    @pl.when(edge_x)
    def _():
        memory_x[...] = jnp.zeros(MEM_X, jnp.float32)
        zeta_x[...] = jnp.zeros(BLOCK, jnp.float32)

    @pl.when(edge_y)
    def _():
        memory_y[...] = jnp.zeros(MEM_Y, jnp.float32)
        zeta_y[...] = jnp.zeros(BLOCK, jnp.float32)

    @pl.when(edge_x | edge_y)
    def _():
        widths = [widths_ref[n].astype(jnp.float32) for n in range(4)]
        keep_x[...] = keep_of(widths[:2], start_x, KEEP_X, 0, NX)
        keep_y[...] = keep_of(widths[2:], start_y, KEEP_Y, 0, NY)
        cells = float(NX * NY) - whole_sum(widths[:2], NX) * whole_sum(widths[2:], NY)
        norm[...] = wide(float(NZ) * cells)

    def owned(px, py):
        lx, ly = (px - start_x, py - start_y)
        return lx, ly, (lx >= 0) & (lx < CX) & (ly >= 0) & (ly < CY)

    def add_receiver(r, count):
        lx, ly, here = owned(rx[r], ry[r])

        @pl.when(here)
        def _():
            table[RECEIVERS + count] = (((lx << 5) + ly) << 14) + (rz[r] << 6) + r

        return count + here.astype(jnp.int32)

    table[0] = lax.fori_loop(0, NREC, add_receiver, 0)

    def add_source(s, count):
        lx, ly, here = owned(sx[s], sy[s])

        @pl.when(here)
        def _():
            table[4 + count] = (((lx << 5) + ly) << 14) + (sz[s] << 6) + s

        return count + here.astype(jnp.int32)

    table[1] = lax.fori_loop(0, NSRC, add_source, 0)
    for copy in copies:
        copy.wait()
    for half in range(2):
        lanes = slice(half * LANES, (half + 1) * LANES)
        field[H : H + CX, half, INSIDE, :] = staged_old[:, :, lanes]
        speed[:, half, :, :] = staged_speed[:, :, lanes]


def inner_kernel(
    step, table, amp, band, current, speed, keep_x, keep_y, norm,
    previous, memory_x_in, memory_y_in, zeta_x_in, zeta_y_in, seen_in,
    following, memory_x, memory_y, zeta_x, zeta_y, seen, bend_z,
):
    _, _, edge_x, edge_y = place()
    halves = [current[H : H + CX, h, INSIDE, :].reshape(CX * CY, LANES) for h in range(2)]
    whole = jnp.concatenate(halves, axis=1)
    high = whole.astype(jnp.bfloat16)
    low = (whole - high.astype(jnp.float32)).astype(jnp.bfloat16)
    bent = jnp.dot(
        jnp.concatenate([high, low], axis=1), band[...], preferred_element_type=jnp.float32
    )
    for h in range(2):
        bend_z[:, h, :, :] = bent[:, h * LANES : (h + 1) * LANES].reshape(CX, CY, LANES)
    source, target = (step % 2, 1 - step % 2)

    def shifted_x(ref, lead, i, inside, k):
        return ref[lead + (i + k, slice(None), inside)]

    def sum_x(ref, lead, i, inside, sign, coef):
        total = 0.0
        for k in range(1, 5):
            up, down = (shifted_x(ref, lead, i, inside, k), shifted_x(ref, lead, i, inside, -k))
            total = total + coef[k - 1] * (up + down if sign > 0 else up - down)
        return total

    def sum_y(ref, i, sign, coef):
        total = 0.0
        for k in range(1, 5):
            up, down = (ref[i, :, LO + k : LO + CY + k, :], ref[i, :, LO - k : LO + CY - k, :])
            total = total + coef[k - 1] * (up + down if sign > 0 else up - down)
        return total

    def row(in_x, in_y, i, energy):
        centre = current[i + H, :, INSIDE, :]
        second_x = sum_x(current, (), i + H, INSIDE, 1, second_coef)
        second_y = sum_y(current, i + H, 1, second_coef)
        laplace = second_x + second_y + (3.0 * centre_coef) * centre + bend_z[i] * (1.0 / COMMON)
        every = slice(0, CY)
        if in_x:
            keep = keep_x[i]
            take = keep - 1.0
            flux = sum_x(memory_x_in, (source,), i + H, every, -1, first_coef)
            bend = second_x + centre_coef * centre + flux
            zeta = keep * zeta_x_in[i] + take * bend
            zeta_x[i] = zeta
            laplace = laplace + (flux + zeta)
            grad = sum_x(current, (), i + H, INSIDE, -1, first_coef)
            memory_x[target, i + H] = keep * memory_x_in[source, i + H] + take * grad
        if in_y:
            keep = keep_y[...]
            take = keep - 1.0
            flux = sum_y(memory_y_in, i, -1, first_coef)
            bend = second_y + centre_coef * centre + flux
            zeta = keep * zeta_y_in[i] + take * bend
            zeta_y[i] = zeta
            laplace = laplace + (flux + zeta)
            grad = sum_y(current, i + H, -1, first_coef)
            memory_y[i, :, INSIDE, :] = keep * memory_y_in[i, :, INSIDE, :] + take * grad
        value = 2.0 * centre - previous[i + H, :, INSIDE, :]
        following[i + H, :, INSIDE, :] = value + speed[i] * laplace
        if step > 0 and (in_x or in_y):
            energy = energy + energy_row(current, i, keep_x, keep_y)
        return energy

    for in_x in (False, True):
        for in_y in (False, True):

            @pl.when((edge_x == in_x) & (edge_y == in_y))
            def _():
                zero = jnp.zeros((CY, LANES), jnp.float32) if in_x or in_y else 0
                body = functools.partial(row, in_x, in_y)
                energy = lax.fori_loop(0, CX, body, zero, unroll=1 if in_x or in_y else 2)
                if step > 0 and (in_x or in_y):
                    note_energy(seen, step - 1, energy, norm)

    lane = lax.broadcasted_iota(jnp.int32, (1, LANES), 1)

    def inject(n, carry):
        code = table[4 + n]
        s, z, ly, lx = (code & 63, (code >> 6) & 255, (code >> 14) & 31, code >> 19)
        at = (lx + H, z >> 7, pl.ds(ly + LO, 1), slice(None))
        following[at] = following[at] + jnp.where(lane == (z & 127), amp[step, s], 0.0)
        return carry

    lax.fori_loop(0, table[1], inject, 0)
    if step > 0:
        note_traces(current, seen, step - 1, table)


def join_kernel(last, *refs):
    if last:
        table, keep_x, keep_y, norm, speed, near_x, far_x, near_y, far_y, _, _ = refs[:11]
        field, seen, beside = refs[11:]
    else:
        speed, near_x, far_x, near_y, far_y, _, field = refs[:7]
        strips, beside = (refs[7:11], refs[11])
    gx, gy, edge_x, edge_y = place()
    mine_x, mine_y = odd()
    halo_x = [jnp.where(mine_x, near_x[...], far_x[...]), jnp.where(mine_x, far_x[...], near_x[...])]
    has = [
        (gx > 0).astype(jnp.float32),
        (gx < lax.axis_size(GX) - 1).astype(jnp.float32),
        (gy > 0).astype(jnp.float32),
        (gy < lax.axis_size(GY) - 1).astype(jnp.float32),
    ]
    low_x, high_x, low_y, high_y = [[e * m for e in second_coef] for m in has]
    beside[:, :, 4:8, :] = jnp.where(mine_y, near_y[...], far_y[...])
    beside[:, :, 8:16, :] = jnp.zeros((CX, 2, 8, LANES), jnp.float32)
    beside[:, :, 16:20, :] = jnp.where(mine_y, far_y[...], near_y[...])

    def ends(i):
        first, final = (0.0, 0.0)
        for k in range(1, 5):
            first = first + low_y[k - 1] * beside[i, :, 8 - k : 16 - k, :]
            final = final + high_y[k - 1] * beside[i, :, 8 + k : 16 + k, :]
        return first, final

    def inside(i, carry):
        first, final = ends(i)
        for at, extra in ((0, first), (16, final)):
            rows = slice(LO + at, LO + at + 8)
            field[i + H, :, rows, :] = (
                field[i + H, :, rows, :] + speed[i, :, at : at + 8, :] * extra
            )
        return carry

    lax.fori_loop(H, CX - H, inside, 0, unroll=4)
    for r in range(H):
        for i, coef, halo in ((r, low_x, halo_x[0]), (CX - H + r, high_x, halo_x[1])):
            across = 0.0
            for k in range(1, 5):
                at = H + i - k if i < H else i + k - CX
                if 0 <= at < H:
                    across = across + coef[k - 1] * halo[at]
            first, final = ends(i)
            for at, extra in ((0, first), (8, None), (16, final)):
                rows = slice(LO + at, LO + at + 8)
                part = across[:, at : at + 8, :]
                part = part if extra is None else part + extra
                field[i + H, :, rows, :] = (
                    field[i + H, :, rows, :] + speed[i, :, at : at + 8, :] * part
                )
    if not last:
        split_strips(field, mine_x, mine_y, *strips)
        return

    @pl.when(edge_x | edge_y)
    def _():
        add = lambda i, summed: summed + energy_row(field, i, keep_x, keep_y)
        zero = jnp.zeros((CY, LANES), jnp.float32)
        note_energy(seen, STEPS - 1, lax.fori_loop(0, CX, add, zero, unroll=4), norm)

    note_traces(field, seen, STEPS - 1, table)


def finish_kernel(field, pressure):
    for half in range(2):
        part = field[H : H + CX, half, INSIDE, :]
        pressure[:, :, half * LANES : (half + 1) * LANES] = part


def report_kernel(*refs):
    parts, (traces, energy) = (refs[:-2], refs[-2:])
    seen = parts[0][...]
    for part in parts[1:]:
        seen = seen + part[...]
    turned = seen.T
    traces[...] = turned[:NREC, :STEPS]
    energy[...] = jnp.sum(turned[:, STEPS:], axis=0, keepdims=True)


def vmem(count):
    return [pl.BlockSpec(memory_space=pltpu.VMEM)] * count


def smem(count):
    return [pl.BlockSpec(memory_space=pltpu.SMEM)] * count


def hbm(count):
    return [pl.BlockSpec(memory_space=pl.ANY)] * count


def shape(*sizes):
    return [jax.ShapeDtypeStruct(size, jnp.float32) for size in sizes]


def limit(mebibytes):
    return pltpu.CompilerParams(vmem_limit_bytes=mebibytes * 1024 * 1024)


def swap(strip, axis, far):
    size = lax.axis_size(axis)
    return lax.ppermute(strip, axis, [(i, (((i + far) ^ 1) - far) % size) for i in range(size)])


def exchange(strips):
    near_x, far_x, near_y, far_y = strips
    return (swap(near_x, GX, 0), swap(far_x, GX, 1), swap(near_y, GY, 0), swap(far_y, GY, 1))


def spread(value, by):
    columns = lax.axis_size(GY)
    pairs = []
    for gx in range(lax.axis_size(GX)):
        for gy in range(columns):
            pairs.append((gx * columns + gy, (gx ^ by[0]) * columns + (gy ^ by[1])))
    return lax.ppermute(value, BOTH, pairs)


def gather_sums(value):
    if (lax.axis_size(GX), lax.axis_size(GY)) != (8, 16):
        return [lax.psum(value, BOTH)]
    parts = [value, spread(value, (0, 1))]
    for flips in (((1, 0), (0, 2), (1, 2)), ((0, 4), (0, 8), (0, 12)), ((2, 0), (4, 0), (6, 0))):
        value = functools.reduce(jnp.add, parts)
        parts = [value] + [spread(value, by) for by in flips]
    return parts


def per_device(
    pressure,
    pressure_old,
    speed_term,
    layer_width,
    source_x,
    source_y,
    source_z,
    source_amp,
    receiver_x,
    receiver_y,
    receiver_z,
):
    staged = pltpu.VMEM(pressure.shape, jnp.float32)
    strips_out = shape(STRIP_X, STRIP_X, STRIP_Y, STRIP_Y)
    current, *strips = pl.pallas_call(
        pack_kernel,
        out_shape=shape(FIELD) + strips_out,
        in_specs=hbm(1),
        out_specs=vmem(5),
        scratch_shapes=[staged, pltpu.SemaphoreType.DMA((1, CHUNKS))],
        compiler_params=limit(8),
    )(pressure)
    previous, speed, *rest = pl.pallas_call(
        begin_kernel,
        out_shape=shape(FIELD, BLOCK, MEM_X, MEM_Y, BLOCK, BLOCK, SEEN, KEEP_X, KEEP_Y, NORM)
        + [jax.ShapeDtypeStruct((TABLE,), jnp.int32)],
        in_specs=smem(7) + hbm(2),
        out_specs=vmem(10) + smem(1),
        scratch_shapes=[staged, staged, pltpu.SemaphoreType.DMA((2, CHUNKS))],
        compiler_params=limit(8),
    )(
        layer_width,
        source_x,
        source_y,
        source_z,
        receiver_x,
        receiver_y,
        receiver_z,
        pressure_old,
        speed_term,
    )
    state, keeps, table = (rest[:5], rest[5:8], rest[8])
    band = jnp.asarray(band_matrix())
    beside = pltpu.VMEM((CX, 2, 24, LANES), jnp.float32)
    for step in range(STEPS):
        halos = exchange(strips)
        following, *state = pl.pallas_call(
            functools.partial(inner_kernel, step),
            out_shape=shape(FIELD, MEM_X, MEM_Y, BLOCK, BLOCK, SEEN),
            in_specs=smem(2) + vmem(12),
            out_specs=vmem(6),
            scratch_shapes=[pltpu.VMEM(BLOCK, jnp.float32)],
            input_output_aliases={8: 0, 9: 1, 10: 2, 11: 3, 12: 4, 13: 5},
            compiler_params=limit(8),
        )(table, source_amp, band, current, speed, *keeps, previous, *state)
        previous = current
        if step < STEPS - 1:
            current, *strips = pl.pallas_call(
                functools.partial(join_kernel, False),
                out_shape=shape(FIELD) + strips_out,
                in_specs=vmem(6),
                out_specs=vmem(5),
                scratch_shapes=[beside],
                input_output_aliases={5: 0},
                compiler_params=limit(4),
            )(speed, *halos, following)
        else:
            current, seen = pl.pallas_call(
                functools.partial(join_kernel, True),
                out_shape=shape(FIELD, SEEN),
                in_specs=smem(1) + vmem(10),
                out_specs=vmem(2),
                scratch_shapes=[beside],
                input_output_aliases={9: 0, 10: 1},
                compiler_params=limit(4),
            )(table, *keeps, speed, *halos, following, state[-1])
    final = pl.pallas_call(
        finish_kernel,
        out_shape=jax.ShapeDtypeStruct(pressure.shape, jnp.float32),
        in_specs=vmem(1),
        out_specs=pl.BlockSpec(memory_space=pltpu.VMEM),
        compiler_params=limit(4),
    )(current)
    parts = gather_sums(seen)
    traces, energy = pl.pallas_call(
        report_kernel,
        out_shape=shape((NREC, STEPS), (1, STEPS)),
        in_specs=vmem(len(parts)),
        out_specs=vmem(2),
        compiler_params=limit(2),
    )(*parts)
    return final, traces, energy.reshape(STEPS)


def solution(mesh):
    block = P(GX, GY, None)
    return jax.shard_map(
        per_device,
        mesh=mesh,
        in_specs=(block, block, block) + (P(),) * 8,
        out_specs=(block, P(), P()),
        check_vma=False,
    )
```

time: 172 us -> 128 us (0.74)
  starting transfers between devices: 82.3 us -> 55.5 us
  Pallas kernels: 61.1 us -> 36.5 us
  waiting for transfers between devices: 13.3 us -> 25.8 us
  local copies, waits for them, and re-layouts: 13.1 us -> 9.23 us
    ppermute x32, starting transfers between devices: 76.1 us -> 42.4 us  [swap(): lax.ppermute(strip, axis, [(i, ((i + far ^ 1) - far) % size) for i in ran...]
    pallas_call x8, Pallas kernels: 54.9 us -> 26.3 us  [per_device(): pl.pallas_call(functools.partial(inner_kernel, step), out_shape=shape(FIE...]
    ppermute x32, waiting for transfers between devices: 0.08 us -> 17 us  [swap(): lax.ppermute(strip, axis, [(i, ((i + far ^ 1) - far) % size) for i in ran...]
    ppermute x10, starting transfers between devices: 6.24 us -> 13.1 us  [spread(): return lax.ppermute(value, BOTH, pairs)]
    ppermute x10, waiting for transfers between devices: 13.2 us -> 8.86 us  [spread(): return lax.ppermute(value, BOTH, pairs)]
    pallas_call x1, Pallas kernels: 0.32 us -> 4.64 us  [per_device(): pl.pallas_call(begin_kernel, out_shape=shape(FIELD, BLOCK, MEM_X, MEM_Y,...]
    unnamed x53 -> x24, local copies, waits for them, and re-layouts: 12.5 us -> 9.23 us
    pallas_call x1, Pallas kernels: 2.77 us -> 0.91 us  [per_device(): pl.pallas_call(functools.partial(join_kernel, True), out_shape=shape(FIEL...]
  transfers between devices with their start and end apart: 42 -> 42, of which waited for: 9 -> 20; matrix products, arithmetic and copies ran while one was open for 0% -> 1% of each run, Pallas kernels for 33% -> 25%
where the time goes in v2:
time: 128 us
  starting transfers between devices  55.5 us (43%)
  Pallas kernels  36.5 us (29%)
  waiting for transfers between devices  25.8 us (20%)
  local copies, waits for them, and re-layouts  9.23 us (7%)
    ppermute x32, starting transfers between devices, swap(): lax.ppermute(strip, axis, [(i, ((i + far ^ 1) - far) % size) for i in ran...  42.4 us
    pallas_call x8, Pallas kernels, per_device(): pl.pallas_call(functools.partial(inner_kernel, step), out_shape=shape(FIE...  26.3 us
    ppermute x32, waiting for transfers between devices, swap(): lax.ppermute(strip, axis, [(i, ((i + far ^ 1) - far) % size) for i in ran...  17 us
    ppermute x10, starting transfers between devices, spread(): return lax.ppermute(value, BOTH, pairs)  13.1 us
    unnamed x24, local copies, waits for them, and re-layouts  9.23 us
    ppermute x10, waiting for transfers between devices, spread(): return lax.ppermute(value, BOTH, pairs)  8.86 us
    pallas_call x1, Pallas kernels, per_device(): pl.pallas_call(begin_kernel, out_shape=shape(FIELD, BLOCK, MEM_X, MEM_Y,...  4.64 us
  transfers between devices with their start and end apart: 42, of which 20 were waited for; matrix products, arithmetic and copies ran while one was open for 1% of the time, Pallas kernels for 25%

profile of v2, /device:TPU:0, one launch (start us, length us, event | category | flops | bytes accessed | tf_op | source)
XLA Modules:
  0.0 128.0 jit_solution(6684509002046362808)
XLA Ops:
  0.7 1.1 copy-done.3
  1.7 0.9 shard_map.140
  2.7 1.7 %collective-permute-start = (f32[4,2,24,128]{3,2,1,0:T(8,128)S(1)}, f32[4,2,24,128]{3,2,1,0:T(8,128)S(1)}, u32[]{:S(2)}, u32[]{:S(2)}) collective-permute-start(f32[4,2,24,128]{3,2,1,0:T(8,128)S(1)} %get-tuple-element.107), channel_id=1, source_target_pairs={{0,16},{16,0},{32,48},{48,32},{64,80},{80,64},{96,112},{112,96},{1... | collective-permute-start | bytes 294920 | tf_op jit(solution)/shard_map/ppermute | solution.py:405
  4.3 3.0 %collective-permute-start.1 = (f32[4,2,24,128]{3,2,1,0:T(8,128)S(1)}, f32[4,2,24,128]{3,2,1,0:T(8,128)S(1)}, u32[]{:S(2)}, u32[]{:S(2)}) collective-permute-start(f32[4,2,24,128]{3,2,1,0:T(8,128)S(1)} %get-tuple-element.108), channel_id=1, source_target_pairs={{0,112},{16,32},{32,16},{48,64},{64,48},{80,96},{96,80},{112,0},{1... | collective-permute-start | bytes 294920 | tf_op jit(solution)/shard_map/ppermute | solution.py:405
  7.3 6.6 %collective-permute-start.3 = (f32[24,2,4,128]{3,2,1,0:T(4,128)S(1)}, f32[24,2,4,128]{3,2,1,0:T(4,128)S(1)}, u32[]{:S(2)}, u32[]{:S(2)}) collective-permute-start(f32[24,2,4,128]{3,2,1,0:T(4,128)S(1)} %get-tuple-element.110), channel_id=1, source_target_pairs={{0,15},{1,2},{2,1},{3,4},{4,3},{5,6},{6,5},{7,8},{8,7},{9,10},{10,... | collective-permute-start | bytes 294920 | tf_op jit(solution)/shard_map/ppermute | solution.py:405
  14.7 1.1 copy-done.1
  15.8 1.1 copy-done.2
  21.4 4.6 %shard_map.139 = (f32[32,2,40,128]{3,2,1,0:T(8,128)S(1)}, f32[24,2,24,128]{3,2,1,0:T(8,128)S(1)}, f32[2,32,2,24,128]{4,3,2,1,0:T(8,128)S(1)}, f32[24,2,40,128]{3...) custom-call(s32[4]{0:T(128)S(1)} %copy-done.4, ...), custom_call_target="tpu_custom_call" | custom-call | tf_op jit(solution)/shard_map/pallas_call | solution.py:455
  26.1 3.2 %shard_map.141 = (f32[32,2,40,128]{3,2,1,0:T(8,128)S(1)}, f32[2,32,2,24,128]{4,3,2,1,0:T(8,128)S(1)}, f32[24,2,40,128]{3,2,1,0:T(8,128)S(1)}, f32[24,2,24,128]{3...) custom-call(s32[72]{0:T(128)S(1)} %get-tuple-element.102.table.refs_, ...), custom_call_target="tpu_custom_call", output_to_operand_aliasing={{0}: (8, {}), {1}: (9, {}), {2}: (10, {}), {3}: (11, {}), {... | custom-call | tf_op jit(solution)/shard_map/pallas_call | solution.py:479
  29.8 1.3 %collective-permute-start.5 = (f32[4,2,24,128]{3,2,1,0:T(8,128)S(1)}, f32[4,2,24,128]{3,2,1,0:T(8,128)S(1)}, u32[]{:S(2)}, u32[]{:S(2)}) collective-permute-start(f32[4,2,24,128]{3,2,1,0:T(8,128)S(1)} %get-tuple-element.120), channel_id=1, source_target_pairs={{0,112},{16,32},{32,16},{48,64},{64,48},{80,96},{96,80},{112,0},{1... | collective-permute-start | bytes 294920 | tf_op jit(solution)/shard_map/ppermute | solution.py:405
  31.4 3.3 %shard_map.143 = (f32[32,2,40,128]{3,2,1,0:T(8,128)S(1)}, f32[2,32,2,24,128]{4,3,2,1,0:T(8,128)S(1)}, f32[24,2,40,128]{3,2,1,0:T(8,128)S(1)}, f32[24,2,24,128]{3...) custom-call(s32[72]{0:T(128)S(1)} %get-tuple-element.102.table.refs_, ...), custom_call_target="tpu_custom_call", output_to_operand_aliasing={{0}: (8, {}), {1}: (9, {}), {2}: (10, {}), {3}: (11, {}), {... | custom-call | tf_op jit(solution)/shard_map/pallas_call | solution.py:479
  35.2 2.2 %collective-permute-done.5.refs_2_ = f32[4,2,24,128]{3,2,1,0:T(8,128)S(1)} collective-permute-done((f32[4,2,24,128]{3,2,1,0:T(8,128)S(1)}, f32[4,2,24,128]{3,2,1,0:T(8,128)S(1)}, u32[]{:S(2)}, u32[]{:S(2)}) %collective-permute-start.5) | collective-permute-done | bytes 98336 | tf_op jit(solution)/shard_map/ppermute | solution.py:405
  37.4 1.3 %collective-permute-done.7.refs_4_ = f32[24,2,4,128]{3,2,1,0:T(4,128)S(1)} collective-permute-done((f32[24,2,4,128]{3,2,1,0:T(4,128)S(1)}, f32[24,2,4,128]{3,2,1,0:T(4,128)S(1)}, u32[]{:S(2)}, u32[]{:S(2)}) %collective-permute-start.7) | collective-permute-done | bytes 98336 | tf_op jit(solution)/shard_map/ppermute | solution.py:405
  39.8 2.3 %collective-permute-start.9 = (f32[4,2,24,128]{3,2,1,0:T(8,128)S(1)}, f32[4,2,24,128]{3,2,1,0:T(8,128)S(1)}, u32[]{:S(2)}, u32[]{:S(2)}) collective-permute-start(f32[4,2,24,128]{3,2,1,0:T(8,128)S(1)} %get-tuple-element.131), channel_id=1, source_target_pairs={{0,112},{16,32},{32,16},{48,64},{64,48},{80,96},{96,80},{112,0},{1... | collective-permute-start | bytes 294920 | tf_op jit(solution)/shard_map/ppermute | solution.py:405
  42.1 2.3 %collective-permute-start.11 = (f32[24,2,4,128]{3,2,1,0:T(4,128)S(1)}, f32[24,2,4,128]{3,2,1,0:T(4,128)S(1)}, u32[]{:S(2)}, u32[]{:S(2)}) collective-permute-start(f32[24,2,4,128]{3,2,1,0:T(4,128)S(1)} %get-tuple-element.133), channel_id=1, source_target_pairs={{0,15},{1,2},{2,1},{3,4},{4,3},{5,6},{6,5},{7,8},{8,7},{9,10},{10,... | collective-permute-start | bytes 294920 | tf_op jit(solution)/shard_map/ppermute | solution.py:405
  44.4 3.3 %shard_map.145 = (f32[32,2,40,128]{3,2,1,0:T(8,128)S(1)}, f32[2,32,2,24,128]{4,3,2,1,0:T(8,128)S(1)}, f32[24,2,40,128]{3,2,1,0:T(8,128)S(1)}, f32[24,2,24,128]{3...) custom-call(s32[72]{0:T(128)S(1)} %get-tuple-element.102.table.refs_, ...), custom_call_target="tpu_custom_call", output_to_operand_aliasing={{0}: (8, {}), {1}: (9, {}), {2}: (10, {}), {3}: (11, {}), {... | custom-call | tf_op jit(solution)/shard_map/pallas_call | solution.py:479
  47.7 2.1 %collective-permute-done.11.refs_4_ = f32[24,2,4,128]{3,2,1,0:T(4,128)S(1)} collective-permute-done((f32[24,2,4,128]{3,2,1,0:T(4,128)S(1)}, f32[24,2,4,128]{3,2,1,0:T(4,128)S(1)}, u32[]{:S(2)}, u32[]{:S(2)}) %collective-permute-start.11) | collective-permute-done | bytes 98336 | tf_op jit(solution)/shard_map/ppermute | solution.py:405
  50.9 1.3 collective-permute-start.13
  52.2 2.7 %collective-permute-start.15 = (f32[24,2,4,128]{3,2,1,0:T(4,128)S(1)}, f32[24,2,4,128]{3,2,1,0:T(4,128)S(1)}, u32[]{:S(2)}, u32[]{:S(2)}) collective-permute-start(f32[24,2,4,128]{3,2,1,0:T(4,128)S(1)} %get-tuple-element.144), channel_id=1, source_target_pairs={{0,15},{1,2},{2,1},{3,4},{4,3},{5,6},{6,5},{7,8},{8,7},{9,10},{10,... | collective-permute-start | bytes 294920 | tf_op jit(solution)/shard_map/ppermute | solution.py:405
  54.9 3.3 %shard_map.147 = (f32[32,2,40,128]{3,2,1,0:T(8,128)S(1)}, f32[2,32,2,24,128]{4,3,2,1,0:T(8,128)S(1)}, f32[24,2,40,128]{3,2,1,0:T(8,128)S(1)}, f32[24,2,24,128]{3...) custom-call(s32[72]{0:T(128)S(1)} %get-tuple-element.102.table.refs_, ...), custom_call_target="tpu_custom_call", output_to_operand_aliasing={{0}: (8, {}), {1}: (9, {}), {2}: (10, {}), {3}: (11, {}), {... | custom-call | tf_op jit(solution)/shard_map/pallas_call | solution.py:479
  58.5 1.3 %collective-permute-done.15.refs_4_ = f32[24,2,4,128]{3,2,1,0:T(4,128)S(1)} collective-permute-done((f32[24,2,4,128]{3,2,1,0:T(4,128)S(1)}, f32[24,2,4,128]{3,2,1,0:T(4,128)S(1)}, u32[]{:S(2)}, u32[]{:S(2)}) %collective-permute-start.15) | collective-permute-done | bytes 98336 | tf_op jit(solution)/shard_map/ppermute | solution.py:405
  60.9 3.5 %collective-permute-start.17 = (f32[4,2,24,128]{3,2,1,0:T(8,128)S(1)}, f32[4,2,24,128]{3,2,1,0:T(8,128)S(1)}, u32[]{:S(2)}, u32[]{:S(2)}) collective-permute-start(f32[4,2,24,128]{3,2,1,0:T(8,128)S(1)} %get-tuple-element.153), channel_id=1, source_target_pairs={{0,112},{16,32},{32,16},{48,64},{64,48},{80,96},{96,80},{112,0},{1... | collective-permute-start | bytes 294920 | tf_op jit(solution)/shard_map/ppermute | solution.py:405
  64.4 1.4 %collective-permute-start.19 = (f32[24,2,4,128]{3,2,1,0:T(4,128)S(1)}, f32[24,2,4,128]{3,2,1,0:T(4,128)S(1)}, u32[]{:S(2)}, u32[]{:S(2)}) collective-permute-start(f32[24,2,4,128]{3,2,1,0:T(4,128)S(1)} %get-tuple-element.155), channel_id=1, source_target_pairs={{0,15},{1,2},{2,1},{3,4},{4,3},{5,6},{6,5},{7,8},{8,7},{9,10},{10,... | collective-permute-start | bytes 294920 | tf_op jit(solution)/shard_map/ppermute | solution.py:405
  65.8 3.3 %shard_map.149 = (f32[32,2,40,128]{3,2,1,0:T(8,128)S(1)}, f32[2,32,2,24,128]{4,3,2,1,0:T(8,128)S(1)}, f32[24,2,40,128]{3,2,1,0:T(8,128)S(1)}, f32[24,2,24,128]{3...) custom-call(s32[72]{0:T(128)S(1)} %get-tuple-element.102.table.refs_, ...), custom_call_target="tpu_custom_call", output_to_operand_aliasing={{0}: (8, {}), {1}: (9, {}), {2}: (10, {}), {3}: (11, {}), {... | custom-call | tf_op jit(solution)/shard_map/pallas_call | solution.py:479
  69.1 3.0 %collective-permute-done.19.refs_4_ = f32[24,2,4,128]{3,2,1,0:T(4,128)S(1)} collective-permute-done((f32[24,2,4,128]{3,2,1,0:T(4,128)S(1)}, f32[24,2,4,128]{3,2,1,0:T(4,128)S(1)}, u32[]{:S(2)}, u32[]{:S(2)}) %collective-permute-start.19) | collective-permute-done | bytes 98336 | tf_op jit(solution)/shard_map/ppermute | solution.py:405
  72.5 1.2 collective-permute-start.21
  73.8 2.3 %collective-permute-start.23 = (f32[24,2,4,128]{3,2,1,0:T(4,128)S(1)}, f32[24,2,4,128]{3,2,1,0:T(4,128)S(1)}, u32[]{:S(2)}, u32[]{:S(2)}) collective-permute-start(f32[24,2,4,128]{3,2,1,0:T(4,128)S(1)} %get-tuple-element.166), channel_id=1, source_target_pairs={{0,15},{1,2},{2,1},{3,4},{4,3},{5,6},{6,5},{7,8},{8,7},{9,10},{10,... | collective-permute-start | bytes 294920 | tf_op jit(solution)/shard_map/ppermute | solution.py:405
  76.0 3.3 %shard_map.151 = (f32[32,2,40,128]{3,2,1,0:T(8,128)S(1)}, f32[2,32,2,24,128]{4,3,2,1,0:T(8,128)S(1)}, f32[24,2,40,128]{3,2,1,0:T(8,128)S(1)}, f32[24,2,24,128]{3...) custom-call(s32[72]{0:T(128)S(1)} %get-tuple-element.102.table.refs_, ...), custom_call_target="tpu_custom_call", output_to_operand_aliasing={{0}: (8, {}), {1}: (9, {}), {2}: (10, {}), {3}: (11, {}), {... | custom-call | tf_op jit(solution)/shard_map/pallas_call | solution.py:479
  80.2 1.3 collective-permute-done.23.refs_4_
  82.5 2.3 %collective-permute-start.25 = (f32[4,2,24,128]{3,2,1,0:T(8,128)S(1)}, f32[4,2,24,128]{3,2,1,0:T(8,128)S(1)}, u32[]{:S(2)}, u32[]{:S(2)}) collective-permute-start(f32[4,2,24,128]{3,2,1,0:T(8,128)S(1)} %get-tuple-element.175), channel_id=1, source_target_pairs={{0,112},{16,32},{32,16},{48,64},{64,48},{80,96},{96,80},{112,0},{1... | collective-permute-start | bytes 294920 | tf_op jit(solution)/shard_map/ppermute | solution.py:405
  84.8 2.3 %collective-permute-start.27 = (f32[24,2,4,128]{3,2,1,0:T(4,128)S(1)}, f32[24,2,4,128]{3,2,1,0:T(4,128)S(1)}, u32[]{:S(2)}, u32[]{:S(2)}) collective-permute-start(f32[24,2,4,128]{3,2,1,0:T(4,128)S(1)} %get-tuple-element.177), channel_id=1, source_target_pairs={{0,15},{1,2},{2,1},{3,4},{4,3},{5,6},{6,5},{7,8},{8,7},{9,10},{10,... | collective-permute-start | bytes 294920 | tf_op jit(solution)/shard_map/ppermute | solution.py:405
  87.1 3.3 %shard_map.153 = (f32[32,2,40,128]{3,2,1,0:T(8,128)S(1)}, f32[2,32,2,24,128]{4,3,2,1,0:T(8,128)S(1)}, f32[24,2,40,128]{3,2,1,0:T(8,128)S(1)}, f32[24,2,24,128]{3...) custom-call(s32[72]{0:T(128)S(1)} %get-tuple-element.102.table.refs_, ...), custom_call_target="tpu_custom_call", output_to_operand_aliasing={{0}: (8, {}), {1}: (9, {}), {2}: (10, {}), {3}: (11, {}), {... | custom-call | tf_op jit(solution)/shard_map/pallas_call | solution.py:479
  90.4 2.1 %collective-permute-done.27.refs_4_ = f32[24,2,4,128]{3,2,1,0:T(4,128)S(1)} collective-permute-done((f32[24,2,4,128]{3,2,1,0:T(4,128)S(1)}, f32[24,2,4,128]{3,2,1,0:T(4,128)S(1)}, u32[]{:S(2)}, u32[]{:S(2)}) %collective-permute-start.27) | collective-permute-done | bytes 98336 | tf_op jit(solution)/shard_map/ppermute | solution.py:405
  93.6 1.7 %collective-permute-start.29 = (f32[4,2,24,128]{3,2,1,0:T(8,128)S(1)}, f32[4,2,24,128]{3,2,1,0:T(8,128)S(1)}, u32[]{:S(2)}, u32[]{:S(2)}) collective-permute-start(f32[4,2,24,128]{3,2,1,0:T(8,128)S(1)} %get-tuple-element.186), channel_id=1, source_target_pairs={{0,112},{16,32},{32,16},{48,64},{64,48},{80,96},{96,80},{112,0},{1... | collective-permute-start | bytes 294920 | tf_op jit(solution)/shard_map/ppermute | solution.py:405
  95.3 2.3 %collective-permute-start.31 = (f32[24,2,4,128]{3,2,1,0:T(4,128)S(1)}, f32[24,2,4,128]{3,2,1,0:T(4,128)S(1)}, u32[]{:S(2)}, u32[]{:S(2)}) collective-permute-start(f32[24,2,4,128]{3,2,1,0:T(4,128)S(1)} %get-tuple-element.188), channel_id=1, source_target_pairs={{0,15},{1,2},{2,1},{3,4},{4,3},{5,6},{6,5},{7,8},{8,7},{9,10},{10,... | collective-permute-start | bytes 294920 | tf_op jit(solution)/shard_map/ppermute | solution.py:405
  97.6 3.3 %shard_map.155 = (f32[32,2,40,128]{3,2,1,0:T(8,128)S(1)}, f32[2,32,2,24,128]{4,3,2,1,0:T(8,128)S(1)}, f32[24,2,40,128]{3,2,1,0:T(8,128)S(1)}, f32[24,2,24,128]{3...) custom-call(s32[72]{0:T(128)S(1)} %get-tuple-element.102.table.refs_, ...), custom_call_target="tpu_custom_call", output_to_operand_aliasing={{0}: (8, {}), {1}: (9, {}), {2}: (10, {}), {3}: (11, {}), {... | custom-call | tf_op jit(solution)/shard_map/pallas_call | solution.py:479
  101.2 1.7 %collective-permute-done.31.refs_8_ = f32[24,2,4,128]{3,2,1,0:T(4,128)S(1)} collective-permute-done((f32[24,2,4,128]{3,2,1,0:T(4,128)S(1)}, f32[24,2,4,128]{3,2,1,0:T(4,128)S(1)}, u32[]{:S(2)}, u32[]{:S(2)}) %collective-permute-start.31) | collective-permute-done | bytes 98336 | tf_op jit(solution)/shard_map/ppermute | solution.py:405
  103.9 1.2 collective-permute-done.32
  105.1 2.3 %collective-permute-start.34 = (f32[16,128]{1,0:T(8,128)S(1)}, f32[16,128]{1,0:T(8,128)S(1)}, u32[]{:S(2)}, u32[]{:S(2)}) collective-permute-start(f32[16,128]{1,0:T(8,128)S(1)} %add.21), channel_id=1, source_target_pairs={{0,2},{1,3},{2,0},{3,1},{4,6},{5,7},{6,4},{7,5},{8,10},{9,11},{10,... | collective-permute-start | bytes 24584 | tf_op jit(solution)/shard_map/ppermute | solution.py:419
  107.4 1.7 %collective-permute-start.33 = (f32[16,128]{1,0:T(8,128)S(1)}, f32[16,128]{1,0:T(8,128)S(1)}, u32[]{:S(2)}, u32[]{:S(2)}) collective-permute-start(f32[16,128]{1,0:T(8,128)S(1)} %add.21), channel_id=1, source_target_pairs={{0,16},{1,17},{2,18},{3,19},{4,20},{5,21},{6,22},{7,23},{8,24},{9,... | collective-permute-start | bytes 24584 | tf_op jit(solution)/shard_map/ppermute | solution.py:419
  111.1 1.8 %collective-permute-start.38 = (f32[16,128]{1,0:T(8,128)S(1)}, f32[16,128]{1,0:T(8,128)S(1)}, u32[]{:S(2)}, u32[]{:S(2)}) collective-permute-start(f32[16,128]{1,0:T(8,128)S(1)} %add_add_fusion.1), channel_id=1, source_target_pairs={{0,12},{1,13},{2,14},{3,15},{4,8},{5,9},{6,10},{7,11},{8,4},{9,5},... | collective-permute-start | bytes 24584 | tf_op jit(solution)/shard_map/ppermute | solution.py:419
  112.9 2.3 %collective-permute-start.36 = (f32[16,128]{1,0:T(8,128)S(1)}, f32[16,128]{1,0:T(8,128)S(1)}, u32[]{:S(2)}, u32[]{:S(2)}) collective-permute-start(f32[16,128]{1,0:T(8,128)S(1)} %add_add_fusion.1), channel_id=1, source_target_pairs={{0,4},{1,5},{2,6},{3,7},{4,0},{5,1},{6,2},{7,3},{8,12},{9,13},{10,... | collective-permute-start | bytes 24584 | tf_op jit(solution)/shard_map/ppermute | solution.py:419
  116.0 2.1 %collective-permute-done.37 = f32[16,128]{1,0:T(8,128)S(1)} collective-permute-done((f32[16,128]{1,0:T(8,128)S(1)}, f32[16,128]{1,0:T(8,128)S(1)}, u32[]{:S(2)}, u32[]{:S(2)}) %collective-permute-start.37) | collective-permute-done | bytes 8224 | tf_op jit(solution)/shard_map/ppermute | solution.py:419
  118.1 1.6 %collective-permute-start.39 = (f32[16,128]{1,0:T(8,128)S(1)}, f32[16,128]{1,0:T(8,128)S(1)}, u32[]{:S(2)}, u32[]{:S(2)}) collective-permute-start(f32[16,128]{1,0:T(8,128)S(1)} %add_add_fusion.refs_0_), channel_id=1, source_target_pairs={{0,32},{1,33},{2,34},{3,35},{4,36},{5,37},{6,38},{7,39},{8,40},{9,... | collective-permute-start | bytes 24584 | tf_op jit(solution)/shard_map/ppermute | solution.py:419
  119.7 2.1 %collective-permute-start.40 = (f32[16,128]{1,0:T(8,128)S(1)}, f32[16,128]{1,0:T(8,128)S(1)}, u32[]{:S(2)}, u32[]{:S(2)}) collective-permute-start(f32[16,128]{1,0:T(8,128)S(1)} %add_add_fusion.refs_0_), channel_id=1, source_target_pairs={{0,64},{1,65},{2,66},{3,67},{4,68},{5,69},{6,70},{7,71},{8,72},{9,... | collective-permute-start | bytes 24584 | tf_op jit(solution)/shard_map/ppermute | solution.py:419
  121.8 1.1 collective-permute-start.41
  123.7 1.2 collective-permute-done.40.refs_2_
  124.9 1.8 %collective-permute-done.41.refs_3_ = f32[16,128]{1,0:T(8,128)S(1)} collective-permute-done((f32[16,128]{1,0:T(8,128)S(1)}, f32[16,128]{1,0:T(8,128)S(1)}, u32[]{:S(2)}, u32[]{:S(2)}) %collective-permute-start.41) | collective-permute-done | bytes 8224 | tf_op jit(solution)/shard_map/ppermute | solution.py:419
  (83 shorter events, 20.0 us)
Async XLA Ops:
  0.6 25.4 %copy-start = (bf16[512,256]{1,0:T(8,128)(2,1)S(1)}, bf16[512,256]{1,0:T(8,128)(2,1)}, u32[]{:S(2)}) copy-start(bf16[512,256]{1,0:T(8,128)(2,1)} %constant.2.clone.band) | copy-start | bytes 786436
  0.6 1.1 copy-start.3
  2.7 26.6 %collective-permute-start = (f32[4,2,24,128]{3,2,1,0:T(8,128)S(1)}, f32[4,2,24,128]{3,2,1,0:T(8,128)S(1)}, u32[]{:S(2)}, u32[]{:S(2)}) collective-permute-start(f32[4,2,24,128]{3,2,1,0:T(8,128)S(1)} %get-tuple-element.107), channel_id=1, source_target_pairs={{0,16},{16,0},{32,48},{48,32},{64,80},{80,64},{96,112},{112,96},{1... | collective-permute-start | bytes 294920 | tf_op jit(solution)/shard_map/ppermute | solution.py:405
  4.3 25.0 %collective-permute-start.1 = (f32[4,2,24,128]{3,2,1,0:T(8,128)S(1)}, f32[4,2,24,128]{3,2,1,0:T(8,128)S(1)}, u32[]{:S(2)}, u32[]{:S(2)}) collective-permute-start(f32[4,2,24,128]{3,2,1,0:T(8,128)S(1)} %get-tuple-element.108), channel_id=1, source_target_pairs={{0,112},{16,32},{32,16},{48,64},{64,48},{80,96},{96,80},{112,0},{1... | collective-permute-start | bytes 294920 | tf_op jit(solution)/shard_map/ppermute | solution.py:405
  7.3 22.0 %collective-permute-start.2 = (f32[24,2,4,128]{3,2,1,0:T(4,128)S(1)}, f32[24,2,4,128]{3,2,1,0:T(4,128)S(1)}, u32[]{:S(2)}, u32[]{:S(2)}) collective-permute-start(f32[24,2,4,128]{3,2,1,0:T(4,128)S(1)} %get-tuple-element.109), channel_id=1, source_target_pairs={{0,1},{1,0},{2,3},{3,2},{4,5},{5,4},{6,7},{7,6},{8,9},{9,8},{10,11... | collective-permute-start | bytes 294920 | tf_op jit(solution)/shard_map/ppermute | solution.py:405
  7.3 22.0 %collective-permute-start.3 = (f32[24,2,4,128]{3,2,1,0:T(4,128)S(1)}, f32[24,2,4,128]{3,2,1,0:T(4,128)S(1)}, u32[]{:S(2)}, u32[]{:S(2)}) collective-permute-start(f32[24,2,4,128]{3,2,1,0:T(4,128)S(1)} %get-tuple-element.110), channel_id=1, source_target_pairs={{0,15},{1,2},{2,1},{3,4},{4,3},{5,6},{6,5},{7,8},{8,7},{9,10},{10,... | collective-permute-start | bytes 294920 | tf_op jit(solution)/shard_map/ppermute | solution.py:405
  14.7 1.1 copy-start.1
  15.8 1.1 copy-start.2
  16.8 0.7 copy-start.4
  17.5 0.7 copy-start.5
  29.7 5.6 %collective-permute-start.4 = (f32[4,2,24,128]{3,2,1,0:T(8,128)S(1)}, f32[4,2,24,128]{3,2,1,0:T(8,128)S(1)}, u32[]{:S(2)}, u32[]{:S(2)}) collective-permute-start(f32[4,2,24,128]{3,2,1,0:T(8,128)S(1)} %get-tuple-element.119), channel_id=1, source_target_pairs={{0,16},{16,0},{32,48},{48,32},{64,80},{80,64},{96,112},{112,96},{1... | collective-permute-start | bytes 294920 | tf_op jit(solution)/shard_map/ppermute | solution.py:405
  29.8 7.7 %collective-permute-start.5 = (f32[4,2,24,128]{3,2,1,0:T(8,128)S(1)}, f32[4,2,24,128]{3,2,1,0:T(8,128)S(1)}, u32[]{:S(2)}, u32[]{:S(2)}) collective-permute-start(f32[4,2,24,128]{3,2,1,0:T(8,128)S(1)} %get-tuple-element.120), channel_id=1, source_target_pairs={{0,112},{16,32},{32,16},{48,64},{64,48},{80,96},{96,80},{112,0},{1... | collective-permute-start | bytes 294920 | tf_op jit(solution)/shard_map/ppermute | solution.py:405
  31.1 6.4 %collective-permute-start.6 = (f32[24,2,4,128]{3,2,1,0:T(4,128)S(1)}, f32[24,2,4,128]{3,2,1,0:T(4,128)S(1)}, u32[]{:S(2)}, u32[]{:S(2)}) collective-permute-start(f32[24,2,4,128]{3,2,1,0:T(4,128)S(1)} %get-tuple-element.121), channel_id=1, source_target_pairs={{0,1},{1,0},{2,3},{3,2},{4,5},{5,4},{6,7},{7,6},{8,9},{9,8},{10,11... | collective-permute-start | bytes 294920 | tf_op jit(solution)/shard_map/ppermute | solution.py:405
  31.1 7.7 %collective-permute-start.7 = (f32[24,2,4,128]{3,2,1,0:T(4,128)S(1)}, f32[24,2,4,128]{3,2,1,0:T(4,128)S(1)}, u32[]{:S(2)}, u32[]{:S(2)}) collective-permute-start(f32[24,2,4,128]{3,2,1,0:T(4,128)S(1)} %get-tuple-element.122), channel_id=1, source_target_pairs={{0,15},{1,2},{2,1},{3,4},{4,3},{5,6},{6,5},{7,8},{8,7},{9,10},{10,... | collective-permute-start | bytes 294920 | tf_op jit(solution)/shard_map/ppermute | solution.py:405
  39.0 8.6 %collective-permute-start.8 = (f32[4,2,24,128]{3,2,1,0:T(8,128)S(1)}, f32[4,2,24,128]{3,2,1,0:T(8,128)S(1)}, u32[]{:S(2)}, u32[]{:S(2)}) collective-permute-start(f32[4,2,24,128]{3,2,1,0:T(8,128)S(1)} %get-tuple-element.130), channel_id=1, source_target_pairs={{0,16},{16,0},{32,48},{48,32},{64,80},{80,64},{96,112},{112,96},{1... | collective-permute-start | bytes 294920 | tf_op jit(solution)/shard_map/ppermute | solution.py:405
  39.8 7.9 %collective-permute-start.9 = (f32[4,2,24,128]{3,2,1,0:T(8,128)S(1)}, f32[4,2,24,128]{3,2,1,0:T(8,128)S(1)}, u32[]{:S(2)}, u32[]{:S(2)}) collective-permute-start(f32[4,2,24,128]{3,2,1,0:T(8,128)S(1)} %get-tuple-element.131), channel_id=1, source_target_pairs={{0,112},{16,32},{32,16},{48,64},{64,48},{80,96},{96,80},{112,0},{1... | collective-permute-start | bytes 294920 | tf_op jit(solution)/shard_map/ppermute | solution.py:405
  42.1 5.6 %collective-permute-start.10 = (f32[24,2,4,128]{3,2,1,0:T(4,128)S(1)}, f32[24,2,4,128]{3,2,1,0:T(4,128)S(1)}, u32[]{:S(2)}, u32[]{:S(2)}) collective-permute-start(f32[24,2,4,128]{3,2,1,0:T(4,128)S(1)} %get-tuple-element.132), channel_id=1, source_target_pairs={{0,1},{1,0},{2,3},{3,2},{4,5},{5,4},{6,7},{7,6},{8,9},{9,8},{10,11... | collective-permute-start | bytes 294920 | tf_op jit(solution)/shard_map/ppermute | solution.py:405
  42.1 7.7 %collective-permute-start.11 = (f32[24,2,4,128]{3,2,1,0:T(4,128)S(1)}, f32[24,2,4,128]{3,2,1,0:T(4,128)S(1)}, u32[]{:S(2)}, u32[]{:S(2)}) collective-permute-start(f32[24,2,4,128]{3,2,1,0:T(4,128)S(1)} %get-tuple-element.133), channel_id=1, source_target_pairs={{0,15},{1,2},{2,1},{3,4},{4,3},{5,6},{6,5},{7,8},{8,7},{9,10},{10,... | collective-permute-start | bytes 294920 | tf_op jit(solution)/shard_map/ppermute | solution.py:405
  50.1 8.1 %collective-permute-start.12 = (f32[4,2,24,128]{3,2,1,0:T(8,128)S(1)}, f32[4,2,24,128]{3,2,1,0:T(8,128)S(1)}, u32[]{:S(2)}, u32[]{:S(2)}) collective-permute-start(f32[4,2,24,128]{3,2,1,0:T(8,128)S(1)} %get-tuple-element.141), channel_id=1, source_target_pairs={{0,16},{16,0},{32,48},{48,32},{64,80},{80,64},{96,112},{112,96},{1... | collective-permute-start | bytes 294920 | tf_op jit(solution)/shard_map/ppermute | solution.py:405
  50.9 7.6 %collective-permute-start.13 = (f32[4,2,24,128]{3,2,1,0:T(8,128)S(1)}, f32[4,2,24,128]{3,2,1,0:T(8,128)S(1)}, u32[]{:S(2)}, u32[]{:S(2)}) collective-permute-start(f32[4,2,24,128]{3,2,1,0:T(8,128)S(1)} %get-tuple-element.142), channel_id=1, source_target_pairs={{0,112},{16,32},{32,16},{48,64},{64,48},{80,96},{96,80},{112,0},{1... | collective-permute-start | bytes 294920 | tf_op jit(solution)/shard_map/ppermute | solution.py:405
  52.1 6.3 %collective-permute-start.14 = (f32[24,2,4,128]{3,2,1,0:T(4,128)S(1)}, f32[24,2,4,128]{3,2,1,0:T(4,128)S(1)}, u32[]{:S(2)}, u32[]{:S(2)}) collective-permute-start(f32[24,2,4,128]{3,2,1,0:T(4,128)S(1)} %get-tuple-element.143), channel_id=1, source_target_pairs={{0,1},{1,0},{2,3},{3,2},{4,5},{5,4},{6,7},{7,6},{8,9},{9,8},{10,11... | collective-permute-start | bytes 294920 | tf_op jit(solution)/shard_map/ppermute | solution.py:405
  52.2 7.7 %collective-permute-start.15 = (f32[24,2,4,128]{3,2,1,0:T(4,128)S(1)}, f32[24,2,4,128]{3,2,1,0:T(4,128)S(1)}, u32[]{:S(2)}, u32[]{:S(2)}) collective-permute-start(f32[24,2,4,128]{3,2,1,0:T(4,128)S(1)} %get-tuple-element.144), channel_id=1, source_target_pairs={{0,15},{1,2},{2,1},{3,4},{4,3},{5,6},{6,5},{7,8},{8,7},{9,10},{10,... | collective-permute-start | bytes 294920 | tf_op jit(solution)/shard_map/ppermute | solution.py:405
  60.1 9.0 %collective-permute-start.16 = (f32[4,2,24,128]{3,2,1,0:T(8,128)S(1)}, f32[4,2,24,128]{3,2,1,0:T(8,128)S(1)}, u32[]{:S(2)}, u32[]{:S(2)}) collective-permute-start(f32[4,2,24,128]{3,2,1,0:T(8,128)S(1)} %get-tuple-element.152), channel_id=1, source_target_pairs={{0,16},{16,0},{32,48},{48,32},{64,80},{80,64},{96,112},{112,96},{1... | collective-permute-start | bytes 294920 | tf_op jit(solution)/shard_map/ppermute | solution.py:405
  60.9 8.2 %collective-permute-start.17 = (f32[4,2,24,128]{3,2,1,0:T(8,128)S(1)}, f32[4,2,24,128]{3,2,1,0:T(8,128)S(1)}, u32[]{:S(2)}, u32[]{:S(2)}) collective-permute-start(f32[4,2,24,128]{3,2,1,0:T(8,128)S(1)} %get-tuple-element.153), channel_id=1, source_target_pairs={{0,112},{16,32},{32,16},{48,64},{64,48},{80,96},{96,80},{112,0},{1... | collective-permute-start | bytes 294920 | tf_op jit(solution)/shard_map/ppermute | solution.py:405
  64.4 4.7 %collective-permute-start.18 = (f32[24,2,4,128]{3,2,1,0:T(4,128)S(1)}, f32[24,2,4,128]{3,2,1,0:T(4,128)S(1)}, u32[]{:S(2)}, u32[]{:S(2)}) collective-permute-start(f32[24,2,4,128]{3,2,1,0:T(4,128)S(1)} %get-tuple-element.154), channel_id=1, source_target_pairs={{0,1},{1,0},{2,3},{3,2},{4,5},{5,4},{6,7},{7,6},{8,9},{9,8},{10,11... | collective-permute-start | bytes 294920 | tf_op jit(solution)/shard_map/ppermute | solution.py:405
  64.4 7.7 %collective-permute-start.19 = (f32[24,2,4,128]{3,2,1,0:T(4,128)S(1)}, f32[24,2,4,128]{3,2,1,0:T(4,128)S(1)}, u32[]{:S(2)}, u32[]{:S(2)}) collective-permute-start(f32[24,2,4,128]{3,2,1,0:T(4,128)S(1)} %get-tuple-element.155), channel_id=1, source_target_pairs={{0,15},{1,2},{2,1},{3,4},{4,3},{5,6},{6,5},{7,8},{8,7},{9,10},{10,... | collective-permute-start | bytes 294920 | tf_op jit(solution)/shard_map/ppermute | solution.py:405
  72.4 7.0 %collective-permute-start.20 = (f32[4,2,24,128]{3,2,1,0:T(8,128)S(1)}, f32[4,2,24,128]{3,2,1,0:T(8,128)S(1)}, u32[]{:S(2)}, u32[]{:S(2)}) collective-permute-start(f32[4,2,24,128]{3,2,1,0:T(8,128)S(1)} %get-tuple-element.163), channel_id=1, source_target_pairs={{0,16},{16,0},{32,48},{48,32},{64,80},{80,64},{96,112},{112,96},{1... | collective-permute-start | bytes 294920 | tf_op jit(solution)/shard_map/ppermute | solution.py:405
  72.5 7.6 %collective-permute-start.21 = (f32[4,2,24,128]{3,2,1,0:T(8,128)S(1)}, f32[4,2,24,128]{3,2,1,0:T(8,128)S(1)}, u32[]{:S(2)}, u32[]{:S(2)}) collective-permute-start(f32[4,2,24,128]{3,2,1,0:T(8,128)S(1)} %get-tuple-element.164), channel_id=1, source_target_pairs={{0,112},{16,32},{32,16},{48,64},{64,48},{80,96},{96,80},{112,0},{1... | collective-permute-start | bytes 294920 | tf_op jit(solution)/shard_map/ppermute | solution.py:405
  73.8 6.4 %collective-permute-start.22 = (f32[24,2,4,128]{3,2,1,0:T(4,128)S(1)}, f32[24,2,4,128]{3,2,1,0:T(4,128)S(1)}, u32[]{:S(2)}, u32[]{:S(2)}) collective-permute-start(f32[24,2,4,128]{3,2,1,0:T(4,128)S(1)} %get-tuple-element.165), channel_id=1, source_target_pairs={{0,1},{1,0},{2,3},{3,2},{4,5},{5,4},{6,7},{7,6},{8,9},{9,8},{10,11... | collective-permute-start | bytes 294920 | tf_op jit(solution)/shard_map/ppermute | solution.py:405
  73.8 7.7 %collective-permute-start.23 = (f32[24,2,4,128]{3,2,1,0:T(4,128)S(1)}, f32[24,2,4,128]{3,2,1,0:T(4,128)S(1)}, u32[]{:S(2)}, u32[]{:S(2)}) collective-permute-start(f32[24,2,4,128]{3,2,1,0:T(4,128)S(1)} %get-tuple-element.166), channel_id=1, source_target_pairs={{0,15},{1,2},{2,1},{3,4},{4,3},{5,6},{6,5},{7,8},{8,7},{9,10},{10,... | collective-permute-start | bytes 294920 | tf_op jit(solution)/shard_map/ppermute | solution.py:405
  81.7 8.6 %collective-permute-start.24 = (f32[4,2,24,128]{3,2,1,0:T(8,128)S(1)}, f32[4,2,24,128]{3,2,1,0:T(8,128)S(1)}, u32[]{:S(2)}, u32[]{:S(2)}) collective-permute-start(f32[4,2,24,128]{3,2,1,0:T(8,128)S(1)} %get-tuple-element.174), channel_id=1, source_target_pairs={{0,16},{16,0},{32,48},{48,32},{64,80},{80,64},{96,112},{112,96},{1... | collective-permute-start | bytes 294920 | tf_op jit(solution)/shard_map/ppermute | solution.py:405
  82.5 7.9 %collective-permute-start.25 = (f32[4,2,24,128]{3,2,1,0:T(8,128)S(1)}, f32[4,2,24,128]{3,2,1,0:T(8,128)S(1)}, u32[]{:S(2)}, u32[]{:S(2)}) collective-permute-start(f32[4,2,24,128]{3,2,1,0:T(8,128)S(1)} %get-tuple-element.175), channel_id=1, source_target_pairs={{0,112},{16,32},{32,16},{48,64},{64,48},{80,96},{96,80},{112,0},{1... | collective-permute-start | bytes 294920 | tf_op jit(solution)/shard_map/ppermute | solution.py:405
  84.8 5.6 %collective-permute-start.26 = (f32[24,2,4,128]{3,2,1,0:T(4,128)S(1)}, f32[24,2,4,128]{3,2,1,0:T(4,128)S(1)}, u32[]{:S(2)}, u32[]{:S(2)}) collective-permute-start(f32[24,2,4,128]{3,2,1,0:T(4,128)S(1)} %get-tuple-element.176), channel_id=1, source_target_pairs={{0,1},{1,0},{2,3},{3,2},{4,5},{5,4},{6,7},{7,6},{8,9},{9,8},{10,11... | collective-permute-start | bytes 294920 | tf_op jit(solution)/shard_map/ppermute | solution.py:405
  84.8 7.7 %collective-permute-start.27 = (f32[24,2,4,128]{3,2,1,0:T(4,128)S(1)}, f32[24,2,4,128]{3,2,1,0:T(4,128)S(1)}, u32[]{:S(2)}, u32[]{:S(2)}) collective-permute-start(f32[24,2,4,128]{3,2,1,0:T(4,128)S(1)} %get-tuple-element.177), channel_id=1, source_target_pairs={{0,15},{1,2},{2,1},{3,4},{4,3},{5,6},{6,5},{7,8},{8,7},{9,10},{10,... | collective-permute-start | bytes 294920 | tf_op jit(solution)/shard_map/ppermute | solution.py:405
  92.8 8.1 %collective-permute-start.28 = (f32[4,2,24,128]{3,2,1,0:T(8,128)S(1)}, f32[4,2,24,128]{3,2,1,0:T(8,128)S(1)}, u32[]{:S(2)}, u32[]{:S(2)}) collective-permute-start(f32[4,2,24,128]{3,2,1,0:T(8,128)S(1)} %get-tuple-element.185), channel_id=1, source_target_pairs={{0,16},{16,0},{32,48},{48,32},{64,80},{80,64},{96,112},{112,96},{1... | collective-permute-start | bytes 294920 | tf_op jit(solution)/shard_map/ppermute | solution.py:405
  93.6 7.6 %collective-permute-start.29 = (f32[4,2,24,128]{3,2,1,0:T(8,128)S(1)}, f32[4,2,24,128]{3,2,1,0:T(8,128)S(1)}, u32[]{:S(2)}, u32[]{:S(2)}) collective-permute-start(f32[4,2,24,128]{3,2,1,0:T(8,128)S(1)} %get-tuple-element.186), channel_id=1, source_target_pairs={{0,112},{16,32},{32,16},{48,64},{64,48},{80,96},{96,80},{112,0},{1... | collective-permute-start | bytes 294920 | tf_op jit(solution)/shard_map/ppermute | solution.py:405
  95.3 5.9 %collective-permute-start.30 = (f32[24,2,4,128]{3,2,1,0:T(4,128)S(1)}, f32[24,2,4,128]{3,2,1,0:T(4,128)S(1)}, u32[]{:S(2)}, u32[]{:S(2)}) collective-permute-start(f32[24,2,4,128]{3,2,1,0:T(4,128)S(1)} %get-tuple-element.187), channel_id=1, source_target_pairs={{0,1},{1,0},{2,3},{3,2},{4,5},{5,4},{6,7},{7,6},{8,9},{9,8},{10,11... | collective-permute-start | bytes 294920 | tf_op jit(solution)/shard_map/ppermute | solution.py:405
  95.3 7.7 %collective-permute-start.31 = (f32[24,2,4,128]{3,2,1,0:T(4,128)S(1)}, f32[24,2,4,128]{3,2,1,0:T(4,128)S(1)}, u32[]{:S(2)}, u32[]{:S(2)}) collective-permute-start(f32[24,2,4,128]{3,2,1,0:T(4,128)S(1)} %get-tuple-element.188), channel_id=1, source_target_pairs={{0,15},{1,2},{2,1},{3,4},{4,3},{5,6},{6,5},{7,8},{8,7},{9,10},{10,... | collective-permute-start | bytes 294920 | tf_op jit(solution)/shard_map/ppermute | solution.py:405
  103.8 1.3 collective-permute-start.32
  105.1 4.9 %collective-permute-start.35 = (f32[16,128]{1,0:T(8,128)S(1)}, f32[16,128]{1,0:T(8,128)S(1)}, u32[]{:S(2)}, u32[]{:S(2)}) collective-permute-start(f32[16,128]{1,0:T(8,128)S(1)} %add.21), channel_id=1, source_target_pairs={{0,18},{1,19},{2,16},{3,17},{4,22},{5,23},{6,20},{7,21},{8,26},{9,... | collective-permute-start | bytes 24584 | tf_op jit(solution)/shard_map/ppermute | solution.py:419
  105.1 5.2 %collective-permute-start.34 = (f32[16,128]{1,0:T(8,128)S(1)}, f32[16,128]{1,0:T(8,128)S(1)}, u32[]{:S(2)}, u32[]{:S(2)}) collective-permute-start(f32[16,128]{1,0:T(8,128)S(1)} %add.21), channel_id=1, source_target_pairs={{0,2},{1,3},{2,0},{3,1},{4,6},{5,7},{6,4},{7,5},{8,10},{9,11},{10,... | collective-permute-start | bytes 24584 | tf_op jit(solution)/shard_map/ppermute | solution.py:419
  107.4 3.7 %collective-permute-start.33 = (f32[16,128]{1,0:T(8,128)S(1)}, f32[16,128]{1,0:T(8,128)S(1)}, u32[]{:S(2)}, u32[]{:S(2)}) collective-permute-start(f32[16,128]{1,0:T(8,128)S(1)} %add.21), channel_id=1, source_target_pairs={{0,16},{1,17},{2,18},{3,19},{4,20},{5,21},{6,22},{7,23},{8,24},{9,... | collective-permute-start | bytes 24584 | tf_op jit(solution)/shard_map/ppermute | solution.py:419
  111.1 4.9 %collective-permute-start.38 = (f32[16,128]{1,0:T(8,128)S(1)}, f32[16,128]{1,0:T(8,128)S(1)}, u32[]{:S(2)}, u32[]{:S(2)}) collective-permute-start(f32[16,128]{1,0:T(8,128)S(1)} %add_add_fusion.1), channel_id=1, source_target_pairs={{0,12},{1,13},{2,14},{3,15},{4,8},{5,9},{6,10},{7,11},{8,4},{9,5},... | collective-permute-start | bytes 24584 | tf_op jit(solution)/shard_map/ppermute | solution.py:419
  112.9 5.2 %collective-permute-start.37 = (f32[16,128]{1,0:T(8,128)S(1)}, f32[16,128]{1,0:T(8,128)S(1)}, u32[]{:S(2)}, u32[]{:S(2)}) collective-permute-start(f32[16,128]{1,0:T(8,128)S(1)} %add_add_fusion.1), channel_id=1, source_target_pairs={{0,8},{1,9},{2,10},{3,11},{4,12},{5,13},{6,14},{7,15},{8,0},{9,1},... | collective-permute-start | bytes 24584 | tf_op jit(solution)/shard_map/ppermute | solution.py:419
  112.9 5.2 %collective-permute-start.36 = (f32[16,128]{1,0:T(8,128)S(1)}, f32[16,128]{1,0:T(8,128)S(1)}, u32[]{:S(2)}, u32[]{:S(2)}) collective-permute-start(f32[16,128]{1,0:T(8,128)S(1)} %add_add_fusion.1), channel_id=1, source_target_pairs={{0,4},{1,5},{2,6},{3,7},{4,0},{5,1},{6,2},{7,3},{8,12},{9,13},{10,... | collective-permute-start | bytes 24584 | tf_op jit(solution)/shard_map/ppermute | solution.py:419
  118.1 5.6 %collective-permute-start.39 = (f32[16,128]{1,0:T(8,128)S(1)}, f32[16,128]{1,0:T(8,128)S(1)}, u32[]{:S(2)}, u32[]{:S(2)}) collective-permute-start(f32[16,128]{1,0:T(8,128)S(1)} %add_add_fusion.refs_0_), channel_id=1, source_target_pairs={{0,32},{1,33},{2,34},{3,35},{4,36},{5,37},{6,38},{7,39},{8,40},{9,... | collective-permute-start | bytes 24584 | tf_op jit(solution)/shard_map/ppermute | solution.py:419
  119.7 5.2 %collective-permute-start.40 = (f32[16,128]{1,0:T(8,128)S(1)}, f32[16,128]{1,0:T(8,128)S(1)}, u32[]{:S(2)}, u32[]{:S(2)}) collective-permute-start(f32[16,128]{1,0:T(8,128)S(1)} %add_add_fusion.refs_0_), channel_id=1, source_target_pairs={{0,64},{1,65},{2,66},{3,67},{4,68},{5,69},{6,70},{7,71},{8,72},{9,... | collective-permute-start | bytes 24584 | tf_op jit(solution)/shard_map/ppermute | solution.py:419
  121.8 4.9 %collective-permute-start.41 = (f32[16,128]{1,0:T(8,128)S(1)}, f32[16,128]{1,0:T(8,128)S(1)}, u32[]{:S(2)}, u32[]{:S(2)}) collective-permute-start(f32[16,128]{1,0:T(8,128)S(1)} %add_add_fusion.refs_0_), channel_id=1, source_target_pairs={{0,96},{1,97},{2,98},{3,99},{4,100},{5,101},{6,102},{7,103},{8,104... | collective-permute-start | bytes 24584 | tf_op jit(solution)/shard_map/ppermute | solution.py:419
  (5 other events, 3.3 us)

commit v3 on v2

--- a/solution.py
+++ b/solution.py
@@ -146,10 +146,18 @@
 
 
 def begin_kernel(
-    widths_ref, sx, sy, sz, rx, ry, rz, old, speed_term,
-    field, speed, memory_x, memory_y, zeta_x, zeta_y, seen, keep_x, keep_y, norm, table,
-    staged_old, staged_speed, sems,
+    widths_far, sx_far, sy_far, sz_far, rx_far, ry_far, rz_far, amp_far, old, speed_term,
+    field, speed, memory_x, memory_y, zeta_x, zeta_y, seen, keep_x, keep_y, norm, table, amps,
+    staged_old, staged_speed, sems, widths_ref, sx, sy, sz, rx, ry, rz, amp, small_sems,
 ):
+    far = (widths_far, sx_far, sy_far, sz_far, rx_far, ry_far, rz_far, amp_far)
+    near = (widths_ref, sx, sy, sz, rx, ry, rz, amp)
+    small = [
+        pltpu.make_async_copy(source, target, small_sems.at[n])
+        for n, (source, target) in enumerate(zip(far, near))
+    ]
+    for copy in small:
+        copy.start()
     copies = fetch([(old, staged_old), (speed_term, staged_speed)], sems)
     gx, gy, edge_x, edge_y = place()
     start_x, start_y = (gx * CX, gy * CY)
@@ -166,10 +174,15 @@
         memory_y[...] = jnp.zeros(MEM_Y, jnp.float32)
         zeta_y[...] = jnp.zeros(BLOCK, jnp.float32)
 
+    for copy in small:
+        copy.wait()
+
     @pl.when(edge_x | edge_y)
     def _():
         widths = [widths_ref[n].astype(jnp.float32) for n in range(4)]
-        keep_x[...] = keep_of(widths[:2], start_x, KEEP_X, 0, NX)
+        keep = keep_of(widths[:2], start_x, KEEP_Y, 0, NX)
+        for i in range(CX):
+            keep_x[i] = jnp.broadcast_to(keep[i : i + 1], KEEP_Y)
         keep_y[...] = keep_of(widths[2:], start_y, KEEP_Y, 0, NY)
         cells = float(NX * NY) - whole_sum(widths[:2], NX) * whole_sum(widths[2:], NY)
         norm[...] = wide(float(NZ) * cells)
@@ -178,27 +191,23 @@
         lx, ly = (px - start_x, py - start_y)
         return lx, ly, (lx >= 0) & (lx < CX) & (ly >= 0) & (ly < CY)
 
-    def add_receiver(r, count):
-        lx, ly, here = owned(rx[r], ry[r])
-
-        @pl.when(here)
-        def _():
-            table[RECEIVERS + count] = (((lx << 5) + ly) << 14) + (rz[r] << 6) + r
-
-        return count + here.astype(jnp.int32)
-
-    table[0] = lax.fori_loop(0, NREC, add_receiver, 0)
-
-    def add_source(s, count):
-        lx, ly, here = owned(sx[s], sy[s])
-
-        @pl.when(here)
-        def _():
-            table[4 + count] = (((lx << 5) + ly) << 14) + (sz[s] << 6) + s
-
-        return count + here.astype(jnp.int32)
-
-    table[1] = lax.fori_loop(0, NSRC, add_source, 0)
+    def note(at, n, px, py, pz):
+        def add(r, count):
+            lx, ly, here = owned(px[r], py[r])
+
+            @pl.when(here)
+            def _():
+                table[at + count] = (((lx << 5) + ly) << 14) + (pz[r] << 6) + r
+
+            return count + here.astype(jnp.int32)
+
+        return lax.fori_loop(0, n, add, 0)
+
+    table[0] = note(RECEIVERS, NREC, rx, ry, rz)
+    table[1] = note(4, NSRC, sx, sy, sz)
+    for t in range(STEPS):
+        for n in range(NSRC):
+            amps[t * NSRC + n] = amp[t, n]
     for copy in copies:
         copy.wait()
     for half in range(2):
@@ -208,7 +217,7 @@
 
 
 def inner_kernel(
-    step, table, amp, band, current, speed, keep_x, keep_y, norm,
+    step, table, amps, band, current, speed, keep_x, keep_y, norm,
     previous, memory_x_in, memory_y_in, zeta_x_in, zeta_y_in, seen_in,
     following, memory_x, memory_y, zeta_x, zeta_y, seen, bend_z,
 ):
@@ -224,64 +233,71 @@
         bend_z[:, h, :, :] = bent[:, h * LANES : (h + 1) * LANES].reshape(CX, CY, LANES)
     source, target = (step % 2, 1 - step % 2)
 
-    def shifted_x(ref, lead, i, inside, k):
-        return ref[lead + (i + k, slice(None), inside)]
-
-    def sum_x(ref, lead, i, inside, sign, coef):
+    def taps(pick, want_first):
+        second, first = (0.0, 0.0)
+        for k in range(1, 5):
+            up, down = (pick(k), pick(-k))
+            second = second + second_coef[k - 1] * (up + down)
+            if want_first:
+                first = first + first_coef[k - 1] * (up - down)
+        return second, first
+
+    def first_only(pick):
         total = 0.0
         for k in range(1, 5):
-            up, down = (shifted_x(ref, lead, i, inside, k), shifted_x(ref, lead, i, inside, -k))
-            total = total + coef[k - 1] * (up + down if sign > 0 else up - down)
+            total = total + first_coef[k - 1] * (pick(k) - pick(-k))
         return total
 
-    def sum_y(ref, i, sign, coef):
-        total = 0.0
-        for k in range(1, 5):
-            up, down = (ref[i, :, LO + k : LO + CY + k, :], ref[i, :, LO - k : LO + CY - k, :])
-            total = total + coef[k - 1] * (up + down if sign > 0 else up - down)
-        return total
-
-    def row(in_x, in_y, i, energy):
-        centre = current[i + H, :, INSIDE, :]
-        second_x = sum_x(current, (), i + H, INSIDE, 1, second_coef)
-        second_y = sum_y(current, i + H, 1, second_coef)
-        laplace = second_x + second_y + (3.0 * centre_coef) * centre + bend_z[i] * (1.0 / COMMON)
-        every = slice(0, CY)
-        if in_x:
-            keep = keep_x[i]
-            take = keep - 1.0
-            flux = sum_x(memory_x_in, (source,), i + H, every, -1, first_coef)
-            bend = second_x + centre_coef * centre + flux
-            zeta = keep * zeta_x_in[i] + take * bend
-            zeta_x[i] = zeta
-            laplace = laplace + (flux + zeta)
-            grad = sum_x(current, (), i + H, INSIDE, -1, first_coef)
-            memory_x[target, i + H] = keep * memory_x_in[source, i + H] + take * grad
-        if in_y:
-            keep = keep_y[...]
-            take = keep - 1.0
-            flux = sum_y(memory_y_in, i, -1, first_coef)
-            bend = second_y + centre_coef * centre + flux
-            zeta = keep * zeta_y_in[i] + take * bend
-            zeta_y[i] = zeta
-            laplace = laplace + (flux + zeta)
-            grad = sum_y(current, i + H, -1, first_coef)
-            memory_y[i, :, INSIDE, :] = keep * memory_y_in[i, :, INSIDE, :] + take * grad
-        value = 2.0 * centre - previous[i + H, :, INSIDE, :]
-        following[i + H, :, INSIDE, :] = value + speed[i] * laplace
-        if step > 0 and (in_x or in_y):
-            energy = energy + energy_row(current, i, keep_x, keep_y)
+    def row(in_x, in_y, damped, i, energy):
+        for h in range(2):
+            centre = current[i + H, h, INSIDE, :]
+            second_x, grad_x = taps(lambda k: current[i + H + k, h, INSIDE, :], in_x)
+            second_y, grad_y = taps(lambda k: current[i + H, h, LO + k : LO + CY + k, :], in_y)
+            laplace = second_x + second_y + (3.0 * centre_coef) * centre
+            laplace = laplace + bend_z[i, h] * (1.0 / COMMON)
+            if in_x:
+                keep = keep_x[i]
+                take = keep - 1.0
+                flux = first_only(lambda k: memory_x_in[source, i + H + k, h])
+                bend = second_x + centre_coef * centre + flux
+                zeta = keep * zeta_x_in[i, h] + take * bend
+                zeta_x[i, h] = zeta
+                laplace = laplace + (flux + zeta)
+                memory_x[target, i + H, h] = keep * memory_x_in[source, i + H, h] + take * grad_x
+            if in_y:
+                keep = keep_y[...]
+                take = keep - 1.0
+                flux = first_only(lambda k: memory_y_in[i, h, LO + k : LO + CY + k, :])
+                bend = second_y + centre_coef * centre + flux
+                zeta = keep * zeta_y_in[i, h] + take * bend
+                zeta_y[i, h] = zeta
+                laplace = laplace + (flux + zeta)
+                kept = keep * memory_y_in[i, h, INSIDE, :] + take * grad_y
+                memory_y[i, h, INSIDE, :] = kept
+            value = 2.0 * centre - previous[i + H, h, INSIDE, :]
+            following[i + H, h, INSIDE, :] = value + speed[i, h] * laplace
+            if step > 0 and damped:
+                energy = energy + (1.0 - keep_x[i] * keep_y[...]) * (centre * centre)
         return energy
 
-    for in_x in (False, True):
-        for in_y in (False, True):
-
-            @pl.when((edge_x == in_x) & (edge_y == in_y))
+    for is_x in (False, True):
+        for is_y in (False, True):
+
+            @pl.when((edge_x == is_x) & (edge_y == is_y))
             def _():
-                zero = jnp.zeros((CY, LANES), jnp.float32) if in_x or in_y else 0
-                body = functools.partial(row, in_x, in_y)
-                energy = lax.fori_loop(0, CX, body, zero, unroll=1 if in_x or in_y else 2)
-                if step > 0 and (in_x or in_y):
+                damped = is_x or is_y
+                energy = jnp.zeros((CY, LANES), jnp.float32) if damped else 0
+                body = functools.partial(row, is_x, is_y, damped)
+                if is_x:
+                    starts_low = lax.axis_index(GX) == 0
+                    first = jnp.where(starts_low, 0, H)
+                    energy = lax.fori_loop(first, first + CX - H, body, energy)
+                    rest = jnp.where(starts_low, CX - H, 0)
+                    body = functools.partial(row, False, is_y, damped)
+                    energy = lax.fori_loop(rest, rest + H, body, energy)
+                else:
+                    energy = lax.fori_loop(0, CX, body, energy, unroll=2)
+                if step > 0 and damped:
                     note_energy(seen, step - 1, energy, norm)
 
     lane = lax.broadcasted_iota(jnp.int32, (1, LANES), 1)
@@ -290,7 +306,7 @@
         code = table[4 + n]
         s, z, ly, lx = (code & 63, (code >> 6) & 255, (code >> 14) & 31, code >> 19)
         at = (lx + H, z >> 7, pl.ds(ly + LO, 1), slice(None))
-        following[at] = following[at] + jnp.where(lane == (z & 127), amp[step, s], 0.0)
+        following[at] = following[at] + jnp.where(lane == (z & 127), amps[step * NSRC + s], 0.0)
         return carry
 
     lax.fori_loop(0, table[1], inject, 0)
@@ -377,7 +393,7 @@
         seen = seen + part[...]
     turned = seen.T
     traces[...] = turned[:NREC, :STEPS]
-    energy[...] = jnp.sum(turned[:, STEPS:], axis=0, keepdims=True)
+    energy[...] = jnp.sum(turned[:, STEPS:], axis=0)
 
 
 def vmem(count):
@@ -389,7 +405,7 @@
 
 
 def hbm(count):
-    return [pl.BlockSpec(memory_space=pl.ANY)] * count
+    return [pl.BlockSpec(memory_space=pltpu.HBM)] * count
 
 
 def shape(*sizes):
@@ -455,10 +471,15 @@
     previous, speed, *rest = pl.pallas_call(
         begin_kernel,
         out_shape=shape(FIELD, BLOCK, MEM_X, MEM_Y, BLOCK, BLOCK, SEEN, KEEP_X, KEEP_Y, NORM)
-        + [jax.ShapeDtypeStruct((TABLE,), jnp.int32)],
-        in_specs=smem(7) + hbm(2),
-        out_specs=vmem(10) + smem(1),
-        scratch_shapes=[staged, staged, pltpu.SemaphoreType.DMA((2, CHUNKS))],
+        + [
+            jax.ShapeDtypeStruct((TABLE,), jnp.int32),
+            jax.ShapeDtypeStruct((STEPS * NSRC,), jnp.float32),
+        ],
+        in_specs=hbm(10),
+        out_specs=vmem(10) + smem(2),
+        scratch_shapes=[staged, staged, pltpu.SemaphoreType.DMA((2, CHUNKS))]
+        + [pltpu.SMEM((n,), jnp.int32) for n in (4, NSRC, NSRC, NSRC, NREC, NREC, NREC)]
+        + [pltpu.SMEM((STEPS, NSRC), jnp.float32), pltpu.SemaphoreType.DMA((8,))],
         compiler_params=limit(8),
     )(
         layer_width,
@@ -468,10 +489,11 @@
         receiver_x,
         receiver_y,
         receiver_z,
+        source_amp,
         pressure_old,
         speed_term,
     )
-    state, keeps, table = (rest[:5], rest[5:8], rest[8])
+    state, keeps, table, amps = (rest[:5], rest[5:8], rest[8], rest[9])
     band = jnp.asarray(band_matrix())
     beside = pltpu.VMEM((CX, 2, 24, LANES), jnp.float32)
     for step in range(STEPS):
@@ -484,7 +506,7 @@
             scratch_shapes=[pltpu.VMEM(BLOCK, jnp.float32)],
             input_output_aliases={8: 0, 9: 1, 10: 2, 11: 3, 12: 4, 13: 5},
             compiler_params=limit(8),
-        )(table, source_amp, band, current, speed, *keeps, previous, *state)
+        )(table, amps, band, current, speed, *keeps, previous, *state)
         previous = current
         if step < STEPS - 1:
             current, *strips = pl.pallas_call(
@@ -516,12 +538,12 @@
     parts = gather_sums(seen)
     traces, energy = pl.pallas_call(
         report_kernel,
-        out_shape=shape((NREC, STEPS), (1, STEPS)),
+        out_shape=shape((NREC, STEPS), (STEPS,)),
         in_specs=vmem(len(parts)),
         out_specs=vmem(2),
         compiler_params=limit(2),
     )(*parts)
-    return final, traces, energy.reshape(STEPS)
+    return final, traces, energy
 
 
 def solution(mesh):

time: 128 us -> 128 us (level)
  Pallas kernels: 36.5 us -> 34.1 us
  waiting for transfers between devices: 25.8 us -> 27.8 us
    ppermute x32, waiting for transfers between devices: 17 us -> 19 us  [swap(): lax.ppermute(strip, axis, [(i, ((i + far ^ 1) - far) % size) for i in ran...]
    pallas_call x8, Pallas kernels: 26.3 us -> 24.3 us  [per_device(): pl.pallas_call(functools.partial(inner_kernel, step), out_shape=shape(FIE...]
  transfers between devices with their start and end apart: 42 -> 42, of which waited for: 20 -> 21; matrix products, arithmetic and copies ran while one was open for 1% -> 1% of each run, Pallas kernels for 25% -> 23%
where the time goes in v3:
time: 128 us; the launch traced here: 127 us
  starting transfers between devices  55.2 us (43%)
  Pallas kernels  34.1 us (27%)
  waiting for transfers between devices  27.8 us (22%)
  local copies, waits for them, and re-layouts  9.23 us (7%)
    ppermute x32, starting transfers between devices, swap(): lax.ppermute(strip, axis, [(i, ((i + far ^ 1) - far) % size) for i in ran...  42.2 us
    pallas_call x8, Pallas kernels, per_device(): pl.pallas_call(functools.partial(inner_kernel, step), out_shape=shape(FIE...  24.3 us
    ppermute x32, waiting for transfers between devices, swap(): lax.ppermute(strip, axis, [(i, ((i + far ^ 1) - far) % size) for i in ran...  19 us
    ppermute x10, starting transfers between devices, spread(): return lax.ppermute(value, BOTH, pairs)  13 us
    unnamed x24, local copies, waits for them, and re-layouts  9.23 us
    ppermute x10, waiting for transfers between devices, spread(): return lax.ppermute(value, BOTH, pairs)  8.83 us
    pallas_call x1, Pallas kernels, per_device(): pl.pallas_call(begin_kernel, out_shape=shape(FIELD, BLOCK, MEM_X, MEM_Y,...  4.22 us
  transfers between devices with their start and end apart: 42, of which 21 were waited for; matrix products, arithmetic and copies ran while one was open for 1% of the time, Pallas kernels for 23%

profile of v3, /device:TPU:0, one launch (start us, length us, event | category | flops | bytes accessed | tf_op | source)
XLA Modules:
  0.0 127.2 jit_solution(10407257275463778651)
XLA Ops:
  0.7 1.1 copy-done.3
  2.7 1.7 %collective-permute-start = (f32[4,2,24,128]{3,2,1,0:T(8,128)S(1)}, f32[4,2,24,128]{3,2,1,0:T(8,128)S(1)}, u32[]{:S(2)}, u32[]{:S(2)}) collective-permute-start(f32[4,2,24,128]{3,2,1,0:T(8,128)S(1)} %get-tuple-element.108), channel_id=1, source_target_pairs={{0,16},{16,0},{32,48},{48,32},{64,80},{80,64},{96,112},{112,96},{1... | collective-permute-start | bytes 294920 | tf_op jit(solution)/shard_map/ppermute | solution.py:421
  4.3 3.0 %collective-permute-start.1 = (f32[4,2,24,128]{3,2,1,0:T(8,128)S(1)}, f32[4,2,24,128]{3,2,1,0:T(8,128)S(1)}, u32[]{:S(2)}, u32[]{:S(2)}) collective-permute-start(f32[4,2,24,128]{3,2,1,0:T(8,128)S(1)} %get-tuple-element.109), channel_id=1, source_target_pairs={{0,112},{16,32},{32,16},{48,64},{64,48},{80,96},{96,80},{112,0},{1... | collective-permute-start | bytes 294920 | tf_op jit(solution)/shard_map/ppermute | solution.py:421
  7.3 6.6 %collective-permute-start.3 = (f32[24,2,4,128]{3,2,1,0:T(4,128)S(1)}, f32[24,2,4,128]{3,2,1,0:T(4,128)S(1)}, u32[]{:S(2)}, u32[]{:S(2)}) collective-permute-start(f32[24,2,4,128]{3,2,1,0:T(4,128)S(1)} %get-tuple-element.111), channel_id=1, source_target_pairs={{0,15},{1,2},{2,1},{3,4},{4,3},{5,6},{6,5},{7,8},{8,7},{9,10},{10,... | collective-permute-start | bytes 294920 | tf_op jit(solution)/shard_map/ppermute | solution.py:421
  14.7 1.1 copy-done.1
  15.8 1.1 copy-done.2
  21.4 4.2 %shard_map.139 = (f32[32,2,40,128]{3,2,1,0:T(8,128)S(1)}, f32[24,2,24,128]{3,2,1,0:T(8,128)S(1)}, f32[2,32,2,24,128]{4,3,2,1,0:T(8,128)S(1)}, f32[24,2,40,128]{3...) custom-call(s32[4]{0:T(128)S(1)} %copy-done.4, ...), custom_call_target="tpu_custom_call" | custom-call | tf_op jit(solution)/shard_map/pallas_call | solution.py:471
  25.7 2.9 %shard_map.141 = (f32[32,2,40,128]{3,2,1,0:T(8,128)S(1)}, f32[2,32,2,24,128]{4,3,2,1,0:T(8,128)S(1)}, f32[24,2,40,128]{3,2,1,0:T(8,128)S(1)}, f32[24,2,24,128]{3...) custom-call(s32[72]{0:T(128)S(1)} %get-tuple-element.103.table.refs_, ...), custom_call_target="tpu_custom_call", output_to_operand_aliasing={{0}: (8, {}), {1}: (9, {}), {2}: (10, {}), {3}: (11, {}), {... | custom-call | tf_op jit(solution)/shard_map/pallas_call | solution.py:501
  29.0 1.4 %collective-permute-start.5 = (f32[4,2,24,128]{3,2,1,0:T(8,128)S(1)}, f32[4,2,24,128]{3,2,1,0:T(8,128)S(1)}, u32[]{:S(2)}, u32[]{:S(2)}) collective-permute-start(f32[4,2,24,128]{3,2,1,0:T(8,128)S(1)} %get-tuple-element.122), channel_id=1, source_target_pairs={{0,112},{16,32},{32,16},{48,64},{64,48},{80,96},{96,80},{112,0},{1... | collective-permute-start | bytes 294920 | tf_op jit(solution)/shard_map/ppermute | solution.py:421
  30.7 3.0 %shard_map.143 = (f32[32,2,40,128]{3,2,1,0:T(8,128)S(1)}, f32[2,32,2,24,128]{4,3,2,1,0:T(8,128)S(1)}, f32[24,2,40,128]{3,2,1,0:T(8,128)S(1)}, f32[24,2,24,128]{3...) custom-call(s32[72]{0:T(128)S(1)} %get-tuple-element.103.table.refs_, ...), custom_call_target="tpu_custom_call", output_to_operand_aliasing={{0}: (8, {}), {1}: (9, {}), {2}: (10, {}), {3}: (11, {}), {... | custom-call | tf_op jit(solution)/shard_map/pallas_call | solution.py:501
  34.5 2.2 %collective-permute-done.5.refs_2_ = f32[4,2,24,128]{3,2,1,0:T(8,128)S(1)} collective-permute-done((f32[4,2,24,128]{3,2,1,0:T(8,128)S(1)}, f32[4,2,24,128]{3,2,1,0:T(8,128)S(1)}, u32[]{:S(2)}, u32[]{:S(2)}) %collective-permute-start.5) | collective-permute-done | bytes 98336 | tf_op jit(solution)/shard_map/ppermute | solution.py:421
  36.7 1.4 %collective-permute-done.7.refs_4_ = f32[24,2,4,128]{3,2,1,0:T(4,128)S(1)} collective-permute-done((f32[24,2,4,128]{3,2,1,0:T(4,128)S(1)}, f32[24,2,4,128]{3,2,1,0:T(4,128)S(1)}, u32[]{:S(2)}, u32[]{:S(2)}) %collective-permute-start.7) | collective-permute-done | bytes 98336 | tf_op jit(solution)/shard_map/ppermute | solution.py:421
  39.1 2.3 %collective-permute-start.9 = (f32[4,2,24,128]{3,2,1,0:T(8,128)S(1)}, f32[4,2,24,128]{3,2,1,0:T(8,128)S(1)}, u32[]{:S(2)}, u32[]{:S(2)}) collective-permute-start(f32[4,2,24,128]{3,2,1,0:T(8,128)S(1)} %get-tuple-element.133), channel_id=1, source_target_pairs={{0,112},{16,32},{32,16},{48,64},{64,48},{80,96},{96,80},{112,0},{1... | collective-permute-start | bytes 294920 | tf_op jit(solution)/shard_map/ppermute | solution.py:421
  41.4 2.3 %collective-permute-start.11 = (f32[24,2,4,128]{3,2,1,0:T(4,128)S(1)}, f32[24,2,4,128]{3,2,1,0:T(4,128)S(1)}, u32[]{:S(2)}, u32[]{:S(2)}) collective-permute-start(f32[24,2,4,128]{3,2,1,0:T(4,128)S(1)} %get-tuple-element.135), channel_id=1, source_target_pairs={{0,15},{1,2},{2,1},{3,4},{4,3},{5,6},{6,5},{7,8},{8,7},{9,10},{10,... | collective-permute-start | bytes 294920 | tf_op jit(solution)/shard_map/ppermute | solution.py:421
  43.6 3.0 %shard_map.145 = (f32[32,2,40,128]{3,2,1,0:T(8,128)S(1)}, f32[2,32,2,24,128]{4,3,2,1,0:T(8,128)S(1)}, f32[24,2,40,128]{3,2,1,0:T(8,128)S(1)}, f32[24,2,24,128]{3...) custom-call(s32[72]{0:T(128)S(1)} %get-tuple-element.103.table.refs_, ...), custom_call_target="tpu_custom_call", output_to_operand_aliasing={{0}: (8, {}), {1}: (9, {}), {2}: (10, {}), {3}: (11, {}), {... | custom-call | tf_op jit(solution)/shard_map/pallas_call | solution.py:501
  46.7 2.3 %collective-permute-done.11.refs_4_ = f32[24,2,4,128]{3,2,1,0:T(4,128)S(1)} collective-permute-done((f32[24,2,4,128]{3,2,1,0:T(4,128)S(1)}, f32[24,2,4,128]{3,2,1,0:T(4,128)S(1)}, u32[]{:S(2)}, u32[]{:S(2)}) %collective-permute-start.11) | collective-permute-done | bytes 98336 | tf_op jit(solution)/shard_map/ppermute | solution.py:421
  50.1 1.3 collective-permute-start.13
  51.4 2.7 %collective-permute-start.15 = (f32[24,2,4,128]{3,2,1,0:T(4,128)S(1)}, f32[24,2,4,128]{3,2,1,0:T(4,128)S(1)}, u32[]{:S(2)}, u32[]{:S(2)}) collective-permute-start(f32[24,2,4,128]{3,2,1,0:T(4,128)S(1)} %get-tuple-element.146), channel_id=1, source_target_pairs={{0,15},{1,2},{2,1},{3,4},{4,3},{5,6},{6,5},{7,8},{8,7},{9,10},{10,... | collective-permute-start | bytes 294920 | tf_op jit(solution)/shard_map/ppermute | solution.py:421
  54.1 3.0 %shard_map.147 = (f32[32,2,40,128]{3,2,1,0:T(8,128)S(1)}, f32[2,32,2,24,128]{4,3,2,1,0:T(8,128)S(1)}, f32[24,2,40,128]{3,2,1,0:T(8,128)S(1)}, f32[24,2,24,128]{3...) custom-call(s32[72]{0:T(128)S(1)} %get-tuple-element.103.table.refs_, ...), custom_call_target="tpu_custom_call", output_to_operand_aliasing={{0}: (8, {}), {1}: (9, {}), {2}: (10, {}), {3}: (11, {}), {... | custom-call | tf_op jit(solution)/shard_map/pallas_call | solution.py:501
  57.8 1.3 %collective-permute-done.15.refs_4_ = f32[24,2,4,128]{3,2,1,0:T(4,128)S(1)} collective-permute-done((f32[24,2,4,128]{3,2,1,0:T(4,128)S(1)}, f32[24,2,4,128]{3,2,1,0:T(4,128)S(1)}, u32[]{:S(2)}, u32[]{:S(2)}) %collective-permute-start.15) | collective-permute-done | bytes 98336 | tf_op jit(solution)/shard_map/ppermute | solution.py:421
  60.1 3.5 %collective-permute-start.17 = (f32[4,2,24,128]{3,2,1,0:T(8,128)S(1)}, f32[4,2,24,128]{3,2,1,0:T(8,128)S(1)}, u32[]{:S(2)}, u32[]{:S(2)}) collective-permute-start(f32[4,2,24,128]{3,2,1,0:T(8,128)S(1)} %get-tuple-element.155), channel_id=1, source_target_pairs={{0,112},{16,32},{32,16},{48,64},{64,48},{80,96},{96,80},{112,0},{1... | collective-permute-start | bytes 294920 | tf_op jit(solution)/shard_map/ppermute | solution.py:421
  63.7 1.4 %collective-permute-start.19 = (f32[24,2,4,128]{3,2,1,0:T(4,128)S(1)}, f32[24,2,4,128]{3,2,1,0:T(4,128)S(1)}, u32[]{:S(2)}, u32[]{:S(2)}) collective-permute-start(f32[24,2,4,128]{3,2,1,0:T(4,128)S(1)} %get-tuple-element.157), channel_id=1, source_target_pairs={{0,15},{1,2},{2,1},{3,4},{4,3},{5,6},{6,5},{7,8},{8,7},{9,10},{10,... | collective-permute-start | bytes 294920 | tf_op jit(solution)/shard_map/ppermute | solution.py:421
  65.0 3.2 %shard_map.149 = (f32[32,2,40,128]{3,2,1,0:T(8,128)S(1)}, f32[2,32,2,24,128]{4,3,2,1,0:T(8,128)S(1)}, f32[24,2,40,128]{3,2,1,0:T(8,128)S(1)}, f32[24,2,24,128]{3...) custom-call(s32[72]{0:T(128)S(1)} %get-tuple-element.103.table.refs_, ...), custom_call_target="tpu_custom_call", output_to_operand_aliasing={{0}: (8, {}), {1}: (9, {}), {2}: (10, {}), {3}: (11, {}), {... | custom-call | tf_op jit(solution)/shard_map/pallas_call | solution.py:501
  68.4 3.0 %collective-permute-done.19.refs_4_ = f32[24,2,4,128]{3,2,1,0:T(4,128)S(1)} collective-permute-done((f32[24,2,4,128]{3,2,1,0:T(4,128)S(1)}, f32[24,2,4,128]{3,2,1,0:T(4,128)S(1)}, u32[]{:S(2)}, u32[]{:S(2)}) %collective-permute-start.19) | collective-permute-done | bytes 98336 | tf_op jit(solution)/shard_map/ppermute | solution.py:421
  71.8 1.3 %collective-permute-start.21 = (f32[4,2,24,128]{3,2,1,0:T(8,128)S(1)}, f32[4,2,24,128]{3,2,1,0:T(8,128)S(1)}, u32[]{:S(2)}, u32[]{:S(2)}) collective-permute-start(f32[4,2,24,128]{3,2,1,0:T(8,128)S(1)} %get-tuple-element.166), channel_id=1, source_target_pairs={{0,112},{16,32},{32,16},{48,64},{64,48},{80,96},{96,80},{112,0},{1... | collective-permute-start | bytes 294920 | tf_op jit(solution)/shard_map/ppermute | solution.py:421
  73.1 2.1 %collective-permute-start.23 = (f32[24,2,4,128]{3,2,1,0:T(4,128)S(1)}, f32[24,2,4,128]{3,2,1,0:T(4,128)S(1)}, u32[]{:S(2)}, u32[]{:S(2)}) collective-permute-start(f32[24,2,4,128]{3,2,1,0:T(4,128)S(1)} %get-tuple-element.168), channel_id=1, source_target_pairs={{0,15},{1,2},{2,1},{3,4},{4,3},{5,6},{6,5},{7,8},{8,7},{9,10},{10,... | collective-permute-start | bytes 294920 | tf_op jit(solution)/shard_map/ppermute | solution.py:421
  75.3 3.0 %shard_map.151 = (f32[32,2,40,128]{3,2,1,0:T(8,128)S(1)}, f32[2,32,2,24,128]{4,3,2,1,0:T(8,128)S(1)}, f32[24,2,40,128]{3,2,1,0:T(8,128)S(1)}, f32[24,2,24,128]{3...) custom-call(s32[72]{0:T(128)S(1)} %get-tuple-element.103.table.refs_, ...), custom_call_target="tpu_custom_call", output_to_operand_aliasing={{0}: (8, {}), {1}: (9, {}), {2}: (10, {}), {3}: (11, {}), {... | custom-call | tf_op jit(solution)/shard_map/pallas_call | solution.py:501
  78.3 1.1 collective-permute-done.21.refs_2_
  79.4 1.4 %collective-permute-done.23.refs_4_ = f32[24,2,4,128]{3,2,1,0:T(4,128)S(1)} collective-permute-done((f32[24,2,4,128]{3,2,1,0:T(4,128)S(1)}, f32[24,2,4,128]{3,2,1,0:T(4,128)S(1)}, u32[]{:S(2)}, u32[]{:S(2)}) %collective-permute-start.23) | collective-permute-done | bytes 98336 | tf_op jit(solution)/shard_map/ppermute | solution.py:421
  81.8 2.4 %collective-permute-start.25 = (f32[4,2,24,128]{3,2,1,0:T(8,128)S(1)}, f32[4,2,24,128]{3,2,1,0:T(8,128)S(1)}, u32[]{:S(2)}, u32[]{:S(2)}) collective-permute-start(f32[4,2,24,128]{3,2,1,0:T(8,128)S(1)} %get-tuple-element.177), channel_id=1, source_target_pairs={{0,112},{16,32},{32,16},{48,64},{64,48},{80,96},{96,80},{112,0},{1... | collective-permute-start | bytes 294920 | tf_op jit(solution)/shard_map/ppermute | solution.py:421
  84.2 2.1 %collective-permute-start.27 = (f32[24,2,4,128]{3,2,1,0:T(4,128)S(1)}, f32[24,2,4,128]{3,2,1,0:T(4,128)S(1)}, u32[]{:S(2)}, u32[]{:S(2)}) collective-permute-start(f32[24,2,4,128]{3,2,1,0:T(4,128)S(1)} %get-tuple-element.179), channel_id=1, source_target_pairs={{0,15},{1,2},{2,1},{3,4},{4,3},{5,6},{6,5},{7,8},{8,7},{9,10},{10,... | collective-permute-start | bytes 294920 | tf_op jit(solution)/shard_map/ppermute | solution.py:421
  86.3 3.0 %shard_map.153 = (f32[32,2,40,128]{3,2,1,0:T(8,128)S(1)}, f32[2,32,2,24,128]{4,3,2,1,0:T(8,128)S(1)}, f32[24,2,40,128]{3,2,1,0:T(8,128)S(1)}, f32[24,2,24,128]{3...) custom-call(s32[72]{0:T(128)S(1)} %get-tuple-element.103.table.refs_, ...), custom_call_target="tpu_custom_call", output_to_operand_aliasing={{0}: (8, {}), {1}: (9, {}), {2}: (10, {}), {3}: (11, {}), {... | custom-call | tf_op jit(solution)/shard_map/pallas_call | solution.py:501
  89.4 2.5 %collective-permute-done.27.refs_4_ = f32[24,2,4,128]{3,2,1,0:T(4,128)S(1)} collective-permute-done((f32[24,2,4,128]{3,2,1,0:T(4,128)S(1)}, f32[24,2,4,128]{3,2,1,0:T(4,128)S(1)}, u32[]{:S(2)}, u32[]{:S(2)}) %collective-permute-start.27) | collective-permute-done | bytes 98336 | tf_op jit(solution)/shard_map/ppermute | solution.py:421
  92.9 1.7 %collective-permute-start.29 = (f32[4,2,24,128]{3,2,1,0:T(8,128)S(1)}, f32[4,2,24,128]{3,2,1,0:T(8,128)S(1)}, u32[]{:S(2)}, u32[]{:S(2)}) collective-permute-start(f32[4,2,24,128]{3,2,1,0:T(8,128)S(1)} %get-tuple-element.188), channel_id=1, source_target_pairs={{0,112},{16,32},{32,16},{48,64},{64,48},{80,96},{96,80},{112,0},{1... | collective-permute-start | bytes 294920 | tf_op jit(solution)/shard_map/ppermute | solution.py:421
  94.5 2.3 %collective-permute-start.31 = (f32[24,2,4,128]{3,2,1,0:T(4,128)S(1)}, f32[24,2,4,128]{3,2,1,0:T(4,128)S(1)}, u32[]{:S(2)}, u32[]{:S(2)}) collective-permute-start(f32[24,2,4,128]{3,2,1,0:T(4,128)S(1)} %get-tuple-element.190), channel_id=1, source_target_pairs={{0,15},{1,2},{2,1},{3,4},{4,3},{5,6},{6,5},{7,8},{8,7},{9,10},{10,... | collective-permute-start | bytes 294920 | tf_op jit(solution)/shard_map/ppermute | solution.py:421
  96.8 3.0 %shard_map.155 = (f32[32,2,40,128]{3,2,1,0:T(8,128)S(1)}, f32[2,32,2,24,128]{4,3,2,1,0:T(8,128)S(1)}, f32[24,2,40,128]{3,2,1,0:T(8,128)S(1)}, f32[24,2,24,128]{3...) custom-call(s32[72]{0:T(128)S(1)} %get-tuple-element.103.table.refs_, ...), custom_call_target="tpu_custom_call", output_to_operand_aliasing={{0}: (8, {}), {1}: (9, {}), {2}: (10, {}), {3}: (11, {}), {... | custom-call | tf_op jit(solution)/shard_map/pallas_call | solution.py:501
  100.5 1.7 %collective-permute-done.31.refs_8_ = f32[24,2,4,128]{3,2,1,0:T(4,128)S(1)} collective-permute-done((f32[24,2,4,128]{3,2,1,0:T(4,128)S(1)}, f32[24,2,4,128]{3,2,1,0:T(4,128)S(1)}, u32[]{:S(2)}, u32[]{:S(2)}) %collective-permute-start.31) | collective-permute-done | bytes 98336 | tf_op jit(solution)/shard_map/ppermute | solution.py:421
  103.2 1.2 collective-permute-done.32
  104.4 2.3 %collective-permute-start.34 = (f32[16,128]{1,0:T(8,128)S(1)}, f32[16,128]{1,0:T(8,128)S(1)}, u32[]{:S(2)}, u32[]{:S(2)}) collective-permute-start(f32[16,128]{1,0:T(8,128)S(1)} %add.21), channel_id=1, source_target_pairs={{0,2},{1,3},{2,0},{3,1},{4,6},{5,7},{6,4},{7,5},{8,10},{9,11},{10,... | collective-permute-start | bytes 24584 | tf_op jit(solution)/shard_map/ppermute | solution.py:435
  106.7 1.8 %collective-permute-start.33 = (f32[16,128]{1,0:T(8,128)S(1)}, f32[16,128]{1,0:T(8,128)S(1)}, u32[]{:S(2)}, u32[]{:S(2)}) collective-permute-start(f32[16,128]{1,0:T(8,128)S(1)} %add.21), channel_id=1, source_target_pairs={{0,16},{1,17},{2,18},{3,19},{4,20},{5,21},{6,22},{7,23},{8,24},{9,... | collective-permute-start | bytes 24584 | tf_op jit(solution)/shard_map/ppermute | solution.py:435
  110.4 1.9 %collective-permute-start.38 = (f32[16,128]{1,0:T(8,128)S(1)}, f32[16,128]{1,0:T(8,128)S(1)}, u32[]{:S(2)}, u32[]{:S(2)}) collective-permute-start(f32[16,128]{1,0:T(8,128)S(1)} %add_add_fusion.1), channel_id=1, source_target_pairs={{0,12},{1,13},{2,14},{3,15},{4,8},{5,9},{6,10},{7,11},{8,4},{9,5},... | collective-permute-start | bytes 24584 | tf_op jit(solution)/shard_map/ppermute | solution.py:435
  112.3 2.2 %collective-permute-start.36 = (f32[16,128]{1,0:T(8,128)S(1)}, f32[16,128]{1,0:T(8,128)S(1)}, u32[]{:S(2)}, u32[]{:S(2)}) collective-permute-start(f32[16,128]{1,0:T(8,128)S(1)} %add_add_fusion.1), channel_id=1, source_target_pairs={{0,4},{1,5},{2,6},{3,7},{4,0},{5,1},{6,2},{7,3},{8,12},{9,13},{10,... | collective-permute-start | bytes 24584 | tf_op jit(solution)/shard_map/ppermute | solution.py:435
  115.2 2.2 %collective-permute-done.37 = f32[16,128]{1,0:T(8,128)S(1)} collective-permute-done((f32[16,128]{1,0:T(8,128)S(1)}, f32[16,128]{1,0:T(8,128)S(1)}, u32[]{:S(2)}, u32[]{:S(2)}) %collective-permute-start.37) | collective-permute-done | bytes 8224 | tf_op jit(solution)/shard_map/ppermute | solution.py:435
  117.4 1.5 %collective-permute-start.39 = (f32[16,128]{1,0:T(8,128)S(1)}, f32[16,128]{1,0:T(8,128)S(1)}, u32[]{:S(2)}, u32[]{:S(2)}) collective-permute-start(f32[16,128]{1,0:T(8,128)S(1)} %add_add_fusion.refs_0_), channel_id=1, source_target_pairs={{0,32},{1,33},{2,34},{3,35},{4,36},{5,37},{6,38},{7,39},{8,40},{9,... | collective-permute-start | bytes 24584 | tf_op jit(solution)/shard_map/ppermute | solution.py:435
  119.0 2.1 %collective-permute-start.40 = (f32[16,128]{1,0:T(8,128)S(1)}, f32[16,128]{1,0:T(8,128)S(1)}, u32[]{:S(2)}, u32[]{:S(2)}) collective-permute-start(f32[16,128]{1,0:T(8,128)S(1)} %add_add_fusion.refs_0_), channel_id=1, source_target_pairs={{0,64},{1,65},{2,66},{3,67},{4,68},{5,69},{6,70},{7,71},{8,72},{9,... | collective-permute-start | bytes 24584 | tf_op jit(solution)/shard_map/ppermute | solution.py:435
  121.0 1.2 collective-permute-start.41
  123.1 1.0 collective-permute-done.40.refs_2_
  124.1 1.8 %collective-permute-done.41.refs_3_ = f32[16,128]{1,0:T(8,128)S(1)} collective-permute-done((f32[16,128]{1,0:T(8,128)S(1)}, f32[16,128]{1,0:T(8,128)S(1)}, u32[]{:S(2)}, u32[]{:S(2)}) %collective-permute-start.41) | collective-permute-done | bytes 8224 | tf_op jit(solution)/shard_map/ppermute | solution.py:435
  (83 shorter events, 20.7 us)
Async XLA Ops:
  0.6 25.0 %copy-start = (bf16[512,256]{1,0:T(8,128)(2,1)S(1)}, bf16[512,256]{1,0:T(8,128)(2,1)}, u32[]{:S(2)}) copy-start(bf16[512,256]{1,0:T(8,128)(2,1)} %constant.2.clone.band) | copy-start | bytes 786436
  0.6 1.1 copy-start.3
  2.7 25.9 %collective-permute-start = (f32[4,2,24,128]{3,2,1,0:T(8,128)S(1)}, f32[4,2,24,128]{3,2,1,0:T(8,128)S(1)}, u32[]{:S(2)}, u32[]{:S(2)}) collective-permute-start(f32[4,2,24,128]{3,2,1,0:T(8,128)S(1)} %get-tuple-element.108), channel_id=1, source_target_pairs={{0,16},{16,0},{32,48},{48,32},{64,80},{80,64},{96,112},{112,96},{1... | collective-permute-start | bytes 294920 | tf_op jit(solution)/shard_map/ppermute | solution.py:421
  4.3 24.2 %collective-permute-start.1 = (f32[4,2,24,128]{3,2,1,0:T(8,128)S(1)}, f32[4,2,24,128]{3,2,1,0:T(8,128)S(1)}, u32[]{:S(2)}, u32[]{:S(2)}) collective-permute-start(f32[4,2,24,128]{3,2,1,0:T(8,128)S(1)} %get-tuple-element.109), channel_id=1, source_target_pairs={{0,112},{16,32},{32,16},{48,64},{64,48},{80,96},{96,80},{112,0},{1... | collective-permute-start | bytes 294920 | tf_op jit(solution)/shard_map/ppermute | solution.py:421
  7.3 21.3 %collective-permute-start.2 = (f32[24,2,4,128]{3,2,1,0:T(4,128)S(1)}, f32[24,2,4,128]{3,2,1,0:T(4,128)S(1)}, u32[]{:S(2)}, u32[]{:S(2)}) collective-permute-start(f32[24,2,4,128]{3,2,1,0:T(4,128)S(1)} %get-tuple-element.110), channel_id=1, source_target_pairs={{0,1},{1,0},{2,3},{3,2},{4,5},{5,4},{6,7},{7,6},{8,9},{9,8},{10,11... | collective-permute-start | bytes 294920 | tf_op jit(solution)/shard_map/ppermute | solution.py:421
  7.3 21.3 %collective-permute-start.3 = (f32[24,2,4,128]{3,2,1,0:T(4,128)S(1)}, f32[24,2,4,128]{3,2,1,0:T(4,128)S(1)}, u32[]{:S(2)}, u32[]{:S(2)}) collective-permute-start(f32[24,2,4,128]{3,2,1,0:T(4,128)S(1)} %get-tuple-element.111), channel_id=1, source_target_pairs={{0,15},{1,2},{2,1},{3,4},{4,3},{5,6},{6,5},{7,8},{8,7},{9,10},{10,... | collective-permute-start | bytes 294920 | tf_op jit(solution)/shard_map/ppermute | solution.py:421
  14.7 1.1 copy-start.1
  15.8 1.1 copy-start.2
  16.8 0.7 copy-start.4
  17.5 0.7 copy-start.5
  28.9 5.6 %collective-permute-start.4 = (f32[4,2,24,128]{3,2,1,0:T(8,128)S(1)}, f32[4,2,24,128]{3,2,1,0:T(8,128)S(1)}, u32[]{:S(2)}, u32[]{:S(2)}) collective-permute-start(f32[4,2,24,128]{3,2,1,0:T(8,128)S(1)} %get-tuple-element.121), channel_id=1, source_target_pairs={{0,16},{16,0},{32,48},{48,32},{64,80},{80,64},{96,112},{112,96},{1... | collective-permute-start | bytes 294920 | tf_op jit(solution)/shard_map/ppermute | solution.py:421
  29.0 7.7 %collective-permute-start.5 = (f32[4,2,24,128]{3,2,1,0:T(8,128)S(1)}, f32[4,2,24,128]{3,2,1,0:T(8,128)S(1)}, u32[]{:S(2)}, u32[]{:S(2)}) collective-permute-start(f32[4,2,24,128]{3,2,1,0:T(8,128)S(1)} %get-tuple-element.122), channel_id=1, source_target_pairs={{0,112},{16,32},{32,16},{48,64},{64,48},{80,96},{96,80},{112,0},{1... | collective-permute-start | bytes 294920 | tf_op jit(solution)/shard_map/ppermute | solution.py:421
  30.4 6.3 %collective-permute-start.6 = (f32[24,2,4,128]{3,2,1,0:T(4,128)S(1)}, f32[24,2,4,128]{3,2,1,0:T(4,128)S(1)}, u32[]{:S(2)}, u32[]{:S(2)}) collective-permute-start(f32[24,2,4,128]{3,2,1,0:T(4,128)S(1)} %get-tuple-element.123), channel_id=1, source_target_pairs={{0,1},{1,0},{2,3},{3,2},{4,5},{5,4},{6,7},{7,6},{8,9},{9,8},{10,11... | collective-permute-start | bytes 294920 | tf_op jit(solution)/shard_map/ppermute | solution.py:421
  30.4 7.7 %collective-permute-start.7 = (f32[24,2,4,128]{3,2,1,0:T(4,128)S(1)}, f32[24,2,4,128]{3,2,1,0:T(4,128)S(1)}, u32[]{:S(2)}, u32[]{:S(2)}) collective-permute-start(f32[24,2,4,128]{3,2,1,0:T(4,128)S(1)} %get-tuple-element.124), channel_id=1, source_target_pairs={{0,15},{1,2},{2,1},{3,4},{4,3},{5,6},{6,5},{7,8},{8,7},{9,10},{10,... | collective-permute-start | bytes 294920 | tf_op jit(solution)/shard_map/ppermute | solution.py:421
  38.4 8.3 %collective-permute-start.8 = (f32[4,2,24,128]{3,2,1,0:T(8,128)S(1)}, f32[4,2,24,128]{3,2,1,0:T(8,128)S(1)}, u32[]{:S(2)}, u32[]{:S(2)}) collective-permute-start(f32[4,2,24,128]{3,2,1,0:T(8,128)S(1)} %get-tuple-element.132), channel_id=1, source_target_pairs={{0,16},{16,0},{32,48},{48,32},{64,80},{80,64},{96,112},{112,96},{1... | collective-permute-start | bytes 294920 | tf_op jit(solution)/shard_map/ppermute | solution.py:421
  39.1 7.6 %collective-permute-start.9 = (f32[4,2,24,128]{3,2,1,0:T(8,128)S(1)}, f32[4,2,24,128]{3,2,1,0:T(8,128)S(1)}, u32[]{:S(2)}, u32[]{:S(2)}) collective-permute-start(f32[4,2,24,128]{3,2,1,0:T(8,128)S(1)} %get-tuple-element.133), channel_id=1, source_target_pairs={{0,112},{16,32},{32,16},{48,64},{64,48},{80,96},{96,80},{112,0},{1... | collective-permute-start | bytes 294920 | tf_op jit(solution)/shard_map/ppermute | solution.py:421
  41.4 5.3 %collective-permute-start.10 = (f32[24,2,4,128]{3,2,1,0:T(4,128)S(1)}, f32[24,2,4,128]{3,2,1,0:T(4,128)S(1)}, u32[]{:S(2)}, u32[]{:S(2)}) collective-permute-start(f32[24,2,4,128]{3,2,1,0:T(4,128)S(1)} %get-tuple-element.134), channel_id=1, source_target_pairs={{0,1},{1,0},{2,3},{3,2},{4,5},{5,4},{6,7},{7,6},{8,9},{9,8},{10,11... | collective-permute-start | bytes 294920 | tf_op jit(solution)/shard_map/ppermute | solution.py:421
  41.4 7.7 %collective-permute-start.11 = (f32[24,2,4,128]{3,2,1,0:T(4,128)S(1)}, f32[24,2,4,128]{3,2,1,0:T(4,128)S(1)}, u32[]{:S(2)}, u32[]{:S(2)}) collective-permute-start(f32[24,2,4,128]{3,2,1,0:T(4,128)S(1)} %get-tuple-element.135), channel_id=1, source_target_pairs={{0,15},{1,2},{2,1},{3,4},{4,3},{5,6},{6,5},{7,8},{8,7},{9,10},{10,... | collective-permute-start | bytes 294920 | tf_op jit(solution)/shard_map/ppermute | solution.py:421
  49.3 7.8 %collective-permute-start.12 = (f32[4,2,24,128]{3,2,1,0:T(8,128)S(1)}, f32[4,2,24,128]{3,2,1,0:T(8,128)S(1)}, u32[]{:S(2)}, u32[]{:S(2)}) collective-permute-start(f32[4,2,24,128]{3,2,1,0:T(8,128)S(1)} %get-tuple-element.143), channel_id=1, source_target_pairs={{0,16},{16,0},{32,48},{48,32},{64,80},{80,64},{96,112},{112,96},{1... | collective-permute-start | bytes 294920 | tf_op jit(solution)/shard_map/ppermute | solution.py:421
  50.1 7.6 %collective-permute-start.13 = (f32[4,2,24,128]{3,2,1,0:T(8,128)S(1)}, f32[4,2,24,128]{3,2,1,0:T(8,128)S(1)}, u32[]{:S(2)}, u32[]{:S(2)}) collective-permute-start(f32[4,2,24,128]{3,2,1,0:T(8,128)S(1)} %get-tuple-element.144), channel_id=1, source_target_pairs={{0,112},{16,32},{32,16},{48,64},{64,48},{80,96},{96,80},{112,0},{1... | collective-permute-start | bytes 294920 | tf_op jit(solution)/shard_map/ppermute | solution.py:421
  51.4 6.3 %collective-permute-start.14 = (f32[24,2,4,128]{3,2,1,0:T(4,128)S(1)}, f32[24,2,4,128]{3,2,1,0:T(4,128)S(1)}, u32[]{:S(2)}, u32[]{:S(2)}) collective-permute-start(f32[24,2,4,128]{3,2,1,0:T(4,128)S(1)} %get-tuple-element.145), channel_id=1, source_target_pairs={{0,1},{1,0},{2,3},{3,2},{4,5},{5,4},{6,7},{7,6},{8,9},{9,8},{10,11... | collective-permute-start | bytes 294920 | tf_op jit(solution)/shard_map/ppermute | solution.py:421
  51.4 7.7 %collective-permute-start.15 = (f32[24,2,4,128]{3,2,1,0:T(4,128)S(1)}, f32[24,2,4,128]{3,2,1,0:T(4,128)S(1)}, u32[]{:S(2)}, u32[]{:S(2)}) collective-permute-start(f32[24,2,4,128]{3,2,1,0:T(4,128)S(1)} %get-tuple-element.146), channel_id=1, source_target_pairs={{0,15},{1,2},{2,1},{3,4},{4,3},{5,6},{6,5},{7,8},{8,7},{9,10},{10,... | collective-permute-start | bytes 294920 | tf_op jit(solution)/shard_map/ppermute | solution.py:421
  59.4 8.8 %collective-permute-start.16 = (f32[4,2,24,128]{3,2,1,0:T(8,128)S(1)}, f32[4,2,24,128]{3,2,1,0:T(8,128)S(1)}, u32[]{:S(2)}, u32[]{:S(2)}) collective-permute-start(f32[4,2,24,128]{3,2,1,0:T(8,128)S(1)} %get-tuple-element.154), channel_id=1, source_target_pairs={{0,16},{16,0},{32,48},{48,32},{64,80},{80,64},{96,112},{112,96},{1... | collective-permute-start | bytes 294920 | tf_op jit(solution)/shard_map/ppermute | solution.py:421
  60.1 8.2 %collective-permute-start.17 = (f32[4,2,24,128]{3,2,1,0:T(8,128)S(1)}, f32[4,2,24,128]{3,2,1,0:T(8,128)S(1)}, u32[]{:S(2)}, u32[]{:S(2)}) collective-permute-start(f32[4,2,24,128]{3,2,1,0:T(8,128)S(1)} %get-tuple-element.155), channel_id=1, source_target_pairs={{0,112},{16,32},{32,16},{48,64},{64,48},{80,96},{96,80},{112,0},{1... | collective-permute-start | bytes 294920 | tf_op jit(solution)/shard_map/ppermute | solution.py:421
  63.7 4.7 %collective-permute-start.18 = (f32[24,2,4,128]{3,2,1,0:T(4,128)S(1)}, f32[24,2,4,128]{3,2,1,0:T(4,128)S(1)}, u32[]{:S(2)}, u32[]{:S(2)}) collective-permute-start(f32[24,2,4,128]{3,2,1,0:T(4,128)S(1)} %get-tuple-element.156), channel_id=1, source_target_pairs={{0,1},{1,0},{2,3},{3,2},{4,5},{5,4},{6,7},{7,6},{8,9},{9,8},{10,11... | collective-permute-start | bytes 294920 | tf_op jit(solution)/shard_map/ppermute | solution.py:421
  63.7 7.7 %collective-permute-start.19 = (f32[24,2,4,128]{3,2,1,0:T(4,128)S(1)}, f32[24,2,4,128]{3,2,1,0:T(4,128)S(1)}, u32[]{:S(2)}, u32[]{:S(2)}) collective-permute-start(f32[24,2,4,128]{3,2,1,0:T(4,128)S(1)} %get-tuple-element.157), channel_id=1, source_target_pairs={{0,15},{1,2},{2,1},{3,4},{4,3},{5,6},{6,5},{7,8},{8,7},{9,10},{10,... | collective-permute-start | bytes 294920 | tf_op jit(solution)/shard_map/ppermute | solution.py:421
  71.6 6.7 %collective-permute-start.20 = (f32[4,2,24,128]{3,2,1,0:T(8,128)S(1)}, f32[4,2,24,128]{3,2,1,0:T(8,128)S(1)}, u32[]{:S(2)}, u32[]{:S(2)}) collective-permute-start(f32[4,2,24,128]{3,2,1,0:T(8,128)S(1)} %get-tuple-element.165), channel_id=1, source_target_pairs={{0,16},{16,0},{32,48},{48,32},{64,80},{80,64},{96,112},{112,96},{1... | collective-permute-start | bytes 294920 | tf_op jit(solution)/shard_map/ppermute | solution.py:421
  71.8 7.6 %collective-permute-start.21 = (f32[4,2,24,128]{3,2,1,0:T(8,128)S(1)}, f32[4,2,24,128]{3,2,1,0:T(8,128)S(1)}, u32[]{:S(2)}, u32[]{:S(2)}) collective-permute-start(f32[4,2,24,128]{3,2,1,0:T(8,128)S(1)} %get-tuple-element.166), channel_id=1, source_target_pairs={{0,112},{16,32},{32,16},{48,64},{64,48},{80,96},{96,80},{112,0},{1... | collective-permute-start | bytes 294920 | tf_op jit(solution)/shard_map/ppermute | solution.py:421
  73.1 6.3 %collective-permute-start.22 = (f32[24,2,4,128]{3,2,1,0:T(4,128)S(1)}, f32[24,2,4,128]{3,2,1,0:T(4,128)S(1)}, u32[]{:S(2)}, u32[]{:S(2)}) collective-permute-start(f32[24,2,4,128]{3,2,1,0:T(4,128)S(1)} %get-tuple-element.167), channel_id=1, source_target_pairs={{0,1},{1,0},{2,3},{3,2},{4,5},{5,4},{6,7},{7,6},{8,9},{9,8},{10,11... | collective-permute-start | bytes 294920 | tf_op jit(solution)/shard_map/ppermute | solution.py:421
  73.1 7.7 %collective-permute-start.23 = (f32[24,2,4,128]{3,2,1,0:T(4,128)S(1)}, f32[24,2,4,128]{3,2,1,0:T(4,128)S(1)}, u32[]{:S(2)}, u32[]{:S(2)}) collective-permute-start(f32[24,2,4,128]{3,2,1,0:T(4,128)S(1)} %get-tuple-element.168), channel_id=1, source_target_pairs={{0,15},{1,2},{2,1},{3,4},{4,3},{5,6},{6,5},{7,8},{8,7},{9,10},{10,... | collective-permute-start | bytes 294920 | tf_op jit(solution)/shard_map/ppermute | solution.py:421
  81.1 8.3 %collective-permute-start.24 = (f32[4,2,24,128]{3,2,1,0:T(8,128)S(1)}, f32[4,2,24,128]{3,2,1,0:T(8,128)S(1)}, u32[]{:S(2)}, u32[]{:S(2)}) collective-permute-start(f32[4,2,24,128]{3,2,1,0:T(8,128)S(1)} %get-tuple-element.176), channel_id=1, source_target_pairs={{0,16},{16,0},{32,48},{48,32},{64,80},{80,64},{96,112},{112,96},{1... | collective-permute-start | bytes 294920 | tf_op jit(solution)/shard_map/ppermute | solution.py:421
  81.8 7.6 %collective-permute-start.25 = (f32[4,2,24,128]{3,2,1,0:T(8,128)S(1)}, f32[4,2,24,128]{3,2,1,0:T(8,128)S(1)}, u32[]{:S(2)}, u32[]{:S(2)}) collective-permute-start(f32[4,2,24,128]{3,2,1,0:T(8,128)S(1)} %get-tuple-element.177), channel_id=1, source_target_pairs={{0,112},{16,32},{32,16},{48,64},{64,48},{80,96},{96,80},{112,0},{1... | collective-permute-start | bytes 294920 | tf_op jit(solution)/shard_map/ppermute | solution.py:421
  84.2 5.2 %collective-permute-start.26 = (f32[24,2,4,128]{3,2,1,0:T(4,128)S(1)}, f32[24,2,4,128]{3,2,1,0:T(4,128)S(1)}, u32[]{:S(2)}, u32[]{:S(2)}) collective-permute-start(f32[24,2,4,128]{3,2,1,0:T(4,128)S(1)} %get-tuple-element.178), channel_id=1, source_target_pairs={{0,1},{1,0},{2,3},{3,2},{4,5},{5,4},{6,7},{7,6},{8,9},{9,8},{10,11... | collective-permute-start | bytes 294920 | tf_op jit(solution)/shard_map/ppermute | solution.py:421
  84.2 7.7 %collective-permute-start.27 = (f32[24,2,4,128]{3,2,1,0:T(4,128)S(1)}, f32[24,2,4,128]{3,2,1,0:T(4,128)S(1)}, u32[]{:S(2)}, u32[]{:S(2)}) collective-permute-start(f32[24,2,4,128]{3,2,1,0:T(4,128)S(1)} %get-tuple-element.179), channel_id=1, source_target_pairs={{0,15},{1,2},{2,1},{3,4},{4,3},{5,6},{6,5},{7,8},{8,7},{9,10},{10,... | collective-permute-start | bytes 294920 | tf_op jit(solution)/shard_map/ppermute | solution.py:421
  92.2 7.7 %collective-permute-start.28 = (f32[4,2,24,128]{3,2,1,0:T(8,128)S(1)}, f32[4,2,24,128]{3,2,1,0:T(8,128)S(1)}, u32[]{:S(2)}, u32[]{:S(2)}) collective-permute-start(f32[4,2,24,128]{3,2,1,0:T(8,128)S(1)} %get-tuple-element.187), channel_id=1, source_target_pairs={{0,16},{16,0},{32,48},{48,32},{64,80},{80,64},{96,112},{112,96},{1... | collective-permute-start | bytes 294920 | tf_op jit(solution)/shard_map/ppermute | solution.py:421
  92.9 7.6 %collective-permute-start.29 = (f32[4,2,24,128]{3,2,1,0:T(8,128)S(1)}, f32[4,2,24,128]{3,2,1,0:T(8,128)S(1)}, u32[]{:S(2)}, u32[]{:S(2)}) collective-permute-start(f32[4,2,24,128]{3,2,1,0:T(8,128)S(1)} %get-tuple-element.188), channel_id=1, source_target_pairs={{0,112},{16,32},{32,16},{48,64},{64,48},{80,96},{96,80},{112,0},{1... | collective-permute-start | bytes 294920 | tf_op jit(solution)/shard_map/ppermute | solution.py:421
  94.5 5.9 %collective-permute-start.30 = (f32[24,2,4,128]{3,2,1,0:T(4,128)S(1)}, f32[24,2,4,128]{3,2,1,0:T(4,128)S(1)}, u32[]{:S(2)}, u32[]{:S(2)}) collective-permute-start(f32[24,2,4,128]{3,2,1,0:T(4,128)S(1)} %get-tuple-element.189), channel_id=1, source_target_pairs={{0,1},{1,0},{2,3},{3,2},{4,5},{5,4},{6,7},{7,6},{8,9},{9,8},{10,11... | collective-permute-start | bytes 294920 | tf_op jit(solution)/shard_map/ppermute | solution.py:421
  94.5 7.7 %collective-permute-start.31 = (f32[24,2,4,128]{3,2,1,0:T(4,128)S(1)}, f32[24,2,4,128]{3,2,1,0:T(4,128)S(1)}, u32[]{:S(2)}, u32[]{:S(2)}) collective-permute-start(f32[24,2,4,128]{3,2,1,0:T(4,128)S(1)} %get-tuple-element.190), channel_id=1, source_target_pairs={{0,15},{1,2},{2,1},{3,4},{4,3},{5,6},{6,5},{7,8},{8,7},{9,10},{10,... | collective-permute-start | bytes 294920 | tf_op jit(solution)/shard_map/ppermute | solution.py:421
  103.2 1.2 collective-permute-start.32
  104.4 4.9 %collective-permute-start.35 = (f32[16,128]{1,0:T(8,128)S(1)}, f32[16,128]{1,0:T(8,128)S(1)}, u32[]{:S(2)}, u32[]{:S(2)}) collective-permute-start(f32[16,128]{1,0:T(8,128)S(1)} %add.21), channel_id=1, source_target_pairs={{0,18},{1,19},{2,16},{3,17},{4,22},{5,23},{6,20},{7,21},{8,26},{9,... | collective-permute-start | bytes 24584 | tf_op jit(solution)/shard_map/ppermute | solution.py:435
  104.4 5.2 %collective-permute-start.34 = (f32[16,128]{1,0:T(8,128)S(1)}, f32[16,128]{1,0:T(8,128)S(1)}, u32[]{:S(2)}, u32[]{:S(2)}) collective-permute-start(f32[16,128]{1,0:T(8,128)S(1)} %add.21), channel_id=1, source_target_pairs={{0,2},{1,3},{2,0},{3,1},{4,6},{5,7},{6,4},{7,5},{8,10},{9,11},{10,... | collective-permute-start | bytes 24584 | tf_op jit(solution)/shard_map/ppermute | solution.py:435
  106.7 3.7 %collective-permute-start.33 = (f32[16,128]{1,0:T(8,128)S(1)}, f32[16,128]{1,0:T(8,128)S(1)}, u32[]{:S(2)}, u32[]{:S(2)}) collective-permute-start(f32[16,128]{1,0:T(8,128)S(1)} %add.21), channel_id=1, source_target_pairs={{0,16},{1,17},{2,18},{3,19},{4,20},{5,21},{6,22},{7,23},{8,24},{9,... | collective-permute-start | bytes 24584 | tf_op jit(solution)/shard_map/ppermute | solution.py:435
  110.4 4.9 %collective-permute-start.38 = (f32[16,128]{1,0:T(8,128)S(1)}, f32[16,128]{1,0:T(8,128)S(1)}, u32[]{:S(2)}, u32[]{:S(2)}) collective-permute-start(f32[16,128]{1,0:T(8,128)S(1)} %add_add_fusion.1), channel_id=1, source_target_pairs={{0,12},{1,13},{2,14},{3,15},{4,8},{5,9},{6,10},{7,11},{8,4},{9,5},... | collective-permute-start | bytes 24584 | tf_op jit(solution)/shard_map/ppermute | solution.py:435
  112.3 5.2 %collective-permute-start.37 = (f32[16,128]{1,0:T(8,128)S(1)}, f32[16,128]{1,0:T(8,128)S(1)}, u32[]{:S(2)}, u32[]{:S(2)}) collective-permute-start(f32[16,128]{1,0:T(8,128)S(1)} %add_add_fusion.1), channel_id=1, source_target_pairs={{0,8},{1,9},{2,10},{3,11},{4,12},{5,13},{6,14},{7,15},{8,0},{9,1},... | collective-permute-start | bytes 24584 | tf_op jit(solution)/shard_map/ppermute | solution.py:435
  112.3 5.2 %collective-permute-start.36 = (f32[16,128]{1,0:T(8,128)S(1)}, f32[16,128]{1,0:T(8,128)S(1)}, u32[]{:S(2)}, u32[]{:S(2)}) collective-permute-start(f32[16,128]{1,0:T(8,128)S(1)} %add_add_fusion.1), channel_id=1, source_target_pairs={{0,4},{1,5},{2,6},{3,7},{4,0},{5,1},{6,2},{7,3},{8,12},{9,13},{10,... | collective-permute-start | bytes 24584 | tf_op jit(solution)/shard_map/ppermute | solution.py:435
  117.4 5.6 %collective-permute-start.39 = (f32[16,128]{1,0:T(8,128)S(1)}, f32[16,128]{1,0:T(8,128)S(1)}, u32[]{:S(2)}, u32[]{:S(2)}) collective-permute-start(f32[16,128]{1,0:T(8,128)S(1)} %add_add_fusion.refs_0_), channel_id=1, source_target_pairs={{0,32},{1,33},{2,34},{3,35},{4,36},{5,37},{6,38},{7,39},{8,40},{9,... | collective-permute-start | bytes 24584 | tf_op jit(solution)/shard_map/ppermute | solution.py:435
  119.0 5.2 %collective-permute-start.40 = (f32[16,128]{1,0:T(8,128)S(1)}, f32[16,128]{1,0:T(8,128)S(1)}, u32[]{:S(2)}, u32[]{:S(2)}) collective-permute-start(f32[16,128]{1,0:T(8,128)S(1)} %add_add_fusion.refs_0_), channel_id=1, source_target_pairs={{0,64},{1,65},{2,66},{3,67},{4,68},{5,69},{6,70},{7,71},{8,72},{9,... | collective-permute-start | bytes 24584 | tf_op jit(solution)/shard_map/ppermute | solution.py:435
  121.0 4.9 %collective-permute-start.41 = (f32[16,128]{1,0:T(8,128)S(1)}, f32[16,128]{1,0:T(8,128)S(1)}, u32[]{:S(2)}, u32[]{:S(2)}) collective-permute-start(f32[16,128]{1,0:T(8,128)S(1)} %add_add_fusion.refs_0_), channel_id=1, source_target_pairs={{0,96},{1,97},{2,98},{3,99},{4,100},{5,101},{6,102},{7,103},{8,104... | collective-permute-start | bytes 24584 | tf_op jit(solution)/shard_map/ppermute | solution.py:435
  (5 other events, 3.3 us)

commit v4 on v3

--- a/solution.py
+++ b/solution.py
@@ -207,7 +207,7 @@
     table[1] = note(4, NSRC, sx, sy, sz)
     for t in range(STEPS):
         for n in range(NSRC):
-            amps[t * NSRC + n] = amp[t, n]
+            amps[t * NSRC + n] = amp[n, t]
     for copy in copies:
         copy.wait()
     for half in range(2):
@@ -391,9 +391,8 @@
     seen = parts[0][...]
     for part in parts[1:]:
         seen = seen + part[...]
-    turned = seen.T
-    traces[...] = turned[:NREC, :STEPS]
-    energy[...] = jnp.sum(turned[:, STEPS:], axis=0)
+    traces[...] = seen[:STEPS, :NREC]
+    energy[...] = jnp.sum(seen[STEPS:].T, axis=0)
 
 
 def vmem(count):
@@ -423,7 +422,9 @@
 
 def exchange(strips):
     near_x, far_x, near_y, far_y = strips
-    return (swap(near_x, GX, 0), swap(far_x, GX, 1), swap(near_y, GY, 0), swap(far_y, GY, 1))
+    far_y = swap(far_y, GY, 1)
+    far_x = swap(far_x, GX, 1)
+    return (swap(near_x, GX, 0), far_x, swap(near_y, GY, 0), far_y)
 
 
 def spread(value, by):
@@ -458,6 +459,10 @@
     receiver_y,
     receiver_z,
 ):
+    stay = lambda value: pltpu.with_memory_space_constraint(value, pltpu.HBM)
+    pressure, pressure_old, speed_term = [stay(v) for v in (pressure, pressure_old, speed_term)]
+    small = [layer_width, source_x, source_y, source_z, receiver_x, receiver_y, receiver_z, source_amp.T]
+    small = [stay(v) for v in small]
     staged = pltpu.VMEM(pressure.shape, jnp.float32)
     strips_out = shape(STRIP_X, STRIP_X, STRIP_Y, STRIP_Y)
     current, *strips = pl.pallas_call(
@@ -479,20 +484,9 @@
         out_specs=vmem(10) + smem(2),
         scratch_shapes=[staged, staged, pltpu.SemaphoreType.DMA((2, CHUNKS))]
         + [pltpu.SMEM((n,), jnp.int32) for n in (4, NSRC, NSRC, NSRC, NREC, NREC, NREC)]
-        + [pltpu.SMEM((STEPS, NSRC), jnp.float32), pltpu.SemaphoreType.DMA((8,))],
+        + [pltpu.SMEM((NSRC, STEPS), jnp.float32), pltpu.SemaphoreType.DMA((8,))],
         compiler_params=limit(8),
-    )(
-        layer_width,
-        source_x,
-        source_y,
-        source_z,
-        receiver_x,
-        receiver_y,
-        receiver_z,
-        source_amp,
-        pressure_old,
-        speed_term,
-    )
+    )(*small, pressure_old, speed_term)
     state, keeps, table, amps = (rest[:5], rest[5:8], rest[8], rest[9])
     band = jnp.asarray(band_matrix())
     beside = pltpu.VMEM((CX, 2, 24, LANES), jnp.float32)
@@ -538,12 +532,12 @@
     parts = gather_sums(seen)
     traces, energy = pl.pallas_call(
         report_kernel,
-        out_shape=shape((NREC, STEPS), (STEPS,)),
+        out_shape=shape((STEPS, NREC), (STEPS,)),
         in_specs=vmem(len(parts)),
         out_specs=vmem(2),
         compiler_params=limit(2),
     )(*parts)
-    return final, traces, energy
+    return final, traces.T, energy
 
 
 def solution(mesh):

time: 128 us -> 118 us (0.922)
  local copies, waits for them, and re-layouts: 9.23 us -> 0.01 us
  Pallas kernels: 34.1 us -> 32.6 us
    unnamed x24 -> x2, local copies, waits for them, and re-layouts: 9.23 us -> 0.01 us
  transfers between devices with their start and end apart: 42 -> 42, of which waited for: 21 -> 22; matrix products, arithmetic and copies ran while one was open for 1% -> 0% of each run, Pallas kernels for 23% -> 24%
where the time goes in v4:
time: 118 us; the launch traced here: 117 us
  starting transfers between devices  55.8 us (47%)
  Pallas kernels  32.6 us (28%)
  waiting for transfers between devices  28.1 us (24%)
    ppermute x32, starting transfers between devices, swap(): lax.ppermute(strip, axis, [(i, ((i + far ^ 1) - far) % size) for i in ran...  42.7 us
    pallas_call x8, Pallas kernels, per_device(): pl.pallas_call(functools.partial(inner_kernel, step), out_shape=shape(FIE...  23.7 us
    ppermute x32, waiting for transfers between devices, swap(): lax.ppermute(strip, axis, [(i, ((i + far ^ 1) - far) % size) for i in ran...  19.5 us
    ppermute x10, starting transfers between devices, spread(): return lax.ppermute(value, BOTH, pairs)  13.1 us
    ppermute x10, waiting for transfers between devices, spread(): return lax.ppermute(value, BOTH, pairs)  8.56 us
    pallas_call x1, Pallas kernels, per_device(): pl.pallas_call(begin_kernel, out_shape=shape(FIELD, BLOCK, MEM_X, MEM_Y,...  3.2 us
  transfers between devices with their start and end apart: 42, of which 22 were waited for; matrix products, arithmetic and copies ran while one was open for 0% of the time, Pallas kernels for 24%

profile of v4, /device:TPU:0, one launch (start us, length us, event | category | flops | bytes accessed | tf_op | source)
XLA Modules:
  0.0 117.4 jit_solution(16264741058455941812)
XLA Ops:
  0.6 1.3 %shard_map.140 = (f32[32,2,40,128]{3,2,1,0:T(8,128)S(1)}, f32[4,2,24,128]{3,2,1,0:T(8,128)S(1)}, f32[4,2,24,128]{3,2,1,0:T(8,128)S(1)}, f32[24,2,4,128]{3,2,1,0:T(4,128)S(1)}, f32[24,2,4,128]{3,2,1,0:T(4,128)S(1)}) custom-call(f32[24,24,256]{2,1,0:T(8,128)} %pressure.1), custom_call_target="tpu_custom_call" | custom-call | tf_op jit(solution)/shard_map/pallas_call | solution.py:468
  1.9 1.7 %collective-permute-start = (f32[4,2,24,128]{3,2,1,0:T(8,128)S(1)}, f32[4,2,24,128]{3,2,1,0:T(8,128)S(1)}, u32[]{:S(2)}, u32[]{:S(2)}) collective-permute-start(f32[4,2,24,128]{3,2,1,0:T(8,128)S(1)} %get-tuple-element.108), channel_id=1, source_target_pairs={{0,16},{16,0},{32,48},{48,32},{64,80},{80,64},{96,112},{112,96},{1... | collective-permute-start | bytes 294920 | tf_op jit(solution)/shard_map/ppermute | solution.py:420
  3.6 3.0 %collective-permute-start.1 = (f32[4,2,24,128]{3,2,1,0:T(8,128)S(1)}, f32[4,2,24,128]{3,2,1,0:T(8,128)S(1)}, u32[]{:S(2)}, u32[]{:S(2)}) collective-permute-start(f32[4,2,24,128]{3,2,1,0:T(8,128)S(1)} %get-tuple-element.109), channel_id=1, source_target_pairs={{0,112},{16,32},{32,16},{48,64},{64,48},{80,96},{96,80},{112,0},{1... | collective-permute-start | bytes 294920 | tf_op jit(solution)/shard_map/ppermute | solution.py:420
  6.6 6.6 %collective-permute-start.3 = (f32[24,2,4,128]{3,2,1,0:T(4,128)S(1)}, f32[24,2,4,128]{3,2,1,0:T(4,128)S(1)}, u32[]{:S(2)}, u32[]{:S(2)}) collective-permute-start(f32[24,2,4,128]{3,2,1,0:T(4,128)S(1)} %get-tuple-element.111), channel_id=1, source_target_pairs={{0,15},{1,2},{2,1},{3,4},{4,3},{5,6},{6,5},{7,8},{8,7},{9,10},{10,... | collective-permute-start | bytes 294920 | tf_op jit(solution)/shard_map/ppermute | solution.py:420
  13.2 3.2 %shard_map.139 = (f32[32,2,40,128]{3,2,1,0:T(8,128)S(1)}, f32[24,2,24,128]{3,2,1,0:T(8,128)S(1)}, f32[2,32,2,24,128]{4,3,2,1,0:T(8,128)S(1)}, f32[24,2,40,128]{3...) custom-call(s32[4]{0:T(128)} %widths_far.1, ...), custom_call_target="tpu_custom_call" | custom-call | tf_op jit(solution)/shard_map/pallas_call | solution.py:476
  16.4 2.9 %shard_map.141 = (f32[32,2,40,128]{3,2,1,0:T(8,128)S(1)}, f32[2,32,2,24,128]{4,3,2,1,0:T(8,128)S(1)}, f32[24,2,40,128]{3,2,1,0:T(8,128)S(1)}, f32[24,2,24,128]{3...) custom-call(s32[72]{0:T(128)S(1)} %get-tuple-element.103.table.refs_, ...), custom_call_target="tpu_custom_call", output_to_operand_aliasing={{0}: (8, {}), {1}: (9, {}), {2}: (10, {}), {3}: (11, {}), {... | custom-call | tf_op jit(solution)/shard_map/pallas_call | solution.py:495
  19.8 1.5 %collective-permute-start.5 = (f32[4,2,24,128]{3,2,1,0:T(8,128)S(1)}, f32[4,2,24,128]{3,2,1,0:T(8,128)S(1)}, u32[]{:S(2)}, u32[]{:S(2)}) collective-permute-start(f32[4,2,24,128]{3,2,1,0:T(8,128)S(1)} %get-tuple-element.122), channel_id=1, source_target_pairs={{0,112},{16,32},{32,16},{48,64},{64,48},{80,96},{96,80},{112,0},{1... | collective-permute-start | bytes 294920 | tf_op jit(solution)/shard_map/ppermute | solution.py:420
  21.3 1.6 %collective-permute-start.7 = (f32[24,2,4,128]{3,2,1,0:T(4,128)S(1)}, f32[24,2,4,128]{3,2,1,0:T(4,128)S(1)}, u32[]{:S(2)}, u32[]{:S(2)}) collective-permute-start(f32[24,2,4,128]{3,2,1,0:T(4,128)S(1)} %get-tuple-element.124), channel_id=1, source_target_pairs={{0,15},{1,2},{2,1},{3,4},{4,3},{5,6},{6,5},{7,8},{8,7},{9,10},{10,... | collective-permute-start | bytes 294920 | tf_op jit(solution)/shard_map/ppermute | solution.py:420
  22.9 3.0 %shard_map.143 = (f32[32,2,40,128]{3,2,1,0:T(8,128)S(1)}, f32[2,32,2,24,128]{4,3,2,1,0:T(8,128)S(1)}, f32[24,2,40,128]{3,2,1,0:T(8,128)S(1)}, f32[24,2,24,128]{3...) custom-call(s32[72]{0:T(128)S(1)} %get-tuple-element.103.table.refs_, ...), custom_call_target="tpu_custom_call", output_to_operand_aliasing={{0}: (8, {}), {1}: (9, {}), {2}: (10, {}), {3}: (11, {}), {... | custom-call | tf_op jit(solution)/shard_map/pallas_call | solution.py:495
  25.9 1.6 %collective-permute-done.5.refs_2_ = f32[4,2,24,128]{3,2,1,0:T(8,128)S(1)} collective-permute-done((f32[4,2,24,128]{3,2,1,0:T(8,128)S(1)}, f32[4,2,24,128]{3,2,1,0:T(8,128)S(1)}, u32[]{:S(2)}, u32[]{:S(2)}) %collective-permute-start.5) | collective-permute-done | bytes 98336 | tf_op jit(solution)/shard_map/ppermute | solution.py:420
  27.4 1.5 %collective-permute-done.7.refs_4_ = f32[24,2,4,128]{3,2,1,0:T(4,128)S(1)} collective-permute-done((f32[24,2,4,128]{3,2,1,0:T(4,128)S(1)}, f32[24,2,4,128]{3,2,1,0:T(4,128)S(1)}, u32[]{:S(2)}, u32[]{:S(2)}) %collective-permute-start.7) | collective-permute-done | bytes 98336 | tf_op jit(solution)/shard_map/ppermute | solution.py:420
  29.8 2.3 %collective-permute-start.9 = (f32[4,2,24,128]{3,2,1,0:T(8,128)S(1)}, f32[4,2,24,128]{3,2,1,0:T(8,128)S(1)}, u32[]{:S(2)}, u32[]{:S(2)}) collective-permute-start(f32[4,2,24,128]{3,2,1,0:T(8,128)S(1)} %get-tuple-element.133), channel_id=1, source_target_pairs={{0,112},{16,32},{32,16},{48,64},{64,48},{80,96},{96,80},{112,0},{1... | collective-permute-start | bytes 294920 | tf_op jit(solution)/shard_map/ppermute | solution.py:420
  32.1 2.3 %collective-permute-start.11 = (f32[24,2,4,128]{3,2,1,0:T(4,128)S(1)}, f32[24,2,4,128]{3,2,1,0:T(4,128)S(1)}, u32[]{:S(2)}, u32[]{:S(2)}) collective-permute-start(f32[24,2,4,128]{3,2,1,0:T(4,128)S(1)} %get-tuple-element.135), channel_id=1, source_target_pairs={{0,15},{1,2},{2,1},{3,4},{4,3},{5,6},{6,5},{7,8},{8,7},{9,10},{10,... | collective-permute-start | bytes 294920 | tf_op jit(solution)/shard_map/ppermute | solution.py:420
  34.4 3.0 %shard_map.145 = (f32[32,2,40,128]{3,2,1,0:T(8,128)S(1)}, f32[2,32,2,24,128]{4,3,2,1,0:T(8,128)S(1)}, f32[24,2,40,128]{3,2,1,0:T(8,128)S(1)}, f32[24,2,24,128]{3...) custom-call(s32[72]{0:T(128)S(1)} %get-tuple-element.103.table.refs_, ...), custom_call_target="tpu_custom_call", output_to_operand_aliasing={{0}: (8, {}), {1}: (9, {}), {2}: (10, {}), {3}: (11, {}), {... | custom-call | tf_op jit(solution)/shard_map/pallas_call | solution.py:495
  37.4 2.3 %collective-permute-done.11.refs_4_ = f32[24,2,4,128]{3,2,1,0:T(4,128)S(1)} collective-permute-done((f32[24,2,4,128]{3,2,1,0:T(4,128)S(1)}, f32[24,2,4,128]{3,2,1,0:T(4,128)S(1)}, u32[]{:S(2)}, u32[]{:S(2)}) %collective-permute-start.11) | collective-permute-done | bytes 98336 | tf_op jit(solution)/shard_map/ppermute | solution.py:420
  40.9 2.0 %collective-permute-start.13 = (f32[4,2,24,128]{3,2,1,0:T(8,128)S(1)}, f32[4,2,24,128]{3,2,1,0:T(8,128)S(1)}, u32[]{:S(2)}, u32[]{:S(2)}) collective-permute-start(f32[4,2,24,128]{3,2,1,0:T(8,128)S(1)} %get-tuple-element.144), channel_id=1, source_target_pairs={{0,112},{16,32},{32,16},{48,64},{64,48},{80,96},{96,80},{112,0},{1... | collective-permute-start | bytes 294920 | tf_op jit(solution)/shard_map/ppermute | solution.py:420
  42.9 2.0 %collective-permute-start.15 = (f32[24,2,4,128]{3,2,1,0:T(4,128)S(1)}, f32[24,2,4,128]{3,2,1,0:T(4,128)S(1)}, u32[]{:S(2)}, u32[]{:S(2)}) collective-permute-start(f32[24,2,4,128]{3,2,1,0:T(4,128)S(1)} %get-tuple-element.146), channel_id=1, source_target_pairs={{0,15},{1,2},{2,1},{3,4},{4,3},{5,6},{6,5},{7,8},{8,7},{9,10},{10,... | collective-permute-start | bytes 294920 | tf_op jit(solution)/shard_map/ppermute | solution.py:420
  44.9 3.0 %shard_map.147 = (f32[32,2,40,128]{3,2,1,0:T(8,128)S(1)}, f32[2,32,2,24,128]{4,3,2,1,0:T(8,128)S(1)}, f32[24,2,40,128]{3,2,1,0:T(8,128)S(1)}, f32[24,2,24,128]{3...) custom-call(s32[72]{0:T(128)S(1)} %get-tuple-element.103.table.refs_, ...), custom_call_target="tpu_custom_call", output_to_operand_aliasing={{0}: (8, {}), {1}: (9, {}), {2}: (10, {}), {3}: (11, {}), {... | custom-call | tf_op jit(solution)/shard_map/pallas_call | solution.py:495
  48.5 2.0 %collective-permute-done.15.refs_4_ = f32[24,2,4,128]{3,2,1,0:T(4,128)S(1)} collective-permute-done((f32[24,2,4,128]{3,2,1,0:T(4,128)S(1)}, f32[24,2,4,128]{3,2,1,0:T(4,128)S(1)}, u32[]{:S(2)}, u32[]{:S(2)}) %collective-permute-start.15) | collective-permute-done | bytes 98336 | tf_op jit(solution)/shard_map/ppermute | solution.py:420
  50.9 3.5 %collective-permute-start.17 = (f32[4,2,24,128]{3,2,1,0:T(8,128)S(1)}, f32[4,2,24,128]{3,2,1,0:T(8,128)S(1)}, u32[]{:S(2)}, u32[]{:S(2)}) collective-permute-start(f32[4,2,24,128]{3,2,1,0:T(8,128)S(1)} %get-tuple-element.155), channel_id=1, source_target_pairs={{0,112},{16,32},{32,16},{48,64},{64,48},{80,96},{96,80},{112,0},{1... | collective-permute-start | bytes 294920 | tf_op jit(solution)/shard_map/ppermute | solution.py:420
  54.4 1.4 %collective-permute-start.19 = (f32[24,2,4,128]{3,2,1,0:T(4,128)S(1)}, f32[24,2,4,128]{3,2,1,0:T(4,128)S(1)}, u32[]{:S(2)}, u32[]{:S(2)}) collective-permute-start(f32[24,2,4,128]{3,2,1,0:T(4,128)S(1)} %get-tuple-element.157), channel_id=1, source_target_pairs={{0,15},{1,2},{2,1},{3,4},{4,3},{5,6},{6,5},{7,8},{8,7},{9,10},{10,... | collective-permute-start | bytes 294920 | tf_op jit(solution)/shard_map/ppermute | solution.py:420
  55.8 3.0 %shard_map.149 = (f32[32,2,40,128]{3,2,1,0:T(8,128)S(1)}, f32[2,32,2,24,128]{4,3,2,1,0:T(8,128)S(1)}, f32[24,2,40,128]{3,2,1,0:T(8,128)S(1)}, f32[24,2,24,128]{3...) custom-call(s32[72]{0:T(128)S(1)} %get-tuple-element.103.table.refs_, ...), custom_call_target="tpu_custom_call", output_to_operand_aliasing={{0}: (8, {}), {1}: (9, {}), {2}: (10, {}), {3}: (11, {}), {... | custom-call | tf_op jit(solution)/shard_map/pallas_call | solution.py:495
  59.1 3.0 %collective-permute-done.19.refs_4_ = f32[24,2,4,128]{3,2,1,0:T(4,128)S(1)} collective-permute-done((f32[24,2,4,128]{3,2,1,0:T(4,128)S(1)}, f32[24,2,4,128]{3,2,1,0:T(4,128)S(1)}, u32[]{:S(2)}, u32[]{:S(2)}) %collective-permute-start.19) | collective-permute-done | bytes 98336 | tf_op jit(solution)/shard_map/ppermute | solution.py:420
  62.7 1.5 %collective-permute-start.21 = (f32[4,2,24,128]{3,2,1,0:T(8,128)S(1)}, f32[4,2,24,128]{3,2,1,0:T(8,128)S(1)}, u32[]{:S(2)}, u32[]{:S(2)}) collective-permute-start(f32[4,2,24,128]{3,2,1,0:T(8,128)S(1)} %get-tuple-element.166), channel_id=1, source_target_pairs={{0,112},{16,32},{32,16},{48,64},{64,48},{80,96},{96,80},{112,0},{1... | collective-permute-start | bytes 294920 | tf_op jit(solution)/shard_map/ppermute | solution.py:420
  64.2 2.0 %collective-permute-start.23 = (f32[24,2,4,128]{3,2,1,0:T(4,128)S(1)}, f32[24,2,4,128]{3,2,1,0:T(4,128)S(1)}, u32[]{:S(2)}, u32[]{:S(2)}) collective-permute-start(f32[24,2,4,128]{3,2,1,0:T(4,128)S(1)} %get-tuple-element.168), channel_id=1, source_target_pairs={{0,15},{1,2},{2,1},{3,4},{4,3},{5,6},{6,5},{7,8},{8,7},{9,10},{10,... | collective-permute-start | bytes 294920 | tf_op jit(solution)/shard_map/ppermute | solution.py:420
  66.2 3.0 %shard_map.151 = (f32[32,2,40,128]{3,2,1,0:T(8,128)S(1)}, f32[2,32,2,24,128]{4,3,2,1,0:T(8,128)S(1)}, f32[24,2,40,128]{3,2,1,0:T(8,128)S(1)}, f32[24,2,24,128]{3...) custom-call(s32[72]{0:T(128)S(1)} %get-tuple-element.103.table.refs_, ...), custom_call_target="tpu_custom_call", output_to_operand_aliasing={{0}: (8, {}), {1}: (9, {}), {2}: (10, {}), {3}: (11, {}), {... | custom-call | tf_op jit(solution)/shard_map/pallas_call | solution.py:495
  69.2 1.1 collective-permute-done.21.refs_2_
  70.3 1.5 %collective-permute-done.23.refs_4_ = f32[24,2,4,128]{3,2,1,0:T(4,128)S(1)} collective-permute-done((f32[24,2,4,128]{3,2,1,0:T(4,128)S(1)}, f32[24,2,4,128]{3,2,1,0:T(4,128)S(1)}, u32[]{:S(2)}, u32[]{:S(2)}) %collective-permute-start.23) | collective-permute-done | bytes 98336 | tf_op jit(solution)/shard_map/ppermute | solution.py:420
  72.7 2.5 %collective-permute-start.25 = (f32[4,2,24,128]{3,2,1,0:T(8,128)S(1)}, f32[4,2,24,128]{3,2,1,0:T(8,128)S(1)}, u32[]{:S(2)}, u32[]{:S(2)}) collective-permute-start(f32[4,2,24,128]{3,2,1,0:T(8,128)S(1)} %get-tuple-element.177), channel_id=1, source_target_pairs={{0,112},{16,32},{32,16},{48,64},{64,48},{80,96},{96,80},{112,0},{1... | collective-permute-start | bytes 294920 | tf_op jit(solution)/shard_map/ppermute | solution.py:420
  75.2 2.0 %collective-permute-start.27 = (f32[24,2,4,128]{3,2,1,0:T(4,128)S(1)}, f32[24,2,4,128]{3,2,1,0:T(4,128)S(1)}, u32[]{:S(2)}, u32[]{:S(2)}) collective-permute-start(f32[24,2,4,128]{3,2,1,0:T(4,128)S(1)} %get-tuple-element.179), channel_id=1, source_target_pairs={{0,15},{1,2},{2,1},{3,4},{4,3},{5,6},{6,5},{7,8},{8,7},{9,10},{10,... | collective-permute-start | bytes 294920 | tf_op jit(solution)/shard_map/ppermute | solution.py:420
  77.3 3.0 %shard_map.153 = (f32[32,2,40,128]{3,2,1,0:T(8,128)S(1)}, f32[2,32,2,24,128]{4,3,2,1,0:T(8,128)S(1)}, f32[24,2,40,128]{3,2,1,0:T(8,128)S(1)}, f32[24,2,24,128]{3...) custom-call(s32[72]{0:T(128)S(1)} %get-tuple-element.103.table.refs_, ...), custom_call_target="tpu_custom_call", output_to_operand_aliasing={{0}: (8, {}), {1}: (9, {}), {2}: (10, {}), {3}: (11, {}), {... | custom-call | tf_op jit(solution)/shard_map/pallas_call | solution.py:495
  80.3 2.6 %collective-permute-done.27.refs_4_ = f32[24,2,4,128]{3,2,1,0:T(4,128)S(1)} collective-permute-done((f32[24,2,4,128]{3,2,1,0:T(4,128)S(1)}, f32[24,2,4,128]{3,2,1,0:T(4,128)S(1)}, u32[]{:S(2)}, u32[]{:S(2)}) %collective-permute-start.27) | collective-permute-done | bytes 98336 | tf_op jit(solution)/shard_map/ppermute | solution.py:420
  83.8 2.0 %collective-permute-start.29 = (f32[4,2,24,128]{3,2,1,0:T(8,128)S(1)}, f32[4,2,24,128]{3,2,1,0:T(8,128)S(1)}, u32[]{:S(2)}, u32[]{:S(2)}) collective-permute-start(f32[4,2,24,128]{3,2,1,0:T(8,128)S(1)} %get-tuple-element.188), channel_id=1, source_target_pairs={{0,112},{16,32},{32,16},{48,64},{64,48},{80,96},{96,80},{112,0},{1... | collective-permute-start | bytes 294920 | tf_op jit(solution)/shard_map/ppermute | solution.py:420
  85.8 2.0 %collective-permute-start.31 = (f32[24,2,4,128]{3,2,1,0:T(4,128)S(1)}, f32[24,2,4,128]{3,2,1,0:T(4,128)S(1)}, u32[]{:S(2)}, u32[]{:S(2)}) collective-permute-start(f32[24,2,4,128]{3,2,1,0:T(4,128)S(1)} %get-tuple-element.190), channel_id=1, source_target_pairs={{0,15},{1,2},{2,1},{3,4},{4,3},{5,6},{6,5},{7,8},{8,7},{9,10},{10,... | collective-permute-start | bytes 294920 | tf_op jit(solution)/shard_map/ppermute | solution.py:420
  87.7 3.0 %shard_map.155 = (f32[32,2,40,128]{3,2,1,0:T(8,128)S(1)}, f32[2,32,2,24,128]{4,3,2,1,0:T(8,128)S(1)}, f32[24,2,40,128]{3,2,1,0:T(8,128)S(1)}, f32[24,2,24,128]{3...) custom-call(s32[72]{0:T(128)S(1)} %get-tuple-element.103.table.refs_, ...), custom_call_target="tpu_custom_call", output_to_operand_aliasing={{0}: (8, {}), {1}: (9, {}), {2}: (10, {}), {3}: (11, {}), {... | custom-call | tf_op jit(solution)/shard_map/pallas_call | solution.py:495
  91.4 2.0 %collective-permute-done.31.refs_8_ = f32[24,2,4,128]{3,2,1,0:T(4,128)S(1)} collective-permute-done((f32[24,2,4,128]{3,2,1,0:T(4,128)S(1)}, f32[24,2,4,128]{3,2,1,0:T(4,128)S(1)}, u32[]{:S(2)}, u32[]{:S(2)}) %collective-permute-start.31) | collective-permute-done | bytes 98336 | tf_op jit(solution)/shard_map/ppermute | solution.py:420
  93.4 0.9 shard_map.156
  94.4 1.2 collective-permute-done.32
  95.6 2.2 %collective-permute-start.34 = (f32[16,128]{1,0:T(8,128)S(1)}, f32[16,128]{1,0:T(8,128)S(1)}, u32[]{:S(2)}, u32[]{:S(2)}) collective-permute-start(f32[16,128]{1,0:T(8,128)S(1)} %add.21), channel_id=1, source_target_pairs={{0,2},{1,3},{2,0},{3,1},{4,6},{5,7},{6,4},{7,5},{8,10},{9,11},{10,... | collective-permute-start | bytes 24584 | tf_op jit(solution)/shard_map/ppermute | solution.py:436
  97.8 1.9 %collective-permute-start.33 = (f32[16,128]{1,0:T(8,128)S(1)}, f32[16,128]{1,0:T(8,128)S(1)}, u32[]{:S(2)}, u32[]{:S(2)}) collective-permute-start(f32[16,128]{1,0:T(8,128)S(1)} %add.21), channel_id=1, source_target_pairs={{0,16},{1,17},{2,18},{3,19},{4,20},{5,21},{6,22},{7,23},{8,24},{9,... | collective-permute-start | bytes 24584 | tf_op jit(solution)/shard_map/ppermute | solution.py:436
  101.4 1.9 %collective-permute-start.38 = (f32[16,128]{1,0:T(8,128)S(1)}, f32[16,128]{1,0:T(8,128)S(1)}, u32[]{:S(2)}, u32[]{:S(2)}) collective-permute-start(f32[16,128]{1,0:T(8,128)S(1)} %add_add_fusion.1), channel_id=1, source_target_pairs={{0,12},{1,13},{2,14},{3,15},{4,8},{5,9},{6,10},{7,11},{8,4},{9,5},... | collective-permute-start | bytes 24584 | tf_op jit(solution)/shard_map/ppermute | solution.py:436
  103.3 2.2 %collective-permute-start.36 = (f32[16,128]{1,0:T(8,128)S(1)}, f32[16,128]{1,0:T(8,128)S(1)}, u32[]{:S(2)}, u32[]{:S(2)}) collective-permute-start(f32[16,128]{1,0:T(8,128)S(1)} %add_add_fusion.1), channel_id=1, source_target_pairs={{0,4},{1,5},{2,6},{3,7},{4,0},{5,1},{6,2},{7,3},{8,12},{9,13},{10,... | collective-permute-start | bytes 24584 | tf_op jit(solution)/shard_map/ppermute | solution.py:436
  106.3 2.2 %collective-permute-done.37 = f32[16,128]{1,0:T(8,128)S(1)} collective-permute-done((f32[16,128]{1,0:T(8,128)S(1)}, f32[16,128]{1,0:T(8,128)S(1)}, u32[]{:S(2)}, u32[]{:S(2)}) %collective-permute-start.37) | collective-permute-done | bytes 8224 | tf_op jit(solution)/shard_map/ppermute | solution.py:436
  108.5 1.4 %collective-permute-start.39 = (f32[16,128]{1,0:T(8,128)S(1)}, f32[16,128]{1,0:T(8,128)S(1)}, u32[]{:S(2)}, u32[]{:S(2)}) collective-permute-start(f32[16,128]{1,0:T(8,128)S(1)} %add_add_fusion.refs_0_), channel_id=1, source_target_pairs={{0,32},{1,33},{2,34},{3,35},{4,36},{5,37},{6,38},{7,39},{8,40},{9,... | collective-permute-start | bytes 24584 | tf_op jit(solution)/shard_map/ppermute | solution.py:436
  109.9 2.1 %collective-permute-start.40 = (f32[16,128]{1,0:T(8,128)S(1)}, f32[16,128]{1,0:T(8,128)S(1)}, u32[]{:S(2)}, u32[]{:S(2)}) collective-permute-start(f32[16,128]{1,0:T(8,128)S(1)} %add_add_fusion.refs_0_), channel_id=1, source_target_pairs={{0,64},{1,65},{2,66},{3,67},{4,68},{5,69},{6,70},{7,71},{8,72},{9,... | collective-permute-start | bytes 24584 | tf_op jit(solution)/shard_map/ppermute | solution.py:436
  112.0 1.3 %collective-permute-start.41 = (f32[16,128]{1,0:T(8,128)S(1)}, f32[16,128]{1,0:T(8,128)S(1)}, u32[]{:S(2)}, u32[]{:S(2)}) collective-permute-start(f32[16,128]{1,0:T(8,128)S(1)} %add_add_fusion.refs_0_), channel_id=1, source_target_pairs={{0,96},{1,97},{2,98},{3,99},{4,100},{5,101},{6,102},{7,103},{8,104... | collective-permute-start | bytes 24584 | tf_op jit(solution)/shard_map/ppermute | solution.py:436
  114.1 0.9 collective-permute-done.40.refs_2_
  115.0 1.8 %collective-permute-done.41.refs_3_ = f32[16,128]{1,0:T(8,128)S(1)} collective-permute-done((f32[16,128]{1,0:T(8,128)S(1)}, f32[16,128]{1,0:T(8,128)S(1)}, u32[]{:S(2)}, u32[]{:S(2)}) %collective-permute-start.41) | collective-permute-done | bytes 8224 | tf_op jit(solution)/shard_map/ppermute | solution.py:436
  (61 shorter events, 11.1 us)
Async XLA Ops:
  0.6 15.8 %copy-start = (bf16[512,256]{1,0:T(8,128)(2,1)S(1)}, bf16[512,256]{1,0:T(8,128)(2,1)}, u32[]{:S(2)}) copy-start(bf16[512,256]{1,0:T(8,128)(2,1)} %constant.2.clone.band) | copy-start | bytes 786436
  1.9 17.4 %collective-permute-start = (f32[4,2,24,128]{3,2,1,0:T(8,128)S(1)}, f32[4,2,24,128]{3,2,1,0:T(8,128)S(1)}, u32[]{:S(2)}, u32[]{:S(2)}) collective-permute-start(f32[4,2,24,128]{3,2,1,0:T(8,128)S(1)} %get-tuple-element.108), channel_id=1, source_target_pairs={{0,16},{16,0},{32,48},{48,32},{64,80},{80,64},{96,112},{112,96},{1... | collective-permute-start | bytes 294920 | tf_op jit(solution)/shard_map/ppermute | solution.py:420
  3.6 15.7 %collective-permute-start.1 = (f32[4,2,24,128]{3,2,1,0:T(8,128)S(1)}, f32[4,2,24,128]{3,2,1,0:T(8,128)S(1)}, u32[]{:S(2)}, u32[]{:S(2)}) collective-permute-start(f32[4,2,24,128]{3,2,1,0:T(8,128)S(1)} %get-tuple-element.109), channel_id=1, source_target_pairs={{0,112},{16,32},{32,16},{48,64},{64,48},{80,96},{96,80},{112,0},{1... | collective-permute-start | bytes 294920 | tf_op jit(solution)/shard_map/ppermute | solution.py:420
  6.6 12.8 %collective-permute-start.2 = (f32[24,2,4,128]{3,2,1,0:T(4,128)S(1)}, f32[24,2,4,128]{3,2,1,0:T(4,128)S(1)}, u32[]{:S(2)}, u32[]{:S(2)}) collective-permute-start(f32[24,2,4,128]{3,2,1,0:T(4,128)S(1)} %get-tuple-element.110), channel_id=1, source_target_pairs={{0,1},{1,0},{2,3},{3,2},{4,5},{5,4},{6,7},{7,6},{8,9},{9,8},{10,11... | collective-permute-start | bytes 294920 | tf_op jit(solution)/shard_map/ppermute | solution.py:420
  6.6 12.8 %collective-permute-start.3 = (f32[24,2,4,128]{3,2,1,0:T(4,128)S(1)}, f32[24,2,4,128]{3,2,1,0:T(4,128)S(1)}, u32[]{:S(2)}, u32[]{:S(2)}) collective-permute-start(f32[24,2,4,128]{3,2,1,0:T(4,128)S(1)} %get-tuple-element.111), channel_id=1, source_target_pairs={{0,15},{1,2},{2,1},{3,4},{4,3},{5,6},{6,5},{7,8},{8,7},{9,10},{10,... | collective-permute-start | bytes 294920 | tf_op jit(solution)/shard_map/ppermute | solution.py:420
  19.7 6.2 %collective-permute-start.4 = (f32[4,2,24,128]{3,2,1,0:T(8,128)S(1)}, f32[4,2,24,128]{3,2,1,0:T(8,128)S(1)}, u32[]{:S(2)}, u32[]{:S(2)}) collective-permute-start(f32[4,2,24,128]{3,2,1,0:T(8,128)S(1)} %get-tuple-element.121), channel_id=1, source_target_pairs={{0,16},{16,0},{32,48},{48,32},{64,80},{80,64},{96,112},{112,96},{1... | collective-permute-start | bytes 294920 | tf_op jit(solution)/shard_map/ppermute | solution.py:420
  19.8 7.7 %collective-permute-start.5 = (f32[4,2,24,128]{3,2,1,0:T(8,128)S(1)}, f32[4,2,24,128]{3,2,1,0:T(8,128)S(1)}, u32[]{:S(2)}, u32[]{:S(2)}) collective-permute-start(f32[4,2,24,128]{3,2,1,0:T(8,128)S(1)} %get-tuple-element.122), channel_id=1, source_target_pairs={{0,112},{16,32},{32,16},{48,64},{64,48},{80,96},{96,80},{112,0},{1... | collective-permute-start | bytes 294920 | tf_op jit(solution)/shard_map/ppermute | solution.py:420
  21.3 6.1 %collective-permute-start.6 = (f32[24,2,4,128]{3,2,1,0:T(4,128)S(1)}, f32[24,2,4,128]{3,2,1,0:T(4,128)S(1)}, u32[]{:S(2)}, u32[]{:S(2)}) collective-permute-start(f32[24,2,4,128]{3,2,1,0:T(4,128)S(1)} %get-tuple-element.123), channel_id=1, source_target_pairs={{0,1},{1,0},{2,3},{3,2},{4,5},{5,4},{6,7},{7,6},{8,9},{9,8},{10,11... | collective-permute-start | bytes 294920 | tf_op jit(solution)/shard_map/ppermute | solution.py:420
  21.3 7.7 %collective-permute-start.7 = (f32[24,2,4,128]{3,2,1,0:T(4,128)S(1)}, f32[24,2,4,128]{3,2,1,0:T(4,128)S(1)}, u32[]{:S(2)}, u32[]{:S(2)}) collective-permute-start(f32[24,2,4,128]{3,2,1,0:T(4,128)S(1)} %get-tuple-element.124), channel_id=1, source_target_pairs={{0,15},{1,2},{2,1},{3,4},{4,3},{5,6},{6,5},{7,8},{8,7},{9,10},{10,... | collective-permute-start | bytes 294920 | tf_op jit(solution)/shard_map/ppermute | solution.py:420
  29.3 8.1 %collective-permute-start.8 = (f32[4,2,24,128]{3,2,1,0:T(8,128)S(1)}, f32[4,2,24,128]{3,2,1,0:T(8,128)S(1)}, u32[]{:S(2)}, u32[]{:S(2)}) collective-permute-start(f32[4,2,24,128]{3,2,1,0:T(8,128)S(1)} %get-tuple-element.132), channel_id=1, source_target_pairs={{0,16},{16,0},{32,48},{48,32},{64,80},{80,64},{96,112},{112,96},{1... | collective-permute-start | bytes 294920 | tf_op jit(solution)/shard_map/ppermute | solution.py:420
  29.8 7.6 %collective-permute-start.9 = (f32[4,2,24,128]{3,2,1,0:T(8,128)S(1)}, f32[4,2,24,128]{3,2,1,0:T(8,128)S(1)}, u32[]{:S(2)}, u32[]{:S(2)}) collective-permute-start(f32[4,2,24,128]{3,2,1,0:T(8,128)S(1)} %get-tuple-element.133), channel_id=1, source_target_pairs={{0,112},{16,32},{32,16},{48,64},{64,48},{80,96},{96,80},{112,0},{1... | collective-permute-start | bytes 294920 | tf_op jit(solution)/shard_map/ppermute | solution.py:420
  32.1 5.3 %collective-permute-start.10 = (f32[24,2,4,128]{3,2,1,0:T(4,128)S(1)}, f32[24,2,4,128]{3,2,1,0:T(4,128)S(1)}, u32[]{:S(2)}, u32[]{:S(2)}) collective-permute-start(f32[24,2,4,128]{3,2,1,0:T(4,128)S(1)} %get-tuple-element.134), channel_id=1, source_target_pairs={{0,1},{1,0},{2,3},{3,2},{4,5},{5,4},{6,7},{7,6},{8,9},{9,8},{10,11... | collective-permute-start | bytes 294920 | tf_op jit(solution)/shard_map/ppermute | solution.py:420
  32.1 7.7 %collective-permute-start.11 = (f32[24,2,4,128]{3,2,1,0:T(4,128)S(1)}, f32[24,2,4,128]{3,2,1,0:T(4,128)S(1)}, u32[]{:S(2)}, u32[]{:S(2)}) collective-permute-start(f32[24,2,4,128]{3,2,1,0:T(4,128)S(1)} %get-tuple-element.135), channel_id=1, source_target_pairs={{0,15},{1,2},{2,1},{3,4},{4,3},{5,6},{6,5},{7,8},{8,7},{9,10},{10,... | collective-permute-start | bytes 294920 | tf_op jit(solution)/shard_map/ppermute | solution.py:420
  40.1 7.7 %collective-permute-start.12 = (f32[4,2,24,128]{3,2,1,0:T(8,128)S(1)}, f32[4,2,24,128]{3,2,1,0:T(8,128)S(1)}, u32[]{:S(2)}, u32[]{:S(2)}) collective-permute-start(f32[4,2,24,128]{3,2,1,0:T(8,128)S(1)} %get-tuple-element.143), channel_id=1, source_target_pairs={{0,16},{16,0},{32,48},{48,32},{64,80},{80,64},{96,112},{112,96},{1... | collective-permute-start | bytes 294920 | tf_op jit(solution)/shard_map/ppermute | solution.py:420
  40.9 7.6 %collective-permute-start.13 = (f32[4,2,24,128]{3,2,1,0:T(8,128)S(1)}, f32[4,2,24,128]{3,2,1,0:T(8,128)S(1)}, u32[]{:S(2)}, u32[]{:S(2)}) collective-permute-start(f32[4,2,24,128]{3,2,1,0:T(8,128)S(1)} %get-tuple-element.144), channel_id=1, source_target_pairs={{0,112},{16,32},{32,16},{48,64},{64,48},{80,96},{96,80},{112,0},{1... | collective-permute-start | bytes 294920 | tf_op jit(solution)/shard_map/ppermute | solution.py:420
  42.9 5.6 %collective-permute-start.14 = (f32[24,2,4,128]{3,2,1,0:T(4,128)S(1)}, f32[24,2,4,128]{3,2,1,0:T(4,128)S(1)}, u32[]{:S(2)}, u32[]{:S(2)}) collective-permute-start(f32[24,2,4,128]{3,2,1,0:T(4,128)S(1)} %get-tuple-element.145), channel_id=1, source_target_pairs={{0,1},{1,0},{2,3},{3,2},{4,5},{5,4},{6,7},{7,6},{8,9},{9,8},{10,11... | collective-permute-start | bytes 294920 | tf_op jit(solution)/shard_map/ppermute | solution.py:420
  42.9 7.7 %collective-permute-start.15 = (f32[24,2,4,128]{3,2,1,0:T(4,128)S(1)}, f32[24,2,4,128]{3,2,1,0:T(4,128)S(1)}, u32[]{:S(2)}, u32[]{:S(2)}) collective-permute-start(f32[24,2,4,128]{3,2,1,0:T(4,128)S(1)} %get-tuple-element.146), channel_id=1, source_target_pairs={{0,15},{1,2},{2,1},{3,4},{4,3},{5,6},{6,5},{7,8},{8,7},{9,10},{10,... | collective-permute-start | bytes 294920 | tf_op jit(solution)/shard_map/ppermute | solution.py:420
  50.8 7.9 %collective-permute-start.16 = (f32[4,2,24,128]{3,2,1,0:T(8,128)S(1)}, f32[4,2,24,128]{3,2,1,0:T(8,128)S(1)}, u32[]{:S(2)}, u32[]{:S(2)}) collective-permute-start(f32[4,2,24,128]{3,2,1,0:T(8,128)S(1)} %get-tuple-element.154), channel_id=1, source_target_pairs={{0,16},{16,0},{32,48},{48,32},{64,80},{80,64},{96,112},{112,96},{1... | collective-permute-start | bytes 294920 | tf_op jit(solution)/shard_map/ppermute | solution.py:420
  50.9 8.2 %collective-permute-start.17 = (f32[4,2,24,128]{3,2,1,0:T(8,128)S(1)}, f32[4,2,24,128]{3,2,1,0:T(8,128)S(1)}, u32[]{:S(2)}, u32[]{:S(2)}) collective-permute-start(f32[4,2,24,128]{3,2,1,0:T(8,128)S(1)} %get-tuple-element.155), channel_id=1, source_target_pairs={{0,112},{16,32},{32,16},{48,64},{64,48},{80,96},{96,80},{112,0},{1... | collective-permute-start | bytes 294920 | tf_op jit(solution)/shard_map/ppermute | solution.py:420
  54.4 4.7 %collective-permute-start.18 = (f32[24,2,4,128]{3,2,1,0:T(4,128)S(1)}, f32[24,2,4,128]{3,2,1,0:T(4,128)S(1)}, u32[]{:S(2)}, u32[]{:S(2)}) collective-permute-start(f32[24,2,4,128]{3,2,1,0:T(4,128)S(1)} %get-tuple-element.156), channel_id=1, source_target_pairs={{0,1},{1,0},{2,3},{3,2},{4,5},{5,4},{6,7},{7,6},{8,9},{9,8},{10,11... | collective-permute-start | bytes 294920 | tf_op jit(solution)/shard_map/ppermute | solution.py:420
  54.4 7.7 %collective-permute-start.19 = (f32[24,2,4,128]{3,2,1,0:T(4,128)S(1)}, f32[24,2,4,128]{3,2,1,0:T(4,128)S(1)}, u32[]{:S(2)}, u32[]{:S(2)}) collective-permute-start(f32[24,2,4,128]{3,2,1,0:T(4,128)S(1)} %get-tuple-element.157), channel_id=1, source_target_pairs={{0,15},{1,2},{2,1},{3,4},{4,3},{5,6},{6,5},{7,8},{8,7},{9,10},{10,... | collective-permute-start | bytes 294920 | tf_op jit(solution)/shard_map/ppermute | solution.py:420
  62.4 6.8 %collective-permute-start.20 = (f32[4,2,24,128]{3,2,1,0:T(8,128)S(1)}, f32[4,2,24,128]{3,2,1,0:T(8,128)S(1)}, u32[]{:S(2)}, u32[]{:S(2)}) collective-permute-start(f32[4,2,24,128]{3,2,1,0:T(8,128)S(1)} %get-tuple-element.165), channel_id=1, source_target_pairs={{0,16},{16,0},{32,48},{48,32},{64,80},{80,64},{96,112},{112,96},{1... | collective-permute-start | bytes 294920 | tf_op jit(solution)/shard_map/ppermute | solution.py:420
  62.7 7.6 %collective-permute-start.21 = (f32[4,2,24,128]{3,2,1,0:T(8,128)S(1)}, f32[4,2,24,128]{3,2,1,0:T(8,128)S(1)}, u32[]{:S(2)}, u32[]{:S(2)}) collective-permute-start(f32[4,2,24,128]{3,2,1,0:T(8,128)S(1)} %get-tuple-element.166), channel_id=1, source_target_pairs={{0,112},{16,32},{32,16},{48,64},{64,48},{80,96},{96,80},{112,0},{1... | collective-permute-start | bytes 294920 | tf_op jit(solution)/shard_map/ppermute | solution.py:420
  64.2 6.2 %collective-permute-start.22 = (f32[24,2,4,128]{3,2,1,0:T(4,128)S(1)}, f32[24,2,4,128]{3,2,1,0:T(4,128)S(1)}, u32[]{:S(2)}, u32[]{:S(2)}) collective-permute-start(f32[24,2,4,128]{3,2,1,0:T(4,128)S(1)} %get-tuple-element.167), channel_id=1, source_target_pairs={{0,1},{1,0},{2,3},{3,2},{4,5},{5,4},{6,7},{7,6},{8,9},{9,8},{10,11... | collective-permute-start | bytes 294920 | tf_op jit(solution)/shard_map/ppermute | solution.py:420
  64.2 7.7 %collective-permute-start.23 = (f32[24,2,4,128]{3,2,1,0:T(4,128)S(1)}, f32[24,2,4,128]{3,2,1,0:T(4,128)S(1)}, u32[]{:S(2)}, u32[]{:S(2)}) collective-permute-start(f32[24,2,4,128]{3,2,1,0:T(4,128)S(1)} %get-tuple-element.168), channel_id=1, source_target_pairs={{0,15},{1,2},{2,1},{3,4},{4,3},{5,6},{6,5},{7,8},{8,7},{9,10},{10,... | collective-permute-start | bytes 294920 | tf_op jit(solution)/shard_map/ppermute | solution.py:420
  72.2 8.1 %collective-permute-start.24 = (f32[4,2,24,128]{3,2,1,0:T(8,128)S(1)}, f32[4,2,24,128]{3,2,1,0:T(8,128)S(1)}, u32[]{:S(2)}, u32[]{:S(2)}) collective-permute-start(f32[4,2,24,128]{3,2,1,0:T(8,128)S(1)} %get-tuple-element.176), channel_id=1, source_target_pairs={{0,16},{16,0},{32,48},{48,32},{64,80},{80,64},{96,112},{112,96},{1... | collective-permute-start | bytes 294920 | tf_op jit(solution)/shard_map/ppermute | solution.py:420
  72.7 7.6 %collective-permute-start.25 = (f32[4,2,24,128]{3,2,1,0:T(8,128)S(1)}, f32[4,2,24,128]{3,2,1,0:T(8,128)S(1)}, u32[]{:S(2)}, u32[]{:S(2)}) collective-permute-start(f32[4,2,24,128]{3,2,1,0:T(8,128)S(1)} %get-tuple-element.177), channel_id=1, source_target_pairs={{0,112},{16,32},{32,16},{48,64},{64,48},{80,96},{96,80},{112,0},{1... | collective-permute-start | bytes 294920 | tf_op jit(solution)/shard_map/ppermute | solution.py:420
  75.2 5.1 %collective-permute-start.26 = (f32[24,2,4,128]{3,2,1,0:T(4,128)S(1)}, f32[24,2,4,128]{3,2,1,0:T(4,128)S(1)}, u32[]{:S(2)}, u32[]{:S(2)}) collective-permute-start(f32[24,2,4,128]{3,2,1,0:T(4,128)S(1)} %get-tuple-element.178), channel_id=1, source_target_pairs={{0,1},{1,0},{2,3},{3,2},{4,5},{5,4},{6,7},{7,6},{8,9},{9,8},{10,11... | collective-permute-start | bytes 294920 | tf_op jit(solution)/shard_map/ppermute | solution.py:420
  75.2 7.7 %collective-permute-start.27 = (f32[24,2,4,128]{3,2,1,0:T(4,128)S(1)}, f32[24,2,4,128]{3,2,1,0:T(4,128)S(1)}, u32[]{:S(2)}, u32[]{:S(2)}) collective-permute-start(f32[24,2,4,128]{3,2,1,0:T(4,128)S(1)} %get-tuple-element.179), channel_id=1, source_target_pairs={{0,15},{1,2},{2,1},{3,4},{4,3},{5,6},{6,5},{7,8},{8,7},{9,10},{10,... | collective-permute-start | bytes 294920 | tf_op jit(solution)/shard_map/ppermute | solution.py:420
  83.2 7.5 %collective-permute-start.28 = (f32[4,2,24,128]{3,2,1,0:T(8,128)S(1)}, f32[4,2,24,128]{3,2,1,0:T(8,128)S(1)}, u32[]{:S(2)}, u32[]{:S(2)}) collective-permute-start(f32[4,2,24,128]{3,2,1,0:T(8,128)S(1)} %get-tuple-element.187), channel_id=1, source_target_pairs={{0,16},{16,0},{32,48},{48,32},{64,80},{80,64},{96,112},{112,96},{1... | collective-permute-start | bytes 294920 | tf_op jit(solution)/shard_map/ppermute | solution.py:420
  83.8 7.6 %collective-permute-start.29 = (f32[4,2,24,128]{3,2,1,0:T(8,128)S(1)}, f32[4,2,24,128]{3,2,1,0:T(8,128)S(1)}, u32[]{:S(2)}, u32[]{:S(2)}) collective-permute-start(f32[4,2,24,128]{3,2,1,0:T(8,128)S(1)} %get-tuple-element.188), channel_id=1, source_target_pairs={{0,112},{16,32},{32,16},{48,64},{64,48},{80,96},{96,80},{112,0},{1... | collective-permute-start | bytes 294920 | tf_op jit(solution)/shard_map/ppermute | solution.py:420
  85.7 5.6 %collective-permute-start.30 = (f32[24,2,4,128]{3,2,1,0:T(4,128)S(1)}, f32[24,2,4,128]{3,2,1,0:T(4,128)S(1)}, u32[]{:S(2)}, u32[]{:S(2)}) collective-permute-start(f32[24,2,4,128]{3,2,1,0:T(4,128)S(1)} %get-tuple-element.189), channel_id=1, source_target_pairs={{0,1},{1,0},{2,3},{3,2},{4,5},{5,4},{6,7},{7,6},{8,9},{9,8},{10,11... | collective-permute-start | bytes 294920 | tf_op jit(solution)/shard_map/ppermute | solution.py:420
  85.8 7.7 %collective-permute-start.31 = (f32[24,2,4,128]{3,2,1,0:T(4,128)S(1)}, f32[24,2,4,128]{3,2,1,0:T(4,128)S(1)}, u32[]{:S(2)}, u32[]{:S(2)}) collective-permute-start(f32[24,2,4,128]{3,2,1,0:T(4,128)S(1)} %get-tuple-element.190), channel_id=1, source_target_pairs={{0,15},{1,2},{2,1},{3,4},{4,3},{5,6},{6,5},{7,8},{8,7},{9,10},{10,... | collective-permute-start | bytes 294920 | tf_op jit(solution)/shard_map/ppermute | solution.py:420
  94.3 1.3 %collective-permute-start.32 = (f32[16,128]{1,0:T(8,128)S(1)}, f32[16,128]{1,0:T(8,128)S(1)}, u32[]{:S(2)}, u32[]{:S(2)}) collective-permute-start(f32[16,128]{1,0:T(8,128)S(1)} %get-tuple-element.200), channel_id=1, source_target_pairs={{0,1},{1,0},{2,3},{3,2},{4,5},{5,4},{6,7},{7,6},{8,9},{9,8},{10,11... | collective-permute-start | bytes 24584 | tf_op jit(solution)/shard_map/ppermute | solution.py:436
  95.6 4.9 %collective-permute-start.35 = (f32[16,128]{1,0:T(8,128)S(1)}, f32[16,128]{1,0:T(8,128)S(1)}, u32[]{:S(2)}, u32[]{:S(2)}) collective-permute-start(f32[16,128]{1,0:T(8,128)S(1)} %add.21), channel_id=1, source_target_pairs={{0,18},{1,19},{2,16},{3,17},{4,22},{5,23},{6,20},{7,21},{8,26},{9,... | collective-permute-start | bytes 24584 | tf_op jit(solution)/shard_map/ppermute | solution.py:436
  95.6 5.2 %collective-permute-start.34 = (f32[16,128]{1,0:T(8,128)S(1)}, f32[16,128]{1,0:T(8,128)S(1)}, u32[]{:S(2)}, u32[]{:S(2)}) collective-permute-start(f32[16,128]{1,0:T(8,128)S(1)} %add.21), channel_id=1, source_target_pairs={{0,2},{1,3},{2,0},{3,1},{4,6},{5,7},{6,4},{7,5},{8,10},{9,11},{10,... | collective-permute-start | bytes 24584 | tf_op jit(solution)/shard_map/ppermute | solution.py:436
  97.8 3.7 %collective-permute-start.33 = (f32[16,128]{1,0:T(8,128)S(1)}, f32[16,128]{1,0:T(8,128)S(1)}, u32[]{:S(2)}, u32[]{:S(2)}) collective-permute-start(f32[16,128]{1,0:T(8,128)S(1)} %add.21), channel_id=1, source_target_pairs={{0,16},{1,17},{2,18},{3,19},{4,20},{5,21},{6,22},{7,23},{8,24},{9,... | collective-permute-start | bytes 24584 | tf_op jit(solution)/shard_map/ppermute | solution.py:436
  101.4 4.9 %collective-permute-start.38 = (f32[16,128]{1,0:T(8,128)S(1)}, f32[16,128]{1,0:T(8,128)S(1)}, u32[]{:S(2)}, u32[]{:S(2)}) collective-permute-start(f32[16,128]{1,0:T(8,128)S(1)} %add_add_fusion.1), channel_id=1, source_target_pairs={{0,12},{1,13},{2,14},{3,15},{4,8},{5,9},{6,10},{7,11},{8,4},{9,5},... | collective-permute-start | bytes 24584 | tf_op jit(solution)/shard_map/ppermute | solution.py:436
  103.3 5.2 %collective-permute-start.37 = (f32[16,128]{1,0:T(8,128)S(1)}, f32[16,128]{1,0:T(8,128)S(1)}, u32[]{:S(2)}, u32[]{:S(2)}) collective-permute-start(f32[16,128]{1,0:T(8,128)S(1)} %add_add_fusion.1), channel_id=1, source_target_pairs={{0,8},{1,9},{2,10},{3,11},{4,12},{5,13},{6,14},{7,15},{8,0},{9,1},... | collective-permute-start | bytes 24584 | tf_op jit(solution)/shard_map/ppermute | solution.py:436
  103.3 5.2 %collective-permute-start.36 = (f32[16,128]{1,0:T(8,128)S(1)}, f32[16,128]{1,0:T(8,128)S(1)}, u32[]{:S(2)}, u32[]{:S(2)}) collective-permute-start(f32[16,128]{1,0:T(8,128)S(1)} %add_add_fusion.1), channel_id=1, source_target_pairs={{0,4},{1,5},{2,6},{3,7},{4,0},{5,1},{6,2},{7,3},{8,12},{9,13},{10,... | collective-permute-start | bytes 24584 | tf_op jit(solution)/shard_map/ppermute | solution.py:436
  108.5 5.6 %collective-permute-start.39 = (f32[16,128]{1,0:T(8,128)S(1)}, f32[16,128]{1,0:T(8,128)S(1)}, u32[]{:S(2)}, u32[]{:S(2)}) collective-permute-start(f32[16,128]{1,0:T(8,128)S(1)} %add_add_fusion.refs_0_), channel_id=1, source_target_pairs={{0,32},{1,33},{2,34},{3,35},{4,36},{5,37},{6,38},{7,39},{8,40},{9,... | collective-permute-start | bytes 24584 | tf_op jit(solution)/shard_map/ppermute | solution.py:436
  109.9 5.2 %collective-permute-start.40 = (f32[16,128]{1,0:T(8,128)S(1)}, f32[16,128]{1,0:T(8,128)S(1)}, u32[]{:S(2)}, u32[]{:S(2)}) collective-permute-start(f32[16,128]{1,0:T(8,128)S(1)} %add_add_fusion.refs_0_), channel_id=1, source_target_pairs={{0,64},{1,65},{2,66},{3,67},{4,68},{5,69},{6,70},{7,71},{8,72},{9,... | collective-permute-start | bytes 24584 | tf_op jit(solution)/shard_map/ppermute | solution.py:436
  112.0 4.9 %collective-permute-start.41 = (f32[16,128]{1,0:T(8,128)S(1)}, f32[16,128]{1,0:T(8,128)S(1)}, u32[]{:S(2)}, u32[]{:S(2)}) collective-permute-start(f32[16,128]{1,0:T(8,128)S(1)} %add_add_fusion.refs_0_), channel_id=1, source_target_pairs={{0,96},{1,97},{2,98},{3,99},{4,100},{5,101},{6,102},{7,103},{8,104... | collective-permute-start | bytes 24584 | tf_op jit(solution)/shard_map/ppermute | solution.py:436

commit v5 on v4

--- a/solution.py
+++ b/solution.py
@@ -120,7 +120,7 @@
     return copies
 
 
-def split_strips(field, mine_x, mine_y, near_x, far_x, near_y, far_y):
+def split_strips(field, mine_x, mine_y, near_x, far_y, far_x, near_y):
     rows = [field[CX : CX + H, :, INSIDE, :], field[H : 2 * H, :, INSIDE, :]]
     near_x[...] = jnp.where(mine_x, rows[1], rows[0])
     far_x[...] = jnp.where(mine_x, rows[0], rows[1])
@@ -134,21 +134,23 @@
     return lax.axis_index(GX) % 2 == 1, lax.axis_index(GY) % 2 == 1
 
 
-def pack_kernel(pressure, field, near_x, far_x, near_y, far_y, staged, sems):
-    copies = fetch([(pressure, staged)], sems)
+def pack_kernel(pressure, old, speed_term, field, near_x, far_y, far_x, near_y, raw_old, raw_speed, staged, sems):
+    copies = fetch([(pressure, staged), (old, raw_old), (speed_term, raw_speed)], sems)
     field[...] = jnp.zeros(FIELD, jnp.float32)
-    for copy in copies:
+    for copy in copies[:CHUNKS]:
         copy.wait()
     for half in range(2):
         part = staged[:, :, half * LANES : (half + 1) * LANES]
         field[H : H + CX, half, INSIDE, :] = part
-    split_strips(field, *odd(), near_x, far_x, near_y, far_y)
+    split_strips(field, *odd(), near_x, far_y, far_x, near_y)
+    for copy in copies[CHUNKS:]:
+        copy.wait()
 
 
 def begin_kernel(
-    widths_far, sx_far, sy_far, sz_far, rx_far, ry_far, rz_far, amp_far, old, speed_term,
+    widths_far, sx_far, sy_far, sz_far, rx_far, ry_far, rz_far, amp_far, raw_old, raw_speed,
     field, speed, memory_x, memory_y, zeta_x, zeta_y, seen, keep_x, keep_y, norm, table, amps,
-    staged_old, staged_speed, sems, widths_ref, sx, sy, sz, rx, ry, rz, amp, small_sems,
+    widths_ref, sx, sy, sz, rx, ry, rz, amp, small_sems,
 ):
     far = (widths_far, sx_far, sy_far, sz_far, rx_far, ry_far, rz_far, amp_far)
     near = (widths_ref, sx, sy, sz, rx, ry, rz, amp)
@@ -158,11 +160,14 @@
     ]
     for copy in small:
         copy.start()
-    copies = fetch([(old, staged_old), (speed_term, staged_speed)], sems)
     gx, gy, edge_x, edge_y = place()
     start_x, start_y = (gx * CX, gy * CY)
     seen[...] = jnp.zeros(SEEN, jnp.float32)
     field[...] = jnp.zeros(FIELD, jnp.float32)
+    for half in range(2):
+        lanes = slice(half * LANES, (half + 1) * LANES)
+        field[H : H + CX, half, INSIDE, :] = raw_old[:, :, lanes]
+        speed[:, half, :, :] = raw_speed[:, :, lanes]
 
     @pl.when(edge_x)
     def _():
@@ -208,12 +213,6 @@
     for t in range(STEPS):
         for n in range(NSRC):
             amps[t * NSRC + n] = amp[n, t]
-    for copy in copies:
-        copy.wait()
-    for half in range(2):
-        lanes = slice(half * LANES, (half + 1) * LANES)
-        field[H : H + CX, half, INSIDE, :] = staged_old[:, :, lanes]
-        speed[:, half, :, :] = staged_speed[:, :, lanes]
 
 
 def inner_kernel(
@@ -316,10 +315,10 @@
 
 def join_kernel(last, *refs):
     if last:
-        table, keep_x, keep_y, norm, speed, near_x, far_x, near_y, far_y, _, _ = refs[:11]
+        table, keep_x, keep_y, norm, speed, near_x, far_y, far_x, near_y, _, _ = refs[:11]
         field, seen, beside = refs[11:]
     else:
-        speed, near_x, far_x, near_y, far_y, _, field = refs[:7]
+        speed, near_x, far_y, far_x, near_y, _, field = refs[:7]
         strips, beside = (refs[7:11], refs[11])
     gx, gy, edge_x, edge_y = place()
     mine_x, mine_y = odd()
@@ -421,10 +420,8 @@
 
 
 def exchange(strips):
-    near_x, far_x, near_y, far_y = strips
-    far_y = swap(far_y, GY, 1)
-    far_x = swap(far_x, GX, 1)
-    return (swap(near_x, GX, 0), far_x, swap(near_y, GY, 0), far_y)
+    near_x, far_y, far_x, near_y = strips
+    return (swap(near_x, GX, 0), swap(far_y, GY, 1), swap(far_x, GX, 1), swap(near_y, GY, 0))
 
 
 def spread(value, by):
@@ -464,15 +461,15 @@
     small = [layer_width, source_x, source_y, source_z, receiver_x, receiver_y, receiver_z, source_amp.T]
     small = [stay(v) for v in small]
     staged = pltpu.VMEM(pressure.shape, jnp.float32)
-    strips_out = shape(STRIP_X, STRIP_X, STRIP_Y, STRIP_Y)
-    current, *strips = pl.pallas_call(
+    strips_out = shape(STRIP_X, STRIP_Y, STRIP_X, STRIP_Y)
+    current, *strips, raw_old, raw_speed = pl.pallas_call(
         pack_kernel,
-        out_shape=shape(FIELD) + strips_out,
-        in_specs=hbm(1),
-        out_specs=vmem(5),
-        scratch_shapes=[staged, pltpu.SemaphoreType.DMA((1, CHUNKS))],
+        out_shape=shape(FIELD) + strips_out + shape(pressure.shape, pressure.shape),
+        in_specs=hbm(3),
+        out_specs=vmem(7),
+        scratch_shapes=[staged, pltpu.SemaphoreType.DMA((3, CHUNKS))],
         compiler_params=limit(8),
-    )(pressure)
+    )(pressure, pressure_old, speed_term)
     previous, speed, *rest = pl.pallas_call(
         begin_kernel,
         out_shape=shape(FIELD, BLOCK, MEM_X, MEM_Y, BLOCK, BLOCK, SEEN, KEEP_X, KEEP_Y, NORM)
@@ -480,13 +477,12 @@
             jax.ShapeDtypeStruct((TABLE,), jnp.int32),
             jax.ShapeDtypeStruct((STEPS * NSRC,), jnp.float32),
         ],
-        in_specs=hbm(10),
+        in_specs=hbm(8) + vmem(2),
         out_specs=vmem(10) + smem(2),
-        scratch_shapes=[staged, staged, pltpu.SemaphoreType.DMA((2, CHUNKS))]
-        + [pltpu.SMEM((n,), jnp.int32) for n in (4, NSRC, NSRC, NSRC, NREC, NREC, NREC)]
+        scratch_shapes=[pltpu.SMEM((n,), jnp.int32) for n in (4, NSRC, NSRC, NSRC, NREC, NREC, NREC)]
         + [pltpu.SMEM((NSRC, STEPS), jnp.float32), pltpu.SemaphoreType.DMA((8,))],
         compiler_params=limit(8),
-    )(*small, pressure_old, speed_term)
+    )(*small, raw_old, raw_speed)
     state, keeps, table, amps = (rest[:5], rest[5:8], rest[8], rest[9])
     band = jnp.asarray(band_matrix())
     beside = pltpu.VMEM((CX, 2, 24, LANES), jnp.float32)

time: 118 us -> 111 us (0.941)
  starting transfers between devices: 55.8 us -> 49.9 us
  waiting for transfers between devices: 28.1 us -> 26.7 us
  Pallas kernels: 32.6 us -> 33.9 us
    ppermute x32, starting transfers between devices: 42.7 us -> 36.9 us  [swap(): lax.ppermute(strip, axis, [(i, ((i + far ^ 1) - far) % size) for i in ran...]
  transfers between devices with their start and end apart: 42 -> 42, of which waited for: 22 -> 22; matrix products, arithmetic and copies ran while one was open for 0% -> 0% of each run, Pallas kernels for 24% -> 26%
where the time goes in v5:
time: 111 us
  starting transfers between devices  49.9 us (45%)
  Pallas kernels  33.9 us (31%)
  waiting for transfers between devices  26.7 us (24%)
    ppermute x32, starting transfers between devices, swap(): lax.ppermute(strip, axis, [(i, ((i + far ^ 1) - far) % size) for i in ran...  36.9 us
    pallas_call x8, Pallas kernels, per_device(): pl.pallas_call(functools.partial(inner_kernel, step), out_shape=shape(FIE...  24.6 us
    ppermute x32, waiting for transfers between devices, swap(): lax.ppermute(strip, axis, [(i, ((i + far ^ 1) - far) % size) for i in ran...  18.8 us
    ppermute x10, starting transfers between devices, spread(): return lax.ppermute(value, BOTH, pairs)  13 us
    ppermute x10, waiting for transfers between devices, spread(): return lax.ppermute(value, BOTH, pairs)  7.89 us
    pallas_call x1, Pallas kernels, per_device(): pl.pallas_call(begin_kernel, out_shape=shape(FIELD, BLOCK, MEM_X, MEM_Y,...  2.98 us
  transfers between devices with their start and end apart: 42, of which 22 were waited for; matrix products, arithmetic and copies ran while one was open for 0% of the time, Pallas kernels for 26%

profile of v5, /device:TPU:0, one launch (start us, length us, event | category | flops | bytes accessed | tf_op | source)
XLA Modules:
  0.0 111.3 jit_solution(16925056691222369611)
XLA Ops:
  0.6 1.7 %shard_map.139 = (f32[32,2,40,128]{3,2,1,0:T(8,128)S(1)}, f32[4,2,24,128]{3,2,1,0:T(8,128)S(1)}, f32[24,2,4,128]{3,2,1,0:T(4,128)S(1)}, f32[4,2,24,128]{3,2,1,0:...) custom-call(f32[24,24,256]{2,1,0:T(8,128)} %pressure.1, ...), custom_call_target="tpu_custom_call" | custom-call | tf_op jit(solution)/shard_map/pallas_call | solution.py:465
  2.3 1.7 %collective-permute-start = (f32[4,2,24,128]{3,2,1,0:T(8,128)S(1)}, f32[4,2,24,128]{3,2,1,0:T(8,128)S(1)}, u32[]{:S(2)}, u32[]{:S(2)}) collective-permute-start(f32[4,2,24,128]{3,2,1,0:T(8,128)S(1)} %get-tuple-element.112), channel_id=1, source_target_pairs={{0,16},{16,0},{32,48},{48,32},{64,80},{80,64},{96,112},{112,96},{1... | collective-permute-start | bytes 294920 | tf_op jit(solution)/shard_map/ppermute | solution.py:419
  4.0 5.4 %collective-permute-start.1 = (f32[24,2,4,128]{3,2,1,0:T(4,128)S(1)}, f32[24,2,4,128]{3,2,1,0:T(4,128)S(1)}, u32[]{:S(2)}, u32[]{:S(2)}) collective-permute-start(f32[24,2,4,128]{3,2,1,0:T(4,128)S(1)} %get-tuple-element.113), channel_id=1, source_target_pairs={{0,15},{1,2},{2,1},{3,4},{4,3},{5,6},{6,5},{7,8},{8,7},{9,10},{10,... | collective-permute-start | bytes 294920 | tf_op jit(solution)/shard_map/ppermute | solution.py:419
  9.3 2.7 %collective-permute-start.2 = (f32[4,2,24,128]{3,2,1,0:T(8,128)S(1)}, f32[4,2,24,128]{3,2,1,0:T(8,128)S(1)}, u32[]{:S(2)}, u32[]{:S(2)}) collective-permute-start(f32[4,2,24,128]{3,2,1,0:T(8,128)S(1)} %get-tuple-element.114), channel_id=1, source_target_pairs={{0,112},{16,32},{32,16},{48,64},{64,48},{80,96},{96,80},{112,0},{1... | collective-permute-start | bytes 294920 | tf_op jit(solution)/shard_map/ppermute | solution.py:419
  12.0 3.0 %shard_map.140 = (f32[32,2,40,128]{3,2,1,0:T(8,128)S(1)}, f32[24,2,24,128]{3,2,1,0:T(8,128)S(1)}, f32[2,32,2,24,128]{4,3,2,1,0:T(8,128)S(1)}, f32[24,2,40,128]{3...) custom-call(s32[4]{0:T(128)} %widths_far.1, ...), custom_call_target="tpu_custom_call" | custom-call | tf_op jit(solution)/shard_map/pallas_call | solution.py:473
  15.0 2.9 %shard_map.141 = (f32[32,2,40,128]{3,2,1,0:T(8,128)S(1)}, f32[2,32,2,24,128]{4,3,2,1,0:T(8,128)S(1)}, f32[24,2,40,128]{3,2,1,0:T(8,128)S(1)}, f32[24,2,24,128]{3...) custom-call(s32[72]{0:T(128)S(1)} %get-tuple-element.107.table.refs_, ...), custom_call_target="tpu_custom_call", output_to_operand_aliasing={{0}: (8, {}), {1}: (9, {}), {2}: (10, {}), {3}: (11, {}), {... | custom-call | tf_op jit(solution)/shard_map/pallas_call | solution.py:491
  18.3 1.9 %collective-permute-start.5 = (f32[24,2,4,128]{3,2,1,0:T(4,128)S(1)}, f32[24,2,4,128]{3,2,1,0:T(4,128)S(1)}, u32[]{:S(2)}, u32[]{:S(2)}) collective-permute-start(f32[24,2,4,128]{3,2,1,0:T(4,128)S(1)} %get-tuple-element.126), channel_id=1, source_target_pairs={{0,15},{1,2},{2,1},{3,4},{4,3},{5,6},{6,5},{7,8},{8,7},{9,10},{10,... | collective-permute-start | bytes 294920 | tf_op jit(solution)/shard_map/ppermute | solution.py:419
  21.0 3.1 %shard_map.143 = (f32[32,2,40,128]{3,2,1,0:T(8,128)S(1)}, f32[2,32,2,24,128]{4,3,2,1,0:T(8,128)S(1)}, f32[24,2,40,128]{3,2,1,0:T(8,128)S(1)}, f32[24,2,24,128]{3...) custom-call(s32[72]{0:T(128)S(1)} %get-tuple-element.107.table.refs_, ...), custom_call_target="tpu_custom_call", output_to_operand_aliasing={{0}: (8, {}), {1}: (9, {}), {2}: (10, {}), {3}: (11, {}), {... | custom-call | tf_op jit(solution)/shard_map/pallas_call | solution.py:491
  24.1 2.6 %collective-permute-done.5.refs_2_ = f32[24,2,4,128]{3,2,1,0:T(4,128)S(1)} collective-permute-done((f32[24,2,4,128]{3,2,1,0:T(4,128)S(1)}, f32[24,2,4,128]{3,2,1,0:T(4,128)S(1)}, u32[]{:S(2)}, u32[]{:S(2)}) %collective-permute-start.5) | collective-permute-done | bytes 98336 | tf_op jit(solution)/shard_map/ppermute | solution.py:419
  27.3 1.1 %collective-permute-start.8 = (f32[4,2,24,128]{3,2,1,0:T(8,128)S(1)}, f32[4,2,24,128]{3,2,1,0:T(8,128)S(1)}, u32[]{:S(2)}, u32[]{:S(2)}) collective-permute-start(f32[4,2,24,128]{3,2,1,0:T(8,128)S(1)} %get-tuple-element.136), channel_id=1, source_target_pairs={{0,16},{16,0},{32,48},{48,32},{64,80},{80,64},{96,112},{112,96},{1... | collective-permute-start | bytes 294920 | tf_op jit(solution)/shard_map/ppermute | solution.py:419
  28.4 3.5 %collective-permute-start.9 = (f32[24,2,4,128]{3,2,1,0:T(4,128)S(1)}, f32[24,2,4,128]{3,2,1,0:T(4,128)S(1)}, u32[]{:S(2)}, u32[]{:S(2)}) collective-permute-start(f32[24,2,4,128]{3,2,1,0:T(4,128)S(1)} %get-tuple-element.137), channel_id=1, source_target_pairs={{0,15},{1,2},{2,1},{3,4},{4,3},{5,6},{6,5},{7,8},{8,7},{9,10},{10,... | collective-permute-start | bytes 294920 | tf_op jit(solution)/shard_map/ppermute | solution.py:419
  32.1 3.1 %shard_map.145 = (f32[32,2,40,128]{3,2,1,0:T(8,128)S(1)}, f32[2,32,2,24,128]{4,3,2,1,0:T(8,128)S(1)}, f32[24,2,40,128]{3,2,1,0:T(8,128)S(1)}, f32[24,2,24,128]{3...) custom-call(s32[72]{0:T(128)S(1)} %get-tuple-element.107.table.refs_, ...), custom_call_target="tpu_custom_call", output_to_operand_aliasing={{0}: (8, {}), {1}: (9, {}), {2}: (10, {}), {3}: (11, {}), {... | custom-call | tf_op jit(solution)/shard_map/pallas_call | solution.py:491
  35.2 1.6 %collective-permute-done.9.refs_2_ = f32[24,2,4,128]{3,2,1,0:T(4,128)S(1)} collective-permute-done((f32[24,2,4,128]{3,2,1,0:T(4,128)S(1)}, f32[24,2,4,128]{3,2,1,0:T(4,128)S(1)}, u32[]{:S(2)}, u32[]{:S(2)}) %collective-permute-start.9) | collective-permute-done | bytes 98336 | tf_op jit(solution)/shard_map/ppermute | solution.py:419
  36.8 1.8 %collective-permute-done.10.refs_3_ = f32[4,2,24,128]{3,2,1,0:T(8,128)S(1)} collective-permute-done((f32[4,2,24,128]{3,2,1,0:T(8,128)S(1)}, f32[4,2,24,128]{3,2,1,0:T(8,128)S(1)}, u32[]{:S(2)}, u32[]{:S(2)}) %collective-permute-start.10) | collective-permute-done | bytes 98336 | tf_op jit(solution)/shard_map/ppermute | solution.py:419
  39.0 1.9 %collective-permute-start.13 = (f32[24,2,4,128]{3,2,1,0:T(4,128)S(1)}, f32[24,2,4,128]{3,2,1,0:T(4,128)S(1)}, u32[]{:S(2)}, u32[]{:S(2)}) collective-permute-start(f32[24,2,4,128]{3,2,1,0:T(4,128)S(1)} %get-tuple-element.148), channel_id=1, source_target_pairs={{0,15},{1,2},{2,1},{3,4},{4,3},{5,6},{6,5},{7,8},{8,7},{9,10},{10,... | collective-permute-start | bytes 294920 | tf_op jit(solution)/shard_map/ppermute | solution.py:419
  40.9 1.2 %collective-permute-start.14 = (f32[4,2,24,128]{3,2,1,0:T(8,128)S(1)}, f32[4,2,24,128]{3,2,1,0:T(8,128)S(1)}, u32[]{:S(2)}, u32[]{:S(2)}) collective-permute-start(f32[4,2,24,128]{3,2,1,0:T(8,128)S(1)} %get-tuple-element.149), channel_id=1, source_target_pairs={{0,112},{16,32},{32,16},{48,64},{64,48},{80,96},{96,80},{112,0},{1... | collective-permute-start | bytes 294920 | tf_op jit(solution)/shard_map/ppermute | solution.py:419
  42.1 3.1 %shard_map.147 = (f32[32,2,40,128]{3,2,1,0:T(8,128)S(1)}, f32[2,32,2,24,128]{4,3,2,1,0:T(8,128)S(1)}, f32[24,2,40,128]{3,2,1,0:T(8,128)S(1)}, f32[24,2,24,128]{3...) custom-call(s32[72]{0:T(128)S(1)} %get-tuple-element.107.table.refs_, ...), custom_call_target="tpu_custom_call", output_to_operand_aliasing={{0}: (8, {}), {1}: (9, {}), {2}: (10, {}), {3}: (11, {}), {... | custom-call | tf_op jit(solution)/shard_map/pallas_call | solution.py:491
  45.2 2.0 %collective-permute-done.13.refs_2_ = f32[24,2,4,128]{3,2,1,0:T(4,128)S(1)} collective-permute-done((f32[24,2,4,128]{3,2,1,0:T(4,128)S(1)}, f32[24,2,4,128]{3,2,1,0:T(4,128)S(1)}, u32[]{:S(2)}, u32[]{:S(2)}) %collective-permute-start.13) | collective-permute-done | bytes 98336 | tf_op jit(solution)/shard_map/ppermute | solution.py:419
  48.0 1.1 collective-permute-start.16
  49.1 2.4 %collective-permute-start.17 = (f32[24,2,4,128]{3,2,1,0:T(4,128)S(1)}, f32[24,2,4,128]{3,2,1,0:T(4,128)S(1)}, u32[]{:S(2)}, u32[]{:S(2)}) collective-permute-start(f32[24,2,4,128]{3,2,1,0:T(4,128)S(1)} %get-tuple-element.159), channel_id=1, source_target_pairs={{0,15},{1,2},{2,1},{3,4},{4,3},{5,6},{6,5},{7,8},{8,7},{9,10},{10,... | collective-permute-start | bytes 294920 | tf_op jit(solution)/shard_map/ppermute | solution.py:419
  51.5 0.9 collective-permute-start.18
  52.4 3.1 %shard_map.149 = (f32[32,2,40,128]{3,2,1,0:T(8,128)S(1)}, f32[2,32,2,24,128]{4,3,2,1,0:T(8,128)S(1)}, f32[24,2,40,128]{3,2,1,0:T(8,128)S(1)}, f32[24,2,24,128]{3...) custom-call(s32[72]{0:T(128)S(1)} %get-tuple-element.107.table.refs_, ...), custom_call_target="tpu_custom_call", output_to_operand_aliasing={{0}: (8, {}), {1}: (9, {}), {2}: (10, {}), {3}: (11, {}), {... | custom-call | tf_op jit(solution)/shard_map/pallas_call | solution.py:491
  55.5 1.2 %collective-permute-done.17.refs_2_ = f32[24,2,4,128]{3,2,1,0:T(4,128)S(1)} collective-permute-done((f32[24,2,4,128]{3,2,1,0:T(4,128)S(1)}, f32[24,2,4,128]{3,2,1,0:T(4,128)S(1)}, u32[]{:S(2)}, u32[]{:S(2)}) %collective-permute-start.17) | collective-permute-done | bytes 98336 | tf_op jit(solution)/shard_map/ppermute | solution.py:419
  56.7 1.5 %collective-permute-done.18.refs_3_ = f32[4,2,24,128]{3,2,1,0:T(8,128)S(1)} collective-permute-done((f32[4,2,24,128]{3,2,1,0:T(8,128)S(1)}, f32[4,2,24,128]{3,2,1,0:T(8,128)S(1)}, u32[]{:S(2)}, u32[]{:S(2)}) %collective-permute-start.18) | collective-permute-done | bytes 98336 | tf_op jit(solution)/shard_map/ppermute | solution.py:419
  58.8 2.1 %collective-permute-start.21 = (f32[24,2,4,128]{3,2,1,0:T(4,128)S(1)}, f32[24,2,4,128]{3,2,1,0:T(4,128)S(1)}, u32[]{:S(2)}, u32[]{:S(2)}) collective-permute-start(f32[24,2,4,128]{3,2,1,0:T(4,128)S(1)} %get-tuple-element.170), channel_id=1, source_target_pairs={{0,15},{1,2},{2,1},{3,4},{4,3},{5,6},{6,5},{7,8},{8,7},{9,10},{10,... | collective-permute-start | bytes 294920 | tf_op jit(solution)/shard_map/ppermute | solution.py:419
  60.9 1.6 %collective-permute-start.22 = (f32[4,2,24,128]{3,2,1,0:T(8,128)S(1)}, f32[4,2,24,128]{3,2,1,0:T(8,128)S(1)}, u32[]{:S(2)}, u32[]{:S(2)}) collective-permute-start(f32[4,2,24,128]{3,2,1,0:T(8,128)S(1)} %get-tuple-element.171), channel_id=1, source_target_pairs={{0,112},{16,32},{32,16},{48,64},{64,48},{80,96},{96,80},{112,0},{1... | collective-permute-start | bytes 294920 | tf_op jit(solution)/shard_map/ppermute | solution.py:419
  62.5 3.1 %shard_map.151 = (f32[32,2,40,128]{3,2,1,0:T(8,128)S(1)}, f32[2,32,2,24,128]{4,3,2,1,0:T(8,128)S(1)}, f32[24,2,40,128]{3,2,1,0:T(8,128)S(1)}, f32[24,2,24,128]{3...) custom-call(s32[72]{0:T(128)S(1)} %get-tuple-element.107.table.refs_, ...), custom_call_target="tpu_custom_call", output_to_operand_aliasing={{0}: (8, {}), {1}: (9, {}), {2}: (10, {}), {3}: (11, {}), {... | custom-call | tf_op jit(solution)/shard_map/pallas_call | solution.py:491
  65.6 1.3 %collective-permute-done.21.refs_2_ = f32[24,2,4,128]{3,2,1,0:T(4,128)S(1)} collective-permute-done((f32[24,2,4,128]{3,2,1,0:T(4,128)S(1)}, f32[24,2,4,128]{3,2,1,0:T(4,128)S(1)}, u32[]{:S(2)}, u32[]{:S(2)}) %collective-permute-start.21) | collective-permute-done | bytes 98336 | tf_op jit(solution)/shard_map/ppermute | solution.py:419
  68.8 2.4 %collective-permute-start.25 = (f32[24,2,4,128]{3,2,1,0:T(4,128)S(1)}, f32[24,2,4,128]{3,2,1,0:T(4,128)S(1)}, u32[]{:S(2)}, u32[]{:S(2)}) collective-permute-start(f32[24,2,4,128]{3,2,1,0:T(4,128)S(1)} %get-tuple-element.181), channel_id=1, source_target_pairs={{0,15},{1,2},{2,1},{3,4},{4,3},{5,6},{6,5},{7,8},{8,7},{9,10},{10,... | collective-permute-start | bytes 294920 | tf_op jit(solution)/shard_map/ppermute | solution.py:419
  72.1 3.1 %shard_map.153 = (f32[32,2,40,128]{3,2,1,0:T(8,128)S(1)}, f32[2,32,2,24,128]{4,3,2,1,0:T(8,128)S(1)}, f32[24,2,40,128]{3,2,1,0:T(8,128)S(1)}, f32[24,2,24,128]{3...) custom-call(s32[72]{0:T(128)S(1)} %get-tuple-element.107.table.refs_, ...), custom_call_target="tpu_custom_call", output_to_operand_aliasing={{0}: (8, {}), {1}: (9, {}), {2}: (10, {}), {3}: (11, {}), {... | custom-call | tf_op jit(solution)/shard_map/pallas_call | solution.py:491
  75.2 1.8 %collective-permute-done.25.refs_2_ = f32[24,2,4,128]{3,2,1,0:T(4,128)S(1)} collective-permute-done((f32[24,2,4,128]{3,2,1,0:T(4,128)S(1)}, f32[24,2,4,128]{3,2,1,0:T(4,128)S(1)}, u32[]{:S(2)}, u32[]{:S(2)}) %collective-permute-start.25) | collective-permute-done | bytes 98336 | tf_op jit(solution)/shard_map/ppermute | solution.py:419
  77.0 1.0 collective-permute-done.26.refs_3_
  78.4 2.7 %collective-permute-start.29 = (f32[24,2,4,128]{3,2,1,0:T(4,128)S(1)}, f32[24,2,4,128]{3,2,1,0:T(4,128)S(1)}, u32[]{:S(2)}, u32[]{:S(2)}) collective-permute-start(f32[24,2,4,128]{3,2,1,0:T(4,128)S(1)} %get-tuple-element.192), channel_id=1, source_target_pairs={{0,15},{1,2},{2,1},{3,4},{4,3},{5,6},{6,5},{7,8},{8,7},{9,10},{10,... | collective-permute-start | bytes 294920 | tf_op jit(solution)/shard_map/ppermute | solution.py:419
  81.1 1.1 collective-permute-start.30
  82.2 3.1 %shard_map.155 = (f32[32,2,40,128]{3,2,1,0:T(8,128)S(1)}, f32[2,32,2,24,128]{4,3,2,1,0:T(8,128)S(1)}, f32[24,2,40,128]{3,2,1,0:T(8,128)S(1)}, f32[24,2,24,128]{3...) custom-call(s32[72]{0:T(128)S(1)} %get-tuple-element.107.table.refs_, ...), custom_call_target="tpu_custom_call", output_to_operand_aliasing={{0}: (8, {}), {1}: (9, {}), {2}: (10, {}), {3}: (11, {}), {... | custom-call | tf_op jit(solution)/shard_map/pallas_call | solution.py:491
  85.3 1.1 %collective-permute-done.29.refs_6_ = f32[24,2,4,128]{3,2,1,0:T(4,128)S(1)} collective-permute-done((f32[24,2,4,128]{3,2,1,0:T(4,128)S(1)}, f32[24,2,4,128]{3,2,1,0:T(4,128)S(1)}, u32[]{:S(2)}, u32[]{:S(2)}) %collective-permute-start.29) | collective-permute-done | bytes 98336 | tf_op jit(solution)/shard_map/ppermute | solution.py:419
  86.5 1.4 %collective-permute-done.30.refs_7_ = f32[4,2,24,128]{3,2,1,0:T(8,128)S(1)} collective-permute-done((f32[4,2,24,128]{3,2,1,0:T(8,128)S(1)}, f32[4,2,24,128]{3,2,1,0:T(8,128)S(1)}, u32[]{:S(2)}, u32[]{:S(2)}) %collective-permute-start.30) | collective-permute-done | bytes 98336 | tf_op jit(solution)/shard_map/ppermute | solution.py:419
  87.9 1.1 shard_map.156
  88.9 1.2 %collective-permute-done.32 = f32[16,128]{1,0:T(8,128)S(1)} collective-permute-done((f32[16,128]{1,0:T(8,128)S(1)}, f32[16,128]{1,0:T(8,128)S(1)}, u32[]{:S(2)}, u32[]{:S(2)}) %collective-permute-start.32) | collective-permute-done | bytes 8224 | tf_op jit(solution)/shard_map/ppermute | solution.py:433
  90.1 2.3 %collective-permute-start.34 = (f32[16,128]{1,0:T(8,128)S(1)}, f32[16,128]{1,0:T(8,128)S(1)}, u32[]{:S(2)}, u32[]{:S(2)}) collective-permute-start(f32[16,128]{1,0:T(8,128)S(1)} %add.21), channel_id=1, source_target_pairs={{0,2},{1,3},{2,0},{3,1},{4,6},{5,7},{6,4},{7,5},{8,10},{9,11},{10,... | collective-permute-start | bytes 24584 | tf_op jit(solution)/shard_map/ppermute | solution.py:433
  92.4 1.8 %collective-permute-start.33 = (f32[16,128]{1,0:T(8,128)S(1)}, f32[16,128]{1,0:T(8,128)S(1)}, u32[]{:S(2)}, u32[]{:S(2)}) collective-permute-start(f32[16,128]{1,0:T(8,128)S(1)} %add.21), channel_id=1, source_target_pairs={{0,16},{1,17},{2,18},{3,19},{4,20},{5,21},{6,22},{7,23},{8,24},{9,... | collective-permute-start | bytes 24584 | tf_op jit(solution)/shard_map/ppermute | solution.py:433
  96.0 1.3 %collective-permute-start.38 = (f32[16,128]{1,0:T(8,128)S(1)}, f32[16,128]{1,0:T(8,128)S(1)}, u32[]{:S(2)}, u32[]{:S(2)}) collective-permute-start(f32[16,128]{1,0:T(8,128)S(1)} %add_add_fusion.1), channel_id=1, source_target_pairs={{0,12},{1,13},{2,14},{3,15},{4,8},{5,9},{6,10},{7,11},{8,4},{9,5},... | collective-permute-start | bytes 24584 | tf_op jit(solution)/shard_map/ppermute | solution.py:433
  97.3 2.8 %collective-permute-start.36 = (f32[16,128]{1,0:T(8,128)S(1)}, f32[16,128]{1,0:T(8,128)S(1)}, u32[]{:S(2)}, u32[]{:S(2)}) collective-permute-start(f32[16,128]{1,0:T(8,128)S(1)} %add_add_fusion.1), channel_id=1, source_target_pairs={{0,4},{1,5},{2,6},{3,7},{4,0},{5,1},{6,2},{7,3},{8,12},{9,13},{10,... | collective-permute-start | bytes 24584 | tf_op jit(solution)/shard_map/ppermute | solution.py:433
  100.9 1.6 %collective-permute-done.37 = f32[16,128]{1,0:T(8,128)S(1)} collective-permute-done((f32[16,128]{1,0:T(8,128)S(1)}, f32[16,128]{1,0:T(8,128)S(1)}, u32[]{:S(2)}, u32[]{:S(2)}) %collective-permute-start.37) | collective-permute-done | bytes 8224 | tf_op jit(solution)/shard_map/ppermute | solution.py:433
  102.5 1.1 collective-permute-start.39
  103.5 2.3 %collective-permute-start.40 = (f32[16,128]{1,0:T(8,128)S(1)}, f32[16,128]{1,0:T(8,128)S(1)}, u32[]{:S(2)}, u32[]{:S(2)}) collective-permute-start(f32[16,128]{1,0:T(8,128)S(1)} %add_add_fusion.refs_0_), channel_id=1, source_target_pairs={{0,64},{1,65},{2,66},{3,67},{4,68},{5,69},{6,70},{7,71},{8,72},{9,... | collective-permute-start | bytes 24584 | tf_op jit(solution)/shard_map/ppermute | solution.py:433
  105.8 1.5 %collective-permute-start.41 = (f32[16,128]{1,0:T(8,128)S(1)}, f32[16,128]{1,0:T(8,128)S(1)}, u32[]{:S(2)}, u32[]{:S(2)}) collective-permute-start(f32[16,128]{1,0:T(8,128)S(1)} %add_add_fusion.refs_0_), channel_id=1, source_target_pairs={{0,96},{1,97},{2,98},{3,99},{4,100},{5,101},{6,102},{7,103},{8,104... | collective-permute-start | bytes 24584 | tf_op jit(solution)/shard_map/ppermute | solution.py:433
  108.7 2.0 %collective-permute-done.41.refs_3_ = f32[16,128]{1,0:T(8,128)S(1)} collective-permute-done((f32[16,128]{1,0:T(8,128)S(1)}, f32[16,128]{1,0:T(8,128)S(1)}, u32[]{:S(2)}, u32[]{:S(2)}) %collective-permute-start.41) | collective-permute-done | bytes 8224 | tf_op jit(solution)/shard_map/ppermute | solution.py:433
  (61 shorter events, 11.6 us)
Async XLA Ops:
  0.6 14.4 %copy-start = (bf16[512,256]{1,0:T(8,128)(2,1)S(1)}, bf16[512,256]{1,0:T(8,128)(2,1)}, u32[]{:S(2)}) copy-start(bf16[512,256]{1,0:T(8,128)(2,1)} %constant.2.clone.band) | copy-start | bytes 786436
  2.3 15.6 %collective-permute-start = (f32[4,2,24,128]{3,2,1,0:T(8,128)S(1)}, f32[4,2,24,128]{3,2,1,0:T(8,128)S(1)}, u32[]{:S(2)}, u32[]{:S(2)}) collective-permute-start(f32[4,2,24,128]{3,2,1,0:T(8,128)S(1)} %get-tuple-element.112), channel_id=1, source_target_pairs={{0,16},{16,0},{32,48},{48,32},{64,80},{80,64},{96,112},{112,96},{1... | collective-permute-start | bytes 294920 | tf_op jit(solution)/shard_map/ppermute | solution.py:419
  4.0 13.9 %collective-permute-start.1 = (f32[24,2,4,128]{3,2,1,0:T(4,128)S(1)}, f32[24,2,4,128]{3,2,1,0:T(4,128)S(1)}, u32[]{:S(2)}, u32[]{:S(2)}) collective-permute-start(f32[24,2,4,128]{3,2,1,0:T(4,128)S(1)} %get-tuple-element.113), channel_id=1, source_target_pairs={{0,15},{1,2},{2,1},{3,4},{4,3},{5,6},{6,5},{7,8},{8,7},{9,10},{10,... | collective-permute-start | bytes 294920 | tf_op jit(solution)/shard_map/ppermute | solution.py:419
  9.3 8.6 %collective-permute-start.2 = (f32[4,2,24,128]{3,2,1,0:T(8,128)S(1)}, f32[4,2,24,128]{3,2,1,0:T(8,128)S(1)}, u32[]{:S(2)}, u32[]{:S(2)}) collective-permute-start(f32[4,2,24,128]{3,2,1,0:T(8,128)S(1)} %get-tuple-element.114), channel_id=1, source_target_pairs={{0,112},{16,32},{32,16},{48,64},{64,48},{80,96},{96,80},{112,0},{1... | collective-permute-start | bytes 294920 | tf_op jit(solution)/shard_map/ppermute | solution.py:419
  12.0 5.9 %collective-permute-start.3 = (f32[24,2,4,128]{3,2,1,0:T(4,128)S(1)}, f32[24,2,4,128]{3,2,1,0:T(4,128)S(1)}, u32[]{:S(2)}, u32[]{:S(2)}) collective-permute-start(f32[24,2,4,128]{3,2,1,0:T(4,128)S(1)} %get-tuple-element.115), channel_id=1, source_target_pairs={{0,1},{1,0},{2,3},{3,2},{4,5},{5,4},{6,7},{7,6},{8,9},{9,8},{10,11... | collective-permute-start | bytes 294920 | tf_op jit(solution)/shard_map/ppermute | solution.py:419
  18.2 5.8 %collective-permute-start.4 = (f32[4,2,24,128]{3,2,1,0:T(8,128)S(1)}, f32[4,2,24,128]{3,2,1,0:T(8,128)S(1)}, u32[]{:S(2)}, u32[]{:S(2)}) collective-permute-start(f32[4,2,24,128]{3,2,1,0:T(8,128)S(1)} %get-tuple-element.125), channel_id=1, source_target_pairs={{0,16},{16,0},{32,48},{48,32},{64,80},{80,64},{96,112},{112,96},{1... | collective-permute-start | bytes 294920 | tf_op jit(solution)/shard_map/ppermute | solution.py:419
  18.3 8.3 %collective-permute-start.5 = (f32[24,2,4,128]{3,2,1,0:T(4,128)S(1)}, f32[24,2,4,128]{3,2,1,0:T(4,128)S(1)}, u32[]{:S(2)}, u32[]{:S(2)}) collective-permute-start(f32[24,2,4,128]{3,2,1,0:T(4,128)S(1)} %get-tuple-element.126), channel_id=1, source_target_pairs={{0,15},{1,2},{2,1},{3,4},{4,3},{5,6},{6,5},{7,8},{8,7},{9,10},{10,... | collective-permute-start | bytes 294920 | tf_op jit(solution)/shard_map/ppermute | solution.py:419
  20.2 6.7 %collective-permute-start.6 = (f32[4,2,24,128]{3,2,1,0:T(8,128)S(1)}, f32[4,2,24,128]{3,2,1,0:T(8,128)S(1)}, u32[]{:S(2)}, u32[]{:S(2)}) collective-permute-start(f32[4,2,24,128]{3,2,1,0:T(8,128)S(1)} %get-tuple-element.127), channel_id=1, source_target_pairs={{0,112},{16,32},{32,16},{48,64},{64,48},{80,96},{96,80},{112,0},{1... | collective-permute-start | bytes 294920 | tf_op jit(solution)/shard_map/ppermute | solution.py:419
  21.0 6.0 %collective-permute-start.7 = (f32[24,2,4,128]{3,2,1,0:T(4,128)S(1)}, f32[24,2,4,128]{3,2,1,0:T(4,128)S(1)}, u32[]{:S(2)}, u32[]{:S(2)}) collective-permute-start(f32[24,2,4,128]{3,2,1,0:T(4,128)S(1)} %get-tuple-element.128), channel_id=1, source_target_pairs={{0,1},{1,0},{2,3},{3,2},{4,5},{5,4},{6,7},{7,6},{8,9},{9,8},{10,11... | collective-permute-start | bytes 294920 | tf_op jit(solution)/shard_map/ppermute | solution.py:419
  27.3 7.9 %collective-permute-start.8 = (f32[4,2,24,128]{3,2,1,0:T(8,128)S(1)}, f32[4,2,24,128]{3,2,1,0:T(8,128)S(1)}, u32[]{:S(2)}, u32[]{:S(2)}) collective-permute-start(f32[4,2,24,128]{3,2,1,0:T(8,128)S(1)} %get-tuple-element.136), channel_id=1, source_target_pairs={{0,16},{16,0},{32,48},{48,32},{64,80},{80,64},{96,112},{112,96},{1... | collective-permute-start | bytes 294920 | tf_op jit(solution)/shard_map/ppermute | solution.py:419
  28.4 8.4 %collective-permute-start.9 = (f32[24,2,4,128]{3,2,1,0:T(4,128)S(1)}, f32[24,2,4,128]{3,2,1,0:T(4,128)S(1)}, u32[]{:S(2)}, u32[]{:S(2)}) collective-permute-start(f32[24,2,4,128]{3,2,1,0:T(4,128)S(1)} %get-tuple-element.137), channel_id=1, source_target_pairs={{0,15},{1,2},{2,1},{3,4},{4,3},{5,6},{6,5},{7,8},{8,7},{9,10},{10,... | collective-permute-start | bytes 294920 | tf_op jit(solution)/shard_map/ppermute | solution.py:419
  31.9 6.7 %collective-permute-start.10 = (f32[4,2,24,128]{3,2,1,0:T(8,128)S(1)}, f32[4,2,24,128]{3,2,1,0:T(8,128)S(1)}, u32[]{:S(2)}, u32[]{:S(2)}) collective-permute-start(f32[4,2,24,128]{3,2,1,0:T(8,128)S(1)} %get-tuple-element.138), channel_id=1, source_target_pairs={{0,112},{16,32},{32,16},{48,64},{64,48},{80,96},{96,80},{112,0},{1... | collective-permute-start | bytes 294920 | tf_op jit(solution)/shard_map/ppermute | solution.py:419
  32.1 6.5 %collective-permute-start.11 = (f32[24,2,4,128]{3,2,1,0:T(4,128)S(1)}, f32[24,2,4,128]{3,2,1,0:T(4,128)S(1)}, u32[]{:S(2)}, u32[]{:S(2)}) collective-permute-start(f32[24,2,4,128]{3,2,1,0:T(4,128)S(1)} %get-tuple-element.139), channel_id=1, source_target_pairs={{0,1},{1,0},{2,3},{3,2},{4,5},{5,4},{6,7},{7,6},{8,9},{9,8},{10,11... | collective-permute-start | bytes 294920 | tf_op jit(solution)/shard_map/ppermute | solution.py:419
  38.9 6.3 %collective-permute-start.12 = (f32[4,2,24,128]{3,2,1,0:T(8,128)S(1)}, f32[4,2,24,128]{3,2,1,0:T(8,128)S(1)}, u32[]{:S(2)}, u32[]{:S(2)}) collective-permute-start(f32[4,2,24,128]{3,2,1,0:T(8,128)S(1)} %get-tuple-element.147), channel_id=1, source_target_pairs={{0,16},{16,0},{32,48},{48,32},{64,80},{80,64},{96,112},{112,96},{1... | collective-permute-start | bytes 294920 | tf_op jit(solution)/shard_map/ppermute | solution.py:419
  39.0 8.2 %collective-permute-start.13 = (f32[24,2,4,128]{3,2,1,0:T(4,128)S(1)}, f32[24,2,4,128]{3,2,1,0:T(4,128)S(1)}, u32[]{:S(2)}, u32[]{:S(2)}) collective-permute-start(f32[24,2,4,128]{3,2,1,0:T(4,128)S(1)} %get-tuple-element.148), channel_id=1, source_target_pairs={{0,15},{1,2},{2,1},{3,4},{4,3},{5,6},{6,5},{7,8},{8,7},{9,10},{10,... | collective-permute-start | bytes 294920 | tf_op jit(solution)/shard_map/ppermute | solution.py:419
  40.9 6.7 %collective-permute-start.14 = (f32[4,2,24,128]{3,2,1,0:T(8,128)S(1)}, f32[4,2,24,128]{3,2,1,0:T(8,128)S(1)}, u32[]{:S(2)}, u32[]{:S(2)}) collective-permute-start(f32[4,2,24,128]{3,2,1,0:T(8,128)S(1)} %get-tuple-element.149), channel_id=1, source_target_pairs={{0,112},{16,32},{32,16},{48,64},{64,48},{80,96},{96,80},{112,0},{1... | collective-permute-start | bytes 294920 | tf_op jit(solution)/shard_map/ppermute | solution.py:419
  42.1 5.5 %collective-permute-start.15 = (f32[24,2,4,128]{3,2,1,0:T(4,128)S(1)}, f32[24,2,4,128]{3,2,1,0:T(4,128)S(1)}, u32[]{:S(2)}, u32[]{:S(2)}) collective-permute-start(f32[24,2,4,128]{3,2,1,0:T(4,128)S(1)} %get-tuple-element.150), channel_id=1, source_target_pairs={{0,1},{1,0},{2,3},{3,2},{4,5},{5,4},{6,7},{7,6},{8,9},{9,8},{10,11... | collective-permute-start | bytes 294920 | tf_op jit(solution)/shard_map/ppermute | solution.py:419
  48.0 7.5 %collective-permute-start.16 = (f32[4,2,24,128]{3,2,1,0:T(8,128)S(1)}, f32[4,2,24,128]{3,2,1,0:T(8,128)S(1)}, u32[]{:S(2)}, u32[]{:S(2)}) collective-permute-start(f32[4,2,24,128]{3,2,1,0:T(8,128)S(1)} %get-tuple-element.158), channel_id=1, source_target_pairs={{0,16},{16,0},{32,48},{48,32},{64,80},{80,64},{96,112},{112,96},{1... | collective-permute-start | bytes 294920 | tf_op jit(solution)/shard_map/ppermute | solution.py:419
  49.1 7.7 %collective-permute-start.17 = (f32[24,2,4,128]{3,2,1,0:T(4,128)S(1)}, f32[24,2,4,128]{3,2,1,0:T(4,128)S(1)}, u32[]{:S(2)}, u32[]{:S(2)}) collective-permute-start(f32[24,2,4,128]{3,2,1,0:T(4,128)S(1)} %get-tuple-element.159), channel_id=1, source_target_pairs={{0,15},{1,2},{2,1},{3,4},{4,3},{5,6},{6,5},{7,8},{8,7},{9,10},{10,... | collective-permute-start | bytes 294920 | tf_op jit(solution)/shard_map/ppermute | solution.py:419
  51.5 6.7 %collective-permute-start.18 = (f32[4,2,24,128]{3,2,1,0:T(8,128)S(1)}, f32[4,2,24,128]{3,2,1,0:T(8,128)S(1)}, u32[]{:S(2)}, u32[]{:S(2)}) collective-permute-start(f32[4,2,24,128]{3,2,1,0:T(8,128)S(1)} %get-tuple-element.160), channel_id=1, source_target_pairs={{0,112},{16,32},{32,16},{48,64},{64,48},{80,96},{96,80},{112,0},{1... | collective-permute-start | bytes 294920 | tf_op jit(solution)/shard_map/ppermute | solution.py:419
  52.4 5.8 %collective-permute-start.19 = (f32[24,2,4,128]{3,2,1,0:T(4,128)S(1)}, f32[24,2,4,128]{3,2,1,0:T(4,128)S(1)}, u32[]{:S(2)}, u32[]{:S(2)}) collective-permute-start(f32[24,2,4,128]{3,2,1,0:T(4,128)S(1)} %get-tuple-element.161), channel_id=1, source_target_pairs={{0,1},{1,0},{2,3},{3,2},{4,5},{5,4},{6,7},{7,6},{8,9},{9,8},{10,11... | collective-permute-start | bytes 294920 | tf_op jit(solution)/shard_map/ppermute | solution.py:419
  58.5 7.1 %collective-permute-start.20 = (f32[4,2,24,128]{3,2,1,0:T(8,128)S(1)}, f32[4,2,24,128]{3,2,1,0:T(8,128)S(1)}, u32[]{:S(2)}, u32[]{:S(2)}) collective-permute-start(f32[4,2,24,128]{3,2,1,0:T(8,128)S(1)} %get-tuple-element.169), channel_id=1, source_target_pairs={{0,16},{16,0},{32,48},{48,32},{64,80},{80,64},{96,112},{112,96},{1... | collective-permute-start | bytes 294920 | tf_op jit(solution)/shard_map/ppermute | solution.py:419
  58.8 8.1 %collective-permute-start.21 = (f32[24,2,4,128]{3,2,1,0:T(4,128)S(1)}, f32[24,2,4,128]{3,2,1,0:T(4,128)S(1)}, u32[]{:S(2)}, u32[]{:S(2)}) collective-permute-start(f32[24,2,4,128]{3,2,1,0:T(4,128)S(1)} %get-tuple-element.170), channel_id=1, source_target_pairs={{0,15},{1,2},{2,1},{3,4},{4,3},{5,6},{6,5},{7,8},{8,7},{9,10},{10,... | collective-permute-start | bytes 294920 | tf_op jit(solution)/shard_map/ppermute | solution.py:419
  60.9 6.7 %collective-permute-start.22 = (f32[4,2,24,128]{3,2,1,0:T(8,128)S(1)}, f32[4,2,24,128]{3,2,1,0:T(8,128)S(1)}, u32[]{:S(2)}, u32[]{:S(2)}) collective-permute-start(f32[4,2,24,128]{3,2,1,0:T(8,128)S(1)} %get-tuple-element.171), channel_id=1, source_target_pairs={{0,112},{16,32},{32,16},{48,64},{64,48},{80,96},{96,80},{112,0},{1... | collective-permute-start | bytes 294920 | tf_op jit(solution)/shard_map/ppermute | solution.py:419
  62.5 5.2 %collective-permute-start.23 = (f32[24,2,4,128]{3,2,1,0:T(4,128)S(1)}, f32[24,2,4,128]{3,2,1,0:T(4,128)S(1)}, u32[]{:S(2)}, u32[]{:S(2)}) collective-permute-start(f32[24,2,4,128]{3,2,1,0:T(4,128)S(1)} %get-tuple-element.172), channel_id=1, source_target_pairs={{0,1},{1,0},{2,3},{3,2},{4,5},{5,4},{6,7},{7,6},{8,9},{9,8},{10,11... | collective-permute-start | bytes 294920 | tf_op jit(solution)/shard_map/ppermute | solution.py:419
  68.0 7.3 %collective-permute-start.24 = (f32[4,2,24,128]{3,2,1,0:T(8,128)S(1)}, f32[4,2,24,128]{3,2,1,0:T(8,128)S(1)}, u32[]{:S(2)}, u32[]{:S(2)}) collective-permute-start(f32[4,2,24,128]{3,2,1,0:T(8,128)S(1)} %get-tuple-element.180), channel_id=1, source_target_pairs={{0,16},{16,0},{32,48},{48,32},{64,80},{80,64},{96,112},{112,96},{1... | collective-permute-start | bytes 294920 | tf_op jit(solution)/shard_map/ppermute | solution.py:419
  68.8 8.2 %collective-permute-start.25 = (f32[24,2,4,128]{3,2,1,0:T(4,128)S(1)}, f32[24,2,4,128]{3,2,1,0:T(4,128)S(1)}, u32[]{:S(2)}, u32[]{:S(2)}) collective-permute-start(f32[24,2,4,128]{3,2,1,0:T(4,128)S(1)} %get-tuple-element.181), channel_id=1, source_target_pairs={{0,15},{1,2},{2,1},{3,4},{4,3},{5,6},{6,5},{7,8},{8,7},{9,10},{10,... | collective-permute-start | bytes 294920 | tf_op jit(solution)/shard_map/ppermute | solution.py:419
  71.3 6.7 %collective-permute-start.26 = (f32[4,2,24,128]{3,2,1,0:T(8,128)S(1)}, f32[4,2,24,128]{3,2,1,0:T(8,128)S(1)}, u32[]{:S(2)}, u32[]{:S(2)}) collective-permute-start(f32[4,2,24,128]{3,2,1,0:T(8,128)S(1)} %get-tuple-element.182), channel_id=1, source_target_pairs={{0,112},{16,32},{32,16},{48,64},{64,48},{80,96},{96,80},{112,0},{1... | collective-permute-start | bytes 294920 | tf_op jit(solution)/shard_map/ppermute | solution.py:419
  72.1 5.9 %collective-permute-start.27 = (f32[24,2,4,128]{3,2,1,0:T(4,128)S(1)}, f32[24,2,4,128]{3,2,1,0:T(4,128)S(1)}, u32[]{:S(2)}, u32[]{:S(2)}) collective-permute-start(f32[24,2,4,128]{3,2,1,0:T(4,128)S(1)} %get-tuple-element.183), channel_id=1, source_target_pairs={{0,1},{1,0},{2,3},{3,2},{4,5},{5,4},{6,7},{7,6},{8,9},{9,8},{10,11... | collective-permute-start | bytes 294920 | tf_op jit(solution)/shard_map/ppermute | solution.py:419
  78.3 7.0 %collective-permute-start.28 = (f32[4,2,24,128]{3,2,1,0:T(8,128)S(1)}, f32[4,2,24,128]{3,2,1,0:T(8,128)S(1)}, u32[]{:S(2)}, u32[]{:S(2)}) collective-permute-start(f32[4,2,24,128]{3,2,1,0:T(8,128)S(1)} %get-tuple-element.191), channel_id=1, source_target_pairs={{0,16},{16,0},{32,48},{48,32},{64,80},{80,64},{96,112},{112,96},{1... | collective-permute-start | bytes 294920 | tf_op jit(solution)/shard_map/ppermute | solution.py:419
  78.4 8.1 %collective-permute-start.29 = (f32[24,2,4,128]{3,2,1,0:T(4,128)S(1)}, f32[24,2,4,128]{3,2,1,0:T(4,128)S(1)}, u32[]{:S(2)}, u32[]{:S(2)}) collective-permute-start(f32[24,2,4,128]{3,2,1,0:T(4,128)S(1)} %get-tuple-element.192), channel_id=1, source_target_pairs={{0,15},{1,2},{2,1},{3,4},{4,3},{5,6},{6,5},{7,8},{8,7},{9,10},{10,... | collective-permute-start | bytes 294920 | tf_op jit(solution)/shard_map/ppermute | solution.py:419
  81.1 6.7 %collective-permute-start.30 = (f32[4,2,24,128]{3,2,1,0:T(8,128)S(1)}, f32[4,2,24,128]{3,2,1,0:T(8,128)S(1)}, u32[]{:S(2)}, u32[]{:S(2)}) collective-permute-start(f32[4,2,24,128]{3,2,1,0:T(8,128)S(1)} %get-tuple-element.193), channel_id=1, source_target_pairs={{0,112},{16,32},{32,16},{48,64},{64,48},{80,96},{96,80},{112,0},{1... | collective-permute-start | bytes 294920 | tf_op jit(solution)/shard_map/ppermute | solution.py:419
  82.2 5.6 %collective-permute-start.31 = (f32[24,2,4,128]{3,2,1,0:T(4,128)S(1)}, f32[24,2,4,128]{3,2,1,0:T(4,128)S(1)}, u32[]{:S(2)}, u32[]{:S(2)}) collective-permute-start(f32[24,2,4,128]{3,2,1,0:T(4,128)S(1)} %get-tuple-element.194), channel_id=1, source_target_pairs={{0,1},{1,0},{2,3},{3,2},{4,5},{5,4},{6,7},{7,6},{8,9},{9,8},{10,11... | collective-permute-start | bytes 294920 | tf_op jit(solution)/shard_map/ppermute | solution.py:419
  88.9 1.2 %collective-permute-start.32 = (f32[16,128]{1,0:T(8,128)S(1)}, f32[16,128]{1,0:T(8,128)S(1)}, u32[]{:S(2)}, u32[]{:S(2)}) collective-permute-start(f32[16,128]{1,0:T(8,128)S(1)} %get-tuple-element.204), channel_id=1, source_target_pairs={{0,1},{1,0},{2,3},{3,2},{4,5},{5,4},{6,7},{7,6},{8,9},{9,8},{10,11... | collective-permute-start | bytes 24584 | tf_op jit(solution)/shard_map/ppermute | solution.py:433
  90.1 4.9 %collective-permute-start.35 = (f32[16,128]{1,0:T(8,128)S(1)}, f32[16,128]{1,0:T(8,128)S(1)}, u32[]{:S(2)}, u32[]{:S(2)}) collective-permute-start(f32[16,128]{1,0:T(8,128)S(1)} %add.21), channel_id=1, source_target_pairs={{0,18},{1,19},{2,16},{3,17},{4,22},{5,23},{6,20},{7,21},{8,26},{9,... | collective-permute-start | bytes 24584 | tf_op jit(solution)/shard_map/ppermute | solution.py:433
  90.1 5.2 %collective-permute-start.34 = (f32[16,128]{1,0:T(8,128)S(1)}, f32[16,128]{1,0:T(8,128)S(1)}, u32[]{:S(2)}, u32[]{:S(2)}) collective-permute-start(f32[16,128]{1,0:T(8,128)S(1)} %add.21), channel_id=1, source_target_pairs={{0,2},{1,3},{2,0},{3,1},{4,6},{5,7},{6,4},{7,5},{8,10},{9,11},{10,... | collective-permute-start | bytes 24584 | tf_op jit(solution)/shard_map/ppermute | solution.py:433
  92.4 3.7 %collective-permute-start.33 = (f32[16,128]{1,0:T(8,128)S(1)}, f32[16,128]{1,0:T(8,128)S(1)}, u32[]{:S(2)}, u32[]{:S(2)}) collective-permute-start(f32[16,128]{1,0:T(8,128)S(1)} %add.21), channel_id=1, source_target_pairs={{0,16},{1,17},{2,18},{3,19},{4,20},{5,21},{6,22},{7,23},{8,24},{9,... | collective-permute-start | bytes 24584 | tf_op jit(solution)/shard_map/ppermute | solution.py:433
  96.0 4.9 %collective-permute-start.38 = (f32[16,128]{1,0:T(8,128)S(1)}, f32[16,128]{1,0:T(8,128)S(1)}, u32[]{:S(2)}, u32[]{:S(2)}) collective-permute-start(f32[16,128]{1,0:T(8,128)S(1)} %add_add_fusion.1), channel_id=1, source_target_pairs={{0,12},{1,13},{2,14},{3,15},{4,8},{5,9},{6,10},{7,11},{8,4},{9,5},... | collective-permute-start | bytes 24584 | tf_op jit(solution)/shard_map/ppermute | solution.py:433
  97.3 5.2 %collective-permute-start.37 = (f32[16,128]{1,0:T(8,128)S(1)}, f32[16,128]{1,0:T(8,128)S(1)}, u32[]{:S(2)}, u32[]{:S(2)}) collective-permute-start(f32[16,128]{1,0:T(8,128)S(1)} %add_add_fusion.1), channel_id=1, source_target_pairs={{0,8},{1,9},{2,10},{3,11},{4,12},{5,13},{6,14},{7,15},{8,0},{9,1},... | collective-permute-start | bytes 24584 | tf_op jit(solution)/shard_map/ppermute | solution.py:433
  97.3 5.2 %collective-permute-start.36 = (f32[16,128]{1,0:T(8,128)S(1)}, f32[16,128]{1,0:T(8,128)S(1)}, u32[]{:S(2)}, u32[]{:S(2)}) collective-permute-start(f32[16,128]{1,0:T(8,128)S(1)} %add_add_fusion.1), channel_id=1, source_target_pairs={{0,4},{1,5},{2,6},{3,7},{4,0},{5,1},{6,2},{7,3},{8,12},{9,13},{10,... | collective-permute-start | bytes 24584 | tf_op jit(solution)/shard_map/ppermute | solution.py:433
  102.5 5.6 %collective-permute-start.39 = (f32[16,128]{1,0:T(8,128)S(1)}, f32[16,128]{1,0:T(8,128)S(1)}, u32[]{:S(2)}, u32[]{:S(2)}) collective-permute-start(f32[16,128]{1,0:T(8,128)S(1)} %add_add_fusion.refs_0_), channel_id=1, source_target_pairs={{0,32},{1,33},{2,34},{3,35},{4,36},{5,37},{6,38},{7,39},{8,40},{9,... | collective-permute-start | bytes 24584 | tf_op jit(solution)/shard_map/ppermute | solution.py:433
  103.5 5.2 %collective-permute-start.40 = (f32[16,128]{1,0:T(8,128)S(1)}, f32[16,128]{1,0:T(8,128)S(1)}, u32[]{:S(2)}, u32[]{:S(2)}) collective-permute-start(f32[16,128]{1,0:T(8,128)S(1)} %add_add_fusion.refs_0_), channel_id=1, source_target_pairs={{0,64},{1,65},{2,66},{3,67},{4,68},{5,69},{6,70},{7,71},{8,72},{9,... | collective-permute-start | bytes 24584 | tf_op jit(solution)/shard_map/ppermute | solution.py:433
  105.8 4.9 %collective-permute-start.41 = (f32[16,128]{1,0:T(8,128)S(1)}, f32[16,128]{1,0:T(8,128)S(1)}, u32[]{:S(2)}, u32[]{:S(2)}) collective-permute-start(f32[16,128]{1,0:T(8,128)S(1)} %add_add_fusion.refs_0_), channel_id=1, source_target_pairs={{0,96},{1,97},{2,98},{3,99},{4,100},{5,101},{6,102},{7,103},{8,104... | collective-permute-start | bytes 24584 | tf_op jit(solution)/shard_map/ppermute | solution.py:433

commit v6 on v5

--- a/solution.py
+++ b/solution.py
@@ -39,8 +39,8 @@
 KEEP_X = (CX, CY, LANES)
 KEEP_Y = (CY, LANES)
 NORM = (1, LANES)
-RECEIVERS = 8
-TABLE = RECEIVERS + NREC
+RECEIVERS = 12
+TABLE = RECEIVERS + NREC + 1
 COMMON = 5040.0
 CHUNKS = 4
 INSIDE = slice(LO, LO + CY)
@@ -199,14 +199,10 @@
     def note(at, n, px, py, pz):
         def add(r, count):
             lx, ly, here = owned(px[r], py[r])
-
-            @pl.when(here)
-            def _():
-                table[at + count] = (((lx << 5) + ly) << 14) + (pz[r] << 6) + r
-
+            table[at + count] = (((lx << 5) + ly) << 14) + (pz[r] << 6) + r
             return count + here.astype(jnp.int32)
 
-        return lax.fori_loop(0, n, add, 0)
+        return lax.fori_loop(0, n, add, 0, unroll=4)
 
     table[0] = note(RECEIVERS, NREC, rx, ry, rz)
     table[1] = note(4, NSRC, sx, sy, sz)
@@ -415,8 +411,18 @@
 
 
 def swap(strip, axis, far):
-    size = lax.axis_size(axis)
-    return lax.ppermute(strip, axis, [(i, (((i + far) ^ 1) - far) % size) for i in range(size)])
+    rows, columns = (lax.axis_size(GX), lax.axis_size(GY))
+    pairs = []
+    for gx in range(rows):
+        for gy in range(columns):
+            to_x = ((gx + far) ^ 1) - far if axis == GX else gx
+            to_y = ((gy + far) ^ 1) - far if axis == GY else gy
+            if not 0 <= to_x < rows:
+                to_x, to_y = (gx, gy ^ 1)
+            if not 0 <= to_y < columns:
+                to_x, to_y = (gx ^ 1, gy)
+            pairs.append((gx * columns + gy, to_x * columns + to_y))
+    return lax.ppermute(strip, BOTH, pairs)
 
 
 def exchange(strips):

time: 111 us -> 105 us (0.946)
  waiting for transfers between devices: 26.7 us -> 12.3 us
  starting transfers between devices: 49.9 us -> 59.4 us
  Pallas kernels: 33.9 us -> 32.5 us
    ppermute x32, waiting for transfers between devices: 18.8 us -> 2.05 us  [swap(): return lax.ppermute(strip, BOTH, pairs)]
    ppermute x32, starting transfers between devices: 36.9 us -> 44.5 us  [swap(): return lax.ppermute(strip, BOTH, pairs)]
    ppermute x10, waiting for transfers between devices: 7.89 us -> 10.2 us  [spread(): return lax.ppermute(value, BOTH, pairs)]
    ppermute x10, starting transfers between devices: 13 us -> 14.9 us  [spread(): return lax.ppermute(value, BOTH, pairs)]
  transfers between devices with their start and end apart: 42 -> 42, of which waited for: 22 -> 12; matrix products, arithmetic and copies ran while one was open for 0% -> 0% of each run, Pallas kernels for 26% -> 26%
where the time goes in v6:
time: 105 us
  starting transfers between devices  59.4 us (57%)
  Pallas kernels  32.5 us (31%)
  waiting for transfers between devices  12.3 us (12%)
    ppermute x32, starting transfers between devices, swap(): return lax.ppermute(strip, BOTH, pairs)  44.5 us
    pallas_call x8, Pallas kernels, per_device(): pl.pallas_call(functools.partial(inner_kernel, step), out_shape=shape(FIE...  24.1 us
    ppermute x10, starting transfers between devices, spread(): return lax.ppermute(value, BOTH, pairs)  14.9 us
    ppermute x10, waiting for transfers between devices, spread(): return lax.ppermute(value, BOTH, pairs)  10.2 us
    pallas_call x7, Pallas kernels, per_device(): pl.pallas_call(functools.partial(join_kernel, False), out_shape=shape(FIE...  2.15 us
    pallas_call x1, Pallas kernels, per_device(): pl.pallas_call(begin_kernel, out_shape=shape(FIELD, BLOCK, MEM_X, MEM_Y,...  2.12 us
  transfers between devices with their start and end apart: 42, of which 12 were waited for; matrix products, arithmetic and copies ran while one was open for 0% of the time, Pallas kernels for 26%

profile of v6, /device:TPU:0, one launch (start us, length us, event | category | flops | bytes accessed | tf_op | source)
XLA Modules:
  0.0 105.0 jit_solution(3123142105528793636)
XLA Ops:
  0.6 1.7 %shard_map.139 = (f32[32,2,40,128]{3,2,1,0:T(8,128)S(1)}, f32[4,2,24,128]{3,2,1,0:T(8,128)S(1)}, f32[24,2,4,128]{3,2,1,0:T(4,128)S(1)}, f32[4,2,24,128]{3,2,1,0:...) custom-call(f32[24,24,256]{2,1,0:T(8,128)} %pressure.1, ...), custom_call_target="tpu_custom_call" | custom-call | tf_op jit(solution)/shard_map/pallas_call | solution.py:471
  2.3 1.7 %collective-permute-start = (f32[4,2,24,128]{3,2,1,0:T(8,128)S(1)}, f32[4,2,24,128]{3,2,1,0:T(8,128)S(1)}, u32[]{:S(2)}, u32[]{:S(2)}) collective-permute-start(f32[4,2,24,128]{3,2,1,0:T(8,128)S(1)} %get-tuple-element.112), channel_id=1, source_target_pairs={{0,16},{1,17},{2,18},{3,19},{4,20},{5,21},{6,22},{7,23},{8,24},{9,... | collective-permute-start | bytes 294920 | tf_op jit(solution)/shard_map/ppermute | solution.py:425
  4.0 0.5 collective-permute-start.1
  4.4 2.4 %collective-permute-start.2 = (f32[4,2,24,128]{3,2,1,0:T(8,128)S(1)}, f32[4,2,24,128]{3,2,1,0:T(8,128)S(1)}, u32[]{:S(2)}, u32[]{:S(2)}) collective-permute-start(f32[4,2,24,128]{3,2,1,0:T(8,128)S(1)} %get-tuple-element.114), channel_id=1, source_target_pairs={{0,1},{1,0},{2,3},{3,2},{4,5},{5,4},{6,7},{7,6},{8,9},{9,8},{10,11... | collective-permute-start | bytes 294920 | tf_op jit(solution)/shard_map/ppermute | solution.py:425
  6.8 2.1 %shard_map.140 = (f32[32,2,40,128]{3,2,1,0:T(8,128)S(1)}, f32[24,2,24,128]{3,2,1,0:T(8,128)S(1)}, f32[2,32,2,24,128]{4,3,2,1,0:T(8,128)S(1)}, f32[24,2,40,128]{3...) custom-call(s32[4]{0:T(128)} %widths_far.1, ...), custom_call_target="tpu_custom_call" | custom-call | tf_op jit(solution)/shard_map/pallas_call | solution.py:479
  8.9 2.9 %shard_map.141 = (f32[32,2,40,128]{3,2,1,0:T(8,128)S(1)}, f32[2,32,2,24,128]{4,3,2,1,0:T(8,128)S(1)}, f32[24,2,40,128]{3,2,1,0:T(8,128)S(1)}, f32[24,2,24,128]{3...) custom-call(s32[77]{0:T(128)S(1)} %get-tuple-element.107.table.refs_, ...), custom_call_target="tpu_custom_call", output_to_operand_aliasing={{0}: (8, {}), {1}: (9, {}), {2}: (10, {}), {3}: (11, {}), {... | custom-call | tf_op jit(solution)/shard_map/pallas_call | solution.py:497
  11.9 0.3 shard_map.142
  12.2 2.2 %collective-permute-start.4 = (f32[4,2,24,128]{3,2,1,0:T(8,128)S(1)}, f32[4,2,24,128]{3,2,1,0:T(8,128)S(1)}, u32[]{:S(2)}, u32[]{:S(2)}) collective-permute-start(f32[4,2,24,128]{3,2,1,0:T(8,128)S(1)} %get-tuple-element.125), channel_id=1, source_target_pairs={{0,16},{1,17},{2,18},{3,19},{4,20},{5,21},{6,22},{7,23},{8,24},{9,... | collective-permute-start | bytes 294920 | tf_op jit(solution)/shard_map/ppermute | solution.py:425
  14.5 2.0 %collective-permute-start.6 = (f32[4,2,24,128]{3,2,1,0:T(8,128)S(1)}, f32[4,2,24,128]{3,2,1,0:T(8,128)S(1)}, u32[]{:S(2)}, u32[]{:S(2)}) collective-permute-start(f32[4,2,24,128]{3,2,1,0:T(8,128)S(1)} %get-tuple-element.127), channel_id=1, source_target_pairs={{0,1},{1,0},{2,3},{3,2},{4,5},{5,4},{6,7},{7,6},{8,9},{9,8},{10,11... | collective-permute-start | bytes 294920 | tf_op jit(solution)/shard_map/ppermute | solution.py:425
  16.4 3.0 %shard_map.143 = (f32[32,2,40,128]{3,2,1,0:T(8,128)S(1)}, f32[2,32,2,24,128]{4,3,2,1,0:T(8,128)S(1)}, f32[24,2,40,128]{3,2,1,0:T(8,128)S(1)}, f32[24,2,24,128]{3...) custom-call(s32[77]{0:T(128)S(1)} %get-tuple-element.107.table.refs_, ...), custom_call_target="tpu_custom_call", output_to_operand_aliasing={{0}: (8, {}), {1}: (9, {}), {2}: (10, {}), {3}: (11, {}), {... | custom-call | tf_op jit(solution)/shard_map/pallas_call | solution.py:497
  19.8 4.5 %collective-permute-start.8 = (f32[4,2,24,128]{3,2,1,0:T(8,128)S(1)}, f32[4,2,24,128]{3,2,1,0:T(8,128)S(1)}, u32[]{:S(2)}, u32[]{:S(2)}) collective-permute-start(f32[4,2,24,128]{3,2,1,0:T(8,128)S(1)} %get-tuple-element.136), channel_id=1, source_target_pairs={{0,16},{1,17},{2,18},{3,19},{4,20},{5,21},{6,22},{7,23},{8,24},{9,... | collective-permute-start | bytes 294920 | tf_op jit(solution)/shard_map/ppermute | solution.py:425
  24.4 2.5 %collective-permute-start.10 = (f32[4,2,24,128]{3,2,1,0:T(8,128)S(1)}, f32[4,2,24,128]{3,2,1,0:T(8,128)S(1)}, u32[]{:S(2)}, u32[]{:S(2)}) collective-permute-start(f32[4,2,24,128]{3,2,1,0:T(8,128)S(1)} %get-tuple-element.138), channel_id=1, source_target_pairs={{0,1},{1,0},{2,3},{3,2},{4,5},{5,4},{6,7},{7,6},{8,9},{9,8},{10,11... | collective-permute-start | bytes 294920 | tf_op jit(solution)/shard_map/ppermute | solution.py:425
  26.8 3.0 %shard_map.145 = (f32[32,2,40,128]{3,2,1,0:T(8,128)S(1)}, f32[2,32,2,24,128]{4,3,2,1,0:T(8,128)S(1)}, f32[24,2,40,128]{3,2,1,0:T(8,128)S(1)}, f32[24,2,24,128]{3...) custom-call(s32[77]{0:T(128)S(1)} %get-tuple-element.107.table.refs_, ...), custom_call_target="tpu_custom_call", output_to_operand_aliasing={{0}: (8, {}), {1}: (9, {}), {2}: (10, {}), {3}: (11, {}), {... | custom-call | tf_op jit(solution)/shard_map/pallas_call | solution.py:497
  29.9 0.3 shard_map.146
  30.2 3.7 %collective-permute-start.12 = (f32[4,2,24,128]{3,2,1,0:T(8,128)S(1)}, f32[4,2,24,128]{3,2,1,0:T(8,128)S(1)}, u32[]{:S(2)}, u32[]{:S(2)}) collective-permute-start(f32[4,2,24,128]{3,2,1,0:T(8,128)S(1)} %get-tuple-element.147), channel_id=1, source_target_pairs={{0,16},{1,17},{2,18},{3,19},{4,20},{5,21},{6,22},{7,23},{8,24},{9,... | collective-permute-start | bytes 294920 | tf_op jit(solution)/shard_map/ppermute | solution.py:425
  34.0 2.0 %collective-permute-start.14 = (f32[4,2,24,128]{3,2,1,0:T(8,128)S(1)}, f32[4,2,24,128]{3,2,1,0:T(8,128)S(1)}, u32[]{:S(2)}, u32[]{:S(2)}) collective-permute-start(f32[4,2,24,128]{3,2,1,0:T(8,128)S(1)} %get-tuple-element.149), channel_id=1, source_target_pairs={{0,1},{1,0},{2,3},{3,2},{4,5},{5,4},{6,7},{7,6},{8,9},{9,8},{10,11... | collective-permute-start | bytes 294920 | tf_op jit(solution)/shard_map/ppermute | solution.py:425
  36.0 3.0 %shard_map.147 = (f32[32,2,40,128]{3,2,1,0:T(8,128)S(1)}, f32[2,32,2,24,128]{4,3,2,1,0:T(8,128)S(1)}, f32[24,2,40,128]{3,2,1,0:T(8,128)S(1)}, f32[24,2,24,128]{3...) custom-call(s32[77]{0:T(128)S(1)} %get-tuple-element.107.table.refs_, ...), custom_call_target="tpu_custom_call", output_to_operand_aliasing={{0}: (8, {}), {1}: (9, {}), {2}: (10, {}), {3}: (11, {}), {... | custom-call | tf_op jit(solution)/shard_map/pallas_call | solution.py:497
  39.0 0.6 collective-permute-done.13.refs_2_
  39.9 3.1 %collective-permute-start.16 = (f32[4,2,24,128]{3,2,1,0:T(8,128)S(1)}, f32[4,2,24,128]{3,2,1,0:T(8,128)S(1)}, u32[]{:S(2)}, u32[]{:S(2)}) collective-permute-start(f32[4,2,24,128]{3,2,1,0:T(8,128)S(1)} %get-tuple-element.158), channel_id=1, source_target_pairs={{0,16},{1,17},{2,18},{3,19},{4,20},{5,21},{6,22},{7,23},{8,24},{9,... | collective-permute-start | bytes 294920 | tf_op jit(solution)/shard_map/ppermute | solution.py:425
  43.1 2.4 %collective-permute-start.18 = (f32[4,2,24,128]{3,2,1,0:T(8,128)S(1)}, f32[4,2,24,128]{3,2,1,0:T(8,128)S(1)}, u32[]{:S(2)}, u32[]{:S(2)}) collective-permute-start(f32[4,2,24,128]{3,2,1,0:T(8,128)S(1)} %get-tuple-element.160), channel_id=1, source_target_pairs={{0,1},{1,0},{2,3},{3,2},{4,5},{5,4},{6,7},{7,6},{8,9},{9,8},{10,11... | collective-permute-start | bytes 294920 | tf_op jit(solution)/shard_map/ppermute | solution.py:425
  45.5 3.0 %shard_map.149 = (f32[32,2,40,128]{3,2,1,0:T(8,128)S(1)}, f32[2,32,2,24,128]{4,3,2,1,0:T(8,128)S(1)}, f32[24,2,40,128]{3,2,1,0:T(8,128)S(1)}, f32[24,2,24,128]{3...) custom-call(s32[77]{0:T(128)S(1)} %get-tuple-element.107.table.refs_, ...), custom_call_target="tpu_custom_call", output_to_operand_aliasing={{0}: (8, {}), {1}: (9, {}), {2}: (10, {}), {3}: (11, {}), {... | custom-call | tf_op jit(solution)/shard_map/pallas_call | solution.py:497
  48.9 3.6 %collective-permute-start.20 = (f32[4,2,24,128]{3,2,1,0:T(8,128)S(1)}, f32[4,2,24,128]{3,2,1,0:T(8,128)S(1)}, u32[]{:S(2)}, u32[]{:S(2)}) collective-permute-start(f32[4,2,24,128]{3,2,1,0:T(8,128)S(1)} %get-tuple-element.169), channel_id=1, source_target_pairs={{0,16},{1,17},{2,18},{3,19},{4,20},{5,21},{6,22},{7,23},{8,24},{9,... | collective-permute-start | bytes 294920 | tf_op jit(solution)/shard_map/ppermute | solution.py:425
  52.7 1.6 %collective-permute-start.22 = (f32[4,2,24,128]{3,2,1,0:T(8,128)S(1)}, f32[4,2,24,128]{3,2,1,0:T(8,128)S(1)}, u32[]{:S(2)}, u32[]{:S(2)}) collective-permute-start(f32[4,2,24,128]{3,2,1,0:T(8,128)S(1)} %get-tuple-element.171), channel_id=1, source_target_pairs={{0,1},{1,0},{2,3},{3,2},{4,5},{5,4},{6,7},{7,6},{8,9},{9,8},{10,11... | collective-permute-start | bytes 294920 | tf_op jit(solution)/shard_map/ppermute | solution.py:425
  54.3 3.0 %shard_map.151 = (f32[32,2,40,128]{3,2,1,0:T(8,128)S(1)}, f32[2,32,2,24,128]{4,3,2,1,0:T(8,128)S(1)}, f32[24,2,40,128]{3,2,1,0:T(8,128)S(1)}, f32[24,2,24,128]{3...) custom-call(s32[77]{0:T(128)S(1)} %get-tuple-element.107.table.refs_, ...), custom_call_target="tpu_custom_call", output_to_operand_aliasing={{0}: (8, {}), {1}: (9, {}), {2}: (10, {}), {3}: (11, {}), {... | custom-call | tf_op jit(solution)/shard_map/pallas_call | solution.py:497
  57.7 4.1 %collective-permute-start.24 = (f32[4,2,24,128]{3,2,1,0:T(8,128)S(1)}, f32[4,2,24,128]{3,2,1,0:T(8,128)S(1)}, u32[]{:S(2)}, u32[]{:S(2)}) collective-permute-start(f32[4,2,24,128]{3,2,1,0:T(8,128)S(1)} %get-tuple-element.180), channel_id=1, source_target_pairs={{0,16},{1,17},{2,18},{3,19},{4,20},{5,21},{6,22},{7,23},{8,24},{9,... | collective-permute-start | bytes 294920 | tf_op jit(solution)/shard_map/ppermute | solution.py:425
  61.9 1.9 %collective-permute-start.26 = (f32[4,2,24,128]{3,2,1,0:T(8,128)S(1)}, f32[4,2,24,128]{3,2,1,0:T(8,128)S(1)}, u32[]{:S(2)}, u32[]{:S(2)}) collective-permute-start(f32[4,2,24,128]{3,2,1,0:T(8,128)S(1)} %get-tuple-element.182), channel_id=1, source_target_pairs={{0,1},{1,0},{2,3},{3,2},{4,5},{5,4},{6,7},{7,6},{8,9},{9,8},{10,11... | collective-permute-start | bytes 294920 | tf_op jit(solution)/shard_map/ppermute | solution.py:425
  63.8 3.0 %shard_map.153 = (f32[32,2,40,128]{3,2,1,0:T(8,128)S(1)}, f32[2,32,2,24,128]{4,3,2,1,0:T(8,128)S(1)}, f32[24,2,40,128]{3,2,1,0:T(8,128)S(1)}, f32[24,2,24,128]{3...) custom-call(s32[77]{0:T(128)S(1)} %get-tuple-element.107.table.refs_, ...), custom_call_target="tpu_custom_call", output_to_operand_aliasing={{0}: (8, {}), {1}: (9, {}), {2}: (10, {}), {3}: (11, {}), {... | custom-call | tf_op jit(solution)/shard_map/pallas_call | solution.py:497
  66.9 0.3 collective-permute-done.25.refs_2_
  67.5 4.1 %collective-permute-start.28 = (f32[4,2,24,128]{3,2,1,0:T(8,128)S(1)}, f32[4,2,24,128]{3,2,1,0:T(8,128)S(1)}, u32[]{:S(2)}, u32[]{:S(2)}) collective-permute-start(f32[4,2,24,128]{3,2,1,0:T(8,128)S(1)} %get-tuple-element.191), channel_id=1, source_target_pairs={{0,16},{1,17},{2,18},{3,19},{4,20},{5,21},{6,22},{7,23},{8,24},{9,... | collective-permute-start | bytes 294920 | tf_op jit(solution)/shard_map/ppermute | solution.py:425
  71.8 1.6 %collective-permute-start.30 = (f32[4,2,24,128]{3,2,1,0:T(8,128)S(1)}, f32[4,2,24,128]{3,2,1,0:T(8,128)S(1)}, u32[]{:S(2)}, u32[]{:S(2)}) collective-permute-start(f32[4,2,24,128]{3,2,1,0:T(8,128)S(1)} %get-tuple-element.193), channel_id=1, source_target_pairs={{0,1},{1,0},{2,3},{3,2},{4,5},{5,4},{6,7},{7,6},{8,9},{9,8},{10,11... | collective-permute-start | bytes 294920 | tf_op jit(solution)/shard_map/ppermute | solution.py:425
  73.3 3.0 %shard_map.155 = (f32[32,2,40,128]{3,2,1,0:T(8,128)S(1)}, f32[2,32,2,24,128]{4,3,2,1,0:T(8,128)S(1)}, f32[24,2,40,128]{3,2,1,0:T(8,128)S(1)}, f32[24,2,24,128]{3...) custom-call(s32[77]{0:T(128)S(1)} %get-tuple-element.107.table.refs_, ...), custom_call_target="tpu_custom_call", output_to_operand_aliasing={{0}: (8, {}), {1}: (9, {}), {2}: (10, {}), {3}: (11, {}), {... | custom-call | tf_op jit(solution)/shard_map/pallas_call | solution.py:497
  76.4 1.0 collective-permute-done.29.refs_6_
  77.4 1.0 shard_map.156
  78.6 0.9 collective-permute-done.32
  79.6 3.7 %collective-permute-start.35 = (f32[16,128]{1,0:T(8,128)S(1)}, f32[16,128]{1,0:T(8,128)S(1)}, u32[]{:S(2)}, u32[]{:S(2)}) collective-permute-start(f32[16,128]{1,0:T(8,128)S(1)} %add.21), channel_id=1, source_target_pairs={{0,18},{1,19},{2,16},{3,17},{4,22},{5,23},{6,20},{7,21},{8,26},{9,... | collective-permute-start | bytes 24584 | tf_op jit(solution)/shard_map/ppermute | solution.py:439
  83.2 1.7 %collective-permute-start.34 = (f32[16,128]{1,0:T(8,128)S(1)}, f32[16,128]{1,0:T(8,128)S(1)}, u32[]{:S(2)}, u32[]{:S(2)}) collective-permute-start(f32[16,128]{1,0:T(8,128)S(1)} %add.21), channel_id=1, source_target_pairs={{0,2},{1,3},{2,0},{3,1},{4,6},{5,7},{6,4},{7,5},{8,10},{9,11},{10,... | collective-permute-start | bytes 24584 | tf_op jit(solution)/shard_map/ppermute | solution.py:439
  84.9 3.5 %collective-permute-done.34 = f32[16,128]{1,0:T(8,128)S(1)} collective-permute-done((f32[16,128]{1,0:T(8,128)S(1)}, f32[16,128]{1,0:T(8,128)S(1)}, u32[]{:S(2)}, u32[]{:S(2)}) %collective-permute-start.34) | collective-permute-done | bytes 8224 | tf_op jit(solution)/shard_map/ppermute | solution.py:439
  88.6 2.5 %collective-permute-start.38 = (f32[16,128]{1,0:T(8,128)S(1)}, f32[16,128]{1,0:T(8,128)S(1)}, u32[]{:S(2)}, u32[]{:S(2)}) collective-permute-start(f32[16,128]{1,0:T(8,128)S(1)} %add_add_fusion.1), channel_id=1, source_target_pairs={{0,12},{1,13},{2,14},{3,15},{4,8},{5,9},{6,10},{7,11},{8,4},{9,5},... | collective-permute-start | bytes 24584 | tf_op jit(solution)/shard_map/ppermute | solution.py:439
  91.0 2.2 %collective-permute-start.37 = (f32[16,128]{1,0:T(8,128)S(1)}, f32[16,128]{1,0:T(8,128)S(1)}, u32[]{:S(2)}, u32[]{:S(2)}) collective-permute-start(f32[16,128]{1,0:T(8,128)S(1)} %add_add_fusion.1), channel_id=1, source_target_pairs={{0,8},{1,9},{2,10},{3,11},{4,12},{5,13},{6,14},{7,15},{8,0},{9,1},... | collective-permute-start | bytes 24584 | tf_op jit(solution)/shard_map/ppermute | solution.py:439
  93.4 2.8 %collective-permute-done.37 = f32[16,128]{1,0:T(8,128)S(1)} collective-permute-done((f32[16,128]{1,0:T(8,128)S(1)}, f32[16,128]{1,0:T(8,128)S(1)}, u32[]{:S(2)}, u32[]{:S(2)}) %collective-permute-start.37) | collective-permute-done | bytes 8224 | tf_op jit(solution)/shard_map/ppermute | solution.py:439
  96.2 0.7 collective-permute-done.36
  96.8 1.2 %collective-permute-start.39 = (f32[16,128]{1,0:T(8,128)S(1)}, f32[16,128]{1,0:T(8,128)S(1)}, u32[]{:S(2)}, u32[]{:S(2)}) collective-permute-start(f32[16,128]{1,0:T(8,128)S(1)} %add_add_fusion.refs_0_), channel_id=1, source_target_pairs={{0,32},{1,33},{2,34},{3,35},{4,36},{5,37},{6,38},{7,39},{8,40},{9,... | collective-permute-start | bytes 24584 | tf_op jit(solution)/shard_map/ppermute | solution.py:439
  98.1 1.5 %collective-permute-start.40 = (f32[16,128]{1,0:T(8,128)S(1)}, f32[16,128]{1,0:T(8,128)S(1)}, u32[]{:S(2)}, u32[]{:S(2)}) collective-permute-start(f32[16,128]{1,0:T(8,128)S(1)} %add_add_fusion.refs_0_), channel_id=1, source_target_pairs={{0,64},{1,65},{2,66},{3,67},{4,68},{5,69},{6,70},{7,71},{8,72},{9,... | collective-permute-start | bytes 24584 | tf_op jit(solution)/shard_map/ppermute | solution.py:439
  99.5 2.0 %collective-permute-start.41 = (f32[16,128]{1,0:T(8,128)S(1)}, f32[16,128]{1,0:T(8,128)S(1)}, u32[]{:S(2)}, u32[]{:S(2)}) collective-permute-start(f32[16,128]{1,0:T(8,128)S(1)} %add_add_fusion.refs_0_), channel_id=1, source_target_pairs={{0,96},{1,97},{2,98},{3,99},{4,100},{5,101},{6,102},{7,103},{8,104... | collective-permute-start | bytes 24584 | tf_op jit(solution)/shard_map/ppermute | solution.py:439
  101.5 0.9 shard_map.157
  102.4 0.8 collective-permute-done.40.refs_2_
  103.2 1.2 %collective-permute-done.41.refs_3_ = f32[16,128]{1,0:T(8,128)S(1)} collective-permute-done((f32[16,128]{1,0:T(8,128)S(1)}, f32[16,128]{1,0:T(8,128)S(1)}, u32[]{:S(2)}, u32[]{:S(2)}) %collective-permute-start.41) | collective-permute-done | bytes 8224 | tf_op jit(solution)/shard_map/ppermute | solution.py:439
  104.4 0.6 shard_map.158
  (61 shorter events, 3.0 us)
Async XLA Ops:
  0.6 8.3 %copy-start = (bf16[512,256]{1,0:T(8,128)(2,1)S(1)}, bf16[512,256]{1,0:T(8,128)(2,1)}, u32[]{:S(2)}) copy-start(bf16[512,256]{1,0:T(8,128)(2,1)} %constant.2.clone.band) | copy-start | bytes 786436
  2.3 9.5 %collective-permute-start = (f32[4,2,24,128]{3,2,1,0:T(8,128)S(1)}, f32[4,2,24,128]{3,2,1,0:T(8,128)S(1)}, u32[]{:S(2)}, u32[]{:S(2)}) collective-permute-start(f32[4,2,24,128]{3,2,1,0:T(8,128)S(1)} %get-tuple-element.112), channel_id=1, source_target_pairs={{0,16},{1,17},{2,18},{3,19},{4,20},{5,21},{6,22},{7,23},{8,24},{9,... | collective-permute-start | bytes 294920 | tf_op jit(solution)/shard_map/ppermute | solution.py:425
  4.0 7.9 %collective-permute-start.1 = (f32[24,2,4,128]{3,2,1,0:T(4,128)S(1)}, f32[24,2,4,128]{3,2,1,0:T(4,128)S(1)}, u32[]{:S(2)}, u32[]{:S(2)}) collective-permute-start(f32[24,2,4,128]{3,2,1,0:T(4,128)S(1)} %get-tuple-element.113), channel_id=1, source_target_pairs={{0,16},{1,2},{2,1},{3,4},{4,3},{5,6},{6,5},{7,8},{8,7},{9,10},{10,... | collective-permute-start | bytes 294920 | tf_op jit(solution)/shard_map/ppermute | solution.py:425
  4.4 7.5 %collective-permute-start.2 = (f32[4,2,24,128]{3,2,1,0:T(8,128)S(1)}, f32[4,2,24,128]{3,2,1,0:T(8,128)S(1)}, u32[]{:S(2)}, u32[]{:S(2)}) collective-permute-start(f32[4,2,24,128]{3,2,1,0:T(8,128)S(1)} %get-tuple-element.114), channel_id=1, source_target_pairs={{0,1},{1,0},{2,3},{3,2},{4,5},{5,4},{6,7},{7,6},{8,9},{9,8},{10,11... | collective-permute-start | bytes 294920 | tf_op jit(solution)/shard_map/ppermute | solution.py:425
  6.8 5.1 %collective-permute-start.3 = (f32[24,2,4,128]{3,2,1,0:T(4,128)S(1)}, f32[24,2,4,128]{3,2,1,0:T(4,128)S(1)}, u32[]{:S(2)}, u32[]{:S(2)}) collective-permute-start(f32[24,2,4,128]{3,2,1,0:T(4,128)S(1)} %get-tuple-element.115), channel_id=1, source_target_pairs={{0,1},{1,0},{2,3},{3,2},{4,5},{5,4},{6,7},{7,6},{8,9},{9,8},{10,11... | collective-permute-start | bytes 294920 | tf_op jit(solution)/shard_map/ppermute | solution.py:425
  12.2 7.3 %collective-permute-start.4 = (f32[4,2,24,128]{3,2,1,0:T(8,128)S(1)}, f32[4,2,24,128]{3,2,1,0:T(8,128)S(1)}, u32[]{:S(2)}, u32[]{:S(2)}) collective-permute-start(f32[4,2,24,128]{3,2,1,0:T(8,128)S(1)} %get-tuple-element.125), channel_id=1, source_target_pairs={{0,16},{1,17},{2,18},{3,19},{4,20},{5,21},{6,22},{7,23},{8,24},{9,... | collective-permute-start | bytes 294920 | tf_op jit(solution)/shard_map/ppermute | solution.py:425
  14.4 5.1 %collective-permute-start.5 = (f32[24,2,4,128]{3,2,1,0:T(4,128)S(1)}, f32[24,2,4,128]{3,2,1,0:T(4,128)S(1)}, u32[]{:S(2)}, u32[]{:S(2)}) collective-permute-start(f32[24,2,4,128]{3,2,1,0:T(4,128)S(1)} %get-tuple-element.126), channel_id=1, source_target_pairs={{0,16},{1,2},{2,1},{3,4},{4,3},{5,6},{6,5},{7,8},{8,7},{9,10},{10,... | collective-permute-start | bytes 294920 | tf_op jit(solution)/shard_map/ppermute | solution.py:425
  14.5 5.0 %collective-permute-start.6 = (f32[4,2,24,128]{3,2,1,0:T(8,128)S(1)}, f32[4,2,24,128]{3,2,1,0:T(8,128)S(1)}, u32[]{:S(2)}, u32[]{:S(2)}) collective-permute-start(f32[4,2,24,128]{3,2,1,0:T(8,128)S(1)} %get-tuple-element.127), channel_id=1, source_target_pairs={{0,1},{1,0},{2,3},{3,2},{4,5},{5,4},{6,7},{7,6},{8,9},{9,8},{10,11... | collective-permute-start | bytes 294920 | tf_op jit(solution)/shard_map/ppermute | solution.py:425
  16.4 3.0 %collective-permute-start.7 = (f32[24,2,4,128]{3,2,1,0:T(4,128)S(1)}, f32[24,2,4,128]{3,2,1,0:T(4,128)S(1)}, u32[]{:S(2)}, u32[]{:S(2)}) collective-permute-start(f32[24,2,4,128]{3,2,1,0:T(4,128)S(1)} %get-tuple-element.128), channel_id=1, source_target_pairs={{0,1},{1,0},{2,3},{3,2},{4,5},{5,4},{6,7},{7,6},{8,9},{9,8},{10,11... | collective-permute-start | bytes 294920 | tf_op jit(solution)/shard_map/ppermute | solution.py:425
  19.8 10.0 %collective-permute-start.8 = (f32[4,2,24,128]{3,2,1,0:T(8,128)S(1)}, f32[4,2,24,128]{3,2,1,0:T(8,128)S(1)}, u32[]{:S(2)}, u32[]{:S(2)}) collective-permute-start(f32[4,2,24,128]{3,2,1,0:T(8,128)S(1)} %get-tuple-element.136), channel_id=1, source_target_pairs={{0,16},{1,17},{2,18},{3,19},{4,20},{5,21},{6,22},{7,23},{8,24},{9,... | collective-permute-start | bytes 294920 | tf_op jit(solution)/shard_map/ppermute | solution.py:425
  24.3 5.6 %collective-permute-start.9 = (f32[24,2,4,128]{3,2,1,0:T(4,128)S(1)}, f32[24,2,4,128]{3,2,1,0:T(4,128)S(1)}, u32[]{:S(2)}, u32[]{:S(2)}) collective-permute-start(f32[24,2,4,128]{3,2,1,0:T(4,128)S(1)} %get-tuple-element.137), channel_id=1, source_target_pairs={{0,16},{1,2},{2,1},{3,4},{4,3},{5,6},{6,5},{7,8},{8,7},{9,10},{10,... | collective-permute-start | bytes 294920 | tf_op jit(solution)/shard_map/ppermute | solution.py:425
  24.4 5.5 %collective-permute-start.10 = (f32[4,2,24,128]{3,2,1,0:T(8,128)S(1)}, f32[4,2,24,128]{3,2,1,0:T(8,128)S(1)}, u32[]{:S(2)}, u32[]{:S(2)}) collective-permute-start(f32[4,2,24,128]{3,2,1,0:T(8,128)S(1)} %get-tuple-element.138), channel_id=1, source_target_pairs={{0,1},{1,0},{2,3},{3,2},{4,5},{5,4},{6,7},{7,6},{8,9},{9,8},{10,11... | collective-permute-start | bytes 294920 | tf_op jit(solution)/shard_map/ppermute | solution.py:425
  26.8 3.0 %collective-permute-start.11 = (f32[24,2,4,128]{3,2,1,0:T(4,128)S(1)}, f32[24,2,4,128]{3,2,1,0:T(4,128)S(1)}, u32[]{:S(2)}, u32[]{:S(2)}) collective-permute-start(f32[24,2,4,128]{3,2,1,0:T(4,128)S(1)} %get-tuple-element.139), channel_id=1, source_target_pairs={{0,1},{1,0},{2,3},{3,2},{4,5},{5,4},{6,7},{7,6},{8,9},{9,8},{10,11... | collective-permute-start | bytes 294920 | tf_op jit(solution)/shard_map/ppermute | solution.py:425
  30.2 8.9 %collective-permute-start.12 = (f32[4,2,24,128]{3,2,1,0:T(8,128)S(1)}, f32[4,2,24,128]{3,2,1,0:T(8,128)S(1)}, u32[]{:S(2)}, u32[]{:S(2)}) collective-permute-start(f32[4,2,24,128]{3,2,1,0:T(8,128)S(1)} %get-tuple-element.147), channel_id=1, source_target_pairs={{0,16},{1,17},{2,18},{3,19},{4,20},{5,21},{6,22},{7,23},{8,24},{9,... | collective-permute-start | bytes 294920 | tf_op jit(solution)/shard_map/ppermute | solution.py:425
  33.9 5.8 %collective-permute-start.13 = (f32[24,2,4,128]{3,2,1,0:T(4,128)S(1)}, f32[24,2,4,128]{3,2,1,0:T(4,128)S(1)}, u32[]{:S(2)}, u32[]{:S(2)}) collective-permute-start(f32[24,2,4,128]{3,2,1,0:T(4,128)S(1)} %get-tuple-element.148), channel_id=1, source_target_pairs={{0,16},{1,2},{2,1},{3,4},{4,3},{5,6},{6,5},{7,8},{8,7},{9,10},{10,... | collective-permute-start | bytes 294920 | tf_op jit(solution)/shard_map/ppermute | solution.py:425
  34.0 5.7 %collective-permute-start.14 = (f32[4,2,24,128]{3,2,1,0:T(8,128)S(1)}, f32[4,2,24,128]{3,2,1,0:T(8,128)S(1)}, u32[]{:S(2)}, u32[]{:S(2)}) collective-permute-start(f32[4,2,24,128]{3,2,1,0:T(8,128)S(1)} %get-tuple-element.149), channel_id=1, source_target_pairs={{0,1},{1,0},{2,3},{3,2},{4,5},{5,4},{6,7},{7,6},{8,9},{9,8},{10,11... | collective-permute-start | bytes 294920 | tf_op jit(solution)/shard_map/ppermute | solution.py:425
  36.0 3.6 %collective-permute-start.15 = (f32[24,2,4,128]{3,2,1,0:T(4,128)S(1)}, f32[24,2,4,128]{3,2,1,0:T(4,128)S(1)}, u32[]{:S(2)}, u32[]{:S(2)}) collective-permute-start(f32[24,2,4,128]{3,2,1,0:T(4,128)S(1)} %get-tuple-element.150), channel_id=1, source_target_pairs={{0,1},{1,0},{2,3},{3,2},{4,5},{5,4},{6,7},{7,6},{8,9},{9,8},{10,11... | collective-permute-start | bytes 294920 | tf_op jit(solution)/shard_map/ppermute | solution.py:425
  39.9 8.6 %collective-permute-start.16 = (f32[4,2,24,128]{3,2,1,0:T(8,128)S(1)}, f32[4,2,24,128]{3,2,1,0:T(8,128)S(1)}, u32[]{:S(2)}, u32[]{:S(2)}) collective-permute-start(f32[4,2,24,128]{3,2,1,0:T(8,128)S(1)} %get-tuple-element.158), channel_id=1, source_target_pairs={{0,16},{1,17},{2,18},{3,19},{4,20},{5,21},{6,22},{7,23},{8,24},{9,... | collective-permute-start | bytes 294920 | tf_op jit(solution)/shard_map/ppermute | solution.py:425
  43.0 5.6 %collective-permute-start.17 = (f32[24,2,4,128]{3,2,1,0:T(4,128)S(1)}, f32[24,2,4,128]{3,2,1,0:T(4,128)S(1)}, u32[]{:S(2)}, u32[]{:S(2)}) collective-permute-start(f32[24,2,4,128]{3,2,1,0:T(4,128)S(1)} %get-tuple-element.159), channel_id=1, source_target_pairs={{0,16},{1,2},{2,1},{3,4},{4,3},{5,6},{6,5},{7,8},{8,7},{9,10},{10,... | collective-permute-start | bytes 294920 | tf_op jit(solution)/shard_map/ppermute | solution.py:425
  43.1 5.5 %collective-permute-start.18 = (f32[4,2,24,128]{3,2,1,0:T(8,128)S(1)}, f32[4,2,24,128]{3,2,1,0:T(8,128)S(1)}, u32[]{:S(2)}, u32[]{:S(2)}) collective-permute-start(f32[4,2,24,128]{3,2,1,0:T(8,128)S(1)} %get-tuple-element.160), channel_id=1, source_target_pairs={{0,1},{1,0},{2,3},{3,2},{4,5},{5,4},{6,7},{7,6},{8,9},{9,8},{10,11... | collective-permute-start | bytes 294920 | tf_op jit(solution)/shard_map/ppermute | solution.py:425
  45.5 3.1 %collective-permute-start.19 = (f32[24,2,4,128]{3,2,1,0:T(4,128)S(1)}, f32[24,2,4,128]{3,2,1,0:T(4,128)S(1)}, u32[]{:S(2)}, u32[]{:S(2)}) collective-permute-start(f32[24,2,4,128]{3,2,1,0:T(4,128)S(1)} %get-tuple-element.161), channel_id=1, source_target_pairs={{0,1},{1,0},{2,3},{3,2},{4,5},{5,4},{6,7},{7,6},{8,9},{9,8},{10,11... | collective-permute-start | bytes 294920 | tf_op jit(solution)/shard_map/ppermute | solution.py:425
  48.9 8.4 %collective-permute-start.20 = (f32[4,2,24,128]{3,2,1,0:T(8,128)S(1)}, f32[4,2,24,128]{3,2,1,0:T(8,128)S(1)}, u32[]{:S(2)}, u32[]{:S(2)}) collective-permute-start(f32[4,2,24,128]{3,2,1,0:T(8,128)S(1)} %get-tuple-element.169), channel_id=1, source_target_pairs={{0,16},{1,17},{2,18},{3,19},{4,20},{5,21},{6,22},{7,23},{8,24},{9,... | collective-permute-start | bytes 294920 | tf_op jit(solution)/shard_map/ppermute | solution.py:425
  52.6 4.8 %collective-permute-start.21 = (f32[24,2,4,128]{3,2,1,0:T(4,128)S(1)}, f32[24,2,4,128]{3,2,1,0:T(4,128)S(1)}, u32[]{:S(2)}, u32[]{:S(2)}) collective-permute-start(f32[24,2,4,128]{3,2,1,0:T(4,128)S(1)} %get-tuple-element.170), channel_id=1, source_target_pairs={{0,16},{1,2},{2,1},{3,4},{4,3},{5,6},{6,5},{7,8},{8,7},{9,10},{10,... | collective-permute-start | bytes 294920 | tf_op jit(solution)/shard_map/ppermute | solution.py:425
  52.7 4.7 %collective-permute-start.22 = (f32[4,2,24,128]{3,2,1,0:T(8,128)S(1)}, f32[4,2,24,128]{3,2,1,0:T(8,128)S(1)}, u32[]{:S(2)}, u32[]{:S(2)}) collective-permute-start(f32[4,2,24,128]{3,2,1,0:T(8,128)S(1)} %get-tuple-element.171), channel_id=1, source_target_pairs={{0,1},{1,0},{2,3},{3,2},{4,5},{5,4},{6,7},{7,6},{8,9},{9,8},{10,11... | collective-permute-start | bytes 294920 | tf_op jit(solution)/shard_map/ppermute | solution.py:425
  54.3 3.0 %collective-permute-start.23 = (f32[24,2,4,128]{3,2,1,0:T(4,128)S(1)}, f32[24,2,4,128]{3,2,1,0:T(4,128)S(1)}, u32[]{:S(2)}, u32[]{:S(2)}) collective-permute-start(f32[24,2,4,128]{3,2,1,0:T(4,128)S(1)} %get-tuple-element.172), channel_id=1, source_target_pairs={{0,1},{1,0},{2,3},{3,2},{4,5},{5,4},{6,7},{7,6},{8,9},{9,8},{10,11... | collective-permute-start | bytes 294920 | tf_op jit(solution)/shard_map/ppermute | solution.py:425
  57.7 9.2 %collective-permute-start.24 = (f32[4,2,24,128]{3,2,1,0:T(8,128)S(1)}, f32[4,2,24,128]{3,2,1,0:T(8,128)S(1)}, u32[]{:S(2)}, u32[]{:S(2)}) collective-permute-start(f32[4,2,24,128]{3,2,1,0:T(8,128)S(1)} %get-tuple-element.180), channel_id=1, source_target_pairs={{0,16},{1,17},{2,18},{3,19},{4,20},{5,21},{6,22},{7,23},{8,24},{9,... | collective-permute-start | bytes 294920 | tf_op jit(solution)/shard_map/ppermute | solution.py:425
  61.8 5.4 %collective-permute-start.25 = (f32[24,2,4,128]{3,2,1,0:T(4,128)S(1)}, f32[24,2,4,128]{3,2,1,0:T(4,128)S(1)}, u32[]{:S(2)}, u32[]{:S(2)}) collective-permute-start(f32[24,2,4,128]{3,2,1,0:T(4,128)S(1)} %get-tuple-element.181), channel_id=1, source_target_pairs={{0,16},{1,2},{2,1},{3,4},{4,3},{5,6},{6,5},{7,8},{8,7},{9,10},{10,... | collective-permute-start | bytes 294920 | tf_op jit(solution)/shard_map/ppermute | solution.py:425
  61.9 5.3 %collective-permute-start.26 = (f32[4,2,24,128]{3,2,1,0:T(8,128)S(1)}, f32[4,2,24,128]{3,2,1,0:T(8,128)S(1)}, u32[]{:S(2)}, u32[]{:S(2)}) collective-permute-start(f32[4,2,24,128]{3,2,1,0:T(8,128)S(1)} %get-tuple-element.182), channel_id=1, source_target_pairs={{0,1},{1,0},{2,3},{3,2},{4,5},{5,4},{6,7},{7,6},{8,9},{9,8},{10,11... | collective-permute-start | bytes 294920 | tf_op jit(solution)/shard_map/ppermute | solution.py:425
  63.8 3.4 %collective-permute-start.27 = (f32[24,2,4,128]{3,2,1,0:T(4,128)S(1)}, f32[24,2,4,128]{3,2,1,0:T(4,128)S(1)}, u32[]{:S(2)}, u32[]{:S(2)}) collective-permute-start(f32[24,2,4,128]{3,2,1,0:T(4,128)S(1)} %get-tuple-element.183), channel_id=1, source_target_pairs={{0,1},{1,0},{2,3},{3,2},{4,5},{5,4},{6,7},{7,6},{8,9},{9,8},{10,11... | collective-permute-start | bytes 294920 | tf_op jit(solution)/shard_map/ppermute | solution.py:425
  67.5 8.8 %collective-permute-start.28 = (f32[4,2,24,128]{3,2,1,0:T(8,128)S(1)}, f32[4,2,24,128]{3,2,1,0:T(8,128)S(1)}, u32[]{:S(2)}, u32[]{:S(2)}) collective-permute-start(f32[4,2,24,128]{3,2,1,0:T(8,128)S(1)} %get-tuple-element.191), channel_id=1, source_target_pairs={{0,16},{1,17},{2,18},{3,19},{4,20},{5,21},{6,22},{7,23},{8,24},{9,... | collective-permute-start | bytes 294920 | tf_op jit(solution)/shard_map/ppermute | solution.py:425
  71.7 5.7 %collective-permute-start.29 = (f32[24,2,4,128]{3,2,1,0:T(4,128)S(1)}, f32[24,2,4,128]{3,2,1,0:T(4,128)S(1)}, u32[]{:S(2)}, u32[]{:S(2)}) collective-permute-start(f32[24,2,4,128]{3,2,1,0:T(4,128)S(1)} %get-tuple-element.192), channel_id=1, source_target_pairs={{0,16},{1,2},{2,1},{3,4},{4,3},{5,6},{6,5},{7,8},{8,7},{9,10},{10,... | collective-permute-start | bytes 294920 | tf_op jit(solution)/shard_map/ppermute | solution.py:425
  71.8 5.6 %collective-permute-start.30 = (f32[4,2,24,128]{3,2,1,0:T(8,128)S(1)}, f32[4,2,24,128]{3,2,1,0:T(8,128)S(1)}, u32[]{:S(2)}, u32[]{:S(2)}) collective-permute-start(f32[4,2,24,128]{3,2,1,0:T(8,128)S(1)} %get-tuple-element.193), channel_id=1, source_target_pairs={{0,1},{1,0},{2,3},{3,2},{4,5},{5,4},{6,7},{7,6},{8,9},{9,8},{10,11... | collective-permute-start | bytes 294920 | tf_op jit(solution)/shard_map/ppermute | solution.py:425
  73.3 4.0 %collective-permute-start.31 = (f32[24,2,4,128]{3,2,1,0:T(4,128)S(1)}, f32[24,2,4,128]{3,2,1,0:T(4,128)S(1)}, u32[]{:S(2)}, u32[]{:S(2)}) collective-permute-start(f32[24,2,4,128]{3,2,1,0:T(4,128)S(1)} %get-tuple-element.194), channel_id=1, source_target_pairs={{0,1},{1,0},{2,3},{3,2},{4,5},{5,4},{6,7},{7,6},{8,9},{9,8},{10,11... | collective-permute-start | bytes 294920 | tf_op jit(solution)/shard_map/ppermute | solution.py:425
  78.4 1.2 %collective-permute-start.32 = (f32[16,128]{1,0:T(8,128)S(1)}, f32[16,128]{1,0:T(8,128)S(1)}, u32[]{:S(2)}, u32[]{:S(2)}) collective-permute-start(f32[16,128]{1,0:T(8,128)S(1)} %get-tuple-element.204), channel_id=1, source_target_pairs={{0,1},{1,0},{2,3},{3,2},{4,5},{5,4},{6,7},{7,6},{8,9},{9,8},{10,11... | collective-permute-start | bytes 24584 | tf_op jit(solution)/shard_map/ppermute | solution.py:439
  79.6 5.4 %collective-permute-start.35 = (f32[16,128]{1,0:T(8,128)S(1)}, f32[16,128]{1,0:T(8,128)S(1)}, u32[]{:S(2)}, u32[]{:S(2)}) collective-permute-start(f32[16,128]{1,0:T(8,128)S(1)} %add.21), channel_id=1, source_target_pairs={{0,18},{1,19},{2,16},{3,17},{4,22},{5,23},{6,20},{7,21},{8,26},{9,... | collective-permute-start | bytes 24584 | tf_op jit(solution)/shard_map/ppermute | solution.py:439
  83.2 5.2 %collective-permute-start.34 = (f32[16,128]{1,0:T(8,128)S(1)}, f32[16,128]{1,0:T(8,128)S(1)}, u32[]{:S(2)}, u32[]{:S(2)}) collective-permute-start(f32[16,128]{1,0:T(8,128)S(1)} %add.21), channel_id=1, source_target_pairs={{0,2},{1,3},{2,0},{3,1},{4,6},{5,7},{6,4},{7,5},{8,10},{9,11},{10,... | collective-permute-start | bytes 24584 | tf_op jit(solution)/shard_map/ppermute | solution.py:439
  84.9 3.7 %collective-permute-start.33 = (f32[16,128]{1,0:T(8,128)S(1)}, f32[16,128]{1,0:T(8,128)S(1)}, u32[]{:S(2)}, u32[]{:S(2)}) collective-permute-start(f32[16,128]{1,0:T(8,128)S(1)} %add.21), channel_id=1, source_target_pairs={{0,16},{1,17},{2,18},{3,19},{4,20},{5,21},{6,22},{7,23},{8,24},{9,... | collective-permute-start | bytes 24584 | tf_op jit(solution)/shard_map/ppermute | solution.py:439
  88.6 4.9 %collective-permute-start.38 = (f32[16,128]{1,0:T(8,128)S(1)}, f32[16,128]{1,0:T(8,128)S(1)}, u32[]{:S(2)}, u32[]{:S(2)}) collective-permute-start(f32[16,128]{1,0:T(8,128)S(1)} %add_add_fusion.1), channel_id=1, source_target_pairs={{0,12},{1,13},{2,14},{3,15},{4,8},{5,9},{6,10},{7,11},{8,4},{9,5},... | collective-permute-start | bytes 24584 | tf_op jit(solution)/shard_map/ppermute | solution.py:439
  91.0 5.2 %collective-permute-start.37 = (f32[16,128]{1,0:T(8,128)S(1)}, f32[16,128]{1,0:T(8,128)S(1)}, u32[]{:S(2)}, u32[]{:S(2)}) collective-permute-start(f32[16,128]{1,0:T(8,128)S(1)} %add_add_fusion.1), channel_id=1, source_target_pairs={{0,8},{1,9},{2,10},{3,11},{4,12},{5,13},{6,14},{7,15},{8,0},{9,1},... | collective-permute-start | bytes 24584 | tf_op jit(solution)/shard_map/ppermute | solution.py:439
  93.2 3.7 %collective-permute-start.36 = (f32[16,128]{1,0:T(8,128)S(1)}, f32[16,128]{1,0:T(8,128)S(1)}, u32[]{:S(2)}, u32[]{:S(2)}) collective-permute-start(f32[16,128]{1,0:T(8,128)S(1)} %add_add_fusion.1), channel_id=1, source_target_pairs={{0,4},{1,5},{2,6},{3,7},{4,0},{5,1},{6,2},{7,3},{8,12},{9,13},{10,... | collective-permute-start | bytes 24584 | tf_op jit(solution)/shard_map/ppermute | solution.py:439
  96.8 5.6 %collective-permute-start.39 = (f32[16,128]{1,0:T(8,128)S(1)}, f32[16,128]{1,0:T(8,128)S(1)}, u32[]{:S(2)}, u32[]{:S(2)}) collective-permute-start(f32[16,128]{1,0:T(8,128)S(1)} %add_add_fusion.refs_0_), channel_id=1, source_target_pairs={{0,32},{1,33},{2,34},{3,35},{4,36},{5,37},{6,38},{7,39},{8,40},{9,... | collective-permute-start | bytes 24584 | tf_op jit(solution)/shard_map/ppermute | solution.py:439
  98.1 5.2 %collective-permute-start.40 = (f32[16,128]{1,0:T(8,128)S(1)}, f32[16,128]{1,0:T(8,128)S(1)}, u32[]{:S(2)}, u32[]{:S(2)}) collective-permute-start(f32[16,128]{1,0:T(8,128)S(1)} %add_add_fusion.refs_0_), channel_id=1, source_target_pairs={{0,64},{1,65},{2,66},{3,67},{4,68},{5,69},{6,70},{7,71},{8,72},{9,... | collective-permute-start | bytes 24584 | tf_op jit(solution)/shard_map/ppermute | solution.py:439
  99.5 4.9 %collective-permute-start.41 = (f32[16,128]{1,0:T(8,128)S(1)}, f32[16,128]{1,0:T(8,128)S(1)}, u32[]{:S(2)}, u32[]{:S(2)}) collective-permute-start(f32[16,128]{1,0:T(8,128)S(1)} %add_add_fusion.refs_0_), channel_id=1, source_target_pairs={{0,96},{1,97},{2,98},{3,99},{4,100},{5,101},{6,102},{7,103},{8,104... | collective-permute-start | bytes 24584 | tf_op jit(solution)/shard_map/ppermute | solution.py:439

commit v7 on v6

--- a/solution.py
+++ b/solution.py
@@ -134,23 +134,21 @@
     return lax.axis_index(GX) % 2 == 1, lax.axis_index(GY) % 2 == 1
 
 
-def pack_kernel(pressure, old, speed_term, field, near_x, far_y, far_x, near_y, raw_old, raw_speed, staged, sems):
-    copies = fetch([(pressure, staged), (old, raw_old), (speed_term, raw_speed)], sems)
+def pack_kernel(pressure, field, near_x, far_y, far_x, near_y, staged, sems):
+    copies = fetch([(pressure, staged)], sems)
     field[...] = jnp.zeros(FIELD, jnp.float32)
-    for copy in copies[:CHUNKS]:
+    for copy in copies:
         copy.wait()
     for half in range(2):
         part = staged[:, :, half * LANES : (half + 1) * LANES]
         field[H : H + CX, half, INSIDE, :] = part
     split_strips(field, *odd(), near_x, far_y, far_x, near_y)
-    for copy in copies[CHUNKS:]:
-        copy.wait()
 
 
 def begin_kernel(
-    widths_far, sx_far, sy_far, sz_far, rx_far, ry_far, rz_far, amp_far, raw_old, raw_speed,
+    widths_far, sx_far, sy_far, sz_far, rx_far, ry_far, rz_far, amp_far, old, speed_term,
     field, speed, memory_x, memory_y, zeta_x, zeta_y, seen, keep_x, keep_y, norm, table, amps,
-    widths_ref, sx, sy, sz, rx, ry, rz, amp, small_sems,
+    raw_old, raw_speed, sems, widths_ref, sx, sy, sz, rx, ry, rz, amp, small_sems,
 ):
     far = (widths_far, sx_far, sy_far, sz_far, rx_far, ry_far, rz_far, amp_far)
     near = (widths_ref, sx, sy, sz, rx, ry, rz, amp)
@@ -160,14 +158,11 @@
     ]
     for copy in small:
         copy.start()
+    copies = fetch([(old, raw_old), (speed_term, raw_speed)], sems)
     gx, gy, edge_x, edge_y = place()
     start_x, start_y = (gx * CX, gy * CY)
     seen[...] = jnp.zeros(SEEN, jnp.float32)
     field[...] = jnp.zeros(FIELD, jnp.float32)
-    for half in range(2):
-        lanes = slice(half * LANES, (half + 1) * LANES)
-        field[H : H + CX, half, INSIDE, :] = raw_old[:, :, lanes]
-        speed[:, half, :, :] = raw_speed[:, :, lanes]
 
     @pl.when(edge_x)
     def _():
@@ -209,6 +204,12 @@
     for t in range(STEPS):
         for n in range(NSRC):
             amps[t * NSRC + n] = amp[n, t]
+    for copy in copies:
+        copy.wait()
+    for half in range(2):
+        lanes = slice(half * LANES, (half + 1) * LANES)
+        field[H : H + CX, half, INSIDE, :] = raw_old[:, :, lanes]
+        speed[:, half, :, :] = raw_speed[:, :, lanes]
 
 
 def inner_kernel(
@@ -468,14 +469,14 @@
     small = [stay(v) for v in small]
     staged = pltpu.VMEM(pressure.shape, jnp.float32)
     strips_out = shape(STRIP_X, STRIP_Y, STRIP_X, STRIP_Y)
-    current, *strips, raw_old, raw_speed = pl.pallas_call(
+    current, *strips = pl.pallas_call(
         pack_kernel,
-        out_shape=shape(FIELD) + strips_out + shape(pressure.shape, pressure.shape),
-        in_specs=hbm(3),
-        out_specs=vmem(7),
-        scratch_shapes=[staged, pltpu.SemaphoreType.DMA((3, CHUNKS))],
+        out_shape=shape(FIELD) + strips_out,
+        in_specs=hbm(1),
+        out_specs=vmem(5),
+        scratch_shapes=[staged, pltpu.SemaphoreType.DMA((1, CHUNKS))],
         compiler_params=limit(8),
-    )(pressure, pressure_old, speed_term)
+    )(pressure)
     previous, speed, *rest = pl.pallas_call(
         begin_kernel,
         out_shape=shape(FIELD, BLOCK, MEM_X, MEM_Y, BLOCK, BLOCK, SEEN, KEEP_X, KEEP_Y, NORM)
@@ -483,12 +484,13 @@
             jax.ShapeDtypeStruct((TABLE,), jnp.int32),
             jax.ShapeDtypeStruct((STEPS * NSRC,), jnp.float32),
         ],
-        in_specs=hbm(8) + vmem(2),
+        in_specs=hbm(10),
         out_specs=vmem(10) + smem(2),
-        scratch_shapes=[pltpu.SMEM((n,), jnp.int32) for n in (4, NSRC, NSRC, NSRC, NREC, NREC, NREC)]
+        scratch_shapes=[staged, staged, pltpu.SemaphoreType.DMA((2, CHUNKS))]
+        + [pltpu.SMEM((n,), jnp.int32) for n in (4, NSRC, NSRC, NSRC, NREC, NREC, NREC)]
         + [pltpu.SMEM((NSRC, STEPS), jnp.float32), pltpu.SemaphoreType.DMA((8,))],
         compiler_params=limit(8),
-    )(*small, raw_old, raw_speed)
+    )(*small, pressure_old, speed_term)
     state, keeps, table, amps = (rest[:5], rest[5:8], rest[8], rest[9])
     band = jnp.asarray(band_matrix())
     beside = pltpu.VMEM((CX, 2, 24, LANES), jnp.float32)

time: 105 us -> 105 us (level)
  starting transfers between devices: 59.4 us -> 57.9 us
  waiting for transfers between devices: 12.3 us -> 13.7 us
    ppermute x32, waiting for transfers between devices: 2.05 us -> 3.43 us  [swap(): return lax.ppermute(strip, BOTH, pairs)]
    ppermute x32, starting transfers between devices: 44.5 us -> 43.4 us  [swap(): return lax.ppermute(strip, BOTH, pairs)]
  transfers between devices with their start and end apart: 42 -> 42, of which waited for: 12 -> 14; matrix products, arithmetic and copies ran while one was open for 0% -> 0% of each run, Pallas kernels for 26% -> 26%
where the time goes in v7:
time: 105 us
  starting transfers between devices  57.9 us (55%)
  Pallas kernels  32.3 us (31%)
  waiting for transfers between devices  13.7 us (13%)
    ppermute x32, starting transfers between devices, swap(): return lax.ppermute(strip, BOTH, pairs)  43.4 us
    pallas_call x8, Pallas kernels, per_device(): pl.pallas_call(functools.partial(inner_kernel, step), out_shape=shape(FIE...  24.1 us
    ppermute x10, starting transfers between devices, spread(): return lax.ppermute(value, BOTH, pairs)  14.5 us
    ppermute x10, waiting for transfers between devices, spread(): return lax.ppermute(value, BOTH, pairs)  10.2 us
    ppermute x32, waiting for transfers between devices, swap(): return lax.ppermute(strip, BOTH, pairs)  3.43 us
    pallas_call x1, Pallas kernels, per_device(): pl.pallas_call(begin_kernel, out_shape=shape(FIELD, BLOCK, MEM_X, MEM_Y,...  2.35 us
    pallas_call x7, Pallas kernels, per_device(): pl.pallas_call(functools.partial(join_kernel, False), out_shape=shape(FIE...  2.14 us
  transfers between devices with their start and end apart: 42, of which 14 were waited for; matrix products, arithmetic and copies ran while one was open for 0% of the time, Pallas kernels for 26%

profile of v7, /device:TPU:0, one launch (start us, length us, event | category | flops | bytes accessed | tf_op | source)
XLA Modules:
  0.0 104.7 jit_solution(3252713958712891706)
XLA Ops:
  0.6 1.3 %shard_map.140 = (f32[32,2,40,128]{3,2,1,0:T(8,128)S(1)}, f32[4,2,24,128]{3,2,1,0:T(8,128)S(1)}, f32[24,2,4,128]{3,2,1,0:T(4,128)S(1)}, f32[4,2,24,128]{3,2,1,0:T(8,128)S(1)}, f32[24,2,4,128]{3,2,1,0:T(4,128)S(1)}) custom-call(f32[24,24,256]{2,1,0:T(8,128)} %pressure.1), custom_call_target="tpu_custom_call" | custom-call | tf_op jit(solution)/shard_map/pallas_call | solution.py:472
  1.9 1.7 %collective-permute-start = (f32[4,2,24,128]{3,2,1,0:T(8,128)S(1)}, f32[4,2,24,128]{3,2,1,0:T(8,128)S(1)}, u32[]{:S(2)}, u32[]{:S(2)}) collective-permute-start(f32[4,2,24,128]{3,2,1,0:T(8,128)S(1)} %get-tuple-element.108), channel_id=1, source_target_pairs={{0,16},{1,17},{2,18},{3,19},{4,20},{5,21},{6,22},{7,23},{8,24},{9,... | collective-permute-start | bytes 294920 | tf_op jit(solution)/shard_map/ppermute | solution.py:426
  3.6 0.5 collective-permute-start.1
  4.0 2.4 %collective-permute-start.2 = (f32[4,2,24,128]{3,2,1,0:T(8,128)S(1)}, f32[4,2,24,128]{3,2,1,0:T(8,128)S(1)}, u32[]{:S(2)}, u32[]{:S(2)}) collective-permute-start(f32[4,2,24,128]{3,2,1,0:T(8,128)S(1)} %get-tuple-element.110), channel_id=1, source_target_pairs={{0,1},{1,0},{2,3},{3,2},{4,5},{5,4},{6,7},{7,6},{8,9},{9,8},{10,11... | collective-permute-start | bytes 294920 | tf_op jit(solution)/shard_map/ppermute | solution.py:426
  6.4 2.3 %shard_map.139 = (f32[32,2,40,128]{3,2,1,0:T(8,128)S(1)}, f32[24,2,24,128]{3,2,1,0:T(8,128)S(1)}, f32[2,32,2,24,128]{4,3,2,1,0:T(8,128)S(1)}, f32[24,2,40,128]{3...) custom-call(s32[4]{0:T(128)} %widths_far.1, ...), custom_call_target="tpu_custom_call" | custom-call | tf_op jit(solution)/shard_map/pallas_call | solution.py:480
  8.8 2.9 %shard_map.141 = (f32[32,2,40,128]{3,2,1,0:T(8,128)S(1)}, f32[2,32,2,24,128]{4,3,2,1,0:T(8,128)S(1)}, f32[24,2,40,128]{3,2,1,0:T(8,128)S(1)}, f32[24,2,24,128]{3...) custom-call(s32[77]{0:T(128)S(1)} %get-tuple-element.103.table.refs_, ...), custom_call_target="tpu_custom_call", output_to_operand_aliasing={{0}: (8, {}), {1}: (9, {}), {2}: (10, {}), {3}: (11, {}), {... | custom-call | tf_op jit(solution)/shard_map/pallas_call | solution.py:499
  12.1 2.2 %collective-permute-start.4 = (f32[4,2,24,128]{3,2,1,0:T(8,128)S(1)}, f32[4,2,24,128]{3,2,1,0:T(8,128)S(1)}, u32[]{:S(2)}, u32[]{:S(2)}) collective-permute-start(f32[4,2,24,128]{3,2,1,0:T(8,128)S(1)} %get-tuple-element.121), channel_id=1, source_target_pairs={{0,16},{1,17},{2,18},{3,19},{4,20},{5,21},{6,22},{7,23},{8,24},{9,... | collective-permute-start | bytes 294920 | tf_op jit(solution)/shard_map/ppermute | solution.py:426
  14.3 1.7 %collective-permute-start.6 = (f32[4,2,24,128]{3,2,1,0:T(8,128)S(1)}, f32[4,2,24,128]{3,2,1,0:T(8,128)S(1)}, u32[]{:S(2)}, u32[]{:S(2)}) collective-permute-start(f32[4,2,24,128]{3,2,1,0:T(8,128)S(1)} %get-tuple-element.123), channel_id=1, source_target_pairs={{0,1},{1,0},{2,3},{3,2},{4,5},{5,4},{6,7},{7,6},{8,9},{9,8},{10,11... | collective-permute-start | bytes 294920 | tf_op jit(solution)/shard_map/ppermute | solution.py:426
  16.1 3.0 %shard_map.143 = (f32[32,2,40,128]{3,2,1,0:T(8,128)S(1)}, f32[2,32,2,24,128]{4,3,2,1,0:T(8,128)S(1)}, f32[24,2,40,128]{3,2,1,0:T(8,128)S(1)}, f32[24,2,24,128]{3...) custom-call(s32[77]{0:T(128)S(1)} %get-tuple-element.103.table.refs_, ...), custom_call_target="tpu_custom_call", output_to_operand_aliasing={{0}: (8, {}), {1}: (9, {}), {2}: (10, {}), {3}: (11, {}), {... | custom-call | tf_op jit(solution)/shard_map/pallas_call | solution.py:499
  19.4 5.0 %collective-permute-start.8 = (f32[4,2,24,128]{3,2,1,0:T(8,128)S(1)}, f32[4,2,24,128]{3,2,1,0:T(8,128)S(1)}, u32[]{:S(2)}, u32[]{:S(2)}) collective-permute-start(f32[4,2,24,128]{3,2,1,0:T(8,128)S(1)} %get-tuple-element.132), channel_id=1, source_target_pairs={{0,16},{1,17},{2,18},{3,19},{4,20},{5,21},{6,22},{7,23},{8,24},{9,... | collective-permute-start | bytes 294920 | tf_op jit(solution)/shard_map/ppermute | solution.py:426
  24.5 2.0 %collective-permute-start.10 = (f32[4,2,24,128]{3,2,1,0:T(8,128)S(1)}, f32[4,2,24,128]{3,2,1,0:T(8,128)S(1)}, u32[]{:S(2)}, u32[]{:S(2)}) collective-permute-start(f32[4,2,24,128]{3,2,1,0:T(8,128)S(1)} %get-tuple-element.134), channel_id=1, source_target_pairs={{0,1},{1,0},{2,3},{3,2},{4,5},{5,4},{6,7},{7,6},{8,9},{9,8},{10,11... | collective-permute-start | bytes 294920 | tf_op jit(solution)/shard_map/ppermute | solution.py:426
  26.4 3.0 %shard_map.145 = (f32[32,2,40,128]{3,2,1,0:T(8,128)S(1)}, f32[2,32,2,24,128]{4,3,2,1,0:T(8,128)S(1)}, f32[24,2,40,128]{3,2,1,0:T(8,128)S(1)}, f32[24,2,24,128]{3...) custom-call(s32[77]{0:T(128)S(1)} %get-tuple-element.103.table.refs_, ...), custom_call_target="tpu_custom_call", output_to_operand_aliasing={{0}: (8, {}), {1}: (9, {}), {2}: (10, {}), {3}: (11, {}), {... | custom-call | tf_op jit(solution)/shard_map/pallas_call | solution.py:499
  29.9 4.5 %collective-permute-start.12 = (f32[4,2,24,128]{3,2,1,0:T(8,128)S(1)}, f32[4,2,24,128]{3,2,1,0:T(8,128)S(1)}, u32[]{:S(2)}, u32[]{:S(2)}) collective-permute-start(f32[4,2,24,128]{3,2,1,0:T(8,128)S(1)} %get-tuple-element.143), channel_id=1, source_target_pairs={{0,16},{1,17},{2,18},{3,19},{4,20},{5,21},{6,22},{7,23},{8,24},{9,... | collective-permute-start | bytes 294920 | tf_op jit(solution)/shard_map/ppermute | solution.py:426
  34.5 1.1 %collective-permute-start.14 = (f32[4,2,24,128]{3,2,1,0:T(8,128)S(1)}, f32[4,2,24,128]{3,2,1,0:T(8,128)S(1)}, u32[]{:S(2)}, u32[]{:S(2)}) collective-permute-start(f32[4,2,24,128]{3,2,1,0:T(8,128)S(1)} %get-tuple-element.145), channel_id=1, source_target_pairs={{0,1},{1,0},{2,3},{3,2},{4,5},{5,4},{6,7},{7,6},{8,9},{9,8},{10,11... | collective-permute-start | bytes 294920 | tf_op jit(solution)/shard_map/ppermute | solution.py:426
  35.6 3.0 %shard_map.147 = (f32[32,2,40,128]{3,2,1,0:T(8,128)S(1)}, f32[2,32,2,24,128]{4,3,2,1,0:T(8,128)S(1)}, f32[24,2,40,128]{3,2,1,0:T(8,128)S(1)}, f32[24,2,24,128]{3...) custom-call(s32[77]{0:T(128)S(1)} %get-tuple-element.103.table.refs_, ...), custom_call_target="tpu_custom_call", output_to_operand_aliasing={{0}: (8, {}), {1}: (9, {}), {2}: (10, {}), {3}: (11, {}), {... | custom-call | tf_op jit(solution)/shard_map/pallas_call | solution.py:499
  38.7 1.4 %collective-permute-done.13.refs_2_ = f32[24,2,4,128]{3,2,1,0:T(4,128)S(1)} collective-permute-done((f32[24,2,4,128]{3,2,1,0:T(4,128)S(1)}, f32[24,2,4,128]{3,2,1,0:T(4,128)S(1)}, u32[]{:S(2)}, u32[]{:S(2)}) %collective-permute-start.13) | collective-permute-done | bytes 98336 | tf_op jit(solution)/shard_map/ppermute | solution.py:426
  40.4 2.7 %collective-permute-start.16 = (f32[4,2,24,128]{3,2,1,0:T(8,128)S(1)}, f32[4,2,24,128]{3,2,1,0:T(8,128)S(1)}, u32[]{:S(2)}, u32[]{:S(2)}) collective-permute-start(f32[4,2,24,128]{3,2,1,0:T(8,128)S(1)} %get-tuple-element.154), channel_id=1, source_target_pairs={{0,16},{1,17},{2,18},{3,19},{4,20},{5,21},{6,22},{7,23},{8,24},{9,... | collective-permute-start | bytes 294920 | tf_op jit(solution)/shard_map/ppermute | solution.py:426
  43.2 2.2 %collective-permute-start.18 = (f32[4,2,24,128]{3,2,1,0:T(8,128)S(1)}, f32[4,2,24,128]{3,2,1,0:T(8,128)S(1)}, u32[]{:S(2)}, u32[]{:S(2)}) collective-permute-start(f32[4,2,24,128]{3,2,1,0:T(8,128)S(1)} %get-tuple-element.156), channel_id=1, source_target_pairs={{0,1},{1,0},{2,3},{3,2},{4,5},{5,4},{6,7},{7,6},{8,9},{9,8},{10,11... | collective-permute-start | bytes 294920 | tf_op jit(solution)/shard_map/ppermute | solution.py:426
  45.4 3.0 %shard_map.149 = (f32[32,2,40,128]{3,2,1,0:T(8,128)S(1)}, f32[2,32,2,24,128]{4,3,2,1,0:T(8,128)S(1)}, f32[24,2,40,128]{3,2,1,0:T(8,128)S(1)}, f32[24,2,24,128]{3...) custom-call(s32[77]{0:T(128)S(1)} %get-tuple-element.103.table.refs_, ...), custom_call_target="tpu_custom_call", output_to_operand_aliasing={{0}: (8, {}), {1}: (9, {}), {2}: (10, {}), {3}: (11, {}), {... | custom-call | tf_op jit(solution)/shard_map/pallas_call | solution.py:499
  49.0 3.7 %collective-permute-start.20 = (f32[4,2,24,128]{3,2,1,0:T(8,128)S(1)}, f32[4,2,24,128]{3,2,1,0:T(8,128)S(1)}, u32[]{:S(2)}, u32[]{:S(2)}) collective-permute-start(f32[4,2,24,128]{3,2,1,0:T(8,128)S(1)} %get-tuple-element.165), channel_id=1, source_target_pairs={{0,16},{1,17},{2,18},{3,19},{4,20},{5,21},{6,22},{7,23},{8,24},{9,... | collective-permute-start | bytes 294920 | tf_op jit(solution)/shard_map/ppermute | solution.py:426
  52.7 1.5 %collective-permute-start.22 = (f32[4,2,24,128]{3,2,1,0:T(8,128)S(1)}, f32[4,2,24,128]{3,2,1,0:T(8,128)S(1)}, u32[]{:S(2)}, u32[]{:S(2)}) collective-permute-start(f32[4,2,24,128]{3,2,1,0:T(8,128)S(1)} %get-tuple-element.167), channel_id=1, source_target_pairs={{0,1},{1,0},{2,3},{3,2},{4,5},{5,4},{6,7},{7,6},{8,9},{9,8},{10,11... | collective-permute-start | bytes 294920 | tf_op jit(solution)/shard_map/ppermute | solution.py:426
  54.2 3.0 %shard_map.151 = (f32[32,2,40,128]{3,2,1,0:T(8,128)S(1)}, f32[2,32,2,24,128]{4,3,2,1,0:T(8,128)S(1)}, f32[24,2,40,128]{3,2,1,0:T(8,128)S(1)}, f32[24,2,24,128]{3...) custom-call(s32[77]{0:T(128)S(1)} %get-tuple-element.103.table.refs_, ...), custom_call_target="tpu_custom_call", output_to_operand_aliasing={{0}: (8, {}), {1}: (9, {}), {2}: (10, {}), {3}: (11, {}), {... | custom-call | tf_op jit(solution)/shard_map/pallas_call | solution.py:499
  57.9 4.2 %collective-permute-start.24 = (f32[4,2,24,128]{3,2,1,0:T(8,128)S(1)}, f32[4,2,24,128]{3,2,1,0:T(8,128)S(1)}, u32[]{:S(2)}, u32[]{:S(2)}) collective-permute-start(f32[4,2,24,128]{3,2,1,0:T(8,128)S(1)} %get-tuple-element.176), channel_id=1, source_target_pairs={{0,16},{1,17},{2,18},{3,19},{4,20},{5,21},{6,22},{7,23},{8,24},{9,... | collective-permute-start | bytes 294920 | tf_op jit(solution)/shard_map/ppermute | solution.py:426
  62.1 1.9 %collective-permute-start.26 = (f32[4,2,24,128]{3,2,1,0:T(8,128)S(1)}, f32[4,2,24,128]{3,2,1,0:T(8,128)S(1)}, u32[]{:S(2)}, u32[]{:S(2)}) collective-permute-start(f32[4,2,24,128]{3,2,1,0:T(8,128)S(1)} %get-tuple-element.178), channel_id=1, source_target_pairs={{0,1},{1,0},{2,3},{3,2},{4,5},{5,4},{6,7},{7,6},{8,9},{9,8},{10,11... | collective-permute-start | bytes 294920 | tf_op jit(solution)/shard_map/ppermute | solution.py:426
  64.0 3.0 %shard_map.153 = (f32[32,2,40,128]{3,2,1,0:T(8,128)S(1)}, f32[2,32,2,24,128]{4,3,2,1,0:T(8,128)S(1)}, f32[24,2,40,128]{3,2,1,0:T(8,128)S(1)}, f32[24,2,24,128]{3...) custom-call(s32[77]{0:T(128)S(1)} %get-tuple-element.103.table.refs_, ...), custom_call_target="tpu_custom_call", output_to_operand_aliasing={{0}: (8, {}), {1}: (9, {}), {2}: (10, {}), {3}: (11, {}), {... | custom-call | tf_op jit(solution)/shard_map/pallas_call | solution.py:499
  67.1 0.6 collective-permute-done.25.refs_2_
  68.0 3.8 %collective-permute-start.28 = (f32[4,2,24,128]{3,2,1,0:T(8,128)S(1)}, f32[4,2,24,128]{3,2,1,0:T(8,128)S(1)}, u32[]{:S(2)}, u32[]{:S(2)}) collective-permute-start(f32[4,2,24,128]{3,2,1,0:T(8,128)S(1)} %get-tuple-element.187), channel_id=1, source_target_pairs={{0,16},{1,17},{2,18},{3,19},{4,20},{5,21},{6,22},{7,23},{8,24},{9,... | collective-permute-start | bytes 294920 | tf_op jit(solution)/shard_map/ppermute | solution.py:426
  71.8 1.8 %collective-permute-start.30 = (f32[4,2,24,128]{3,2,1,0:T(8,128)S(1)}, f32[4,2,24,128]{3,2,1,0:T(8,128)S(1)}, u32[]{:S(2)}, u32[]{:S(2)}) collective-permute-start(f32[4,2,24,128]{3,2,1,0:T(8,128)S(1)} %get-tuple-element.189), channel_id=1, source_target_pairs={{0,1},{1,0},{2,3},{3,2},{4,5},{5,4},{6,7},{7,6},{8,9},{9,8},{10,11... | collective-permute-start | bytes 294920 | tf_op jit(solution)/shard_map/ppermute | solution.py:426
  73.7 3.0 %shard_map.155 = (f32[32,2,40,128]{3,2,1,0:T(8,128)S(1)}, f32[2,32,2,24,128]{4,3,2,1,0:T(8,128)S(1)}, f32[24,2,40,128]{3,2,1,0:T(8,128)S(1)}, f32[24,2,24,128]{3...) custom-call(s32[77]{0:T(128)S(1)} %get-tuple-element.103.table.refs_, ...), custom_call_target="tpu_custom_call", output_to_operand_aliasing={{0}: (8, {}), {1}: (9, {}), {2}: (10, {}), {3}: (11, {}), {... | custom-call | tf_op jit(solution)/shard_map/pallas_call | solution.py:499
  76.7 0.8 collective-permute-done.29.refs_6_
  77.5 1.0 shard_map.156
  78.5 0.4 collective-permute-start.32
  78.9 0.8 collective-permute-done.32
  79.7 3.5 %collective-permute-start.35 = (f32[16,128]{1,0:T(8,128)S(1)}, f32[16,128]{1,0:T(8,128)S(1)}, u32[]{:S(2)}, u32[]{:S(2)}) collective-permute-start(f32[16,128]{1,0:T(8,128)S(1)} %add.21), channel_id=1, source_target_pairs={{0,18},{1,19},{2,16},{3,17},{4,22},{5,23},{6,20},{7,21},{8,26},{9,... | collective-permute-start | bytes 24584 | tf_op jit(solution)/shard_map/ppermute | solution.py:440
  83.3 1.5 %collective-permute-start.34 = (f32[16,128]{1,0:T(8,128)S(1)}, f32[16,128]{1,0:T(8,128)S(1)}, u32[]{:S(2)}, u32[]{:S(2)}) collective-permute-start(f32[16,128]{1,0:T(8,128)S(1)} %add.21), channel_id=1, source_target_pairs={{0,2},{1,3},{2,0},{3,1},{4,6},{5,7},{6,4},{7,5},{8,10},{9,11},{10,... | collective-permute-start | bytes 24584 | tf_op jit(solution)/shard_map/ppermute | solution.py:440
  84.9 3.5 %collective-permute-done.34 = f32[16,128]{1,0:T(8,128)S(1)} collective-permute-done((f32[16,128]{1,0:T(8,128)S(1)}, f32[16,128]{1,0:T(8,128)S(1)}, u32[]{:S(2)}, u32[]{:S(2)}) %collective-permute-start.34) | collective-permute-done | bytes 8224 | tf_op jit(solution)/shard_map/ppermute | solution.py:440
  88.4 2.2 %collective-permute-start.38 = (f32[16,128]{1,0:T(8,128)S(1)}, f32[16,128]{1,0:T(8,128)S(1)}, u32[]{:S(2)}, u32[]{:S(2)}) collective-permute-start(f32[16,128]{1,0:T(8,128)S(1)} %add_add_fusion.1), channel_id=1, source_target_pairs={{0,12},{1,13},{2,14},{3,15},{4,8},{5,9},{6,10},{7,11},{8,4},{9,5},... | collective-permute-start | bytes 24584 | tf_op jit(solution)/shard_map/ppermute | solution.py:440
  90.6 2.2 %collective-permute-start.37 = (f32[16,128]{1,0:T(8,128)S(1)}, f32[16,128]{1,0:T(8,128)S(1)}, u32[]{:S(2)}, u32[]{:S(2)}) collective-permute-start(f32[16,128]{1,0:T(8,128)S(1)} %add_add_fusion.1), channel_id=1, source_target_pairs={{0,8},{1,9},{2,10},{3,11},{4,12},{5,13},{6,14},{7,15},{8,0},{9,1},... | collective-permute-start | bytes 24584 | tf_op jit(solution)/shard_map/ppermute | solution.py:440
  92.8 0.6 collective-permute-done.38
  93.4 2.4 %collective-permute-done.37 = f32[16,128]{1,0:T(8,128)S(1)} collective-permute-done((f32[16,128]{1,0:T(8,128)S(1)}, f32[16,128]{1,0:T(8,128)S(1)}, u32[]{:S(2)}, u32[]{:S(2)}) %collective-permute-start.37) | collective-permute-done | bytes 8224 | tf_op jit(solution)/shard_map/ppermute | solution.py:440
  95.8 0.7 collective-permute-done.36
  96.5 1.2 %collective-permute-start.39 = (f32[16,128]{1,0:T(8,128)S(1)}, f32[16,128]{1,0:T(8,128)S(1)}, u32[]{:S(2)}, u32[]{:S(2)}) collective-permute-start(f32[16,128]{1,0:T(8,128)S(1)} %add_add_fusion.refs_0_), channel_id=1, source_target_pairs={{0,32},{1,33},{2,34},{3,35},{4,36},{5,37},{6,38},{7,39},{8,40},{9,... | collective-permute-start | bytes 24584 | tf_op jit(solution)/shard_map/ppermute | solution.py:440
  97.7 1.5 %collective-permute-start.40 = (f32[16,128]{1,0:T(8,128)S(1)}, f32[16,128]{1,0:T(8,128)S(1)}, u32[]{:S(2)}, u32[]{:S(2)}) collective-permute-start(f32[16,128]{1,0:T(8,128)S(1)} %add_add_fusion.refs_0_), channel_id=1, source_target_pairs={{0,64},{1,65},{2,66},{3,67},{4,68},{5,69},{6,70},{7,71},{8,72},{9,... | collective-permute-start | bytes 24584 | tf_op jit(solution)/shard_map/ppermute | solution.py:440
  99.2 1.9 %collective-permute-start.41 = (f32[16,128]{1,0:T(8,128)S(1)}, f32[16,128]{1,0:T(8,128)S(1)}, u32[]{:S(2)}, u32[]{:S(2)}) collective-permute-start(f32[16,128]{1,0:T(8,128)S(1)} %add_add_fusion.refs_0_), channel_id=1, source_target_pairs={{0,96},{1,97},{2,98},{3,99},{4,100},{5,101},{6,102},{7,103},{8,104... | collective-permute-start | bytes 24584 | tf_op jit(solution)/shard_map/ppermute | solution.py:440
  101.2 0.9 shard_map.157
  102.0 0.8 collective-permute-done.40.refs_2_
  102.9 1.2 %collective-permute-done.41.refs_3_ = f32[16,128]{1,0:T(8,128)S(1)} collective-permute-done((f32[16,128]{1,0:T(8,128)S(1)}, f32[16,128]{1,0:T(8,128)S(1)}, u32[]{:S(2)}, u32[]{:S(2)}) %collective-permute-start.41) | collective-permute-done | bytes 8224 | tf_op jit(solution)/shard_map/ppermute | solution.py:440
  104.1 0.6 shard_map.158
  (61 shorter events, 3.6 us)
Async XLA Ops:
  0.6 8.2 %copy-start = (bf16[512,256]{1,0:T(8,128)(2,1)S(1)}, bf16[512,256]{1,0:T(8,128)(2,1)}, u32[]{:S(2)}) copy-start(bf16[512,256]{1,0:T(8,128)(2,1)} %constant.2.clone.band) | copy-start | bytes 786436
  1.9 9.8 %collective-permute-start = (f32[4,2,24,128]{3,2,1,0:T(8,128)S(1)}, f32[4,2,24,128]{3,2,1,0:T(8,128)S(1)}, u32[]{:S(2)}, u32[]{:S(2)}) collective-permute-start(f32[4,2,24,128]{3,2,1,0:T(8,128)S(1)} %get-tuple-element.108), channel_id=1, source_target_pairs={{0,16},{1,17},{2,18},{3,19},{4,20},{5,21},{6,22},{7,23},{8,24},{9,... | collective-permute-start | bytes 294920 | tf_op jit(solution)/shard_map/ppermute | solution.py:426
  3.6 8.1 %collective-permute-start.1 = (f32[24,2,4,128]{3,2,1,0:T(4,128)S(1)}, f32[24,2,4,128]{3,2,1,0:T(4,128)S(1)}, u32[]{:S(2)}, u32[]{:S(2)}) collective-permute-start(f32[24,2,4,128]{3,2,1,0:T(4,128)S(1)} %get-tuple-element.109), channel_id=1, source_target_pairs={{0,16},{1,2},{2,1},{3,4},{4,3},{5,6},{6,5},{7,8},{8,7},{9,10},{10,... | collective-permute-start | bytes 294920 | tf_op jit(solution)/shard_map/ppermute | solution.py:426
  4.0 7.7 %collective-permute-start.2 = (f32[4,2,24,128]{3,2,1,0:T(8,128)S(1)}, f32[4,2,24,128]{3,2,1,0:T(8,128)S(1)}, u32[]{:S(2)}, u32[]{:S(2)}) collective-permute-start(f32[4,2,24,128]{3,2,1,0:T(8,128)S(1)} %get-tuple-element.110), channel_id=1, source_target_pairs={{0,1},{1,0},{2,3},{3,2},{4,5},{5,4},{6,7},{7,6},{8,9},{9,8},{10,11... | collective-permute-start | bytes 294920 | tf_op jit(solution)/shard_map/ppermute | solution.py:426
  6.4 5.3 %collective-permute-start.3 = (f32[24,2,4,128]{3,2,1,0:T(4,128)S(1)}, f32[24,2,4,128]{3,2,1,0:T(4,128)S(1)}, u32[]{:S(2)}, u32[]{:S(2)}) collective-permute-start(f32[24,2,4,128]{3,2,1,0:T(4,128)S(1)} %get-tuple-element.111), channel_id=1, source_target_pairs={{0,1},{1,0},{2,3},{3,2},{4,5},{5,4},{6,7},{7,6},{8,9},{9,8},{10,11... | collective-permute-start | bytes 294920 | tf_op jit(solution)/shard_map/ppermute | solution.py:426
  12.1 7.1 %collective-permute-start.4 = (f32[4,2,24,128]{3,2,1,0:T(8,128)S(1)}, f32[4,2,24,128]{3,2,1,0:T(8,128)S(1)}, u32[]{:S(2)}, u32[]{:S(2)}) collective-permute-start(f32[4,2,24,128]{3,2,1,0:T(8,128)S(1)} %get-tuple-element.121), channel_id=1, source_target_pairs={{0,16},{1,17},{2,18},{3,19},{4,20},{5,21},{6,22},{7,23},{8,24},{9,... | collective-permute-start | bytes 294920 | tf_op jit(solution)/shard_map/ppermute | solution.py:426
  14.3 4.9 %collective-permute-start.5 = (f32[24,2,4,128]{3,2,1,0:T(4,128)S(1)}, f32[24,2,4,128]{3,2,1,0:T(4,128)S(1)}, u32[]{:S(2)}, u32[]{:S(2)}) collective-permute-start(f32[24,2,4,128]{3,2,1,0:T(4,128)S(1)} %get-tuple-element.122), channel_id=1, source_target_pairs={{0,16},{1,2},{2,1},{3,4},{4,3},{5,6},{6,5},{7,8},{8,7},{9,10},{10,... | collective-permute-start | bytes 294920 | tf_op jit(solution)/shard_map/ppermute | solution.py:426
  14.3 4.8 %collective-permute-start.6 = (f32[4,2,24,128]{3,2,1,0:T(8,128)S(1)}, f32[4,2,24,128]{3,2,1,0:T(8,128)S(1)}, u32[]{:S(2)}, u32[]{:S(2)}) collective-permute-start(f32[4,2,24,128]{3,2,1,0:T(8,128)S(1)} %get-tuple-element.123), channel_id=1, source_target_pairs={{0,1},{1,0},{2,3},{3,2},{4,5},{5,4},{6,7},{7,6},{8,9},{9,8},{10,11... | collective-permute-start | bytes 294920 | tf_op jit(solution)/shard_map/ppermute | solution.py:426
  16.1 3.0 %collective-permute-start.7 = (f32[24,2,4,128]{3,2,1,0:T(4,128)S(1)}, f32[24,2,4,128]{3,2,1,0:T(4,128)S(1)}, u32[]{:S(2)}, u32[]{:S(2)}) collective-permute-start(f32[24,2,4,128]{3,2,1,0:T(4,128)S(1)} %get-tuple-element.124), channel_id=1, source_target_pairs={{0,1},{1,0},{2,3},{3,2},{4,5},{5,4},{6,7},{7,6},{8,9},{9,8},{10,11... | collective-permute-start | bytes 294920 | tf_op jit(solution)/shard_map/ppermute | solution.py:426
  19.4 10.0 %collective-permute-start.8 = (f32[4,2,24,128]{3,2,1,0:T(8,128)S(1)}, f32[4,2,24,128]{3,2,1,0:T(8,128)S(1)}, u32[]{:S(2)}, u32[]{:S(2)}) collective-permute-start(f32[4,2,24,128]{3,2,1,0:T(8,128)S(1)} %get-tuple-element.132), channel_id=1, source_target_pairs={{0,16},{1,17},{2,18},{3,19},{4,20},{5,21},{6,22},{7,23},{8,24},{9,... | collective-permute-start | bytes 294920 | tf_op jit(solution)/shard_map/ppermute | solution.py:426
  24.4 5.2 %collective-permute-start.9 = (f32[24,2,4,128]{3,2,1,0:T(4,128)S(1)}, f32[24,2,4,128]{3,2,1,0:T(4,128)S(1)}, u32[]{:S(2)}, u32[]{:S(2)}) collective-permute-start(f32[24,2,4,128]{3,2,1,0:T(4,128)S(1)} %get-tuple-element.133), channel_id=1, source_target_pairs={{0,16},{1,2},{2,1},{3,4},{4,3},{5,6},{6,5},{7,8},{8,7},{9,10},{10,... | collective-permute-start | bytes 294920 | tf_op jit(solution)/shard_map/ppermute | solution.py:426
  24.5 5.1 %collective-permute-start.10 = (f32[4,2,24,128]{3,2,1,0:T(8,128)S(1)}, f32[4,2,24,128]{3,2,1,0:T(8,128)S(1)}, u32[]{:S(2)}, u32[]{:S(2)}) collective-permute-start(f32[4,2,24,128]{3,2,1,0:T(8,128)S(1)} %get-tuple-element.134), channel_id=1, source_target_pairs={{0,1},{1,0},{2,3},{3,2},{4,5},{5,4},{6,7},{7,6},{8,9},{9,8},{10,11... | collective-permute-start | bytes 294920 | tf_op jit(solution)/shard_map/ppermute | solution.py:426
  26.4 3.1 %collective-permute-start.11 = (f32[24,2,4,128]{3,2,1,0:T(4,128)S(1)}, f32[24,2,4,128]{3,2,1,0:T(4,128)S(1)}, u32[]{:S(2)}, u32[]{:S(2)}) collective-permute-start(f32[24,2,4,128]{3,2,1,0:T(4,128)S(1)} %get-tuple-element.135), channel_id=1, source_target_pairs={{0,1},{1,0},{2,3},{3,2},{4,5},{5,4},{6,7},{7,6},{8,9},{9,8},{10,11... | collective-permute-start | bytes 294920 | tf_op jit(solution)/shard_map/ppermute | solution.py:426
  29.9 8.8 %collective-permute-start.12 = (f32[4,2,24,128]{3,2,1,0:T(8,128)S(1)}, f32[4,2,24,128]{3,2,1,0:T(8,128)S(1)}, u32[]{:S(2)}, u32[]{:S(2)}) collective-permute-start(f32[4,2,24,128]{3,2,1,0:T(8,128)S(1)} %get-tuple-element.143), channel_id=1, source_target_pairs={{0,16},{1,17},{2,18},{3,19},{4,20},{5,21},{6,22},{7,23},{8,24},{9,... | collective-permute-start | bytes 294920 | tf_op jit(solution)/shard_map/ppermute | solution.py:426
  34.4 5.7 %collective-permute-start.13 = (f32[24,2,4,128]{3,2,1,0:T(4,128)S(1)}, f32[24,2,4,128]{3,2,1,0:T(4,128)S(1)}, u32[]{:S(2)}, u32[]{:S(2)}) collective-permute-start(f32[24,2,4,128]{3,2,1,0:T(4,128)S(1)} %get-tuple-element.144), channel_id=1, source_target_pairs={{0,16},{1,2},{2,1},{3,4},{4,3},{5,6},{6,5},{7,8},{8,7},{9,10},{10,... | collective-permute-start | bytes 294920 | tf_op jit(solution)/shard_map/ppermute | solution.py:426
  34.5 5.6 %collective-permute-start.14 = (f32[4,2,24,128]{3,2,1,0:T(8,128)S(1)}, f32[4,2,24,128]{3,2,1,0:T(8,128)S(1)}, u32[]{:S(2)}, u32[]{:S(2)}) collective-permute-start(f32[4,2,24,128]{3,2,1,0:T(8,128)S(1)} %get-tuple-element.145), channel_id=1, source_target_pairs={{0,1},{1,0},{2,3},{3,2},{4,5},{5,4},{6,7},{7,6},{8,9},{9,8},{10,11... | collective-permute-start | bytes 294920 | tf_op jit(solution)/shard_map/ppermute | solution.py:426
  35.6 4.5 %collective-permute-start.15 = (f32[24,2,4,128]{3,2,1,0:T(4,128)S(1)}, f32[24,2,4,128]{3,2,1,0:T(4,128)S(1)}, u32[]{:S(2)}, u32[]{:S(2)}) collective-permute-start(f32[24,2,4,128]{3,2,1,0:T(4,128)S(1)} %get-tuple-element.146), channel_id=1, source_target_pairs={{0,1},{1,0},{2,3},{3,2},{4,5},{5,4},{6,7},{7,6},{8,9},{9,8},{10,11... | collective-permute-start | bytes 294920 | tf_op jit(solution)/shard_map/ppermute | solution.py:426
  40.4 8.0 %collective-permute-start.16 = (f32[4,2,24,128]{3,2,1,0:T(8,128)S(1)}, f32[4,2,24,128]{3,2,1,0:T(8,128)S(1)}, u32[]{:S(2)}, u32[]{:S(2)}) collective-permute-start(f32[4,2,24,128]{3,2,1,0:T(8,128)S(1)} %get-tuple-element.154), channel_id=1, source_target_pairs={{0,16},{1,17},{2,18},{3,19},{4,20},{5,21},{6,22},{7,23},{8,24},{9,... | collective-permute-start | bytes 294920 | tf_op jit(solution)/shard_map/ppermute | solution.py:426
  43.1 5.5 %collective-permute-start.17 = (f32[24,2,4,128]{3,2,1,0:T(4,128)S(1)}, f32[24,2,4,128]{3,2,1,0:T(4,128)S(1)}, u32[]{:S(2)}, u32[]{:S(2)}) collective-permute-start(f32[24,2,4,128]{3,2,1,0:T(4,128)S(1)} %get-tuple-element.155), channel_id=1, source_target_pairs={{0,16},{1,2},{2,1},{3,4},{4,3},{5,6},{6,5},{7,8},{8,7},{9,10},{10,... | collective-permute-start | bytes 294920 | tf_op jit(solution)/shard_map/ppermute | solution.py:426
  43.2 5.4 %collective-permute-start.18 = (f32[4,2,24,128]{3,2,1,0:T(8,128)S(1)}, f32[4,2,24,128]{3,2,1,0:T(8,128)S(1)}, u32[]{:S(2)}, u32[]{:S(2)}) collective-permute-start(f32[4,2,24,128]{3,2,1,0:T(8,128)S(1)} %get-tuple-element.156), channel_id=1, source_target_pairs={{0,1},{1,0},{2,3},{3,2},{4,5},{5,4},{6,7},{7,6},{8,9},{9,8},{10,11... | collective-permute-start | bytes 294920 | tf_op jit(solution)/shard_map/ppermute | solution.py:426
  45.4 3.2 %collective-permute-start.19 = (f32[24,2,4,128]{3,2,1,0:T(4,128)S(1)}, f32[24,2,4,128]{3,2,1,0:T(4,128)S(1)}, u32[]{:S(2)}, u32[]{:S(2)}) collective-permute-start(f32[24,2,4,128]{3,2,1,0:T(4,128)S(1)} %get-tuple-element.157), channel_id=1, source_target_pairs={{0,1},{1,0},{2,3},{3,2},{4,5},{5,4},{6,7},{7,6},{8,9},{9,8},{10,11... | collective-permute-start | bytes 294920 | tf_op jit(solution)/shard_map/ppermute | solution.py:426
  49.0 8.3 %collective-permute-start.20 = (f32[4,2,24,128]{3,2,1,0:T(8,128)S(1)}, f32[4,2,24,128]{3,2,1,0:T(8,128)S(1)}, u32[]{:S(2)}, u32[]{:S(2)}) collective-permute-start(f32[4,2,24,128]{3,2,1,0:T(8,128)S(1)} %get-tuple-element.165), channel_id=1, source_target_pairs={{0,16},{1,17},{2,18},{3,19},{4,20},{5,21},{6,22},{7,23},{8,24},{9,... | collective-permute-start | bytes 294920 | tf_op jit(solution)/shard_map/ppermute | solution.py:426
  52.6 4.9 %collective-permute-start.21 = (f32[24,2,4,128]{3,2,1,0:T(4,128)S(1)}, f32[24,2,4,128]{3,2,1,0:T(4,128)S(1)}, u32[]{:S(2)}, u32[]{:S(2)}) collective-permute-start(f32[24,2,4,128]{3,2,1,0:T(4,128)S(1)} %get-tuple-element.166), channel_id=1, source_target_pairs={{0,16},{1,2},{2,1},{3,4},{4,3},{5,6},{6,5},{7,8},{8,7},{9,10},{10,... | collective-permute-start | bytes 294920 | tf_op jit(solution)/shard_map/ppermute | solution.py:426
  52.7 4.8 %collective-permute-start.22 = (f32[4,2,24,128]{3,2,1,0:T(8,128)S(1)}, f32[4,2,24,128]{3,2,1,0:T(8,128)S(1)}, u32[]{:S(2)}, u32[]{:S(2)}) collective-permute-start(f32[4,2,24,128]{3,2,1,0:T(8,128)S(1)} %get-tuple-element.167), channel_id=1, source_target_pairs={{0,1},{1,0},{2,3},{3,2},{4,5},{5,4},{6,7},{7,6},{8,9},{9,8},{10,11... | collective-permute-start | bytes 294920 | tf_op jit(solution)/shard_map/ppermute | solution.py:426
  54.2 3.4 %collective-permute-start.23 = (f32[24,2,4,128]{3,2,1,0:T(4,128)S(1)}, f32[24,2,4,128]{3,2,1,0:T(4,128)S(1)}, u32[]{:S(2)}, u32[]{:S(2)}) collective-permute-start(f32[24,2,4,128]{3,2,1,0:T(4,128)S(1)} %get-tuple-element.168), channel_id=1, source_target_pairs={{0,1},{1,0},{2,3},{3,2},{4,5},{5,4},{6,7},{7,6},{8,9},{9,8},{10,11... | collective-permute-start | bytes 294920 | tf_op jit(solution)/shard_map/ppermute | solution.py:426
  57.9 9.2 %collective-permute-start.24 = (f32[4,2,24,128]{3,2,1,0:T(8,128)S(1)}, f32[4,2,24,128]{3,2,1,0:T(8,128)S(1)}, u32[]{:S(2)}, u32[]{:S(2)}) collective-permute-start(f32[4,2,24,128]{3,2,1,0:T(8,128)S(1)} %get-tuple-element.176), channel_id=1, source_target_pairs={{0,16},{1,17},{2,18},{3,19},{4,20},{5,21},{6,22},{7,23},{8,24},{9,... | collective-permute-start | bytes 294920 | tf_op jit(solution)/shard_map/ppermute | solution.py:426
  62.0 5.6 %collective-permute-start.25 = (f32[24,2,4,128]{3,2,1,0:T(4,128)S(1)}, f32[24,2,4,128]{3,2,1,0:T(4,128)S(1)}, u32[]{:S(2)}, u32[]{:S(2)}) collective-permute-start(f32[24,2,4,128]{3,2,1,0:T(4,128)S(1)} %get-tuple-element.177), channel_id=1, source_target_pairs={{0,16},{1,2},{2,1},{3,4},{4,3},{5,6},{6,5},{7,8},{8,7},{9,10},{10,... | collective-permute-start | bytes 294920 | tf_op jit(solution)/shard_map/ppermute | solution.py:426
  62.1 5.5 %collective-permute-start.26 = (f32[4,2,24,128]{3,2,1,0:T(8,128)S(1)}, f32[4,2,24,128]{3,2,1,0:T(8,128)S(1)}, u32[]{:S(2)}, u32[]{:S(2)}) collective-permute-start(f32[4,2,24,128]{3,2,1,0:T(8,128)S(1)} %get-tuple-element.178), channel_id=1, source_target_pairs={{0,1},{1,0},{2,3},{3,2},{4,5},{5,4},{6,7},{7,6},{8,9},{9,8},{10,11... | collective-permute-start | bytes 294920 | tf_op jit(solution)/shard_map/ppermute | solution.py:426
  64.0 3.6 %collective-permute-start.27 = (f32[24,2,4,128]{3,2,1,0:T(4,128)S(1)}, f32[24,2,4,128]{3,2,1,0:T(4,128)S(1)}, u32[]{:S(2)}, u32[]{:S(2)}) collective-permute-start(f32[24,2,4,128]{3,2,1,0:T(4,128)S(1)} %get-tuple-element.179), channel_id=1, source_target_pairs={{0,1},{1,0},{2,3},{3,2},{4,5},{5,4},{6,7},{7,6},{8,9},{9,8},{10,11... | collective-permute-start | bytes 294920 | tf_op jit(solution)/shard_map/ppermute | solution.py:426
  68.0 8.7 %collective-permute-start.28 = (f32[4,2,24,128]{3,2,1,0:T(8,128)S(1)}, f32[4,2,24,128]{3,2,1,0:T(8,128)S(1)}, u32[]{:S(2)}, u32[]{:S(2)}) collective-permute-start(f32[4,2,24,128]{3,2,1,0:T(8,128)S(1)} %get-tuple-element.187), channel_id=1, source_target_pairs={{0,16},{1,17},{2,18},{3,19},{4,20},{5,21},{6,22},{7,23},{8,24},{9,... | collective-permute-start | bytes 294920 | tf_op jit(solution)/shard_map/ppermute | solution.py:426
  71.7 5.8 %collective-permute-start.29 = (f32[24,2,4,128]{3,2,1,0:T(4,128)S(1)}, f32[24,2,4,128]{3,2,1,0:T(4,128)S(1)}, u32[]{:S(2)}, u32[]{:S(2)}) collective-permute-start(f32[24,2,4,128]{3,2,1,0:T(4,128)S(1)} %get-tuple-element.188), channel_id=1, source_target_pairs={{0,16},{1,2},{2,1},{3,4},{4,3},{5,6},{6,5},{7,8},{8,7},{9,10},{10,... | collective-permute-start | bytes 294920 | tf_op jit(solution)/shard_map/ppermute | solution.py:426
  71.8 5.7 %collective-permute-start.30 = (f32[4,2,24,128]{3,2,1,0:T(8,128)S(1)}, f32[4,2,24,128]{3,2,1,0:T(8,128)S(1)}, u32[]{:S(2)}, u32[]{:S(2)}) collective-permute-start(f32[4,2,24,128]{3,2,1,0:T(8,128)S(1)} %get-tuple-element.189), channel_id=1, source_target_pairs={{0,1},{1,0},{2,3},{3,2},{4,5},{5,4},{6,7},{7,6},{8,9},{9,8},{10,11... | collective-permute-start | bytes 294920 | tf_op jit(solution)/shard_map/ppermute | solution.py:426
  73.7 3.8 %collective-permute-start.31 = (f32[24,2,4,128]{3,2,1,0:T(4,128)S(1)}, f32[24,2,4,128]{3,2,1,0:T(4,128)S(1)}, u32[]{:S(2)}, u32[]{:S(2)}) collective-permute-start(f32[24,2,4,128]{3,2,1,0:T(4,128)S(1)} %get-tuple-element.190), channel_id=1, source_target_pairs={{0,1},{1,0},{2,3},{3,2},{4,5},{5,4},{6,7},{7,6},{8,9},{9,8},{10,11... | collective-permute-start | bytes 294920 | tf_op jit(solution)/shard_map/ppermute | solution.py:426
  78.5 1.2 %collective-permute-start.32 = (f32[16,128]{1,0:T(8,128)S(1)}, f32[16,128]{1,0:T(8,128)S(1)}, u32[]{:S(2)}, u32[]{:S(2)}) collective-permute-start(f32[16,128]{1,0:T(8,128)S(1)} %get-tuple-element.200), channel_id=1, source_target_pairs={{0,1},{1,0},{2,3},{3,2},{4,5},{5,4},{6,7},{7,6},{8,9},{9,8},{10,11... | collective-permute-start | bytes 24584 | tf_op jit(solution)/shard_map/ppermute | solution.py:440
  79.7 5.2 %collective-permute-start.35 = (f32[16,128]{1,0:T(8,128)S(1)}, f32[16,128]{1,0:T(8,128)S(1)}, u32[]{:S(2)}, u32[]{:S(2)}) collective-permute-start(f32[16,128]{1,0:T(8,128)S(1)} %add.21), channel_id=1, source_target_pairs={{0,18},{1,19},{2,16},{3,17},{4,22},{5,23},{6,20},{7,21},{8,26},{9,... | collective-permute-start | bytes 24584 | tf_op jit(solution)/shard_map/ppermute | solution.py:440
  83.3 5.2 %collective-permute-start.34 = (f32[16,128]{1,0:T(8,128)S(1)}, f32[16,128]{1,0:T(8,128)S(1)}, u32[]{:S(2)}, u32[]{:S(2)}) collective-permute-start(f32[16,128]{1,0:T(8,128)S(1)} %add.21), channel_id=1, source_target_pairs={{0,2},{1,3},{2,0},{3,1},{4,6},{5,7},{6,4},{7,5},{8,10},{9,11},{10,... | collective-permute-start | bytes 24584 | tf_op jit(solution)/shard_map/ppermute | solution.py:440
  84.7 3.7 %collective-permute-start.33 = (f32[16,128]{1,0:T(8,128)S(1)}, f32[16,128]{1,0:T(8,128)S(1)}, u32[]{:S(2)}, u32[]{:S(2)}) collective-permute-start(f32[16,128]{1,0:T(8,128)S(1)} %add.21), channel_id=1, source_target_pairs={{0,16},{1,17},{2,18},{3,19},{4,20},{5,21},{6,22},{7,23},{8,24},{9,... | collective-permute-start | bytes 24584 | tf_op jit(solution)/shard_map/ppermute | solution.py:440
  88.4 5.0 %collective-permute-start.38 = (f32[16,128]{1,0:T(8,128)S(1)}, f32[16,128]{1,0:T(8,128)S(1)}, u32[]{:S(2)}, u32[]{:S(2)}) collective-permute-start(f32[16,128]{1,0:T(8,128)S(1)} %add_add_fusion.1), channel_id=1, source_target_pairs={{0,12},{1,13},{2,14},{3,15},{4,8},{5,9},{6,10},{7,11},{8,4},{9,5},... | collective-permute-start | bytes 24584 | tf_op jit(solution)/shard_map/ppermute | solution.py:440
  90.6 5.2 %collective-permute-start.37 = (f32[16,128]{1,0:T(8,128)S(1)}, f32[16,128]{1,0:T(8,128)S(1)}, u32[]{:S(2)}, u32[]{:S(2)}) collective-permute-start(f32[16,128]{1,0:T(8,128)S(1)} %add_add_fusion.1), channel_id=1, source_target_pairs={{0,8},{1,9},{2,10},{3,11},{4,12},{5,13},{6,14},{7,15},{8,0},{9,1},... | collective-permute-start | bytes 24584 | tf_op jit(solution)/shard_map/ppermute | solution.py:440
  92.8 3.7 %collective-permute-start.36 = (f32[16,128]{1,0:T(8,128)S(1)}, f32[16,128]{1,0:T(8,128)S(1)}, u32[]{:S(2)}, u32[]{:S(2)}) collective-permute-start(f32[16,128]{1,0:T(8,128)S(1)} %add_add_fusion.1), channel_id=1, source_target_pairs={{0,4},{1,5},{2,6},{3,7},{4,0},{5,1},{6,2},{7,3},{8,12},{9,13},{10,... | collective-permute-start | bytes 24584 | tf_op jit(solution)/shard_map/ppermute | solution.py:440
  96.5 5.6 %collective-permute-start.39 = (f32[16,128]{1,0:T(8,128)S(1)}, f32[16,128]{1,0:T(8,128)S(1)}, u32[]{:S(2)}, u32[]{:S(2)}) collective-permute-start(f32[16,128]{1,0:T(8,128)S(1)} %add_add_fusion.refs_0_), channel_id=1, source_target_pairs={{0,32},{1,33},{2,34},{3,35},{4,36},{5,37},{6,38},{7,39},{8,40},{9,... | collective-permute-start | bytes 24584 | tf_op jit(solution)/shard_map/ppermute | solution.py:440
  97.7 5.2 %collective-permute-start.40 = (f32[16,128]{1,0:T(8,128)S(1)}, f32[16,128]{1,0:T(8,128)S(1)}, u32[]{:S(2)}, u32[]{:S(2)}) collective-permute-start(f32[16,128]{1,0:T(8,128)S(1)} %add_add_fusion.refs_0_), channel_id=1, source_target_pairs={{0,64},{1,65},{2,66},{3,67},{4,68},{5,69},{6,70},{7,71},{8,72},{9,... | collective-permute-start | bytes 24584 | tf_op jit(solution)/shard_map/ppermute | solution.py:440
  99.2 4.9 %collective-permute-start.41 = (f32[16,128]{1,0:T(8,128)S(1)}, f32[16,128]{1,0:T(8,128)S(1)}, u32[]{:S(2)}, u32[]{:S(2)}) collective-permute-start(f32[16,128]{1,0:T(8,128)S(1)} %add_add_fusion.refs_0_), channel_id=1, source_target_pairs={{0,96},{1,97},{2,98},{3,99},{4,100},{5,101},{6,102},{7,103},{8,104... | collective-permute-start | bytes 24584 | tf_op jit(solution)/shard_map/ppermute | solution.py:440
